TPU v7x, 32 devices: a whole 2x2x4 slice. The times are simulated.
32 devices in a mesh: dp: 4 (over y, core), expert: 8 (over z, x).
Axes of the slice: x: 2, y: 2, z: 4, core: 2. Of those that a mesh axis runs over, the one named last changes fastest.
Arguments:
- tokens: bfloat16 [8192, 2048], P(('dp', 'expert')), may hold values from -6 to 6
- grad_out: bfloat16 [8192, 2048], P(('dp', 'expert')), may hold values from -6 to 6
- routes: int32 [8192, 3], P(('dp', 'expert')), may hold values from 0 to 7, all different within a row; in each aligned block of 256 rows (0 to 255, 256 to 511, ...) at most 108 rows name the same one
- gate_values: float32 [8192, 3], P(('dp', 'expert')), may hold values from 0.1 to 0.5
- parents: int32 [4, 8], P('dp'), may hold values from 0 to 6, as said below
- attn_gain: bfloat16 [2048], P(('dp', 'expert')), may hold values from 0.5 to 1.5
- w_query: bfloat16 [2048, 3072], P(('dp', 'expert')), may hold values from -0.125 to 0.125
- w_latent: bfloat16 [2048, 576], P(('dp', 'expert')), may hold values from -0.125 to 0.125
- latent_gain: bfloat16 [512], P(('dp', 'expert')), may hold values from 0.5 to 1.5
- w_expand: bfloat16 [512, 4096], P(('dp', 'expert')), may hold values from -0.25 to 0.25
- w_output: bfloat16 [2048, 2048], P(('dp', 'expert')), may hold values from -0.75 to 0.75
- ffn_gain: bfloat16 [2048], P(('dp', 'expert')), may hold values from 0.5 to 1.5
- shared_gate: bfloat16 [2048, 2816], P(('dp', 'expert')), may hold values from -0.125 to 0.125
- shared_up: bfloat16 [2048, 2816], P(('dp', 'expert')), may hold values from -0.125 to 0.125
- shared_down: bfloat16 [2816, 2048], P(('dp', 'expert')), may hold values from -0.21875 to 0.21875
- expert_gate: bfloat16 [8, 2048, 1408], P('expert'), may hold values from -0.125 to 0.125
- expert_up: bfloat16 [8, 2048, 1408], P('expert'), may hold values from -0.125 to 0.125
- expert_down: bfloat16 [8, 1408, 2048], P('expert'), may hold values from -0.3125 to 0.3125
Outputs:
- block_out: bfloat16 [8192, 2048], P(('dp', 'expert'))
- grad_tokens: float32 [8192, 2048], P(('dp', 'expert'))
- grad_attn_gain: float32 [2048], P(('dp', 'expert'))
- grad_w_query: float32 [2048, 3072], P(('dp', 'expert'))
- grad_w_latent: float32 [2048, 576], P(('dp', 'expert'))
- grad_latent_gain: float32 [512], P(('dp', 'expert'))
- grad_w_expand: float32 [512, 4096], P(('dp', 'expert'))
- grad_w_output: float32 [2048, 2048], P(('dp', 'expert'))
- grad_ffn_gain: float32 [2048], P(('dp', 'expert'))
- grad_shared_gate: float32 [2048, 2816], P(('dp', 'expert'))
- grad_shared_up: float32 [2048, 2816], P(('dp', 'expert'))
- grad_shared_down: float32 [2816, 2048], P(('dp', 'expert'))
- grad_expert_gate: float32 [8, 2048, 1408], P('expert', 'dp')
- grad_expert_up: float32 [8, 2048, 1408], P('expert', 'dp')
- grad_expert_down: float32 [8, 1408, 2048], P('expert', None, 'dp')
Inputs may be any that keep to these rules, and one draw needn't show every extreme that they name: `routes`: each token's 3 entries are different experts; among the tokens of one device no expert is named more than 108 times, a bound that some block reaches. parents[t, 0] = 0 (segment 0 is the root), 0 <= parents[t, s] < s for s >= 1, and the last segment's parent is the segment before it.
All inputs are finite; a program needn't handle non-finite values.
Results may differ from a plain program's by a relative error of at most 0.02.
Values may be sent and summed in bfloat16 or wider, within the bound.
A program may use at most 384 MiB of HBM per device.

v0:
```python
import jax
import jax.numpy as jnp
from jax import lax
from jax.sharding import PartitionSpec as P

HEADS = 16
NOPE = 128
ROPE = 64
KV = 512
VD = 128
SEG = 256


epsilon = 1e-06
highest = lax.Precision.HIGHEST


def norm_rows(values, gain_vec):
    return (
        values * lax.rsqrt(jnp.mean(values * values, axis=-1, keepdims=True) + epsilon) * gain_vec
    )


def rotate(values, cos_table, sin_table):
    half_width = values.shape[-1] // 2
    first_half = values[..., :half_width]
    second_half = values[..., half_width:]
    return jnp.concatenate(
        [
            first_half * cos_table - second_half * sin_table,
            second_half * cos_table + first_half * sin_table,
        ],
        axis=-1,
    )


def gating(gate_part, up_part):
    return jax.nn.silu(gate_part) * up_part


def ancestry(parent_row, seg_count):
    identity = jnp.eye(seg_count, dtype=jnp.float32)
    parent_hot = (parent_row[:, None] == jnp.arange(seg_count, dtype=jnp.int32)[None, :]).astype(
        jnp.float32
    )

    def grow(turn_index, reachable):
        return jnp.maximum(identity, jnp.dot(parent_hot, reachable))

    return lax.fori_loop(0, seg_count, grow, identity)


def matmul(left, right):
    return jnp.dot(left, right, preferred_element_type=jnp.float32)


def dot_last(left, right):
    return lax.dot_general(
        left, right, (((1,), (1,)), ((), ())), preferred_element_type=jnp.float32
    )


def dot_first(left, right):
    return lax.dot_general(
        left, right, (((0,), (0,)), ((), ())), preferred_element_type=jnp.float32
    )


def exact_last(left, right):
    return lax.dot_general(
        left, right, (((1,), (1,)), ((), ())), precision=highest, preferred_element_type=jnp.float32
    )


def exact_first(left, right):
    return lax.dot_general(
        left, right, (((0,), (0,)), ((), ())), precision=highest, preferred_element_type=jnp.float32
    )


def per_device(
    tokens,
    grad_out,
    routes,
    gate_values,
    parents,
    attn_gain,
    w_query,
    w_latent,
    latent_gain,
    w_expand,
    w_output,
    ffn_gain,
    shared_gate,
    shared_up,
    shared_down,
    expert_gate,
    expert_up,
    expert_down,
):
    (
        attn_gain,
        w_query,
        w_latent,
        latent_gain,
        w_expand,
        w_output,
        ffn_gain,
        shared_gate,
        shared_up,
        shared_down,
    ) = (
        lax.all_gather(attn_gain, ("dp", "expert"), axis=0, tiled=True),
        lax.all_gather(w_query, ("dp", "expert"), axis=0, tiled=True),
        lax.all_gather(w_latent, ("dp", "expert"), axis=0, tiled=True),
        lax.all_gather(latent_gain, ("dp", "expert"), axis=0, tiled=True),
        lax.all_gather(w_expand, ("dp", "expert"), axis=0, tiled=True),
        lax.all_gather(w_output, ("dp", "expert"), axis=0, tiled=True),
        lax.all_gather(ffn_gain, ("dp", "expert"), axis=0, tiled=True),
        lax.all_gather(shared_gate, ("dp", "expert"), axis=0, tiled=True),
        lax.all_gather(shared_up, ("dp", "expert"), axis=0, tiled=True),
        lax.all_gather(shared_down, ("dp", "expert"), axis=0, tiled=True),
    )
    tok_dev = tokens.shape[0]
    model_width = tokens.shape[1]
    group_size = lax.axis_size("expert")
    group_rank = lax.axis_index("expert")
    tree_len = tok_dev * group_size
    seg_count = parents.shape[1]
    per_token = routes.shape[1]
    capacity = tok_dev * per_token * 9 // (8 * group_size)
    score_scale = (NOPE + ROPE) ** (-0.5)
    reachable = ancestry(parents[0], seg_count)
    seg_depth = jnp.sum(reachable, axis=1) - 1.0
    own_index = group_rank * tok_dev + jnp.arange(tok_dev, dtype=jnp.int32)
    seg_query = own_index // SEG
    off_query = own_index % SEG
    query_hot = (seg_query[:, None] == jnp.arange(seg_count, dtype=jnp.int32)[None, :]).astype(
        jnp.float32
    )
    reach_query = jnp.dot(query_hot, reachable)
    positions = jnp.dot(query_hot, seg_depth[:, None])[:, 0] * SEG + off_query.astype(jnp.float32)
    half_width = ROPE // 2
    freq = 10000.0 ** (-2.0 * jnp.arange(half_width, dtype=jnp.float32) / ROPE)
    angle = positions[:, None] * freq[None, :]
    cos_table = jnp.cos(angle)
    sin_table = jnp.sin(angle)

    def allowed_block(block_start, key_count):
        key_index = block_start + jnp.arange(key_count, dtype=jnp.int32)
        seg_key = key_index // SEG
        off_key = key_index % SEG
        key_hot = (seg_key[None, :] == jnp.arange(seg_count, dtype=jnp.int32)[:, None]).astype(
            jnp.float32
        )
        reach_key = jnp.dot(reach_query, key_hot) > 0.5
        same_seg = seg_query[:, None] == seg_key[None, :]
        return reach_key & ~same_seg | same_seg & (off_key[None, :] <= off_query[:, None])

    tokens_f = tokens.astype(jnp.float32)
    first_normed, first_norm_back = jax.vjp(norm_rows, tokens_f, attn_gain.astype(jnp.float32))
    first_bf = first_normed.astype(jnp.bfloat16)
    query_lin = matmul(first_bf, w_query).reshape(tok_dev, HEADS, NOPE + ROPE)

    def query_rope(query_in):
        return jnp.concatenate(
            [
                query_in[..., :NOPE],
                rotate(query_in[..., NOPE:], cos_table[:, None, :], sin_table[:, None, :]),
            ],
            axis=-1,
        )

    query_rot, query_back = jax.vjp(query_rope, query_lin)
    query_bf = query_rot.astype(jnp.bfloat16)
    latent = matmul(first_bf, w_latent)

    def latent_parts(latent_in, gain_vec):
        return (
            norm_rows(latent_in[:, :KV], gain_vec),
            rotate(latent_in[:, KV:], cos_table, sin_table),
        )

    (latent_normed, rope_key), latent_back = jax.vjp(
        latent_parts, latent, latent_gain.astype(jnp.float32)
    )
    latent_bf = latent_normed.astype(jnp.bfloat16)
    rope_bf = rope_key.astype(jnp.bfloat16)
    latent_all, rope_all = (
        lax.all_gather(latent_bf, "expert", axis=0, tiled=True),
        lax.all_gather(rope_bf, "expert", axis=0, tiled=True),
    )
    keys_all = matmul(latent_all, w_expand).astype(jnp.bfloat16)
    key_block = min(512, tree_len)
    block_count = tree_len // key_block
    key_blocks = keys_all.reshape(block_count, key_block, HEADS, NOPE + VD)
    rope_blocks = rope_all.reshape(block_count, key_block, ROPE)
    block_starts = jnp.arange(block_count, dtype=jnp.int32) * key_block

    def block_scores(keys_now, rope_now, block_start):
        score = (
            jnp.einsum(
                "qhd,khd->hqk",
                query_bf[..., :NOPE],
                keys_now[..., :NOPE],
                preferred_element_type=jnp.float32,
            )
            + jnp.einsum(
                "qhr,kr->hqk", query_bf[..., NOPE:], rope_now, preferred_element_type=jnp.float32
            )
        ) * score_scale
        return (score, allowed_block(block_start, key_block))

    def stats_step(carry, pieces):
        top_now, total = carry
        score, allowed = block_scores(*pieces)
        masked = jnp.where(allowed[None], score, -1e30)
        new_top = jnp.maximum(top_now, jnp.max(masked, axis=-1))
        total = total * jnp.exp(top_now - new_top) + jnp.sum(
            jnp.where(allowed[None], jnp.exp(score - new_top[..., None]), 0.0), axis=-1
        )
        return ((new_top, total), None)

    start_top = jnp.full((HEADS, tok_dev), -1e30, jnp.float32)
    (row_top, row_total), unused = lax.scan(
        stats_step,
        (start_top, jnp.zeros((HEADS, tok_dev), jnp.float32)),
        (key_blocks, rope_blocks, block_starts),
    )
    log_total = row_top + jnp.log(row_total)

    def value_step(accumulated, pieces):
        score, allowed = block_scores(*pieces)
        probability = jnp.where(allowed[None], jnp.exp(score - log_total[..., None]), 0.0).astype(
            jnp.bfloat16
        )
        return (
            accumulated
            + jnp.einsum(
                "hqk,khd->qhd",
                probability,
                pieces[0][..., NOPE:],
                preferred_element_type=jnp.float32,
            ),
            None,
        )

    attended, unused = lax.scan(
        value_step,
        jnp.zeros((tok_dev, HEADS, VD), jnp.float32),
        (key_blocks, rope_blocks, block_starts),
    )
    attended_bf = attended.reshape(tok_dev, HEADS * VD).astype(jnp.bfloat16)
    resid = tokens_f + matmul(attended_bf, w_output)
    second_normed, second_norm_back = jax.vjp(norm_rows, resid, ffn_gain.astype(jnp.float32))
    second_bf = second_normed.astype(jnp.bfloat16)
    shared_act, shared_gating_back = jax.vjp(
        gating, matmul(second_bf, shared_gate), matmul(second_bf, shared_up)
    )
    shared_bf = shared_act.astype(jnp.bfloat16)
    shared_result = matmul(shared_bf, shared_down)
    flat_routes = routes.reshape(-1)
    route_hot = (flat_routes[:, None] == jnp.arange(group_size, dtype=jnp.int32)[None, :]).astype(
        jnp.int32
    )
    slot_number = jnp.sum((jnp.cumsum(route_hot, axis=0) - 1) * route_hot, axis=1)
    slot_index = flat_routes * capacity + slot_number
    token_of = jnp.arange(tok_dev * per_token, dtype=jnp.int32) // per_token
    send_rows = (
        jnp.zeros((group_size * capacity, model_width), jnp.bfloat16)
        .at[slot_index]
        .set(second_bf[token_of])
    )
    expert_rows = lax.all_to_all(
        send_rows.reshape(group_size, capacity, model_width),
        "expert",
        split_axis=0,
        concat_axis=0,
        tiled=True,
    ).reshape(group_size * capacity, model_width)
    activated, expert_gating_back = jax.vjp(
        gating, matmul(expert_rows, expert_gate[0]), matmul(expert_rows, expert_up[0])
    )
    activated_bf = activated.astype(jnp.bfloat16)
    expert_result = matmul(activated_bf, expert_down[0]).astype(jnp.bfloat16)
    returned = lax.all_to_all(
        expert_result.reshape(group_size, capacity, model_width),
        "expert",
        split_axis=0,
        concat_axis=0,
        tiled=True,
    ).reshape(group_size * capacity, model_width)
    picked = returned[slot_index].astype(jnp.float32).reshape(tok_dev, per_token, model_width)
    routed = jnp.sum(gate_values[..., None] * picked, axis=1)
    block_out = (resid + shared_result + routed).astype(jnp.bfloat16)
    grad_f = grad_out.astype(jnp.float32)
    gated_grad = (gate_values[..., None] * grad_f[:, None, :]).reshape(
        tok_dev * per_token, model_width
    )
    send_grads = (
        jnp.zeros((group_size * capacity, model_width), jnp.float32)
        .at[slot_index]
        .set(gated_grad)
        .astype(jnp.bfloat16)
    )
    expert_grad_rows = lax.all_to_all(
        send_grads.reshape(group_size, capacity, model_width),
        "expert",
        split_axis=0,
        concat_axis=0,
        tiled=True,
    ).reshape(group_size * capacity, model_width)
    grad_activated = dot_last(expert_grad_rows, expert_down[0]).astype(jnp.bfloat16)
    grad_e_down = dot_first(activated_bf, expert_grad_rows)
    grad_e_gate_part, grad_e_up_part = expert_gating_back(grad_activated.astype(jnp.float32))
    grad_e_gate_part = grad_e_gate_part.astype(jnp.bfloat16)
    grad_e_up_part = grad_e_up_part.astype(jnp.bfloat16)
    grad_e_gate = dot_first(expert_rows, grad_e_gate_part)
    grad_e_up = dot_first(expert_rows, grad_e_up_part)
    grad_rows = (
        dot_last(grad_e_gate_part, expert_gate[0]) + dot_last(grad_e_up_part, expert_up[0])
    ).astype(jnp.bfloat16)
    grad_returned = lax.all_to_all(
        grad_rows.reshape(group_size, capacity, model_width),
        "expert",
        split_axis=0,
        concat_axis=0,
        tiled=True,
    ).reshape(group_size * capacity, model_width)
    grad_second = jnp.sum(
        grad_returned[slot_index].astype(jnp.float32).reshape(tok_dev, per_token, model_width),
        axis=1,
    )
    grad_e_gate, grad_e_up, grad_e_down = (
        lax.psum_scatter(
            grad_e_gate.astype(jnp.bfloat16), "dp", scatter_dimension=0, tiled=True
        ).astype(jnp.float32),
        lax.psum_scatter(
            grad_e_up.astype(jnp.bfloat16), "dp", scatter_dimension=0, tiled=True
        ).astype(jnp.float32),
        lax.psum_scatter(
            grad_e_down.astype(jnp.bfloat16), "dp", scatter_dimension=1, tiled=True
        ).astype(jnp.float32),
    )
    grad_shared_act = dot_last(grad_out, shared_down).astype(jnp.bfloat16)
    grad_s_down = dot_first(shared_bf, grad_out)
    grad_s_gate_part, grad_s_up_part = shared_gating_back(grad_shared_act.astype(jnp.float32))
    grad_s_gate_part = grad_s_gate_part.astype(jnp.bfloat16)
    grad_s_up_part = grad_s_up_part.astype(jnp.bfloat16)
    grad_s_gate = dot_first(second_bf, grad_s_gate_part)
    grad_s_up = dot_first(second_bf, grad_s_up_part)
    grad_second = (
        grad_second + dot_last(grad_s_gate_part, shared_gate) + dot_last(grad_s_up_part, shared_up)
    )
    grad_resid_norm, grad_f_gain = second_norm_back(grad_second)
    grad_resid = grad_f + grad_resid_norm
    grad_attn_out = grad_resid.astype(jnp.bfloat16)
    grad_w_out = dot_first(attended_bf, grad_attn_out)
    grad_attended = dot_last(grad_attn_out, w_output).reshape(tok_dev, HEADS, VD)
    grad_attended_bf = grad_attended.astype(jnp.bfloat16)
    row_delta = jnp.sum(grad_attended_bf.astype(jnp.float32) * attended, axis=-1).T

    def grad_step(query_grad, pieces):
        keys_now, rope_now, block_start = pieces
        score, allowed = block_scores(keys_now, rope_now, block_start)
        probability = jnp.where(allowed[None], jnp.exp(score - log_total[..., None]), 0.0)
        grad_prob = jnp.einsum(
            "qhd,khd->hqk",
            grad_attended_bf,
            keys_now[..., NOPE:],
            preferred_element_type=jnp.float32,
        )
        grad_score = (probability * (grad_prob - row_delta[..., None])).astype(jnp.bfloat16)
        query_grad = query_grad + jnp.concatenate(
            [
                jnp.einsum(
                    "hqk,khd->qhd",
                    grad_score,
                    keys_now[..., :NOPE],
                    preferred_element_type=jnp.float32,
                ),
                jnp.einsum("hqk,kr->qhr", grad_score, rope_now, preferred_element_type=jnp.float32),
            ],
            axis=-1,
        )
        grad_key = (
            jnp.einsum(
                "hqk,qhd->khd", grad_score, query_bf[..., :NOPE], preferred_element_type=jnp.float32
            )
            * score_scale
        )
        grad_rope = (
            jnp.einsum(
                "hqk,qhr->kr", grad_score, query_bf[..., NOPE:], preferred_element_type=jnp.float32
            )
            * score_scale
        )
        grad_value = jnp.einsum(
            "hqk,qhd->khd",
            probability.astype(jnp.bfloat16),
            grad_attended_bf,
            preferred_element_type=jnp.float32,
        )
        grad_pair = jnp.concatenate([grad_key, grad_value], axis=-1).reshape(
            key_block, HEADS * (NOPE + VD)
        )
        return (query_grad, (grad_pair, grad_rope))

    query_grad, (grad_pairs, grad_ropes) = lax.scan(
        grad_step,
        jnp.zeros((tok_dev, HEADS, NOPE + ROPE), jnp.float32),
        (key_blocks, rope_blocks, block_starts),
    )
    pairs_flat = grad_pairs.reshape(tree_len, HEADS * (NOPE + VD))
    ropes_flat = grad_ropes.reshape(tree_len, ROPE)
    expand_f = w_expand.astype(jnp.float32)
    grad_w_exp = exact_first(latent_all.astype(jnp.float32), pairs_flat)
    grad_latent_partial = exact_last(pairs_flat, expand_f)
    grad_latent_normed, grad_rope_own = (
        lax.psum_scatter(
            grad_latent_partial.astype(jnp.bfloat16), "expert", scatter_dimension=0, tiled=True
        ).astype(jnp.float32),
        lax.psum_scatter(
            ropes_flat.astype(jnp.bfloat16), "expert", scatter_dimension=0, tiled=True
        ).astype(jnp.float32),
    )
    grad_latent, grad_l_gain = latent_back((grad_latent_normed, grad_rope_own))
    grad_latent_bf = grad_latent.astype(jnp.bfloat16)
    (grad_query_lin,) = query_back(query_grad * score_scale)
    grad_query_bf = grad_query_lin.reshape(tok_dev, HEADS * (NOPE + ROPE)).astype(jnp.bfloat16)
    grad_w_q = dot_first(first_bf, grad_query_bf)
    grad_w_lat = dot_first(first_bf, grad_latent_bf)
    grad_first = dot_last(grad_query_bf, w_query) + dot_last(grad_latent_bf, w_latent)
    grad_tokens_norm, grad_a_gain = first_norm_back(grad_first)
    grad_tokens = grad_resid + grad_tokens_norm
    (
        grad_a_gain,
        grad_w_q,
        grad_w_lat,
        grad_l_gain,
        grad_w_exp,
        grad_w_out,
        grad_f_gain,
        grad_s_gate,
        grad_s_up,
        grad_s_down,
    ) = (
        lax.psum_scatter(grad_a_gain, ("dp", "expert"), scatter_dimension=0, tiled=True),
        lax.psum_scatter(grad_w_q, ("dp", "expert"), scatter_dimension=0, tiled=True),
        lax.psum_scatter(grad_w_lat, ("dp", "expert"), scatter_dimension=0, tiled=True),
        lax.psum_scatter(grad_l_gain, ("dp", "expert"), scatter_dimension=0, tiled=True),
        lax.psum_scatter(grad_w_exp, ("dp", "expert"), scatter_dimension=0, tiled=True),
        lax.psum_scatter(grad_w_out, ("dp", "expert"), scatter_dimension=0, tiled=True),
        lax.psum_scatter(grad_f_gain, ("dp", "expert"), scatter_dimension=0, tiled=True),
        lax.psum_scatter(grad_s_gate, ("dp", "expert"), scatter_dimension=0, tiled=True),
        lax.psum_scatter(grad_s_up, ("dp", "expert"), scatter_dimension=0, tiled=True),
        lax.psum_scatter(grad_s_down, ("dp", "expert"), scatter_dimension=0, tiled=True),
    )
    return (
        block_out,
        grad_tokens,
        grad_a_gain,
        grad_w_q,
        grad_w_lat,
        grad_l_gain,
        grad_w_exp,
        grad_w_out,
        grad_f_gain,
        grad_s_gate,
        grad_s_up,
        grad_s_down,
        grad_e_gate[None],
        grad_e_up[None],
        grad_e_down[None],
    )


def solution(mesh):
    placed = (
        P(("dp", "expert"), None),
        P(("dp", "expert"), None),
        P(("dp", "expert"), None),
        P(("dp", "expert"), None),
        P("dp", None),
        P(("dp", "expert")),
        P(("dp", "expert"), None),
        P(("dp", "expert"), None),
        P(("dp", "expert")),
        P(("dp", "expert"), None),
        P(("dp", "expert"), None),
        P(("dp", "expert")),
        P(("dp", "expert"), None),
        P(("dp", "expert"), None),
        P(("dp", "expert"), None),
        P("expert", None, None),
        P("expert", None, None),
        P("expert", None, None),
    )
    return jax.shard_map(
        per_device,
        mesh=mesh,
        in_specs=placed,
        out_specs=(
            P(("dp", "expert"), None),
            P(("dp", "expert"), None),
            P(("dp", "expert")),
            P(("dp", "expert"), None),
            P(("dp", "expert"), None),
            P(("dp", "expert")),
            P(("dp", "expert"), None),
            P(("dp", "expert"), None),
            P(("dp", "expert")),
            P(("dp", "expert"), None),
            P(("dp", "expert"), None),
            P(("dp", "expert"), None),
            P("expert", "dp", None),
            P("expert", "dp", None),
            P("expert", None, "dp"),
        ),
        check_vma=False,
    )
```

profile of v0, /device:TPU:0, one launch (start us, length us, event | category | flops | bytes accessed | tf_op | source)
XLA Modules:
  0.0 3826.1 jit_solution(12708452995534273941)
XLA Ops:
  11.3 42.2 %all-reduce.14 = (bf16[2048]{0:T(1024)(128)(2,1)S(1)}, bf16[512]{0:T(512)(128)(2,1)S(1)}, bf16[2048]{0:T(1024)(128)(2,1)}) all-reduce(bf16[2048]{0:T(1024)(128)(2,1)S(1)} %dynamic-update-slice, bf16[512]{0:T(512)(128)(2,1)S(1)} %dynamic-update-slice.1, ...), channel_id=1, replica_groups=mesh['dp'=4,'expert'=8] {'dp','expert'}, use_global_device_ids=true, to_apply=%add.7 | all-reduce | flops 4608 | bytes 18432
  55.6 16.2 all-gather.9.cloned.1.call-done
  88.7 10.8 mul.478
  100.2 15.2 scatter_custom_fusion.1
  133.1 116.7 %all_gather.42 = bf16[2048,64]{0,1:T(8,128)(2,1)S(1)} all-gather(bf16[256,64]{0,1:T(8,128)(2,1)S(1)} %pad_maximum_fusion.2), channel_id=1, replica_groups=mesh['dp'=4,'expert'=8] {'expert'}, dimensions={0}, use_global_device_ids=true | all-gather | bytes 294912 | tf_op jit(solution)/shard_map/all_gather | solution.py:191
  249.9 15.0 convolution_convert_fusion
  264.9 10.5 copy.205
  275.4 12.0 copy.147
  287.4 54.2 %all-gather.15.cloned.1.call-done = bf16[2048,3072]{1,0:T(8,128)(2,1)} async-done(((bf16[64,3072]{1,0:T(8,128)(2,1)}), bf16[2048,3072]{1,0:T(8,128)(2,1)}) %all-gather.15.cloned.1.call-update) | async-done | bytes 12582928 | tf_op jit(solution)/shard_map/all_gather | solution.py:114
  354.1 66.5 %while.63 = (s32[]{:T(128)}, f32[16,256]{1,0:T(8,128)S(1)}, f32[16,256]{1,0:T(8,128)}, s32[4]{0:T(128)}, bf16[256,8]{1,0:T(8,128)(2,1)}, /*index=5*/bf16[4,512,1...) while((s32[]{:T(128)}, f32[16,256]{1,0:T(8,128)S(1)}, ...), condition=%wide.region_8.9_spmd.clone.clone.clone, body=%wide.region_5.8_spmd.clone.clone.clone.sunk | while | flops 823045120 | bytes 49578192 | solution.py:225
  421.3 95.8 %while.64 = (s32[]{:T(128)}, f32[256,16,128]{0,2,1:T(8,128)}, bf16[4,512,16,256]{3,1,2,0:T(8,128)(2,1)}, s32[4]{0:T(128)}, bf16[256,8]{1,0:T(8,128)(2,1)}, /*ind...) while((s32[]{:T(128)}, f32[256,16,128]{0,2,1:T(8,128)}, ...), condition=%wide.region_10.11_spmd.clone.clone.clone, body=%wide.region_9.10_spmd.clone.clone.clone.sunk | while | flops 1356749824 | bytes 55410868 | solution.py:248
  507.9 9.2 bitcast_add_fusion.5
  527.8 23.0 scatter_custom_fusion
  565.1 11.6 fusion.140
  576.8 103.9 %all-to-all-done = bf16[8,108,2048]{2,1,0:T(8,128)(2,1)} async-done(((bf16[8,108,2048]{2,1,0:T(8,128)(2,1)}), bf16[8,108,2048]{2,1,0:T(8,128)(2,1)}, u32[]{:S(2)}, u32[]{:S(2)}) %all-to-all-start) | async-done | bytes 3538976 | tf_op jit(solution)/shard_map/all_to_all | solution.py:274
  685.3 9.6 fusion.124
  695.0 12.4 fusion.133
  733.0 9.0 fusion.216
  742.0 9.0 fusion.215
  751.0 24.9 all-gather.23.cloned.1.call-done
  775.9 12.5 multiply_convert_fusion.1
  788.4 37.4 all-to-all-done.3
  830.9 9.6 gather_fusion.1
  840.5 9.7 reshape.441
  850.2 10.0 reduce_sum.171
  887.8 199.5 %while.65 = (s32[]{:T(128)}, f32[256,16,192]{0,2,1:T(8,128)}, f32[4,512,4096]{2,1,0:T(8,128)}, bf16[4,512,64]{1,2,0:T(8,128)(2,1)}, bf16[4,512,16,256]{3,1,2,0:T...) while((s32[]{:T(128)}, f32[256,16,192]{0,2,1:T(8,128)}, ...), condition=%wide.region_22.23_spmd.clone.clone.clone, body=%wide.region_21.22_spmd.clone.clone.clone.sunk | while | flops 3515014144 | bytes 216711536 | solution.py:409
  921.1 8.9 copy.215
  1089.1 32.6 convolution_convert_fusion.5
  1121.7 9.7 convolution_convert_fusion.1
  1133.4 10.6 convolution_convert_fusion.3
  1144.1 11.8 convolution_convert_fusion.2
  1157.2 64.0 %reduce-scatter.15.cloned.1.call-done = bf16[256,512]{0,1:T(8,128)(2,1)} async-done(((bf16[2048,512]{0,1:T(8,128)(2,1)}), bf16[256,512]{0,1:T(8,128)(2,1)}) %reduce-scatter.15.cloned.1.call-update) | async-done | bytes 262160 | tf_op jit(solution)/shard_map/reduce_scatter | solution.py:420
  1230.3 33.4 fusion.218
  1278.3 12.4 fusion.207
  1292.6 10.2 fusion.220
  1304.1 9.5 fusion.219
  1315.3 9.5 fusion.221
  1340.6 84.4 %all-to-all-done.1 = bf16[8,108,2048]{2,1,0:T(8,128)(2,1)} async-done(((bf16[8,108,2048]{2,1,0:T(8,128)(2,1)}), bf16[8,108,2048]{2,1,0:T(8,128)(2,1)}, u32[]{:S(2)}, u32[]{:S(2)}) %all-to-all-start.1) | async-done | bytes 3538976 | tf_op jit(solution)/shard_map/all_to_all | solution.py:286
  1432.4 9.7 reshape.440
  1442.1 11.5 multiply_reduce_fusion
  1472.1 42.4 %all-reduce.13 = (f32[2048]{0:T(1024)S(1)}, f32[512]{0:T(512)S(1)}, f32[2048]{0:T(1024)S(1)}) all-reduce(f32[2048]{0:T(1024)S(1)} %get-tuple-element.901, f32[512]{0:T(512)S(1)} %copy-done.72, f32[2048]{0:T(1024)S(1)} %copy-done.73), channel_id=4, replica_groups=mesh['dp'=4,'expert'=8] {'dp','expert'}, use_global_device_ids=true, to_apply=%region_28.29.clone | all-reduce | flops 4608 | bytes 36864
  1529.4 17.7 reduce-scatter.19.cloned.1.call-done
  1547.1 187.0 %reduce-scatter.21.cloned.1.call-done = f32[16,4096]{1,0:T(8,128)} async-done(((f32[512,4096]{1,0:T(8,128)}), f32[16,4096]{1,0:T(8,128)}) %reduce-scatter.21.cloned.1.call-update) | async-done | bytes 262160 | tf_op jit(solution)/shard_map/reduce_scatter | solution.py:452
  1734.1 359.8 %reduce-scatter.23.cloned.1.call-done = f32[64,2048]{1,0:T(8,128)} async-done(((f32[2048,2048]{1,0:T(8,128)}), f32[64,2048]{1,0:T(8,128)}) %reduce-scatter.23.cloned.1.call-update) | async-done | bytes 524304 | tf_op jit(solution)/shard_map/reduce_scatter | solution.py:453
  2093.9 252.7 %reduce-scatter.17.cloned.1.call-done = f32[64,3072]{1,0:T(8,128)} async-done(((f32[2048,3072]{1,0:T(8,128)}), f32[64,3072]{1,0:T(8,128)}) %reduce-scatter.17.cloned.1.call-update) | async-done | bytes 786448 | tf_op jit(solution)/shard_map/reduce_scatter | solution.py:449
  2346.6 490.4 %reduce-scatter.27.cloned.1.call-done = f32[64,2816]{1,0:T(8,128)} async-done(((f32[2048,2816]{1,0:T(8,128)}), f32[64,2816]{1,0:T(8,128)}) %reduce-scatter.27.cloned.1.call-update) | async-done | bytes 720912 | tf_op jit(solution)/shard_map/reduce_scatter | solution.py:456
  2837.0 491.0 %reduce-scatter.25.cloned.1.call-done = f32[64,2816]{1,0:T(8,128)} async-done(((f32[2048,2816]{1,0:T(8,128)}), f32[64,2816]{1,0:T(8,128)}) %reduce-scatter.25.cloned.1.call-update) | async-done | bytes 720912 | tf_op jit(solution)/shard_map/reduce_scatter | solution.py:455
  3328.0 490.8 %reduce-scatter.29.cloned.1.call-done = f32[88,2048]{1,0:T(8,128)} async-done(((f32[2816,2048]{1,0:T(8,128)}), f32[88,2048]{1,0:T(8,128)}) %reduce-scatter.29.cloned.1.call-update) | async-done | bytes 720912 | tf_op jit(solution)/shard_map/reduce_scatter | solution.py:457
  (555 shorter events, 566.6 us)
Async XLA Ops:
  7.2 64.6 %all-gather.9.cloned.1.call-start = ((), (), s32[]{:S(2)}) async-start(), calls=%async_computation.16 | async-start | bytes 2703360 | tf_op jit(solution)/shard_map/all_gather | solution.py:115
  7.9 242.0 %all-gather.13.cloned.1.call-start = ((), (), s32[]{:S(2)}) async-start(), calls=%async_computation.18 | async-start | bytes 4325376 | tf_op jit(solution)/shard_map/all_gather | solution.py:117
  8.7 241.2 %all-gather.11.cloned.1.call-start = ((), (), s32[]{:S(2)}) async-start(), calls=%async_computation.17 | async-start | bytes 2359296 | tf_op jit(solution)/shard_map/all_gather | solution.py:190
  53.5 23.8 copy-start.59
  55.5 24.2 copy-start.63
  55.6 25.2 copy-start.74
  55.6 27.7 copy-start.19
  77.3 264.4 %all-gather.15.cloned.1.call-start = ((), (), s32[]{:S(2)}) async-start(), calls=%async_computation.19 | async-start | bytes 12976128 | tf_op jit(solution)/shard_map/all_gather | solution.py:114
  77.9 441.9 %all-gather.17.cloned.1.call-start = ((), (), s32[]{:S(2)}) async-start(), calls=%async_computation.20 | async-start | bytes 8650752 | tf_op jit(solution)/shard_map/all_gather | solution.py:118
  78.5 654.6 %all-gather.21.cloned.1.call-start = ((), (), s32[]{:S(2)}) async-start(), calls=%async_computation.22 | async-start | bytes 11894784 | tf_op jit(solution)/shard_map/all_gather | solution.py:121
  79.0 663.0 %all-gather.19.cloned.1.call-start = ((), (), s32[]{:S(2)}) async-start(), calls=%async_computation.21 | async-start | bytes 11894784 | tf_op jit(solution)/shard_map/all_gather | solution.py:120
  122.1 433.3 %all-to-all-start.2 = ((bf16[8,108,2048]{2,1,0:T(8,128)(2,1)}), bf16[8,108,2048]{2,1,0:T(8,128)(2,1)}, u32[]{:S(2)}, u32[]{:S(2)}) async-start(bf16[8,108,2048]{2,1,0:T(8,128)(2,1)} %reshape.435), calls=%async_computation.2 | async-start | bytes 7340032 | tf_op jit(solution)/shard_map/all_to_all | solution.py:306
  126.7 649.2 %all-gather.23.cloned.1.call-start = ((), (), s32[]{:S(2)}) async-start(), calls=%async_computation.23 | async-start | bytes 11894784 | tf_op jit(solution)/shard_map/all_gather | solution.py:122
  133.0 216.8 %copy-start.49 = (f32[256,32]{0,1:T(8,128)}, f32[256,32]{0,1:T(8,128)S(1)}, u32[]{:S(2)}) copy-start(f32[256,32]{0,1:T(8,128)S(1)} %get-tuple-element.1006) | copy-start | bytes 98308
  133.1 216.8 %copy-start.51 = (f32[256,32]{0,1:T(8,128)}, f32[256,32]{0,1:T(8,128)S(1)}, u32[]{:S(2)}) copy-start(f32[256,32]{0,1:T(8,128)S(1)} %get-tuple-element.1007) | copy-start | bytes 98308
  275.4 66.3 %copy-start.6 = (bf16[256,2048]{1,0:T(8,128)(2,1)S(1)}, bf16[256,2048]{1,0:T(8,128)(2,1)}, u32[]{:S(2)}) copy-start(bf16[256,2048]{1,0:T(8,128)(2,1)} %param.26) | copy-start | bytes 3145732
  275.4 66.3 %copy-start.47 = (f32[2048]{0:T(1024)S(1)}, f32[2048]{0:T(1024)}, u32[]{:S(2)}) copy-start(f32[2048]{0:T(1024)} %copy-done.46) | copy-start | bytes 24580
  275.4 66.3 %copy-start.55 = (f32[256]{0:T(256)S(1)}, f32[256]{0:T(256)}, u32[]{:S(2)}) copy-start(f32[256]{0:T(256)} %copy-done.54) | copy-start | bytes 3076
  527.8 214.2 %copy-start.16 = (bf16[256,2048]{1,0:T(8,128)(2,1)}, bf16[256,2048]{1,0:T(8,128)(2,1)S(1)}, u32[]{:S(2)}) copy-start(bf16[256,2048]{1,0:T(8,128)(2,1)S(1)} %multiply_convert_fusion.3) | copy-start | bytes 3145732
  555.4 125.2 %all-to-all-start = ((bf16[8,108,2048]{2,1,0:T(8,128)(2,1)}), bf16[8,108,2048]{2,1,0:T(8,128)(2,1)}, u32[]{:S(2)}, u32[]{:S(2)}) async-start(bf16[8,108,2048]{2,1,0:T(8,128)(2,1)} %reshape.431), calls=%async_computation | async-start | bytes 7340032 | tf_op jit(solution)/shard_map/all_to_all | solution.py:274
  685.3 31.0 slice-start.2
  728.4 97.4 %all-to-all-start.3 = ((bf16[8,108,2048]{2,1,0:T(8,128)(2,1)}), bf16[8,108,2048]{2,1,0:T(8,128)(2,1)}, u32[]{:S(2)}, u32[]{:S(2)}) async-start(bf16[8,108,2048]{2,1,0:T(8,128)(2,1)} %reshape.437), calls=%async_computation.3 | async-start | bytes 7340032 | tf_op jit(solution)/shard_map/all_to_all | solution.py:323
  732.9 423.2 %reduce-scatter.13.cloned.1.call-start = ((), (), s32[]{:S(2)}) async-start(), calls=%async_computation.24 | async-start | bytes 294912 | tf_op jit(solution)/shard_map/reduce_scatter | solution.py:423
  733.0 97.9 %copy-start.57 = (s32[1024]{0:T(1024)}, s32[1024]{0:T(1024)S(1)}, u32[]{:S(2)}) copy-start(s32[1024]{0:T(1024)S(1)} %pad_clamp_fusion) | copy-start | bytes 12292
  1089.0 132.2 %reduce-scatter.15.cloned.1.call-start = ((), (), s32[]{:S(2)}) async-start(), calls=%async_computation.25 | async-start | bytes 2359296 | tf_op jit(solution)/shard_map/reduce_scatter | solution.py:420
  1089.1 32.6 copy-start.30
  1121.7 398.1 %reduce-scatter.35.cloned.1.call-start = ((), (), s32[]{:S(2)}) async-start(), calls=%async_computation.35 | async-start | bytes 7208960 | tf_op jit(solution)/shard_map/reduce_scatter | solution.py:341
  1131.5 391.6 %reduce-scatter.31.cloned.1.call-start = ((), (), s32[]{:S(2)}) async-start(), calls=%async_computation.33 | async-start | bytes 7208960 | tf_op jit(solution)/shard_map/reduce_scatter | solution.py:335
  1144.1 382.1 %reduce-scatter.33.cloned.1.call-start = ((), (), s32[]{:S(2)}) async-start(), calls=%async_computation.34 | async-start | bytes 7208960 | tf_op jit(solution)/shard_map/reduce_scatter | solution.py:338
  1155.9 65.3 %copy-start.23 = (f32[256,576]{0,1:T(8,128)S(1)}, f32[256,576]{0,1:T(8,128)}, u32[]{:S(2)}) copy-start(f32[256,576]{0,1:T(8,128)} %copy-done.22) | copy-start | bytes 1769476
  1155.9 65.3 %copy-start.60 = (f32[512]{0:T(512)S(1)}, f32[512]{0:T(512)}, u32[]{:S(2)}) copy-start(f32[512]{0:T(512)} %copy-done.59) | copy-start | bytes 6148
  1155.9 65.3 %copy-start.62 = (f32[256]{0:T(256)S(1)}, f32[256]{0:T(256)}, u32[]{:S(2)}) copy-start(f32[256]{0:T(256)} %copy-done.61) | copy-start | bytes 3076
  1155.9 67.0 %copy-start.71 = (f32[256]{0:T(256)S(1)}, f32[256]{0:T(256)}, u32[]{:S(2)}) copy-start(f32[256]{0:T(256)} %copy-done.70) | copy-start | bytes 3076
  1156.0 68.9 %copy-start.7 = (bf16[256,2048]{1,0:T(8,128)(2,1)S(1)}, bf16[256,2048]{1,0:T(8,128)(2,1)}, u32[]{:S(2)}) copy-start(bf16[256,2048]{1,0:T(8,128)(2,1)} %param.26) | copy-start | bytes 3145732
  1156.0 68.9 %copy-start.48 = (f32[2048]{0:T(1024)S(1)}, f32[2048]{0:T(1024)}, u32[]{:S(2)}) copy-start(f32[2048]{0:T(1024)} %copy-done.46) | copy-start | bytes 24580
  1156.0 68.9 %copy-start.56 = (f32[256]{0:T(256)S(1)}, f32[256]{0:T(256)}, u32[]{:S(2)}) copy-start(f32[256]{0:T(256)} %copy-done.54) | copy-start | bytes 3076
  1156.0 391.1 %reduce-scatter.19.cloned.1.call-start = ((), (), s32[]{:S(2)}) async-start(), calls=%async_computation.27 | async-start | bytes 5406720 | tf_op jit(solution)/shard_map/reduce_scatter | solution.py:450
  1157.2 71.3 %copy-start.40 = (f32[256,64]{0,1:T(8,128)}, f32[256,64]{0,1:T(8,128)S(1)}, u32[]{:S(2)}) copy-start(f32[256,64]{0,1:T(8,128)S(1)} %pad_add_fusion.1) | copy-start | bytes 196612
  1228.5 505.6 %reduce-scatter.21.cloned.1.call-start = ((), (), s32[]{:S(2)}) async-start(), calls=%async_computation.28 | async-start | bytes 8650752 | tf_op jit(solution)/shard_map/reduce_scatter | solution.py:452
  1263.8 830.1 %reduce-scatter.23.cloned.1.call-start = ((), (), s32[]{:S(2)}) async-start(), calls=%async_computation.29 | async-start | bytes 17301504 | tf_op jit(solution)/shard_map/reduce_scatter | solution.py:453
  1273.8 1072.8 %reduce-scatter.17.cloned.1.call-start = ((), (), s32[]{:S(2)}) async-start(), calls=%async_computation.26 | async-start | bytes 25952256 | tf_op jit(solution)/shard_map/reduce_scatter | solution.py:449
  1290.8 1546.2 %reduce-scatter.27.cloned.1.call-start = ((), (), s32[]{:S(2)}) async-start(), calls=%async_computation.31 | async-start | bytes 23789568 | tf_op jit(solution)/shard_map/reduce_scatter | solution.py:456
  1302.8 2025.2 %reduce-scatter.25.cloned.1.call-start = ((), (), s32[]{:S(2)}) async-start(), calls=%async_computation.30 | async-start | bytes 23789568 | tf_op jit(solution)/shard_map/reduce_scatter | solution.py:455
  1313.6 2505.2 %reduce-scatter.29.cloned.1.call-start = ((), (), s32[]{:S(2)}) async-start(), calls=%async_computation.32 | async-start | bytes 23789568 | tf_op jit(solution)/shard_map/reduce_scatter | solution.py:457
  1335.8 89.2 %all-to-all-start.1 = ((bf16[8,108,2048]{2,1,0:T(8,128)(2,1)}), bf16[8,108,2048]{2,1,0:T(8,128)(2,1)}, u32[]{:S(2)}, u32[]{:S(2)}) async-start(bf16[8,108,2048]{2,1,0:T(8,128)(2,1)} %reshape.433), calls=%async_computation.1 | async-start | bytes 7340032 | tf_op jit(solution)/shard_map/all_to_all | solution.py:286
  1340.6 87.5 %copy-start.58 = (s32[1024]{0:T(1024)S(1)}, s32[1024]{0:T(1024)}, u32[]{:S(2)}) copy-start(s32[1024]{0:T(1024)} %copy-done.57) | copy-start | bytes 12292
  1469.4 46.8 %copy-start.69 = (f32[256]{0:T(256)S(1)}, f32[256]{0:T(256)}, u32[]{:S(2)}) copy-start(f32[256]{0:T(256)} %copy-done.68) | copy-start | bytes 3076
  1469.4 46.8 %copy-start.12 = (f32[256,2048]{1,0:T(8,128)S(1)}, f32[256,2048]{1,0:T(8,128)}, u32[]{:S(2)}) copy-start(f32[256,2048]{1,0:T(8,128)} %copy-done.10) | copy-start | bytes 6291460
  (89 other events, 396.8 us)
Sparse Core Ops, SparseCore 0:
  10.9 60.8 all-gather.8
  74.8 62.8 all-gather.12
  140.3 101.7 all-gather.10
  244.9 96.6 all-gather.14
  344.5 75.6 all-gather.16
  422.9 89.8 all-gather.20
  515.6 142.2 all-gather.18
  660.8 115.0 all-gather.22
  1089.1 60.6 reduce-scatter.12
  1153.8 67.3 reduce-scatter.14
  1223.7 53.8 reduce-scatter.34
  1280.2 54.8 reduce-scatter.30
  1337.6 54.8 reduce-scatter.32
  1395.3 151.7 reduce-scatter.18
  1549.9 184.1 reduce-scatter.20
  1736.9 356.9 reduce-scatter.22
  2101.9 244.6 reduce-scatter.16
  2349.3 487.6 reduce-scatter.26
  2839.9 488.0 reduce-scatter.24
  3330.7 488.0 reduce-scatter.28
where the time goes:
time: 3840 us; the launch traced here: 3830 us
  waiting for transfers between devices  2680 us (70%)
  matrix products  465 us (12%)
  local copies, waits for them, and re-layouts  324 us (8%)
  blocking collectives  201 us (5%)
  other arithmetic  111 us (3%)
    reduce_scatter x1, waiting for transfers between devices, per_device(): lax.psum_scatter(grad_s_gate, ('dp', 'expert'), scatter_dimension=0, tile...  491 us
    reduce_scatter x1, waiting for transfers between devices, per_device(): lax.psum_scatter(grad_s_down, ('dp', 'expert'), scatter_dimension=0, tile...  491 us
    reduce_scatter x1, waiting for transfers between devices, per_device(): lax.psum_scatter(grad_s_up, ('dp', 'expert'), scatter_dimension=0, tiled=...  490 us
    reduce_scatter x1, waiting for transfers between devices, per_device(): lax.psum_scatter(grad_w_out, ('dp', 'expert'), scatter_dimension=0, tiled...  360 us
    reduce_scatter x1, waiting for transfers between devices, per_device(): lax.psum_scatter(grad_w_q, ('dp', 'expert'), scatter_dimension=0, tiled=T...  253 us
    reduce_scatter x1, waiting for transfers between devices, per_device(): lax.psum_scatter(grad_w_exp, ('dp', 'expert'), scatter_dimension=0, tiled...  187 us
    all_gather x1, blocking collectives, per_device(): lax.all_gather(rope_bf, 'expert', axis=0, tiled=True)  117 us
    all_to_all x1, waiting for transfers between devices, per_device(): lax.all_to_all(send_rows.reshape(group_size, capacity, model_width), 'exp...  104 us
  transfers between devices with their start and end apart: 24, of which 14 were waited for; matrix products, arithmetic and copies ran while one was open for 16% of the time, Pallas kernels for 0%

commit v1 on v0

v1 whole, which is shorter than its diff:
```python
import functools

import jax
import jax.numpy as jnp
from jax import lax
from jax.experimental import pallas as pl
from jax.experimental.pallas import tpu as pltpu
from jax.sharding import PartitionSpec as P

HEADS = 16
NOPE = 128
ROPE = 64
KV = 512
VD = 128
SEG = 256
KEY = 256

epsilon = 1e-06
bf16 = jnp.bfloat16
f32 = jnp.float32
EVERY = ("dp", "expert")
MESH = pl.DeviceIdType.MESH
VMEM_LIMIT = 60 << 20
WIRE = pl.CostEstimate(flops=0, bytes_accessed=300_000_000, transcendentals=0)


def norm_rows(values, gain_vec):
    return (
        values * lax.rsqrt(jnp.mean(values * values, axis=-1, keepdims=True) + epsilon) * gain_vec
    )


def rotate(values, cos_table, sin_table):
    half_width = values.shape[-1] // 2
    first_half = values[..., :half_width]
    second_half = values[..., half_width:]
    return jnp.concatenate(
        [
            first_half * cos_table - second_half * sin_table,
            second_half * cos_table + first_half * sin_table,
        ],
        axis=-1,
    )


def gating(gate_part, up_part):
    return jax.nn.silu(gate_part) * up_part


def ancestry(parent_row, seg_count):
    identity = jnp.eye(seg_count, dtype=f32)
    parent_hot = (parent_row[:, None] == jnp.arange(seg_count, dtype=jnp.int32)[None, :]).astype(
        f32
    )
    reachable = identity
    for _ in range(seg_count - 1):
        reachable = jnp.maximum(identity, jnp.dot(parent_hot, reachable))
    return reachable


def matmul(left, right):
    return jnp.dot(left, right, preferred_element_type=f32)


def dot_last(left, right):
    return lax.dot_general(left, right, (((1,), (1,)), ((), ())), preferred_element_type=f32)


def dot_first(left, right):
    return lax.dot_general(left, right, (((0,), (0,)), ((), ())), preferred_element_type=f32)


def greet(rank, last):
    barrier = pltpu.get_barrier_semaphore()
    a = rank // 2

    def hail(other):
        pl.semaphore_signal(barrier, inc=1, device_id={"expert": other}, device_id_type=MESH)

    hail(rank + 1 - 2 * (rank % 2))

    @pl.when(a < last)
    def _():
        hail(rank + 2)

    @pl.when(a > 0)
    def _():
        hail(rank - 2)

    pl.semaphore_wait(barrier, 1 + (a + last - 1) // last + (2 * last - 1 - a) // last)


def gather_kernel(chunks, x_ref, o_ref, sx, rx, su, ru, sd, rd):
    rank = lax.axis_index("expert")
    last = o_ref.shape[0] // 2 - 1
    a = rank // 2
    side = rank + 1 - 2 * (rank % 2)
    rows = x_ref.shape[0] // chunks
    greet(rank, last)

    def piece(ref, c):
        return ref.at[pl.ds(c * rows, rows)]

    def to(src, block, c, send, recv, target):
        return pltpu.make_async_remote_copy(
            src_ref=src,
            dst_ref=piece(o_ref.at[block], c),
            send_sem=send,
            recv_sem=recv,
            device_id={"expert": target},
            device_id_type=MESH,
        )

    for c in range(chunks):
        own = piece(x_ref, c)
        to(own, rank, c, sx.at[0, c], rx.at[0, c], side).start()

        @pl.when(a < last)
        def _():
            to(own, rank, c, su.at[0, c], ru.at[0, c], rank + 2).start()

        @pl.when(a > 0)
        def _():
            to(own, rank, c, sd.at[0, c], rd.at[0, c], rank - 2).start()

    for s in range(1, last + 1):
        for c in range(chunks):

            @pl.when(a >= s)
            def _():
                block = rank - 2 * s
                src = piece(o_ref.at[block], c)
                to(src, block, c, su.at[s - 1, c], ru.at[s - 1, c], rank + 2).wait_recv()
                to(src, block, c, sx.at[s, c], rx.at[s, c], side).start()

                @pl.when(a < last)
                def _():
                    to(src, block, c, su.at[s, c], ru.at[s, c], rank + 2).start()

            @pl.when(a + s <= last)
            def _():
                block = rank + 2 * s
                src = piece(o_ref.at[block], c)
                to(src, block, c, sd.at[s - 1, c], rd.at[s - 1, c], rank - 2).wait_recv()
                to(src, block, c, sx.at[last + s, c], rx.at[last + s, c], side).start()

                @pl.when(a > 0)
                def _():
                    to(src, block, c, sd.at[s, c], rd.at[s, c], rank - 2).start()

    o_ref[rank] = x_ref[...]
    for c in range(chunks):
        own = piece(x_ref, c)
        to(own, side, c, sx.at[0, c], rx.at[0, c], side).wait()

        @pl.when(a < last)
        def _():
            to(own, rank, c, su.at[0, c], ru.at[0, c], rank + 2).wait_send()

        @pl.when(a > 0)
        def _():
            to(own, rank, c, sd.at[0, c], rd.at[0, c], rank - 2).wait_send()

    for s in range(1, last + 1):
        for c in range(chunks):

            @pl.when(a >= s)
            def _():
                block = rank - 2 * s
                src = piece(o_ref.at[block], c)
                to(src, side - 2 * s, c, sx.at[s, c], rx.at[s, c], side).wait()

                @pl.when(a < last)
                def _():
                    to(src, block, c, su.at[s, c], ru.at[s, c], rank + 2).wait_send()

            @pl.when(a + s <= last)
            def _():
                block = rank + 2 * s
                src = piece(o_ref.at[block], c)
                to(src, side + 2 * s, c, sx.at[last + s, c], rx.at[last + s, c], side).wait()

                @pl.when(a > 0)
                def _():
                    to(src, block, c, sd.at[s, c], rd.at[s, c], rank - 2).wait_send()


def gather_rows(x, count, call_id, chunks=2):
    half = count // 2
    dma = pltpu.SemaphoreType.DMA
    return pl.pallas_call(
        functools.partial(gather_kernel, chunks),
        out_shape=jax.ShapeDtypeStruct((count,) + x.shape, x.dtype),
        in_specs=[pl.BlockSpec(memory_space=pltpu.VMEM)],
        out_specs=pl.BlockSpec(memory_space=pltpu.VMEM),
        scratch_shapes=[dma((2 * half, chunks))] * 2 + [dma((half, chunks))] * 4,
        compiler_params=pltpu.CompilerParams(
            collective_id=call_id, has_side_effects=True, vmem_limit_bytes=VMEM_LIMIT
        ),
        cost_estimate=WIRE,
        name="gather_rows",
    )(x)


def reduce_kernel(chunks, p_ref, o_ref, rx, st, ru, rd, acc, sxs, rxs, sus, rus, sds, rds):
    rank = lax.axis_index("expert")
    last = p_ref.shape[0] // 2 - 1
    a = rank // 2
    b = rank % 2
    rows = p_ref.shape[1] // chunks
    greet(rank, last)
    h = a // 2
    order = [3 - 3 * h, 2 - h, 4 * h + 1 - a, a]

    def cut(ref, c):
        return ref.at[pl.ds(c * rows, rows)]

    def copy(src, dst, send, recv, target):
        return pltpu.make_async_remote_copy(
            src_ref=src,
            dst_ref=dst,
            send_sem=send,
            recv_sem=recv,
            device_id={"expert": target},
            device_id_type=MESH,
        )

    def across(t, c):
        return copy(
            cut(p_ref.at[2 * t + 1 - b], c),
            cut(rx.at[t], c),
            sxs.at[t, c],
            rxs.at[t, c],
            rank + 1 - 2 * b,
        )

    def upward(t, c):
        return copy(cut(st.at[t], c), cut(ru.at[t], c), sus.at[t, c], rus.at[t, c], rank + 2)

    def downward(t, c):
        return copy(cut(st.at[t], c), cut(rd.at[t], c), sds.at[t, c], rds.at[t, c], rank - 2)

    for t in order:
        for c in range(chunks):
            across(t, c).start()
    for t in order:
        for c in range(chunks):
            across(t, c).wait_recv()
            acc[...] = cut(p_ref.at[2 * t + b], c)[...].astype(f32) + cut(rx.at[t], c)[...].astype(
                f32
            )

            @pl.when((t >= a) & (a > 0))
            def _():
                upward(t, c).wait_recv()
                acc[...] += cut(ru.at[t], c)[...].astype(f32)

            @pl.when((t <= a) & (a < last))
            def _():
                downward(t, c).wait_recv()
                acc[...] += cut(rd.at[t], c)[...].astype(f32)

            @pl.when(t == a)
            def _():
                cut(o_ref, c)[...] = acc[...]

            @pl.when(t > a)
            def _():
                cut(st.at[t], c)[...] = acc[...].astype(st.dtype)
                upward(t, c).start()

            @pl.when(t < a)
            def _():
                cut(st.at[t], c)[...] = acc[...].astype(st.dtype)
                downward(t, c).start()

    for t in order:
        for c in range(chunks):
            across(t, c).wait_send()

            @pl.when(t > a)
            def _():
                upward(t, c).wait_send()

            @pl.when(t < a)
            def _():
                downward(t, c).wait_send()


def reduce_rows(p, call_id, chunks=4):
    count, rows, width = p.shape
    half = count // 2
    buf = pltpu.VMEM((half, rows, width), p.dtype)
    sem = pltpu.SemaphoreType.DMA((half, chunks))
    return pl.pallas_call(
        functools.partial(reduce_kernel, chunks),
        out_shape=jax.ShapeDtypeStruct((rows, width), f32),
        in_specs=[pl.BlockSpec(memory_space=pltpu.VMEM)],
        out_specs=pl.BlockSpec(memory_space=pltpu.VMEM),
        scratch_shapes=[buf] * 4 + [pltpu.VMEM((rows // chunks, width), f32)] + [sem] * 6,
        compiler_params=pltpu.CompilerParams(
            collective_id=call_id, has_side_effects=True, vmem_limit_bytes=VMEM_LIMIT
        ),
        cost_estimate=WIRE,
        name="reduce_rows",
    )(p)


def triangle():
    keys = lax.broadcasted_iota(jnp.int32, (SEG, SEG), 0)
    queries = lax.broadcasted_iota(jnp.int32, (SEG, SEG), 1)
    return keys <= queries


def attend_kernel(
    heads, segs, scale, reach_ref, q_ref, k_ref, v_ref, out_ref, full_ref, log_ref, m_s, l_s, acc_s
):
    i = pl.program_id(0)
    diag = triangle()

    def score(h, j):
        keys = k_ref[pl.ds(j * SEG, SEG), h * KEY : (h + 1) * KEY]
        return dot_last(keys, q_ref[:, h * KEY : (h + 1) * KEY]) * scale

    def weigh(h, j, weights):
        vals = v_ref[pl.ds(j * SEG, SEG), h * VD : (h + 1) * VD]
        return dot_first(vals, weights.astype(bf16))

    for h in range(heads):
        s = jnp.where(diag, score(h, i), -1e30)
        top = jnp.max(s, axis=0, keepdims=True)
        w = jnp.where(diag, jnp.exp(s - top), 0.0)
        m_s[h : h + 1] = top
        l_s[h : h + 1] = jnp.sum(w, axis=0, keepdims=True)
        acc_s[h] = weigh(h, i, w)

    def step(j, carry):
        @pl.when(reach_ref[i * segs + j] > 0)
        def _():
            for h in range(heads):
                s = score(h, j)
                old = m_s[h : h + 1]
                top = jnp.maximum(old, jnp.max(s, axis=0, keepdims=True))
                w = jnp.exp(s - top)
                fade = jnp.exp(old - top)
                m_s[h : h + 1] = top
                l_s[h : h + 1] = l_s[h : h + 1] * fade + jnp.sum(w, axis=0, keepdims=True)
                acc_s[h] = acc_s[h] * fade + weigh(h, j, w)

        return carry

    lax.fori_loop(0, i, step, 0)
    for h in range(heads):
        total = l_s[h : h + 1]
        rows = (acc_s[h] * (1.0 / total)).T
        full_ref[:, h * VD : (h + 1) * VD] = rows
        out_ref[:, h * VD : (h + 1) * VD] = rows.astype(bf16)
        log_ref[h : h + 1] = m_s[h : h + 1] + jnp.log(total)


def attend(reach, q, k, v, scale):
    tree = q.shape[0]
    segs = tree // SEG
    heads = q.shape[1] // KEY
    whole = lambda width: pl.BlockSpec((tree, width), lambda i, r: (0, 0))
    part = lambda width: pl.BlockSpec((SEG, width), lambda i, r: (i, 0))
    return pl.pallas_call(
        functools.partial(attend_kernel, heads, segs, scale),
        grid_spec=pltpu.PrefetchScalarGridSpec(
            num_scalar_prefetch=1,
            grid=(segs,),
            in_specs=[part(heads * KEY), whole(heads * KEY), whole(heads * VD)],
            out_specs=[
                part(heads * VD),
                part(heads * VD),
                pl.BlockSpec((heads, SEG), lambda i, r: (0, i)),
            ],
            scratch_shapes=[
                pltpu.VMEM((heads, SEG), f32),
                pltpu.VMEM((heads, SEG), f32),
                pltpu.VMEM((heads, VD, SEG), f32),
            ],
        ),
        out_shape=[
            jax.ShapeDtypeStruct((tree, heads * VD), bf16),
            jax.ShapeDtypeStruct((tree, heads * VD), f32),
            jax.ShapeDtypeStruct((heads, tree), f32),
        ],
        compiler_params=pltpu.CompilerParams(vmem_limit_bytes=VMEM_LIMIT),
        name="attend",
    )(reach, q, k, v)


def attend_back_kernel(
    heads,
    segs,
    scale,
    reach_ref,
    q_ref,
    k_ref,
    v_ref,
    g_ref,
    log_ref,
    delta_ref,
    dq_ref,
    dkv_ref,
    dr_ref,
    dk_s,
    dv_s,
):
    j = pl.program_id(0)
    diag = triangle()

    @pl.when(j == 0)
    def _():
        dq_ref[...] = jnp.zeros_like(dq_ref)

    dk_s[...] = jnp.zeros_like(dk_s)
    dv_s[...] = jnp.zeros_like(dv_s)

    def block(i, masked):
        rows = pl.ds(i * SEG, SEG)
        for h in range(heads):
            kcols = slice(h * KEY, (h + 1) * KEY)
            vcols = slice(h * VD, (h + 1) * VD)
            q = q_ref[rows, kcols]
            k = k_ref[:, kcols]
            g = g_ref[rows, vcols]
            s = dot_last(k, q) * scale
            w = jnp.exp(s - log_ref[h : h + 1, rows])
            if masked:
                w = jnp.where(diag, w, 0.0)
            dw = dot_last(v_ref[:, vcols], g)
            ds = (w * (dw - delta_ref[h : h + 1, rows])).astype(bf16)
            dv_s[h] += matmul(w.astype(bf16), g)
            dk_s[h] += matmul(ds, q)
            dq_ref[rows, kcols] += dot_first(ds, k)

    block(j, True)

    def step(i, carry):
        @pl.when(reach_ref[i * segs + j] > 0)
        def _():
            block(i, False)

        return carry

    lax.fori_loop(j + 1, segs, step, 0)
    rope = jnp.zeros((SEG, KEY - NOPE), f32)
    for h in range(heads):
        dkv_ref[:, h * KEY : h * KEY + NOPE] = (dk_s[h, :, :NOPE] * scale).astype(bf16)
        dkv_ref[:, h * KEY + NOPE : (h + 1) * KEY] = dv_s[h].astype(bf16)
        rope = rope + dk_s[h, :, NOPE:]
    dr_ref[...] = rope * scale


def attend_back(reach, q, k, v, g, log_total, delta, scale):
    tree = q.shape[0]
    segs = tree // SEG
    heads = q.shape[1] // KEY
    whole = lambda width: pl.BlockSpec((tree, width), lambda j, r: (0, 0))
    part = lambda width: pl.BlockSpec((SEG, width), lambda j, r: (j, 0))
    lane = pl.BlockSpec((heads, tree), lambda j, r: (0, 0))
    return pl.pallas_call(
        functools.partial(attend_back_kernel, heads, segs, scale),
        grid_spec=pltpu.PrefetchScalarGridSpec(
            num_scalar_prefetch=1,
            grid=(segs,),
            in_specs=[
                whole(heads * KEY),
                part(heads * KEY),
                part(heads * VD),
                whole(heads * VD),
                lane,
                lane,
            ],
            out_specs=[whole(heads * KEY), part(heads * KEY), part(KEY - NOPE)],
            scratch_shapes=[
                pltpu.VMEM((heads, SEG, KEY), f32),
                pltpu.VMEM((heads, SEG, VD), f32),
            ],
        ),
        out_shape=[
            jax.ShapeDtypeStruct((tree, heads * KEY), f32),
            jax.ShapeDtypeStruct((tree, heads * KEY), bf16),
            jax.ShapeDtypeStruct((tree, KEY - NOPE), f32),
        ],
        compiler_params=pltpu.CompilerParams(vmem_limit_bytes=VMEM_LIMIT),
        name="attend_back",
    )(reach, q, k, v, g, log_total, delta)


def per_device(
    tokens,
    grad_out,
    routes,
    gate_values,
    parents,
    attn_gain,
    w_query,
    w_latent,
    latent_gain,
    w_expand,
    w_output,
    ffn_gain,
    shared_gate,
    shared_up,
    shared_down,
    expert_gate,
    expert_up,
    expert_down,
):
    group = lax.axis_size("expert")
    spread = lax.axis_size("dp")
    rank = lax.axis_index("expert")
    tok_dev, width = tokens.shape
    tree = tok_dev * group
    segs = parents.shape[1]
    per_token = routes.shape[1]
    capacity = tok_dev * per_token * 9 // (8 * group)
    slots = -(-capacity // 16) * 16
    scale = (NOPE + ROPE) ** (-0.5)
    mine = HEADS // group
    rows_w = w_query.shape[0]
    rows_l = w_expand.shape[0]
    ff_cut = shared_down.shape[0]
    ff_own = ff_cut * spread
    ff_pad = -(-ff_own // 128) * 128
    q_own = mine * KEY
    e_own = mine * (NOPE + VD)
    e_fold = rows_l * e_own // rows_w

    x_all = gather_rows(tokens, group, 0).reshape(tree, width)
    g_all = lax.all_gather(grad_out, "expert", axis=0, tiled=True)

    wq_cut = jnp.pad(
        w_query.reshape(rows_w, group, mine, NOPE + ROPE),
        ((0, 0), (0, 0), (0, 0), (0, KEY - NOPE - ROPE)),
    ).reshape(rows_w, group, q_own)

    def ff_columns(weight):
        cut = weight.reshape(rows_w, spread, group, ff_cut).transpose(0, 2, 1, 3)
        return jnp.pad(
            cut.reshape(rows_w, group, ff_own), ((0, 0), (0, 0), (0, ff_pad - ff_own))
        )

    we_cut = (
        w_expand.reshape(rows_l, group, e_own).transpose(1, 0, 2).reshape(group, rows_w, e_fold)
    )
    packed = jnp.concatenate(
        [
            wq_cut.transpose(1, 0, 2),
            we_cut,
            ff_columns(shared_gate).transpose(1, 0, 2),
            ff_columns(shared_up).transpose(1, 0, 2),
        ],
        axis=2,
    )
    packed = lax.all_to_all(packed, "expert", split_axis=0, concat_axis=0, tiled=True)
    packed = lax.all_gather(packed, "dp", axis=0, tiled=True).reshape(width, -1)
    wq = packed[:, :q_own]
    we = packed[:, q_own : q_own + e_fold].reshape(KV, e_own)
    sg = packed[:, q_own + e_fold : q_own + e_fold + ff_pad]
    su = packed[:, q_own + e_fold + ff_pad :]
    sd = lax.all_gather(shared_down, "dp", axis=0, tiled=True)
    sd = jnp.pad(sd, ((0, ff_pad - ff_own), (0, 0)))

    lat_w = KV + ROPE
    gains = jnp.stack(
        [attn_gain, ffn_gain, jnp.pad(latent_gain, (0, rows_w - rows_l))], axis=1
    )
    gains = jnp.pad(gains, ((0, 0), (0, ROPE - 3)))
    lat_pack = lax.all_gather(
        jnp.concatenate([w_latent, gains], axis=1), EVERY, axis=0, tiled=True
    )
    wl = lat_pack[:, :lat_w]
    a_gain = lat_pack[:, lat_w].astype(f32)
    f_gain = lat_pack[:, lat_w + 1].astype(f32)
    l_gain = lat_pack[:, lat_w + 2].reshape(-1, rows_w)[:, :rows_l].reshape(KV).astype(f32)
    wo = lax.all_gather(w_output, EVERY, axis=0, tiled=True)

    reachable = ancestry(parents[0], segs)
    depth = jnp.sum(reachable, axis=1) - 1.0
    reach = reachable.astype(jnp.int32).reshape(segs * segs)
    positions = (depth[:, None] * SEG + jnp.arange(SEG, dtype=f32)[None, :]).reshape(tree)
    half_width = ROPE // 2
    freq = 10000.0 ** (-2.0 * jnp.arange(half_width, dtype=f32) / ROPE)
    angle = positions[:, None] * freq[None, :]
    cos_table = jnp.cos(angle)
    sin_table = jnp.sin(angle)

    def own(values):
        return lax.dynamic_slice_in_dim(values, rank * tok_dev, tok_dev, 0)

    h1 = norm_rows(x_all.astype(f32), a_gain).astype(bf16)
    query = matmul(h1, wq).reshape(tree, mine, KEY)

    def query_rope(query_in):
        return jnp.concatenate(
            [
                query_in[..., :NOPE],
                rotate(
                    query_in[..., NOPE : NOPE + ROPE], cos_table[:, None, :], sin_table[:, None, :]
                ),
                jnp.zeros(query_in.shape[:-1] + (KEY - NOPE - ROPE,), f32),
            ],
            axis=-1,
        )

    def query_rope_back(grad):
        return jnp.concatenate(
            [
                grad[..., :NOPE],
                rotate(
                    grad[..., NOPE : NOPE + ROPE], cos_table[:, None, :], -sin_table[:, None, :]
                ),
                jnp.zeros(grad.shape[:-1] + (KEY - NOPE - ROPE,), f32),
            ],
            axis=-1,
        )

    q_att = query_rope(query).astype(bf16).reshape(tree, q_own)
    latent = matmul(h1, wl)
    ckv = norm_rows(latent[:, :KV], l_gain).astype(bf16)
    krope = rotate(latent[:, KV:], cos_table, sin_table).astype(bf16)
    kv = matmul(ckv, we).astype(bf16).reshape(tree, mine, NOPE + VD)
    k_att = jnp.concatenate(
        [
            kv[..., :NOPE],
            jnp.broadcast_to(krope[:, None, :], (tree, mine, ROPE)),
            jnp.zeros((tree, mine, KEY - NOPE - ROPE), bf16),
        ],
        axis=-1,
    ).reshape(tree, q_own)
    v_att = kv[..., NOPE:].reshape(tree, mine * VD)
    attn_heads, attended, log_total = attend(reach, q_att, k_att, v_att, scale)
    attn_own = lax.all_to_all(attn_heads, "expert", split_axis=0, concat_axis=1, tiled=True)
    tokens_f = tokens.astype(f32)
    resid = tokens_f + matmul(attn_own, wo)
    second_normed, second_norm_back = jax.vjp(norm_rows, resid, f_gain)

    h2 = gather_rows(second_normed.astype(bf16), group, 2)
    expert_ids = jnp.arange(group, dtype=jnp.int32)
    gate_of = jnp.sum(
        jnp.where(routes[:, :, None] == expert_ids[None, None, :], gate_values[:, :, None], 0.0),
        axis=1,
    )
    gate_of = lax.all_to_all(gate_of.T, "expert", split_axis=0, concat_axis=0, tiled=True)
    routed = gate_of > 0.0
    upto = (
        jnp.arange(tok_dev, dtype=jnp.int32)[:, None]
        <= jnp.arange(tok_dev, dtype=jnp.int32)[None, :]
    )
    place = matmul(routed.astype(bf16), upto.astype(bf16)).astype(jnp.int32) - 1
    chosen = (
        place[:, None, :] == jnp.arange(slots, dtype=jnp.int32)[None, :, None]
    ) & routed[:, None, :]
    pick = chosen.astype(bf16)
    slot_gate = jnp.sum(jnp.where(chosen, gate_of[:, None, :], 0.0), axis=2).reshape(-1, 1)

    def take(rows):
        return jnp.einsum("bst,btd->bsd", pick, rows, preferred_element_type=f32).reshape(
            group * slots, width
        )

    def give(rows):
        return jnp.einsum(
            "bst,bsd->btd", pick, rows.reshape(group, slots, width), preferred_element_type=f32
        ).reshape(tree, width)

    h2_flat = h2.reshape(tree, width)
    e_rows = take(h2).astype(bf16)
    activated, e_gating_back = jax.vjp(
        gating, matmul(e_rows, expert_gate[0]), matmul(e_rows, expert_up[0])
    )
    activated = activated.astype(bf16)
    e_result = (matmul(activated, expert_down[0]).astype(bf16).astype(f32) * slot_gate).astype(
        bf16
    )
    s_act, s_gating_back = jax.vjp(gating, matmul(h2_flat, sg), matmul(h2_flat, su))
    s_act = s_act.astype(bf16)
    out_part = (matmul(s_act, sd) + give(e_result)).astype(bf16).reshape(group, tok_dev, width)

    e_grad = (take(g_all.reshape(group, tok_dev, width)) * slot_gate).astype(bf16)
    grad_e_act = dot_last(e_grad, expert_down[0]).astype(bf16)
    grad_e_down = dot_first(activated, e_grad).astype(bf16)
    grad_e_gate_part, grad_e_up_part = e_gating_back(grad_e_act.astype(f32))
    grad_e_gate_part = grad_e_gate_part.astype(bf16)
    grad_e_up_part = grad_e_up_part.astype(bf16)
    grad_e_gate = dot_first(e_rows, grad_e_gate_part).astype(bf16)
    grad_e_up = dot_first(e_rows, grad_e_up_part).astype(bf16)
    grad_rows = (
        dot_last(grad_e_gate_part, expert_gate[0]) + dot_last(grad_e_up_part, expert_up[0])
    ).astype(bf16)
    grad_s_act = dot_last(g_all, sd).astype(bf16)
    grad_s_down = dot_first(s_act, g_all).astype(bf16)
    grad_s_gate_part, grad_s_up_part = s_gating_back(grad_s_act.astype(f32))
    grad_s_gate_part = grad_s_gate_part.astype(bf16)
    grad_s_up_part = grad_s_up_part.astype(bf16)
    grad_s_cols = jnp.concatenate(
        [dot_first(h2_flat, grad_s_gate_part), dot_first(h2_flat, grad_s_up_part)], axis=1
    ).astype(bf16)
    second_part = (
        (give(grad_rows) + dot_last(grad_s_gate_part, sg) + dot_last(grad_s_up_part, su))
        .astype(bf16)
        .reshape(group, tok_dev, width)
    )
    out_sum = lax.psum_scatter(
        out_part.reshape(tree, width), "expert", scatter_dimension=0, tiled=True
    )
    block_out = (resid + out_sum.astype(f32)).astype(bf16)
    (second_part, grad_e_gate, grad_e_up, grad_e_down, grad_s_down, grad_s_cols) = (
        lax.optimization_barrier(
            (second_part, grad_e_gate, grad_e_up, grad_e_down, grad_s_down, grad_s_cols)
        )
    )
    grad_second = reduce_rows(second_part, 3)

    grad_e_gate = lax.psum_scatter(grad_e_gate, "dp", scatter_dimension=0, tiled=True)
    grad_e_up = lax.psum_scatter(grad_e_up, "dp", scatter_dimension=0, tiled=True)
    grad_e_down = lax.psum_scatter(grad_e_down, "dp", scatter_dimension=1, tiled=True)
    grad_s_down = lax.psum_scatter(grad_s_down[:ff_own], "dp", scatter_dimension=0, tiled=True)

    def spread_columns(grads):
        summed = lax.psum_scatter(grads, "dp", scatter_dimension=0, tiled=True)
        return lax.all_to_all(
            summed.reshape(group, rows_w, -1), "expert", split_axis=0, concat_axis=0, tiled=True
        )

    grad_s_cols = spread_columns(grad_s_cols)

    def ff_restore(cut):
        return (
            cut[:, :, :ff_own]
            .reshape(group, rows_w, spread, ff_cut)
            .transpose(1, 2, 0, 3)
            .reshape(rows_w, -1)
            .astype(f32)
        )

    grad_s_gate = ff_restore(grad_s_cols[:, :, :ff_pad])
    grad_s_up = ff_restore(grad_s_cols[:, :, ff_pad:])

    grad_f = grad_out.astype(f32)
    grad_resid_norm, grad_f_gain = second_norm_back(grad_second)
    grad_resid = grad_f + grad_resid_norm
    grad_attn_out = grad_resid.astype(bf16)
    grad_w_out = lax.psum_scatter(
        dot_first(attn_own, grad_attn_out).astype(bf16), "dp", scatter_dimension=0, tiled=True
    )
    grad_w_out = lax.psum_scatter(
        grad_w_out, "expert", scatter_dimension=0, tiled=True
    ).astype(f32)
    grad_attended = dot_last(grad_attn_out, wo).astype(bf16)
    grad_heads = lax.all_to_all(grad_attended, "expert", split_axis=1, concat_axis=0, tiled=True)
    delta = jnp.sum(
        (grad_heads.astype(f32) * attended).reshape(tree, mine, VD), axis=-1
    ).T
    grad_q, grad_kv, grad_krope = attend_back(
        reach, q_att, k_att, v_att, grad_heads, log_total, delta, scale
    )
    grad_w_exp = dot_first(ckv, grad_kv)
    lat_part = (
        jnp.concatenate([dot_last(grad_kv, we), grad_krope], axis=1)
        .astype(bf16)
        .reshape(group, tok_dev, -1)
    )
    grad_lat_sum = reduce_rows(lat_part, 5)

    def latent_parts(latent_in, gain_vec):
        return (
            norm_rows(latent_in[:, :KV], gain_vec),
            rotate(latent_in[:, KV:], own(cos_table), own(sin_table)),
        )

    unused, latent_back = jax.vjp(latent_parts, own(latent), l_gain)
    grad_latent, grad_l_gain = latent_back(
        (grad_lat_sum[:, :KV], grad_lat_sum[:, KV : KV + ROPE])
    )
    grad_latent = grad_latent.astype(bf16)
    grad_w_lat = dot_first(own(h1), grad_latent)
    grad_gains = jnp.stack(
        [
            grad_f_gain,
            jnp.pad(grad_l_gain.reshape(-1, rows_l), ((0, 0), (0, rows_w - rows_l))).reshape(width),
        ],
        axis=1,
    )
    lat_grads = lax.psum_scatter(
        jnp.concatenate(
            [grad_w_lat, jnp.pad(grad_gains, ((0, 0), (0, ROPE - 2)))], axis=1
        ).astype(bf16),
        EVERY,
        scatter_dimension=0,
        tiled=True,
    ).astype(f32)
    grad_w_lat = lat_grads[:, :lat_w]
    grad_f_gain = lat_grads[:, lat_w]
    grad_l_gain = lat_grads[:rows_l, lat_w + 1]

    grad_q_lin = (
        query_rope_back((grad_q * scale).reshape(tree, mine, KEY)).astype(bf16).reshape(tree, q_own)
    )
    grad_a_cols = jnp.concatenate(
        [dot_first(h1, grad_q_lin), grad_w_exp.reshape(width, e_fold)], axis=1
    ).astype(bf16)
    grad_a_cols = spread_columns(grad_a_cols)
    grad_w_q = (
        grad_a_cols[:, :, :q_own]
        .reshape(group, rows_w, mine, KEY)[..., : NOPE + ROPE]
        .transpose(1, 0, 2, 3)
        .reshape(rows_w, -1)
        .astype(f32)
    )
    grad_w_exp = (
        grad_a_cols[:, :, q_own:]
        .reshape(group, rows_l, e_own)
        .transpose(1, 0, 2)
        .reshape(rows_l, -1)
        .astype(f32)
    )
    grad_a_gain = (
        jnp.sum(grad_w_q * w_query.astype(f32), axis=1)
        + jnp.sum(grad_w_lat * w_latent.astype(f32), axis=1)
    ) / attn_gain.astype(f32)

    first_part = dot_last(grad_q_lin, wq).astype(bf16).reshape(group, tok_dev, width)
    grad_first = reduce_rows(first_part, 6) + dot_last(grad_latent, wl)
    unused, first_norm_back = jax.vjp(
        lambda v: norm_rows(v, a_gain), tokens_f
    )
    (grad_tokens_norm,) = first_norm_back(grad_first)
    grad_tokens = grad_resid + grad_tokens_norm
    return (
        block_out,
        grad_tokens,
        grad_a_gain,
        grad_w_q,
        grad_w_lat,
        grad_l_gain,
        grad_w_exp,
        grad_w_out,
        grad_f_gain,
        grad_s_gate,
        grad_s_up,
        grad_s_down.astype(f32),
        grad_e_gate.astype(f32)[None],
        grad_e_up.astype(f32)[None],
        grad_e_down.astype(f32)[None],
    )


def solution(mesh):
    placed = (
        P(EVERY, None),
        P(EVERY, None),
        P(EVERY, None),
        P(EVERY, None),
        P("dp", None),
        P(EVERY),
        P(EVERY, None),
        P(EVERY, None),
        P(EVERY),
        P(EVERY, None),
        P(EVERY, None),
        P(EVERY),
        P(EVERY, None),
        P(EVERY, None),
        P(EVERY, None),
        P("expert", None, None),
        P("expert", None, None),
        P("expert", None, None),
    )
    return jax.shard_map(
        per_device,
        mesh=mesh,
        in_specs=placed,
        out_specs=(
            P(EVERY, None),
            P(EVERY, None),
            P(EVERY),
            P(EVERY, None),
            P(EVERY, None),
            P(EVERY),
            P(EVERY, None),
            P(EVERY, None),
            P(EVERY),
            P(EVERY, None),
            P(EVERY, None),
            P(EVERY, None),
            P("expert", "dp", None),
            P("expert", "dp", None),
            P("expert", None, "dp"),
        ),
        check_vma=False,
    )
```

time: 3840 us -> 1290 us (0.34)
  waiting for transfers between devices: 2680 us -> 165 us
  Pallas kernels: 0 us -> 534 us
  local copies, waits for them, and re-layouts: 324 us -> 114 us
  matrix products: 465 us -> 263 us
  blocking collectives: 201 us -> 49.3 us
    reduce_scatter x12 -> x9, waiting for transfers between devices: 2350 us -> 77.4 us  [the longest x1 59.2 us: per_device(): lax.psum_scatter(grad_w_out, 'expert', scatter_dimension=0, tiled=True)]
    pallas_call x0 -> x7, Pallas kernels: none -> 534 us  [the longest x3 274 us: reduce_rows(): pl.pallas_call(functools.partial(reduce_kernel, chunks), out_shape=jax.Sh...]
    dot_general x82 -> x19, matrix products: 307 us -> 103 us  [the longest x11 76 us: matmul(): return jnp.dot(left, right, preferred_element_type=f32)]
    all_to_all x4 -> x5, waiting for transfers between devices: 226 us -> 44.7 us  [the longest x1 21.2 us: per_device(): lax.all_to_all(grad_attended, 'expert', split_axis=1, concat_axis=0, tile...]
    all_gather x1 -> x0, blocking collectives: 117 us -> none  [per_device(): lax.all_gather(rope_bf, 'expert', axis=0, tiled=True)]
    unnamed x2 -> x0, blocking collectives: 84.6 us -> none
    dynamic_update_slice x8 -> x0, local copies, waits for them, and re-layouts: 66.5 us -> none  [per_device(): lax.scan(grad_step, jnp.zeros((tok_dev, HEADS, NOPE + ROPE), jnp.float32)...]
    all_gather x8 -> x5, waiting for transfers between devices: 95.4 us -> 30 us  [the longest x1 29.9 us: per_device(): wo = lax.all_gather(w_output, EVERY, axis=0, tiled=True)]
  transfers between devices with their start and end apart: 24 -> 20, of which waited for: 14 -> 8; matrix products, arithmetic and copies ran while one was open for 16% -> 31% of each run, Pallas kernels for 0% -> 34%
where the time goes in v1:
time: 1290 us; the launch traced here: 1280 us
  Pallas kernels  534 us (41%)
  matrix products  263 us (20%)
  waiting for transfers between devices  165 us (13%)
  local copies, waits for them, and re-layouts  114 us (9%)
  other arithmetic  112 us (9%)
  blocking collectives  49.3 us (4%)
  starting transfers between devices  25.2 us (2%)
  between operations  15.8 us (1%)
    pallas_call x3, Pallas kernels, reduce_rows(): pl.pallas_call(functools.partial(reduce_kernel, chunks), out_shape=jax.Sh...  274 us
    pallas_call x2, Pallas kernels, gather_rows(): pl.pallas_call(functools.partial(gather_kernel, chunks), out_shape=jax.Sh...  208 us
    dot_general x10, matrix products, dot_last(): lax.dot_general(left, right, (((1,), (1,)), ((), ())), preferred_element_...  90.5 us
    dot_general x11, matrix products, matmul(): return jnp.dot(left, right, preferred_element_type=f32)  76 us
    dot_general x10, matrix products, dot_first(): lax.dot_general(left, right, (((0,), (0,)), ((), ())), preferred_element_...  69.2 us
    reduce_scatter x1, waiting for transfers between devices, per_device(): lax.psum_scatter(grad_w_out, 'expert', scatter_dimension=0, tiled=True)  59.2 us
    all_to_all x1, blocking collectives, per_device(): lax.all_to_all(packed, 'expert', split_axis=0, concat_axis=0, tiled=True)  49.3 us
    unnamed x166, local copies, waits for them, and re-layouts  30.8 us
  transfers between devices with their start and end apart: 20, of which 8 were waited for; matrix products, arithmetic and copies ran while one was open for 31% of the time, Pallas kernels for 34%

profile of v1, /device:TPU:0, one launch (start us, length us, event | category | flops | bytes accessed | tf_op | source)
XLA Modules:
  0.0 1278.3 jit_solution(5581007452798404223)
XLA Ops:
  18.4 49.3 %all_to_all.65 = bf16[8,64,1408]{2,1,0:T(8,128)(2,1)} all-to-all(bf16[8,64,1408]{2,1,0:T(8,128)(2,1)S(1)} %pad_maximum_fusion.4), channel_id=1, replica_groups=mesh['dp'=4,'expert'=8] {'expert'}, dimensions={0} | all-to-all | bytes 2883584 | tf_op jit(solution)/shard_map/all_to_all | solution.py:559
  74.2 108.7 %gather_rows.2 = bf16[8,256,2048]{2,1,0:T(8,128)(2,1)} custom-call(bf16[256,2048]{1,0:T(8,128)(2,1)} %x_ref.1), custom_call_target="tpu_custom_call" | custom-call | bytes 300000000 | tf_op jit(solution)/shard_map/gather_rows/pallas_call | solution.py:191
  194.0 8.8 fusion.4
  202.8 7.9 fusion.37
  214.5 7.6 fusion.53
  227.3 8.7 multiply_convert_fusion
  242.3 7.8 fusion.115
  267.4 25.4 %attend.1 = (bf16[2048,256]{1,0:T(8,128)(2,1)}, f32[2048,256]{1,0:T(8,128)}, f32[2,2048]{1,0:T(2,128)}) custom-call(s32[64]{0:T(128)} %reshape.427.reach_ref, bf16[2048,512]{1,0:T(8,128)(2,1)} %copy.289.q_ref, bf16[2048,512]{1,0:T(8,128)(2,1)} %bitcast.209, bf16[2048,256]{1,0:T(8,128)(2,1)} %copy.310.v_ref), custom_call_target="tpu_custom_call" | custom-call | tf_op jit(solution)/shard_map/attend/pallas_call | solution.py:367
  299.8 9.7 convolution_convert_fusion.12
  314.1 10.1 fusion.23
  324.2 7.6 all-to-all-done.1
  331.8 29.9 %all-gather.10.cloned.1.call-done = bf16[2048,2048]{1,0:T(8,128)(2,1)} async-done(((bf16[64,2048]{1,0:T(8,128)(2,1)}), bf16[2048,2048]{1,0:T(8,128)(2,1)}) %all-gather.10.cloned.1.call-update) | async-done | bytes 8388624 | tf_op jit(solution)/shard_map/all_gather | solution.py:580
  361.7 5.8 multiply_reduce_fusion.4
  370.2 98.9 %gather_rows.3 = bf16[8,256,2048]{2,1,0:T(8,128)(2,1)} custom-call(bf16[256,2048]{1,0:T(8,128)(2,1)} %multiply_convert_fusion.6.x_ref), custom_call_target="tpu_custom_call" | custom-call | bytes 300000000 | tf_op jit(solution)/shard_map/gather_rows/pallas_call | solution.py:191
  477.4 6.2 fusion.47
  483.6 7.8 fusion.12
  491.4 13.8 %fusion.21 = (bf16[896,1408]{1,0:T(8,128)(2,1)}, bf16[896,1408]{1,0:T(8,128)(2,1)}, f32[896,1408]{1,0:T(8,128)}) fusion(f32[896,1408]{1,0:T(8,128)} %fusion.12, bf16[896,1408]{1,0:T(8,128)(2,1)} %fusion.23, bf16[896,2048]{1,0:T(8,128)(2,1)S(1)} %bitcast.223, bf16[1,2048,1408]{2,1,0:T(8,128)(2,1)} %param.33), kind=kOutput, calls=%fused_computation.38 | convolution fusion | flops 5186306048 | bytes 27099136 | tf_op jit(solution)/shard_map/dot_general | solution.py:62
  505.2 7.8 multiply_convert_fusion.2
  513.0 8.2 fusion.67
  521.2 7.2 fusion.32
  528.5 10.2 fusion.2
  539.2 5.6 fusion.5
  544.8 7.1 convolution_convert_fusion.10
  558.0 12.4 fusion.49
  570.4 11.7 fusion.10
  582.2 8.6 add_convert_fusion
  590.8 8.2 fusion.63
  603.6 8.6 convolution_convert_fusion.2
  612.2 10.7 convolution_convert_fusion
  622.9 12.8 convolution_convert_fusion.1
  635.7 16.0 %fusion.1 = bf16[2048,2048]{1,0:T(8,128)(2,1)} fusion(f32[2048,2048]{1,0:T(8,128)} %fusion.49, f32[8,256,2048]{2,1,0:T(8,128)} %fusion.63, bf16[2048,1408]{1,0:T(8,128)(2,1)} %bitcast.232, bf16[384,2048]{0,1:T(8,128)(2,1)} %convolution_convert_fusion.12, f32[2048,384]{1,0:T(8,128)S(1)} %copy-done.22), kind=kOutput, calls=%fused_computation.2 | convolution fusion | flops 3239313408 | bytes 48234496 | tf_op jit(solution)/shard_map/dot_general | solution.py:66
  655.7 98.6 %reduce_rows.3 = f32[256,2048]{1,0:T(8,128)} custom-call(bf16[8,256,2048]{2,1,0:T(8,128)(2,1)} %bitcast.205), custom_call_target="tpu_custom_call" | custom-call | bytes 300000000 | tf_op jit(solution)/shard_map/reduce_rows/pallas_call | solution.py:295
  761.8 5.7 convolution_convert_fusion.3
  769.1 5.8 convolution_convert_fusion.13
  775.9 5.9 all-to-all-start.3
  784.7 21.2 %all-to-all-done.3 = bf16[256,8,256]{2,0,1:T(8,128)(2,1)S(1)} async-done(((bf16[256,8,256]{2,0,1:T(8,128)(2,1)}), bf16[256,8,256]{2,0,1:T(8,128)(2,1)S(1)}, u32[]{:S(2)}, u32[]{:S(2)}) %all-to-all-start.3) | async-done | bytes 1048608 | tf_op jit(solution)/shard_map/all_to_all | solution.py:755
  812.7 5.6 reduce_sum.171
  820.5 27.3 %attend_back.1 = (f32[2048,512]{1,0:T(8,128)}, bf16[2048,512]{1,0:T(8,128)(2,1)}, f32[2048,128]{1,0:T(8,128)}) custom-call(s32[64]{0:T(128)} %reshape.427.reach_ref, bf16[2048,512]{1,0:T(8,128)(2,1)} %copy.289.q_ref, bf16[2048,512]{1,0:T(8,128)(2,1)} %bitcast.210, bf16[2048,256]{1,0:T(8,128)(2,1)} %copy.310.v_ref, bf16[2048,256]{1,0:T(8,128)(2,1)} %bitcast.213, ...), custom_call_target="tpu_custom_call" | custom-call | tf_op jit(solution)/shard_map/attend_back/pallas_call | solution.py:464
  857.9 5.9 reshape.450
  884.7 6.0 maximum_convert_fusion
  891.2 9.7 convolution_convert_fusion.7
  913.4 30.8 %reduce_rows.5 = f32[256,640]{1,0:T(8,128)} custom-call(bf16[8,256,640]{2,1,0:T(8,128)(2,1)} %pad_maximum_fusion.1.p_ref), custom_call_target="tpu_custom_call" | custom-call | bytes 300000000 | tf_op jit(solution)/shard_map/reduce_rows/pallas_call | solution.py:295
  966.5 14.1 %all-to-all-done.5 = bf16[8,64,768]{2,1,0:T(8,128)(2,1)S(1)} async-done(((bf16[8,64,768]{2,1,0:T(8,128)(2,1)}), bf16[8,64,768]{2,1,0:T(8,128)(2,1)S(1)}, u32[]{:S(2)}, u32[]{:S(2)}) %all-to-all-start.5) | async-done | bytes 786464 | tf_op jit(solution)/shard_map/all_to_all | solution.py:726
  1000.4 18.1 %reduce-scatter.25.cloned.1.call-done = bf16[512,1408]{1,0:T(8,128)(2,1)} async-done(((bf16[2048,1408]{1,0:T(8,128)(2,1)}), bf16[512,1408]{1,0:T(8,128)(2,1)}) %reduce-scatter.25.cloned.1.call-update) | async-done | bytes 1441808 | tf_op jit(solution)/shard_map/reduce_scatter | solution.py:719
  1021.8 8.4 convolution_convert_fusion.4
  1030.3 144.6 %reduce_rows.4 = f32[256,2048]{1,0:T(8,128)} custom-call(bf16[8,256,2048]{2,1,0:T(8,128)(2,1)} %bitcast.216), custom_call_target="tpu_custom_call" | custom-call | bytes 300000000 | tf_op jit(solution)/shard_map/reduce_rows/pallas_call | solution.py:295
  1190.3 9.5 reduce-scatter.31.cloned.1.call-done
  1210.3 59.2 %reduce-scatter.19.cloned.1.call-done = bf16[64,2048]{1,0:T(8,128)(2,1)} async-done(((bf16[512,2048]{1,0:T(8,128)(2,1)}), bf16[64,2048]{1,0:T(8,128)(2,1)}) %reduce-scatter.19.cloned.1.call-update) | async-done | bytes 262160 | tf_op jit(solution)/shard_map/reduce_scatter | solution.py:751
  (362 shorter events, 236.9 us)
Async XLA Ops:
  7.2 183.2 %all-gather.6.cloned.1.call-start = ((), (), s32[]{:S(2)}) async-start(), calls=%async_computation.16 | async-start | bytes 2703360 | tf_op jit(solution)/shard_map/all_gather | solution.py:573
  10.4 225.6 %all-gather.8.cloned.1.call-start = ((), (), s32[]{:S(2)}) async-start(), calls=%async_computation.17 | async-start | bytes 7208960 | tf_op jit(solution)/shard_map/all_gather | solution.py:560
  18.4 50.7 %copy-start.53 = (f32[256,3]{0,1:T(4,128)S(1)}, f32[256,3]{0,1:T(4,128)}, u32[]{:S(2)}) copy-start(f32[256,3]{0,1:T(4,128)} %param.21) | copy-start | bytes 9220
  18.4 50.7 %copy-start.54 = (s32[256,3]{0,1:T(4,128)S(1)}, s32[256,3]{0,1:T(4,128)}, u32[]{:S(2)}) copy-start(s32[256,3]{0,1:T(4,128)} %param.20) | copy-start | bytes 9220
  18.4 55.7 %copy-start.56 = (s32[1,8]{1,0:T(1,128)S(1)}, s32[1,8]{1,0:T(1,128)}, u32[]{:S(2)}) copy-start(s32[1,8]{1,0:T(1,128)} %param.22) | copy-start | bytes 100
  67.7 232.0 %all-gather.12.cloned.1.call-start = ((), (), s32[]{:S(2)}) async-start(), calls=%async_computation.19 | async-start | bytes 1802240 | tf_op jit(solution)/shard_map/all_gather | solution.py:565
  68.5 231.3 %all-gather.14.cloned.1.call-start = ((), (), s32[]{:S(2)}) async-start(), calls=%async_computation.21 | async-start | bytes 9437184 | tf_op jit(solution)/shard_map/all_gather | solution.py:534
  69.7 120.2 %all-to-all-start.2 = ((f32[8,1,256]{2,1,0:T(1,128)}), f32[8,1,256]{2,1,0:T(1,128)S(1)}, u32[]{:S(2)}, u32[]{:S(2)}) async-start(f32[8,1,256]{2,1,0:T(1,128)} %copy.267), calls=%async_computation.2 | async-start | bytes 16384 | tf_op jit(solution)/shard_map/all_to_all | solution.py:648
  73.5 288.3 %all-gather.10.cloned.1.call-start = ((), (), s32[]{:S(2)}) async-start(), calls=%async_computation.18 | async-start | bytes 8650752 | tf_op jit(solution)/shard_map/all_gather | solution.py:580
  192.1 59.3 %copy-start.45 = (f32[512]{0:T(512)}, f32[512]{0:T(512)S(1)}, u32[]{:S(2)}) copy-start(f32[512]{0:T(512)S(1)} %reshape.459) | copy-start | bytes 6148
  194.0 33.3 %copy-start.41 = (f32[2048]{0:T(1024)}, f32[2048]{0:T(1024)S(1)}, u32[]{:S(2)}) copy-start(f32[2048]{0:T(1024)S(1)} %get-tuple-element.147) | copy-start | bytes 24580
  194.0 173.6 %copy-start.43 = (f32[2048]{0:T(1024)}, f32[2048]{0:T(1024)S(1)}, u32[]{:S(2)}) copy-start(f32[2048]{0:T(1024)S(1)} %get-tuple-element.146) | copy-start | bytes 24580
  222.5 33.0 %copy-start.24 = (f32[2048,32]{0,1:T(8,128)}, f32[2048,32]{0,1:T(8,128)S(1)}, u32[]{:S(2)}) copy-start(f32[2048,32]{0,1:T(8,128)S(1)} %copy.258) | copy-start | bytes 786436
  226.2 25.2 %copy-start.51 = (f32[2048]{0:T(1024)}, f32[2048]{0:T(1024)S(1)}, u32[]{:S(2)}) copy-start(f32[2048]{0:T(1024)S(1)} %add_rsqrt_fusion) | copy-start | bytes 24580
  295.2 36.7 %all-to-all-start.1 = ((bf16[8,256,256]{1,2,0:T(8,128)(2,1)}), bf16[8,256,256]{1,2,0:T(8,128)(2,1)S(1)}, u32[]{:S(2)}, u32[]{:S(2)}) async-start(bf16[8,256,256]{1,2,0:T(8,128)(2,1)} %copy.266), calls=%async_computation.1 | async-start | bytes 2097152 | tf_op jit(solution)/shard_map/all_to_all | solution.py:637
  299.7 456.9 %reduce-scatter.13.cloned.1.call-start = ((), (), s32[]{:S(2)}) async-start(), calls=%async_computation.20 | async-start | bytes 9437184 | tf_op jit(solution)/shard_map/reduce_scatter | solution.py:708
  314.1 47.6 %copy-start.6 = (bf16[256,2048]{1,0:T(8,128)(2,1)S(1)}, bf16[256,2048]{1,0:T(8,128)(2,1)}, u32[]{:S(2)}) copy-start(bf16[256,2048]{1,0:T(8,128)(2,1)} %x_ref.1) | copy-start | bytes 3145732
  331.8 35.8 %copy-start.8 = (bf16[8,256,256]{1,2,0:T(8,128)(2,1)}, bf16[8,256,256]{1,2,0:T(8,128)(2,1)S(1)}, u32[]{:S(2)}) copy-start(bf16[8,256,256]{1,2,0:T(8,128)(2,1)S(1)} %all-to-all-done.1) | copy-start | bytes 3145732
  367.6 101.5 %copy-start.49 = (f32[256]{0:T(256)}, f32[256]{0:T(256)S(1)}, u32[]{:S(2)}) copy-start(f32[256]{0:T(256)S(1)} %get-tuple-element.186) | copy-start | bytes 3076
  367.6 101.5 %copy-start.47 = (f32[256]{0:T(256)}, f32[256]{0:T(256)S(1)}, u32[]{:S(2)}) copy-start(f32[256]{0:T(256)S(1)} %fusion.98) | copy-start | bytes 3076
  370.2 103.8 %slice-start.6 = ((s8[5767168]{0:T(1024)(128)(4,1)}), s8[1572864]{0:T(1024)(128)(4,1)S(1)}, s32[]{:S(2)}) async-start(s8[5767168]{0:T(1024)(128)(4,1)} %bitcast.234), calls=%async_computation.37 | async-start | bytes 3145728
  469.1 14.4 %slice-start.10 = ((s8[5767168]{0:T(1024)(128)(4,1)}), s8[1572864]{0:T(1024)(128)(4,1)S(1)}, s32[]{:S(2)}) async-start(s8[5767168]{0:T(1024)(128)(4,1)} %bitcast.266), calls=%async_computation.41 | async-start | bytes 3145728
  473.9 17.5 %copy-start.11 = (bf16[8,112,2048]{2,1,0:T(8,128)(2,1)}, bf16[8,112,2048]{2,1,0:T(8,128)(2,1)S(1)}, u32[]{:S(2)}) copy-start(bf16[8,112,2048]{2,1,0:T(8,128)(2,1)S(1)} %convolution_convert_fusion.5) | copy-start | bytes 11010052
  483.6 21.6 %slice-start.8 = ((s8[5767168]{0:T(1024)(128)(4,1)}), s8[4194304]{0:T(1024)(128)(4,1)S(1)}, s32[]{:S(2)}) async-start(s8[5767168]{0:T(1024)(128)(4,1)} %bitcast.264), calls=%async_computation.39 | async-start | bytes 8388608
  538.7 418.5 %reduce-scatter.21.cloned.1.call-start = ((), (), s32[]{:S(2)}) async-start(), calls=%async_computation.25 | async-start | bytes 3932160 | tf_op jit(solution)/shard_map/reduce_scatter | solution.py:725
  558.0 24.2 %slice-start.12 = ((s8[5767168]{0:T(1024)(128)(4,1)}), s8[4194304]{0:T(1024)(128)(4,1)S(1)}, s32[]{:S(2)}) async-start(s8[5767168]{0:T(1024)(128)(4,1)} %bitcast.268), calls=%async_computation.43 | async-start | bytes 8388608
  570.4 28.6 %slice-start.2 = ((s8[8388608]{0:T(1024)(128)(4,1)}), s8[4194304]{0:T(1024)(128)(4,1)S(1)}, s32[]{:S(2)}) async-start(s8[8388608]{0:T(1024)(128)(4,1)} %bitcast.207), calls=%async_computation.33 | async-start | bytes 8388608
  582.2 16.9 %slice-start.3 = ((s8[8388608]{0:T(1024)(128)(4,1)}), s8[4194304]{0:T(1024)(128)(4,1)S(1)}, s32[]{:S(2)}) async-start(s8[8388608]{0:T(1024)(128)(4,1)} %bitcast.207), calls=%async_computation.34 | async-start | bytes 8388608
  651.7 312.8 %reduce-scatter.23.cloned.1.call-start = ((), (), s32[]{:S(2)}) async-start(), calls=%async_computation.26 | async-start | bytes 1802240 | tf_op jit(solution)/shard_map/reduce_scatter | solution.py:722
  654.3 339.6 %reduce-scatter.29.cloned.1.call-start = ((), (), s32[]{:S(2)}) async-start(), calls=%async_computation.29 | async-start | bytes 7208960 | tf_op jit(solution)/shard_map/reduce_scatter | solution.py:721
  655.1 342.2 %reduce-scatter.27.cloned.1.call-start = ((), (), s32[]{:S(2)}) async-start(), calls=%async_computation.28 | async-start | bytes 7208960 | tf_op jit(solution)/shard_map/reduce_scatter | solution.py:720
  655.7 98.7 %copy-start.2 = (f32[256,2048]{1,0:T(8,128)S(1)}, f32[256,2048]{1,0:T(8,128)}, u32[]{:S(2)}) copy-start(f32[256,2048]{1,0:T(8,128)} %copy-done.1) | copy-start | bytes 6291460
  655.7 98.7 %copy-start.44 = (f32[2048]{0:T(1024)S(1)}, f32[2048]{0:T(1024)}, u32[]{:S(2)}) copy-start(f32[2048]{0:T(1024)} %copy-done.43) | copy-start | bytes 24580
  655.7 98.7 %copy-start.48 = (f32[256]{0:T(256)S(1)}, f32[256]{0:T(256)}, u32[]{:S(2)}) copy-start(f32[256]{0:T(256)} %copy-done.47) | copy-start | bytes 3076
  655.7 344.7 %reduce-scatter.17.cloned.1.call-start = ((), (), s32[]{:S(2)}) async-start(), calls=%async_computation.23 | async-start | bytes 10485760 | tf_op jit(solution)/shard_map/reduce_scatter | solution.py:748
  767.5 251.1 %reduce-scatter.25.cloned.1.call-start = ((), (), s32[]{:S(2)}) async-start(), calls=%async_computation.27 | async-start | bytes 7208960 | tf_op jit(solution)/shard_map/reduce_scatter | solution.py:719
  775.9 30.0 %all-to-all-start.3 = ((bf16[256,8,256]{2,0,1:T(8,128)(2,1)}), bf16[256,8,256]{2,0,1:T(8,128)(2,1)S(1)}, u32[]{:S(2)}, u32[]{:S(2)}) async-start(bf16[256,8,256]{2,0,1:T(8,128)(2,1)} %bitcast.240), calls=%async_computation.4 | async-start | bytes 2097152 | tf_op jit(solution)/shard_map/all_to_all | solution.py:755
  781.8 397.8 %reduce-scatter.15.cloned.1.call-start = ((), (), s32[]{:S(2)}) async-start(), calls=%async_computation.22 | async-start | bytes 3276800 | tf_op jit(solution)/shard_map/reduce_scatter | solution.py:725
  820.5 27.3 %copy-start.46 = (f32[512]{0:T(512)S(1)}, f32[512]{0:T(512)}, u32[]{:S(2)}) copy-start(f32[512]{0:T(512)} %copy-done.45) | copy-start | bytes 6148
  820.5 27.3 %copy-start.52 = (f32[2048]{0:T(1024)S(1)}, f32[2048]{0:T(1024)}, u32[]{:S(2)}) copy-start(f32[2048]{0:T(1024)} %copy-done.51) | copy-start | bytes 24580
  902.6 297.1 %reduce-scatter.31.cloned.1.call-start = ((), (), s32[]{:S(2)}) async-start(), calls=%async_computation.30 | async-start | bytes 2703360
  959.5 21.1 %all-to-all-start.5 = ((bf16[8,64,768]{2,1,0:T(8,128)(2,1)}), bf16[8,64,768]{2,1,0:T(8,128)(2,1)S(1)}, u32[]{:S(2)}, u32[]{:S(2)}) async-start(bf16[8,64,768]{2,1,0:T(8,128)(2,1)} %bitcast.51), calls=%async_computation.10 | async-start | bytes 1572864 | tf_op jit(solution)/shard_map/all_to_all | solution.py:726
  964.1 305.4 %reduce-scatter.19.cloned.1.call-start = ((), (), s32[]{:S(2)}) async-start(), calls=%async_computation.24 | async-start | bytes 2359296 | tf_op jit(solution)/shard_map/reduce_scatter | solution.py:751
  1030.2 144.6 %copy-start.7 = (bf16[256,2048]{1,0:T(8,128)(2,1)S(1)}, bf16[256,2048]{1,0:T(8,128)(2,1)}, u32[]{:S(2)}) copy-start(bf16[256,2048]{1,0:T(8,128)(2,1)} %x_ref.1) | copy-start | bytes 3145732
  1030.2 144.6 %copy-start.18 = (f32[256,512]{1,0:T(8,128)S(1)}, f32[256,512]{1,0:T(8,128)}, u32[]{:S(2)}) copy-start(f32[256,512]{1,0:T(8,128)} %copy-done.17) | copy-start | bytes 1572868
  1030.3 144.6 %copy-start.42 = (f32[2048]{0:T(1024)S(1)}, f32[2048]{0:T(1024)}, u32[]{:S(2)}) copy-start(f32[2048]{0:T(1024)} %copy-done.41) | copy-start | bytes 24580
  1181.9 22.7 %all-to-all-start.4 = ((bf16[8,64,640]{2,1,0:T(8,128)(2,1)}), bf16[8,64,640]{2,1,0:T(8,128)(2,1)}, u32[]{:S(2)}, u32[]{:S(2)}) async-start(bf16[8,64,640]{2,1,0:T(8,128)(2,1)} %bitcast.242), calls=%async_computation.6 | async-start | bytes 1310720 | tf_op jit(solution)/shard_map/all_to_all | solution.py:726
  1209.5 61.7 %copy-start.23 = (f32[64,3072]{1,0:T(8,128)}, f32[64,3072]{1,0:T(8,128)S(1)}, u32[]{:S(2)}) copy-start(f32[64,3072]{1,0:T(8,128)S(1)} %reshape.461) | copy-start | bytes 2359300
  (47 other events, 293.8 us)
Sparse Core Ops, SparseCore 0:
  11.5 64.5 all-gather.5
  77.7 42.3 all-gather.7
  121.6 18.9 all-gather.11
  142.6 129.0 all-gather.13
  274.5 87.1 all-gather.9
  538.8 158.6 reduce-scatter.12
  700.3 40.9 reduce-scatter.20
  744.4 27.3 reduce-scatter.22
  774.5 54.8 reduce-scatter.28
  831.8 54.8 reduce-scatter.26
  889.5 71.7 reduce-scatter.16
  963.6 54.8 reduce-scatter.24
  1021.2 34.6 reduce-scatter.14
  1058.1 141.6 reduce-scatter.30
  1203.1 66.2 reduce-scatter.18

commit v2 on v1

--- a/solution.py
+++ b/solution.py
@@ -90,48 +90,55 @@
     pl.semaphore_wait(barrier, 1 + (a + last - 1) // last + (2 * last - 1 - a) // last)
 
 
-def gather_kernel(chunks, x_ref, o_ref, sx, rx, su, ru, sd, rd):
-    rank = lax.axis_index("expert")
-    last = o_ref.shape[0] // 2 - 1
-    a = rank // 2
-    side = rank + 1 - 2 * (rank % 2)
-    rows = x_ref.shape[0] // chunks
-    greet(rank, last)
-
-    def piece(ref, c):
-        return ref.at[pl.ds(c * rows, rows)]
-
-    def to(src, block, c, send, recv, target):
+class Chain:
+    def __init__(self, chunks, x_ref, o_ref, sx, rx, su, ru, sd, rd):
+        self.chunks, self.x, self.o = chunks, x_ref, o_ref
+        self.sems = (sx, rx, su, ru, sd, rd)
+        self.rank = lax.axis_index("expert")
+        self.last = o_ref.shape[0] // 2 - 1
+        self.a = self.rank // 2
+        self.side = self.rank + 1 - 2 * (self.rank % 2)
+        self.rows = x_ref.shape[0] // chunks
+
+    def piece(self, ref, c):
+        return ref.at[pl.ds(c * self.rows, self.rows)]
+
+    def to(self, src, block, c, send, recv, target):
         return pltpu.make_async_remote_copy(
             src_ref=src,
-            dst_ref=piece(o_ref.at[block], c),
+            dst_ref=self.piece(self.o.at[block], c),
             send_sem=send,
             recv_sem=recv,
             device_id={"expert": target},
             device_id_type=MESH,
         )
 
-    for c in range(chunks):
-        own = piece(x_ref, c)
-        to(own, rank, c, sx.at[0, c], rx.at[0, c], side).start()
-
-        @pl.when(a < last)
-        def _():
-            to(own, rank, c, su.at[0, c], ru.at[0, c], rank + 2).start()
-
-        @pl.when(a > 0)
-        def _():
-            to(own, rank, c, sd.at[0, c], rd.at[0, c], rank - 2).start()
-
-    for s in range(1, last + 1):
-        for c in range(chunks):
+    def start(self):
+        sx, rx, su, ru, sd, rd = self.sems
+        rank, a, last, to = self.rank, self.a, self.last, self.to
+        for c in range(self.chunks):
+            own = self.piece(self.x, c)
+            to(own, rank, c, sx.at[0, c], rx.at[0, c], self.side).start()
+
+            @pl.when(a < last)
+            def _():
+                to(own, rank, c, su.at[0, c], ru.at[0, c], rank + 2).start()
+
+            @pl.when(a > 0)
+            def _():
+                to(own, rank, c, sd.at[0, c], rd.at[0, c], rank - 2).start()
+
+    def step(self, s):
+        sx, rx, su, ru, sd, rd = self.sems
+        rank, a, last, to = self.rank, self.a, self.last, self.to
+        for c in range(self.chunks):
 
             @pl.when(a >= s)
             def _():
                 block = rank - 2 * s
-                src = piece(o_ref.at[block], c)
+                src = self.piece(self.o.at[block], c)
                 to(src, block, c, su.at[s - 1, c], ru.at[s - 1, c], rank + 2).wait_recv()
-                to(src, block, c, sx.at[s, c], rx.at[s, c], side).start()
+                to(src, block, c, sx.at[s, c], rx.at[s, c], self.side).start()
 
                 @pl.when(a < last)
                 def _():
@@ -140,66 +147,212 @@
             @pl.when(a + s <= last)
             def _():
                 block = rank + 2 * s
-                src = piece(o_ref.at[block], c)
+                src = self.piece(self.o.at[block], c)
                 to(src, block, c, sd.at[s - 1, c], rd.at[s - 1, c], rank - 2).wait_recv()
-                to(src, block, c, sx.at[last + s, c], rx.at[last + s, c], side).start()
+                to(src, block, c, sx.at[last + s, c], rx.at[last + s, c], self.side).start()
 
                 @pl.when(a > 0)
                 def _():
                     to(src, block, c, sd.at[s, c], rd.at[s, c], rank - 2).start()
 
-    o_ref[rank] = x_ref[...]
-    for c in range(chunks):
-        own = piece(x_ref, c)
-        to(own, side, c, sx.at[0, c], rx.at[0, c], side).wait()
-
-        @pl.when(a < last)
-        def _():
-            to(own, rank, c, su.at[0, c], ru.at[0, c], rank + 2).wait_send()
-
-        @pl.when(a > 0)
-        def _():
-            to(own, rank, c, sd.at[0, c], rd.at[0, c], rank - 2).wait_send()
-
-    for s in range(1, last + 1):
-        for c in range(chunks):
-
-            @pl.when(a >= s)
+    def finish(self):
+        sx, rx, su, ru, sd, rd = self.sems
+        rank, a, last, to, side = self.rank, self.a, self.last, self.to, self.side
+        for c in range(self.chunks):
+            own = self.piece(self.x, c)
+            to(own, side, c, sx.at[0, c], rx.at[0, c], side).wait()
+
+            @pl.when(a < last)
             def _():
-                block = rank - 2 * s
-                src = piece(o_ref.at[block], c)
-                to(src, side - 2 * s, c, sx.at[s, c], rx.at[s, c], side).wait()
-
-                @pl.when(a < last)
+                to(own, rank, c, su.at[0, c], ru.at[0, c], rank + 2).wait_send()
+
+            @pl.when(a > 0)
+            def _():
+                to(own, rank, c, sd.at[0, c], rd.at[0, c], rank - 2).wait_send()
+
+        for s in range(1, last + 1):
+            for c in range(self.chunks):
+
+                @pl.when(a >= s)
                 def _():
-                    to(src, block, c, su.at[s, c], ru.at[s, c], rank + 2).wait_send()
-
-            @pl.when(a + s <= last)
-            def _():
-                block = rank + 2 * s
-                src = piece(o_ref.at[block], c)
-                to(src, side + 2 * s, c, sx.at[last + s, c], rx.at[last + s, c], side).wait()
-
-                @pl.when(a > 0)
+                    block = rank - 2 * s
+                    src = self.piece(self.o.at[block], c)
+                    to(src, side - 2 * s, c, sx.at[s, c], rx.at[s, c], side).wait()
+
+                    @pl.when(a < last)
+                    def _():
+                        to(src, block, c, su.at[s, c], ru.at[s, c], rank + 2).wait_send()
+
+                @pl.when(a + s <= last)
                 def _():
-                    to(src, block, c, sd.at[s, c], rd.at[s, c], rank - 2).wait_send()
-
-
-def gather_rows(x, count, call_id, chunks=2):
+                    block = rank + 2 * s
+                    src = self.piece(self.o.at[block], c)
+                    to(src, side + 2 * s, c, sx.at[last + s, c], rx.at[last + s, c], side).wait()
+
+                    @pl.when(a > 0)
+                    def _():
+                        to(src, block, c, sd.at[s, c], rd.at[s, c], rank - 2).wait_send()
+
+
+def chain_sems(count, chunks):
     half = count // 2
     dma = pltpu.SemaphoreType.DMA
+    return [dma((2 * half, chunks))] * 2 + [dma((half, chunks))] * 4
+
+
+def gather_kernel(chunks, x_ref, o_ref, *sems):
+    chain = Chain(chunks, x_ref, o_ref, *sems)
+    greet(chain.rank, chain.last)
+    chain.start()
+    o_ref[chain.rank] = x_ref[...]
+    for s in range(1, chain.last + 1):
+        chain.step(s)
+    chain.finish()
+
+
+def prologue_kernel(
+    chunks,
+    x_ref,
+    w_ref,
+    d_ref,
+    t_ref,
+    o_ref,
+    pk_ref,
+    do_ref,
+    to_ref,
+    wa_s,
+    wa_r,
+    ta_s,
+    ta_r,
+    wp_s,
+    wp_r,
+    dp_s,
+    dp_r,
+    *sems,
+):
+    group, spread = o_ref.shape[0], pk_ref.shape[0]
+    chain = Chain(chunks, x_ref, o_ref, *sems)
+    rank, line = chain.rank, lax.axis_index("dp")
+    barrier = pltpu.get_barrier_semaphore()
+    for k in range(1, group):
+        pl.semaphore_signal(
+            barrier,
+            inc=1,
+            device_id={"expert": lax.rem(rank + k, group)},
+            device_id_type=MESH,
+        )
+    for k in range(1, spread):
+        pl.semaphore_signal(
+            barrier, inc=1, device_id={"dp": lax.rem(line + k, spread)}, device_id_type=MESH
+        )
+    pl.semaphore_wait(barrier, group + spread - 2)
+
+    def cut(k):
+        peer = lax.rem(rank + k, group)
+        return pltpu.make_async_remote_copy(
+            src_ref=w_ref.at[peer],
+            dst_ref=pk_ref.at[line, rank],
+            send_sem=wa_s.at[k - 1],
+            recv_sem=wa_r.at[k - 1],
+            device_id={"expert": peer},
+            device_id_type=MESH,
+        )
+
+    def gates(k):
+        peer = lax.rem(rank + k, group)
+        return pltpu.make_async_remote_copy(
+            src_ref=t_ref.at[peer],
+            dst_ref=to_ref.at[rank],
+            send_sem=ta_s.at[k - 1],
+            recv_sem=ta_r.at[k - 1],
+            device_id={"expert": peer},
+            device_id_type=MESH,
+        )
+
+    def along(src, dst, send, recv, k):
+        return pltpu.make_async_remote_copy(
+            src_ref=src,
+            dst_ref=dst,
+            send_sem=send.at[k - 1],
+            recv_sem=recv.at[k - 1],
+            device_id={"dp": lax.rem(line + k, spread)},
+            device_id_type=MESH,
+        )
+
+    for k in range(1, group):
+        cut(k).start()
+        gates(k).start()
+    chain.start()
+    for k in range(1, spread):
+        along(d_ref, do_ref.at[line], dp_s, dp_r, k).start()
+    pk_ref[line, rank] = w_ref[rank]
+    do_ref[line] = d_ref[...]
+    to_ref[rank] = t_ref[rank]
+    o_ref[rank] = x_ref[...]
+    for k in range(1, group):
+        cut(k).wait_recv()
+    for k in range(1, spread):
+        along(pk_ref.at[line], pk_ref.at[line], wp_s, wp_r, k).start()
+    for s in range(1, chain.last + 1):
+        chain.step(s)
+    chain.finish()
+    for k in range(1, group):
+        cut(k).wait_send()
+        gates(k).wait()
+    for k in range(1, spread):
+        along(d_ref, do_ref.at[line], dp_s, dp_r, k).wait()
+        along(pk_ref.at[line], pk_ref.at[line], wp_s, wp_r, k).wait()
+
+
+def prologue(x, cuts, down, gates, spread, call_id, chunks=2):
+    group = cuts.shape[0]
+    dma = pltpu.SemaphoreType.DMA
+    vmem = pl.BlockSpec(memory_space=pltpu.VMEM)
+    return pl.pallas_call(
+        functools.partial(prologue_kernel, chunks),
+        out_shape=[
+            jax.ShapeDtypeStruct((group,) + x.shape, x.dtype),
+            jax.ShapeDtypeStruct((spread,) + cuts.shape, cuts.dtype),
+            jax.ShapeDtypeStruct((spread,) + down.shape, down.dtype),
+            jax.ShapeDtypeStruct(gates.shape, gates.dtype),
+        ],
+        in_specs=[vmem] * 4,
+        out_specs=[vmem] * 4,
+        scratch_shapes=[dma((group - 1,))] * 4
+        + [dma((spread - 1,))] * 4
+        + chain_sems(group, chunks),
+        compiler_params=pltpu.CompilerParams(
+            collective_id=call_id, has_side_effects=True, vmem_limit_bytes=VMEM_LIMIT
+        ),
+        cost_estimate=WIRE,
+        name="prologue",
+    )(x, cuts, down, gates)
+
+
+def gather_rows(x, count, call_id, chunks=2):
     return pl.pallas_call(
         functools.partial(gather_kernel, chunks),
         out_shape=jax.ShapeDtypeStruct((count,) + x.shape, x.dtype),
         in_specs=[pl.BlockSpec(memory_space=pltpu.VMEM)],
         out_specs=pl.BlockSpec(memory_space=pltpu.VMEM),
-        scratch_shapes=[dma((2 * half, chunks))] * 2 + [dma((half, chunks))] * 4,
+        scratch_shapes=chain_sems(count, chunks),
         compiler_params=pltpu.CompilerParams(
             collective_id=call_id, has_side_effects=True, vmem_limit_bytes=VMEM_LIMIT
         ),
         cost_estimate=WIRE,
         name="gather_rows",
     )(x)
+
+
+def ring_pairs(group):
+    half = group // 2
+    side = [(r, r + 1 - 2 * (r % 2)) for r in range(group)]
+    onward = [(2 * a + b, 2 * ((a + 1) % half) + b) for a in range(half) for b in range(2)]
+    return side, onward
+
+
+def tie(*values):
+    return lax.optimization_barrier(values)
 
 
 def reduce_kernel(chunks, p_ref, o_ref, rx, st, ru, rd, acc, sxs, rxs, sus, rus, sds, rds):
@@ -304,6 +457,107 @@
         cost_estimate=WIRE,
         name="reduce_rows",
     )(p)
+
+
+def swap_halves(values):
+    lane = lax.broadcasted_iota(jnp.int32, values.shape, 1)
+    half = ROPE // 2
+    return jnp.where(lane < half, pltpu.roll(values, KEY - NOPE - half, 1), pltpu.roll(values, half, 1))
+
+
+def turns(seg_cos, seg_sin, off_cos, off_sin):
+    lane = lax.broadcasted_iota(jnp.int32, off_cos.shape, 1)
+    sine = seg_sin * off_cos + seg_cos * off_sin
+    return seg_cos * off_cos - seg_sin * off_sin, jnp.where(lane < ROPE // 2, -sine, sine)
+
+
+def project_kernel(
+    heads,
+    x_ref,
+    wq_ref,
+    wl_ref,
+    we_ref,
+    ag_ref,
+    lg_ref,
+    sc_ref,
+    ss_ref,
+    oc_ref,
+    os_ref,
+    h1_ref,
+    q_ref,
+    k_ref,
+    v_ref,
+    lat_ref,
+    ckv_ref,
+):
+    i = pl.program_id(0)
+    x = x_ref[...].astype(f32)
+    power = jnp.mean(x * x, axis=-1, keepdims=True)
+    h1 = (x * lax.rsqrt(power + epsilon) * ag_ref[...]).astype(bf16)
+    h1_ref[...] = h1
+    cosine, sine = turns(sc_ref[pl.ds(i, 1)], ss_ref[pl.ds(i, 1)], oc_ref[...], os_ref[...])
+
+    def turn(values):
+        return (values * cosine + swap_halves(values) * sine).astype(bf16)
+
+    query = matmul(h1, wq_ref[...])
+    for h in range(heads):
+        at = h * KEY
+        q_ref[:, at : at + NOPE] = query[:, at : at + NOPE].astype(bf16)
+        q_ref[:, at + NOPE : at + KEY] = turn(query[:, at + NOPE : at + KEY])
+    latent = matmul(h1, wl_ref[...])
+    lat_ref[...] = latent
+    low = latent[:, :KV]
+    power = jnp.mean(low * low, axis=-1, keepdims=True)
+    ckv = (low * lax.rsqrt(power + epsilon) * lg_ref[...]).astype(bf16)
+    ckv_ref[...] = ckv
+    krope = turn(latent[:, KV:])
+    kv = matmul(ckv, we_ref[...]).astype(bf16)
+    for h in range(heads):
+        at = h * KEY
+        k_ref[:, at : at + NOPE] = kv[:, at : at + NOPE]
+        k_ref[:, at + NOPE : at + KEY] = krope
+        v_ref[:, h * VD : (h + 1) * VD] = kv[:, at + NOPE : at + KEY]
+
+
+def project(x, packed, lat_pack, we, a_gain, l_gain, tables, heads):
+    tree, width = x.shape
+    segs = tree // SEG
+    lat_width = lat_pack.shape[1]
+    fixed = lambda arr: pl.BlockSpec(arr.shape, lambda i: (0, 0))
+    part = lambda cols: pl.BlockSpec((SEG, cols), lambda i: (i, 0))
+    return pl.pallas_call(
+        functools.partial(project_kernel, heads),
+        grid=(segs,),
+        in_specs=[
+            part(width),
+            pl.BlockSpec((width, heads * KEY), lambda i: (0, 0)),
+            fixed(lat_pack),
+            fixed(we),
+            fixed(a_gain),
+            fixed(l_gain),
+        ]
+        + [fixed(table) for table in tables],
+        out_specs=[
+            part(width),
+            part(heads * KEY),
+            part(heads * KEY),
+            part(heads * VD),
+            part(lat_width),
+            part(KV),
+        ],
+        out_shape=[
+            jax.ShapeDtypeStruct((tree, width), bf16),
+            jax.ShapeDtypeStruct((tree, heads * KEY), bf16),
+            jax.ShapeDtypeStruct((tree, heads * KEY), bf16),
+            jax.ShapeDtypeStruct((tree, heads * VD), bf16),
+            jax.ShapeDtypeStruct((tree, lat_width), f32),
+            jax.ShapeDtypeStruct((tree, KV), bf16),
+        ],
+        compiler_params=pltpu.CompilerParams(vmem_limit_bytes=VMEM_LIMIT),
+        cost_estimate=pl.CostEstimate(flops=0, bytes_accessed=60_000_000, transcendentals=0),
+        name="project",
+    )(x, packed, lat_pack, we, a_gain, l_gain, *tables)
 
 
 def triangle():
@@ -387,6 +641,7 @@
             jax.ShapeDtypeStruct((heads, tree), f32),
         ],
         compiler_params=pltpu.CompilerParams(vmem_limit_bytes=VMEM_LIMIT),
+        cost_estimate=pl.CostEstimate(flops=0, bytes_accessed=70_000_000, transcendentals=0),
         name="attend",
     )(reach, q, k, v)
 
@@ -400,20 +655,36 @@
     k_ref,
     v_ref,
     g_ref,
+    att_ref,
     log_ref,
-    delta_ref,
-    dq_ref,
+    we_ref,
+    sc_ref,
+    ss_ref,
+    oc_ref,
+    os_ref,
+    gq_ref,
     dkv_ref,
-    dr_ref,
+    lat_ref,
+    dq_s,
     dk_s,
     dv_s,
+    delta_s,
 ):
     j = pl.program_id(0)
     diag = triangle()
 
     @pl.when(j == 0)
     def _():
-        dq_ref[...] = jnp.zeros_like(dq_ref)
+        def prepare(i, carry):
+            rows = pl.ds(i * SEG, SEG)
+            for h in range(heads):
+                vcols = slice(h * VD, (h + 1) * VD)
+                both = g_ref[rows, vcols].astype(f32) * att_ref[rows, vcols]
+                delta_s[h : h + 1, rows] = jnp.sum(both.T, axis=0, keepdims=True)
+            dq_s[rows] = jnp.zeros((SEG, heads * KEY), f32)
+            return carry
+
+        lax.fori_loop(0, segs, prepare, 0)
 
     dk_s[...] = jnp.zeros_like(dk_s)
     dv_s[...] = jnp.zeros_like(dv_s)
@@ -431,10 +702,10 @@
             if masked:
                 w = jnp.where(diag, w, 0.0)
             dw = dot_last(v_ref[:, vcols], g)
-            ds = (w * (dw - delta_ref[h : h + 1, rows])).astype(bf16)
+            ds = (w * (dw - delta_s[h : h + 1, rows])).astype(bf16)
             dv_s[h] += matmul(w.astype(bf16), g)
             dk_s[h] += matmul(ds, q)
-            dq_ref[rows, kcols] += dot_first(ds, k)
+            dq_s[rows, kcols] += dot_first(ds, k)
 
     block(j, True)
 
@@ -451,16 +722,36 @@
         dkv_ref[:, h * KEY : h * KEY + NOPE] = (dk_s[h, :, :NOPE] * scale).astype(bf16)
         dkv_ref[:, h * KEY + NOPE : (h + 1) * KEY] = dv_s[h].astype(bf16)
         rope = rope + dk_s[h, :, NOPE:]
-    dr_ref[...] = rope * scale
-
-
-def attend_back(reach, q, k, v, g, log_total, delta, scale):
+    lat_ref[:, :KV] = dot_last(dkv_ref[...], we_ref[...]).astype(bf16)
+    lat_ref[:, KV:] = (rope * scale).astype(bf16)
+
+    @pl.when(j == segs - 1)
+    def _():
+        def finish(i, carry):
+            rows = pl.ds(i * SEG, SEG)
+            cosine, sine = turns(
+                sc_ref[pl.ds(i, 1)], ss_ref[pl.ds(i, 1)], oc_ref[...], os_ref[...]
+            )
+            for h in range(heads):
+                at = h * KEY
+                gq_ref[rows, at : at + NOPE] = (dq_s[rows, at : at + NOPE] * scale).astype(bf16)
+                turned = dq_s[rows, at + NOPE : at + KEY] * scale
+                gq_ref[rows, at + NOPE : at + KEY] = (
+                    turned * cosine - swap_halves(turned) * sine
+                ).astype(bf16)
+            return carry
+
+        lax.fori_loop(0, segs, finish, 0)
+
+
+def attend_back(reach, q, k, v, g, attended, log_total, we, tables, scale):
     tree = q.shape[0]
     segs = tree // SEG
     heads = q.shape[1] // KEY
     whole = lambda width: pl.BlockSpec((tree, width), lambda j, r: (0, 0))
     part = lambda width: pl.BlockSpec((SEG, width), lambda j, r: (j, 0))
-    lane = pl.BlockSpec((heads, tree), lambda j, r: (0, 0))
+    fixed = lambda arr: pl.BlockSpec(arr.shape, lambda j, r: (0, 0))
+    lat_width = KV + KEY - NOPE
     return pl.pallas_call(
         functools.partial(attend_back_kernel, heads, segs, scale),
         grid_spec=pltpu.PrefetchScalarGridSpec(
@@ -471,23 +762,28 @@
                 part(heads * KEY),
                 part(heads * VD),
                 whole(heads * VD),
-                lane,
-                lane,
-            ],
-            out_specs=[whole(heads * KEY), part(heads * KEY), part(KEY - NOPE)],
+                whole(heads * VD),
+                fixed(log_total),
+                fixed(we),
+            ]
+            + [fixed(table) for table in tables],
+            out_specs=[whole(heads * KEY), part(heads * KEY), part(lat_width)],
             scratch_shapes=[
+                pltpu.VMEM((tree, heads * KEY), f32),
                 pltpu.VMEM((heads, SEG, KEY), f32),
                 pltpu.VMEM((heads, SEG, VD), f32),
+                pltpu.VMEM((heads, tree), f32),
             ],
         ),
         out_shape=[
-            jax.ShapeDtypeStruct((tree, heads * KEY), f32),
             jax.ShapeDtypeStruct((tree, heads * KEY), bf16),
-            jax.ShapeDtypeStruct((tree, KEY - NOPE), f32),
+            jax.ShapeDtypeStruct((tree, heads * KEY), bf16),
+            jax.ShapeDtypeStruct((tree, lat_width), bf16),
         ],
         compiler_params=pltpu.CompilerParams(vmem_limit_bytes=VMEM_LIMIT),
+        cost_estimate=pl.CostEstimate(flops=0, bytes_accessed=90_000_000, transcendentals=0),
         name="attend_back",
-    )(reach, q, k, v, g, log_total, delta)
+    )(reach, q, k, v, g, attended, log_total, we, *tables)
 
 
 def per_device(
@@ -530,9 +826,6 @@
     e_own = mine * (NOPE + VD)
     e_fold = rows_l * e_own // rows_w
 
-    x_all = gather_rows(tokens, group, 0).reshape(tree, width)
-    g_all = lax.all_gather(grad_out, "expert", axis=0, tiled=True)
-
     wq_cut = jnp.pad(
         w_query.reshape(rows_w, group, mine, NOPE + ROPE),
         ((0, 0), (0, 0), (0, 0), (0, KEY - NOPE - ROPE)),
@@ -556,14 +849,22 @@
         ],
         axis=2,
     )
-    packed = lax.all_to_all(packed, "expert", split_axis=0, concat_axis=0, tiled=True)
-    packed = lax.all_gather(packed, "dp", axis=0, tiled=True).reshape(width, -1)
+    expert_ids = jnp.arange(group, dtype=jnp.int32)
+    gate_of = jnp.sum(
+        jnp.where(routes[:, :, None] == expert_ids[None, None, :], gate_values[:, :, None], 0.0),
+        axis=1,
+    ).T
+    gate_of = jnp.broadcast_to(gate_of[:, None, :], (group, 8, tok_dev))
+    x_all, packed, sd, gate_of = prologue(tokens, packed, shared_down, gate_of, spread, 0)
+    x_all, parents, gate_of = lax.optimization_barrier(
+        (x_all.reshape(tree, width), parents, gate_of[:, 0])
+    )
+    packed = packed.reshape(width, -1)
     wq = packed[:, :q_own]
     we = packed[:, q_own : q_own + e_fold].reshape(KV, e_own)
     sg = packed[:, q_own + e_fold : q_own + e_fold + ff_pad]
     su = packed[:, q_own + e_fold + ff_pad :]
-    sd = lax.all_gather(shared_down, "dp", axis=0, tiled=True)
-    sd = jnp.pad(sd, ((0, ff_pad - ff_own), (0, 0)))
+    sd = jnp.pad(sd.reshape(ff_own, width), ((0, ff_pad - ff_own), (0, 0)))
 
     lat_w = KV + ROPE
     gains = jnp.stack(
@@ -578,74 +879,78 @@
     f_gain = lat_pack[:, lat_w + 1].astype(f32)
     l_gain = lat_pack[:, lat_w + 2].reshape(-1, rows_w)[:, :rows_l].reshape(KV).astype(f32)
     wo = lax.all_gather(w_output, EVERY, axis=0, tiled=True)
-
     reachable = ancestry(parents[0], segs)
     depth = jnp.sum(reachable, axis=1) - 1.0
     reach = reachable.astype(jnp.int32).reshape(segs * segs)
-    positions = (depth[:, None] * SEG + jnp.arange(SEG, dtype=f32)[None, :]).reshape(tree)
     half_width = ROPE // 2
     freq = 10000.0 ** (-2.0 * jnp.arange(half_width, dtype=f32) / ROPE)
-    angle = positions[:, None] * freq[None, :]
-    cos_table = jnp.cos(angle)
-    sin_table = jnp.sin(angle)
+    seg_angle = (depth * SEG)[:, None] * freq[None, :]
+    off_angle = jnp.arange(SEG, dtype=f32)[:, None] * freq[None, :]
+
+    def lanes(values):
+        return jnp.pad(
+            jnp.concatenate([values, values], axis=1), ((0, 0), (0, KEY - NOPE - ROPE))
+        )
+
+    tables = [
+        lanes(jnp.cos(seg_angle)),
+        lanes(jnp.sin(seg_angle)),
+        lanes(jnp.cos(off_angle)),
+        lanes(jnp.sin(off_angle)),
+    ]
+    seg_cos = lax.dynamic_slice_in_dim(tables[0], rank, 1, 0)[:, :half_width]
+    seg_sin = lax.dynamic_slice_in_dim(tables[1], rank, 1, 0)[:, :half_width]
+    off_cos = tables[2][:, :half_width]
+    off_sin = tables[3][:, :half_width]
+    own_cos = seg_cos * off_cos - seg_sin * off_sin
+    own_sin = seg_sin * off_cos + seg_cos * off_sin
 
     def own(values):
         return lax.dynamic_slice_in_dim(values, rank * tok_dev, tok_dev, 0)
 
-    h1 = norm_rows(x_all.astype(f32), a_gain).astype(bf16)
-    query = matmul(h1, wq).reshape(tree, mine, KEY)
-
-    def query_rope(query_in):
-        return jnp.concatenate(
-            [
-                query_in[..., :NOPE],
-                rotate(
-                    query_in[..., NOPE : NOPE + ROPE], cos_table[:, None, :], sin_table[:, None, :]
-                ),
-                jnp.zeros(query_in.shape[:-1] + (KEY - NOPE - ROPE,), f32),
-            ],
-            axis=-1,
-        )
-
-    def query_rope_back(grad):
-        return jnp.concatenate(
-            [
-                grad[..., :NOPE],
-                rotate(
-                    grad[..., NOPE : NOPE + ROPE], cos_table[:, None, :], -sin_table[:, None, :]
-                ),
-                jnp.zeros(grad.shape[:-1] + (KEY - NOPE - ROPE,), f32),
-            ],
-            axis=-1,
-        )
-
-    q_att = query_rope(query).astype(bf16).reshape(tree, q_own)
-    latent = matmul(h1, wl)
-    ckv = norm_rows(latent[:, :KV], l_gain).astype(bf16)
-    krope = rotate(latent[:, KV:], cos_table, sin_table).astype(bf16)
-    kv = matmul(ckv, we).astype(bf16).reshape(tree, mine, NOPE + VD)
-    k_att = jnp.concatenate(
-        [
-            kv[..., :NOPE],
-            jnp.broadcast_to(krope[:, None, :], (tree, mine, ROPE)),
-            jnp.zeros((tree, mine, KEY - NOPE - ROPE), bf16),
-        ],
-        axis=-1,
-    ).reshape(tree, q_own)
-    v_att = kv[..., NOPE:].reshape(tree, mine * VD)
+    h1, q_att, k_att, v_att, latent, ckv = project(
+        x_all, packed, lat_pack, we, a_gain[None], l_gain[None], tables, mine
+    )
+    side, ring = ring_pairs(group)
+
+    def across(values):
+        return lax.ppermute(values, "expert", side)
+
+    def onward(values):
+        return lax.ppermute(values, "expert", ring)
+
+    def sum_with(mine, *others):
+        total = mine.astype(f32)
+        for other in others:
+            total = total + other.astype(f32)
+        return total
+
+    q_att, g0 = tie(q_att, grad_out)
+    g1, g0_side = onward(g0), across(g0)
     attn_heads, attended, log_total = attend(reach, q_att, k_att, v_att, scale)
+    attn_heads, g1, g0_side = tie(attn_heads, g1, g0_side)
+    g2, g1_side = onward(g1), across(g1)
     attn_own = lax.all_to_all(attn_heads, "expert", split_axis=0, concat_axis=1, tiled=True)
+    attn_own, g2, g1_side = tie(attn_own, g2, g1_side)
+    g3, g2_side = onward(g2), across(g2)
     tokens_f = tokens.astype(f32)
     resid = tokens_f + matmul(attn_own, wo)
     second_normed, second_norm_back = jax.vjp(norm_rows, resid, f_gain)
-
-    h2 = gather_rows(second_normed.astype(bf16), group, 2)
-    expert_ids = jnp.arange(group, dtype=jnp.int32)
-    gate_of = jnp.sum(
-        jnp.where(routes[:, :, None] == expert_ids[None, None, :], gate_values[:, :, None], 0.0),
-        axis=1,
-    )
-    gate_of = lax.all_to_all(gate_of.T, "expert", split_axis=0, concat_axis=0, tiled=True)
+    h0, g3, g2_side = tie(second_normed.astype(bf16), g3, g2_side)
+
+    half = group // 2
+    h1_back, h0_side = tie(onward(h0), across(h0))
+    h2_back, h1_side, g3_side = onward(h1_back), across(h1_back), across(g3)
+    gate_of = jnp.concatenate(
+        [
+            lax.dynamic_slice_in_dim(
+                gate_of, 2 * lax.rem(rank // 2 - s + half, half) + lax.rem(rank + k, 2), 1, 0
+            )
+            for s in range(half)
+            for k in range(2)
+        ],
+        axis=0,
+    )
     routed = gate_of > 0.0
     upto = (
         jnp.arange(tok_dev, dtype=jnp.int32)[:, None]
@@ -655,79 +960,112 @@
     chosen = (
         place[:, None, :] == jnp.arange(slots, dtype=jnp.int32)[None, :, None]
     ) & routed[:, None, :]
-    pick = chosen.astype(bf16)
-    slot_gate = jnp.sum(jnp.where(chosen, gate_of[:, None, :], 0.0), axis=2).reshape(-1, 1)
-
-    def take(rows):
-        return jnp.einsum("bst,btd->bsd", pick, rows, preferred_element_type=f32).reshape(
-            group * slots, width
-        )
-
-    def give(rows):
-        return jnp.einsum(
-            "bst,bsd->btd", pick, rows.reshape(group, slots, width), preferred_element_type=f32
-        ).reshape(tree, width)
-
-    h2_flat = h2.reshape(tree, width)
-    e_rows = take(h2).astype(bf16)
-    activated, e_gating_back = jax.vjp(
-        gating, matmul(e_rows, expert_gate[0]), matmul(e_rows, expert_up[0])
-    )
-    activated = activated.astype(bf16)
-    e_result = (matmul(activated, expert_down[0]).astype(bf16).astype(f32) * slot_gate).astype(
-        bf16
-    )
-    s_act, s_gating_back = jax.vjp(gating, matmul(h2_flat, sg), matmul(h2_flat, su))
-    s_act = s_act.astype(bf16)
-    out_part = (matmul(s_act, sd) + give(e_result)).astype(bf16).reshape(group, tok_dev, width)
-
-    e_grad = (take(g_all.reshape(group, tok_dev, width)) * slot_gate).astype(bf16)
-    grad_e_act = dot_last(e_grad, expert_down[0]).astype(bf16)
+    pick_all = chosen.astype(bf16)
+    gates_all = jnp.sum(jnp.where(chosen, gate_of[:, None, :], 0.0), axis=2)
+
+    def experts(s, h2, g_rows):
+        pick = pick_all[2 * s : 2 * s + 2]
+        slot_gate = gates_all[2 * s : 2 * s + 2].reshape(2 * slots, 1)
+
+        def take(rows):
+            return jnp.einsum("bst,btd->bsd", pick, rows, preferred_element_type=f32).reshape(
+                2 * slots, width
+            )
+
+        def give(rows):
+            return jnp.einsum(
+                "bst,bsd->btd", pick, rows.reshape(2, slots, width), preferred_element_type=f32
+            ).reshape(2 * tok_dev, width)
+
+        h2 = jnp.stack(h2)
+        e_rows = take(h2).astype(bf16)
+        activated, e_gating_back = jax.vjp(
+            gating, matmul(e_rows, expert_gate[0]), matmul(e_rows, expert_up[0])
+        )
+        activated = activated.astype(bf16)
+        e_result = (
+            matmul(activated, expert_down[0]).astype(bf16).astype(f32) * slot_gate
+        ).astype(bf16)
+        h2 = h2.reshape(2 * tok_dev, width)
+        s_act, s_gating_back = jax.vjp(gating, matmul(h2, sg), matmul(h2, su))
+        s_act = s_act.astype(bf16)
+        out_part = (matmul(s_act, sd) + give(e_result)).astype(bf16)
+
+        g_rows = jnp.stack(g_rows)
+        e_grad = (take(g_rows) * slot_gate).astype(bf16)
+        g_rows = g_rows.reshape(2 * tok_dev, width)
+        grad_e_act = dot_last(e_grad, expert_down[0]).astype(bf16)
+        grad_gate_part, grad_up_part = e_gating_back(grad_e_act.astype(f32))
+        grad_gate_part = grad_gate_part.astype(bf16)
+        grad_up_part = grad_up_part.astype(bf16)
+        grad_rows = (
+            dot_last(grad_gate_part, expert_gate[0]) + dot_last(grad_up_part, expert_up[0])
+        ).astype(bf16)
+        grad_s_act = dot_last(g_rows, sd).astype(bf16)
+        grad_s_gate_part, grad_s_up_part = s_gating_back(grad_s_act.astype(f32))
+        grad_s_gate_part = grad_s_gate_part.astype(bf16)
+        grad_s_up_part = grad_s_up_part.astype(bf16)
+        second_part = (
+            give(grad_rows) + dot_last(grad_s_gate_part, sg) + dot_last(grad_s_up_part, su)
+        ).astype(bf16)
+        return (
+            out_part[:tok_dev],
+            out_part[tok_dev:],
+            second_part[:tok_dev],
+            second_part[tok_dev:],
+            (
+                e_rows,
+                activated,
+                e_grad,
+                grad_gate_part,
+                grad_up_part,
+                h2,
+                s_act,
+                g_rows,
+                jnp.concatenate([grad_s_gate_part, grad_s_up_part], axis=1),
+            ),
+        )
+
+    o0, o0_far, n0, n0_far, kept0 = experts(0, (h0, h0_side), (g0, g0_side))
+    n0, h2_back, h1_side, g3_side = tie(n0, h2_back, h1_side, g3_side)
+    h3_back, h2_side = onward(h2_back), across(h2_back)
+    o1, o1_far, n1, n1_far, kept1 = experts(1, (h1_back, h1_side), (g1, g1_side))
+    n1, n1_far, h3_back, h2_side = tie(n1, n1_far, h3_back, h2_side)
+    h3_side, n1_in = across(h3_back), across(n1_far)
+    o2, o2_far, n2, n2_far, kept2 = experts(2, (h2_back, h2_side), (g2, g2_side))
+    n2, n2_far, h3_side, n1_in = tie(n2, n2_far, h3_side, n1_in)
+    ring1, n2_in = onward(sum_with(n1, n1_in).astype(bf16)), across(n2_far)
+    o3, o3_far, n3, n3_far, kept3 = experts(3, (h3_back, h3_side), (g3, g3_side))
+    kept = [kept0, kept1, kept2, kept3]
+    n3, n3_far, ring1, n2_in = tie(n3, n3_far, ring1, n2_in)
+    ring2, n3_in = onward(sum_with(n2, n2_in, ring1).astype(bf16)), across(n3_far)
+    e_rows, activated, e_grad, grad_gate_part, grad_up_part = (
+        jnp.concatenate([pieces[k] for pieces in kept], axis=0) for k in range(5)
+    )
+    grad_e_gate = dot_first(e_rows, grad_gate_part).astype(bf16)
+    grad_e_up = dot_first(e_rows, grad_up_part).astype(bf16)
+    grad_e_gate, grad_e_up, ring2, n3_in, activated = tie(
+        grad_e_gate, grad_e_up, ring2, n3_in, activated
+    )
+    ring3, n0_in = onward(sum_with(n3, n3_in, ring2).astype(bf16)), across(n0_far)
     grad_e_down = dot_first(activated, e_grad).astype(bf16)
-    grad_e_gate_part, grad_e_up_part = e_gating_back(grad_e_act.astype(f32))
-    grad_e_gate_part = grad_e_gate_part.astype(bf16)
-    grad_e_up_part = grad_e_up_part.astype(bf16)
-    grad_e_gate = dot_first(e_rows, grad_e_gate_part).astype(bf16)
-    grad_e_up = dot_first(e_rows, grad_e_up_part).astype(bf16)
-    grad_rows = (
-        dot_last(grad_e_gate_part, expert_gate[0]) + dot_last(grad_e_up_part, expert_up[0])
-    ).astype(bf16)
-    grad_s_act = dot_last(g_all, sd).astype(bf16)
-    grad_s_down = dot_first(s_act, g_all).astype(bf16)
-    grad_s_gate_part, grad_s_up_part = s_gating_back(grad_s_act.astype(f32))
-    grad_s_gate_part = grad_s_gate_part.astype(bf16)
-    grad_s_up_part = grad_s_up_part.astype(bf16)
-    grad_s_cols = jnp.concatenate(
-        [dot_first(h2_flat, grad_s_gate_part), dot_first(h2_flat, grad_s_up_part)], axis=1
-    ).astype(bf16)
-    second_part = (
-        (give(grad_rows) + dot_last(grad_s_gate_part, sg) + dot_last(grad_s_up_part, su))
-        .astype(bf16)
-        .reshape(group, tok_dev, width)
-    )
-    out_sum = lax.psum_scatter(
-        out_part.reshape(tree, width), "expert", scatter_dimension=0, tiled=True
-    )
-    block_out = (resid + out_sum.astype(f32)).astype(bf16)
-    (second_part, grad_e_gate, grad_e_up, grad_e_down, grad_s_down, grad_s_cols) = (
-        lax.optimization_barrier(
-            (second_part, grad_e_gate, grad_e_up, grad_e_down, grad_s_down, grad_s_cols)
-        )
-    )
-    grad_second = reduce_rows(second_part, 3)
+    grad_s_down = sum(dot_first(pieces[6], pieces[7]) for pieces in kept).astype(bf16)
+    grad_s_cols = sum(dot_first(pieces[5], pieces[8]) for pieces in kept).astype(bf16)
+    grad_e_down, grad_s_down, grad_s_cols, ring3, n0_in, o1_far, o2_far, o3_far, o0_far = tie(
+        grad_e_down, grad_s_down, grad_s_cols, ring3, n0_in, o1_far, o2_far, o3_far, o0_far
+    )
+    grad_second = sum_with(n0, n0_in, ring3)
+    o1_in = across(o1_far)
 
     grad_e_gate = lax.psum_scatter(grad_e_gate, "dp", scatter_dimension=0, tiled=True)
     grad_e_up = lax.psum_scatter(grad_e_up, "dp", scatter_dimension=0, tiled=True)
     grad_e_down = lax.psum_scatter(grad_e_down, "dp", scatter_dimension=1, tiled=True)
     grad_s_down = lax.psum_scatter(grad_s_down[:ff_own], "dp", scatter_dimension=0, tiled=True)
 
-    def spread_columns(grads):
-        summed = lax.psum_scatter(grads, "dp", scatter_dimension=0, tiled=True)
-        return lax.all_to_all(
-            summed.reshape(group, rows_w, -1), "expert", split_axis=0, concat_axis=0, tiled=True
-        )
-
-    grad_s_cols = spread_columns(grad_s_cols)
+    def sum_columns(grads):
+        return lax.psum_scatter(grads, "dp", scatter_dimension=0, tiled=True)
+
+    grad_s_cols = sum_columns(grad_s_cols)
 
     def ff_restore(cut):
         return (
@@ -738,39 +1076,33 @@
             .astype(f32)
         )
 
-    grad_s_gate = ff_restore(grad_s_cols[:, :, :ff_pad])
-    grad_s_up = ff_restore(grad_s_cols[:, :, ff_pad:])
-
     grad_f = grad_out.astype(f32)
     grad_resid_norm, grad_f_gain = second_norm_back(grad_second)
     grad_resid = grad_f + grad_resid_norm
     grad_attn_out = grad_resid.astype(bf16)
-    grad_w_out = lax.psum_scatter(
-        dot_first(attn_own, grad_attn_out).astype(bf16), "dp", scatter_dimension=0, tiled=True
-    )
-    grad_w_out = lax.psum_scatter(
-        grad_w_out, "expert", scatter_dimension=0, tiled=True
-    ).astype(f32)
+    grad_w_out = dot_first(attn_own, grad_attn_out).astype(bf16)
     grad_attended = dot_last(grad_attn_out, wo).astype(bf16)
+    grad_attended, grad_w_out, o1_in = tie(grad_attended, grad_w_out, o1_in)
+    ring1, o2_in = onward(sum_with(o1, o1_in).astype(bf16)), across(o2_far)
     grad_heads = lax.all_to_all(grad_attended, "expert", split_axis=1, concat_axis=0, tiled=True)
-    delta = jnp.sum(
-        (grad_heads.astype(f32) * attended).reshape(tree, mine, VD), axis=-1
-    ).T
-    grad_q, grad_kv, grad_krope = attend_back(
-        reach, q_att, k_att, v_att, grad_heads, log_total, delta, scale
-    )
+    grad_heads, grad_e_gate, ring1, o2_in = tie(grad_heads, grad_e_gate, ring1, o2_in)
+    ring2, o3_in = onward(sum_with(o2, o2_in, ring1).astype(bf16)), across(o3_far)
+    grad_w_out = lax.psum_scatter(grad_w_out, "dp", scatter_dimension=0, tiled=True)
+    grad_q_lin, grad_kv, lat_part = attend_back(
+        reach, q_att, k_att, v_att, grad_heads, attended, log_total, we, tables, scale
+    )
+    lat_part, grad_e_up, ring2, o3_in = tie(lat_part, grad_e_up, ring2, o3_in)
+    ring3, o0_in = onward(sum_with(o3, o3_in, ring2).astype(bf16)), across(o0_far)
     grad_w_exp = dot_first(ckv, grad_kv)
-    lat_part = (
-        jnp.concatenate([dot_last(grad_kv, we), grad_krope], axis=1)
-        .astype(bf16)
-        .reshape(group, tok_dev, -1)
-    )
-    grad_lat_sum = reduce_rows(lat_part, 5)
+    lat_part = lat_part.reshape(group, tok_dev, -1)
+    grad_lat_sum = reduce_rows(lat_part, 5, 2)
+    grad_lat_sum, ring3, o0_in = tie(grad_lat_sum, ring3, o0_in)
+    block_out = (resid + sum_with(o0, o0_in, ring3)).astype(bf16)
 
     def latent_parts(latent_in, gain_vec):
         return (
             norm_rows(latent_in[:, :KV], gain_vec),
-            rotate(latent_in[:, KV:], own(cos_table), own(sin_table)),
+            rotate(latent_in[:, KV : KV + ROPE], own_cos, own_sin),
         )
 
     unused, latent_back = jax.vjp(latent_parts, own(latent), l_gain)
@@ -778,7 +1110,7 @@
         (grad_lat_sum[:, :KV], grad_lat_sum[:, KV : KV + ROPE])
     )
     grad_latent = grad_latent.astype(bf16)
-    grad_w_lat = dot_first(own(h1), grad_latent)
+    grad_w_lat = dot_first(own(h1), grad_latent)[:, :KV + ROPE]
     grad_gains = jnp.stack(
         [
             grad_f_gain,
@@ -790,21 +1122,38 @@
         jnp.concatenate(
             [grad_w_lat, jnp.pad(grad_gains, ((0, 0), (0, ROPE - 2)))], axis=1
         ).astype(bf16),
-        EVERY,
+        "dp",
         scatter_dimension=0,
         tiled=True,
-    ).astype(f32)
-    grad_w_lat = lat_grads[:, :lat_w]
-    grad_f_gain = lat_grads[:, lat_w]
-    grad_l_gain = lat_grads[:rows_l, lat_w + 1]
-
-    grad_q_lin = (
-        query_rope_back((grad_q * scale).reshape(tree, mine, KEY)).astype(bf16).reshape(tree, q_own)
-    )
+    )
+
     grad_a_cols = jnp.concatenate(
         [dot_first(h1, grad_q_lin), grad_w_exp.reshape(width, e_fold)], axis=1
     ).astype(bf16)
-    grad_a_cols = spread_columns(grad_a_cols)
+    grad_a_cols = sum_columns(grad_a_cols)
+    first_part = dot_last(grad_q_lin, wq).astype(bf16).reshape(group, tok_dev, width)
+    first_part, grad_e_down, grad_s_down, grad_s_cols = lax.optimization_barrier(
+        (first_part, grad_e_down, grad_s_down, grad_s_cols)
+    )
+    first_sum = reduce_rows(first_part, 6)
+    first_sum, rest, cols = lax.optimization_barrier(
+        (
+            first_sum,
+            jnp.concatenate([grad_w_out, lat_grads], axis=1),
+            jnp.concatenate([grad_s_cols, grad_a_cols], axis=1),
+        )
+    )
+    cols = lax.all_to_all(
+        cols.reshape(group, rows_w, -1), "expert", split_axis=0, concat_axis=0, tiled=True
+    )
+    rest = reduce_rows(rest.reshape(group, rows_w, -1), 7, max(1, rows_w // 32))
+    grad_w_out = rest[:, :width]
+    grad_w_lat = rest[:, width : width + lat_w]
+    grad_f_gain = rest[:, width + lat_w]
+    grad_l_gain = rest[:rows_l, width + lat_w + 1]
+    grad_s_gate = ff_restore(cols[:, :, :ff_pad])
+    grad_s_up = ff_restore(cols[:, :, ff_pad : 2 * ff_pad])
+    grad_a_cols = cols[:, :, 2 * ff_pad :]
     grad_w_q = (
         grad_a_cols[:, :, :q_own]
         .reshape(group, rows_w, mine, KEY)[..., : NOPE + ROPE]
@@ -824,8 +1173,7 @@
         + jnp.sum(grad_w_lat * w_latent.astype(f32), axis=1)
     ) / attn_gain.astype(f32)
 
-    first_part = dot_last(grad_q_lin, wq).astype(bf16).reshape(group, tok_dev, width)
-    grad_first = reduce_rows(first_part, 6) + dot_last(grad_latent, wl)
+    grad_first = first_sum + dot_last(grad_latent[:, :lat_w], wl)
     unused, first_norm_back = jax.vjp(
         lambda v: norm_rows(v, a_gain), tokens_f
     )

time: 1290 us -> 1040 us (0.81)
  Pallas kernels: 534 us -> 399 us
  matrix products: 263 us -> 212 us
  blocking collectives: 49.3 us -> 0 us
  waiting for transfers between devices: 165 us -> 210 us
  local copies, waits for them, and re-layouts: 114 us -> 71.6 us
  other arithmetic: 112 us -> 82.8 us
  starting transfers between devices: 25.2 us -> 42.9 us
    ppermute x0 -> x28, waiting for transfers between devices: none -> 199 us  [the longest x16 107 us: across(): return lax.ppermute(values, 'expert', side)]
    pallas_call x3, Pallas kernels: 274 us -> 181 us  [reduce_rows(): pl.pallas_call(functools.partial(reduce_kernel, chunks), out_shape=jax.Sh...]
    reduce_scatter x5 -> x4, waiting for transfers between devices: 59.2 us -> 0.01 us  [the longest x2 0.01 us: sum_columns(): return lax.psum_scatter(grads, 'dp', scatter_dimension=0, tiled=True)]
    all_to_all x1 -> x0, blocking collectives: 49.3 us -> none  [per_device(): lax.all_to_all(packed, 'expert', split_axis=0, concat_axis=0, tiled=True)]
    pallas_call x2, Pallas kernels: 208 us -> 166 us  [the longest x1 146 us: prologue(): pl.pallas_call(functools.partial(prologue_kernel, chunks), out_shape=[jax...]
    all_gather x1, waiting for transfers between devices: 29.9 us -> 0.01 us  [per_device(): wo = lax.all_gather(w_output, EVERY, axis=0, tiled=True)]
    ppermute x0 -> x28, starting transfers between devices: none -> 28.5 us  [the longest x16 20.1 us: across(): return lax.ppermute(values, 'expert', side)]
    dot_general x11 -> x26, matrix products: 76 us -> 48.8 us  [matmul(): return jnp.dot(left, right, preferred_element_type=f32)]
  transfers between devices with their start and end apart: 20 -> 41, of which waited for: 8 -> 18; matrix products, arithmetic and copies ran while one was open for 31% -> 27% of each run, Pallas kernels for 34% -> 39%
where the time goes in v2:
time: 1040 us
  Pallas kernels  399 us (38%)
  matrix products  212 us (20%)
  waiting for transfers between devices  210 us (20%)
  other arithmetic  82.8 us (8%)
  local copies, waits for them, and re-layouts  71.6 us (7%)
  starting transfers between devices  42.9 us (4%)
  between operations  16.6 us (2%)
    pallas_call x3, Pallas kernels, reduce_rows(): pl.pallas_call(functools.partial(reduce_kernel, chunks), out_shape=jax.Sh...  181 us
    pallas_call x1, Pallas kernels, prologue(): pl.pallas_call(functools.partial(prologue_kernel, chunks), out_shape=[jax...  146 us
    ppermute x16, waiting for transfers between devices, across(): return lax.ppermute(values, 'expert', side)  107 us
    ppermute x12, waiting for transfers between devices, onward(): return lax.ppermute(values, 'expert', ring)  92.2 us
    dot_general x27, matrix products, dot_last(): lax.dot_general(left, right, (((1,), (1,)), ((), ())), preferred_element_...  77 us
    dot_general x15, matrix products, dot_first(): lax.dot_general(left, right, (((0,), (0,)), ((), ())), preferred_element_...  64.9 us
    dot_general x26, matrix products, matmul(): return jnp.dot(left, right, preferred_element_type=f32)  48.8 us
    pallas_call x1, Pallas kernels, attend_back(): pl.pallas_call(functools.partial(attend_back_kernel, heads, segs, scale),...  29 us
  transfers between devices with their start and end apart: 41, of which 18 were waited for; matrix products, arithmetic and copies ran while one was open for 27% of the time, Pallas kernels for 39%

profile of v2, /device:TPU:0, one launch (start us, length us, event | category | flops | bytes accessed | tf_op | source)
XLA Modules:
  0.0 1035.4 jit_solution(8641390226537754576)
XLA Ops:
  19.9 145.8 %prologue.1 = (bf16[8,256,2048]{2,1,0:T(8,128)(2,1)}, bf16[4,8,64,1408]{3,2,1,0:T(8,128)(2,1)}, bf16[4,88,2048]{2,1,0:T(8,128)(2,1)}, f32[8,8,256]{2,1,0:T(8,128)}) custom-call(bf16[256,2048]{1,0:T(8,128)(2,1)} %x_ref.1, bf16[8,64,1408]{2,1,0:T(8,128)(2,1)} %pad_maximum_fusion.12.w_ref, bf16[88,2048]{1,0:T(8,128)(2,1)} %d_ref.1, ...), custom_call_target="tpu_custom_call" | custom-call | bytes 300000000 | tf_op jit(solution)/shard_map/prologue/pallas_call | solution.py:311
  177.6 20.4 %project.1 = (bf16[2048,2048]{1,0:T(8,128)(2,1)}, bf16[2048,512]{1,0:T(8,128)(2,1)}, bf16[2048,512]{1,0:T(8,128)(2,1)}, bf16[2048,256]{1,0:T(8,128)(2,1)}, f32[2...) custom-call(bf16[2048,2048]{1,0:T(8,128)(2,1)} %bitcast.432, bf16[2048,1408]{1,0:T(8,128)(2,1)} %bitcast.385, ...), custom_call_target="tpu_custom_call" | custom-call | bytes 60000000 | tf_op jit(solution)/shard_map/project/pallas_call | solution.py:529
  201.7 22.3 %attend.1 = (bf16[2048,256]{1,0:T(8,128)(2,1)}, f32[2048,256]{1,0:T(8,128)}, f32[2,2048]{1,0:T(2,128)}) custom-call(s32[64]{0:T(128)} %reshape.426.reach_ref, bf16[2048,512]{1,0:T(8,128)(2,1)} %get-tuple-element.104.q_ref, bf16[2048,512]{1,0:T(8,128)(2,1)} %get-tuple-element.105.k_ref, bf16[2048,256]{1,0:T(8,128)(2,1)} %get-tuple-element.106.v_ref), custom_call_target="tpu_custom_call" | custom-call | bytes 70000000 | tf_op jit(solution)/shard_map/attend/pallas_call | solution.py:621
  226.7 5.0 all-to-all-start
  245.4 28.8 %collective-permute-done.2 = bf16[256,2048]{1,0:T(8,128)(2,1)S(1)} collective-permute-done((bf16[256,2048]{1,0:T(8,128)(2,1)}, bf16[256,2048]{1,0:T(8,128)(2,1)S(1)}, u32[]{:S(2)}, u32[]{:S(2)}) %collective-permute-start.2) | collective-permute-done | bytes 1048608 | tf_op jit(solution)/shard_map/ppermute | solution.py:920
  275.2 3.8 all-to-all-done
  281.9 4.1 multiply_convert_fusion.3
  290.9 5.8 multiply_reduce_fusion.2
  297.0 6.5 collective-permute-done.4
  317.5 10.9 %collective-permute-done.6 = bf16[256,2048]{1,0:T(8,128)(2,1)S(1)} collective-permute-done((bf16[256,2048]{1,0:T(8,128)(2,1)S(1)}, bf16[256,2048]{1,0:T(8,128)(2,1)S(1)}, u32[]{:S(2)}, u32[]{:S(2)}) %collective-permute-start.6) | collective-permute-done | bytes 1048608 | tf_op jit(solution)/shard_map/ppermute | solution.py:920
  328.5 3.4 collective-permute-done.7
  345.7 4.6 fusion.92
  355.0 19.4 %collective-permute-done.9 = bf16[256,2048]{1,0:T(8,128)(2,1)S(1)} collective-permute-done((bf16[256,2048]{1,0:T(8,128)(2,1)S(1)}, bf16[256,2048]{1,0:T(8,128)(2,1)S(1)}, u32[]{:S(2)}, u32[]{:S(2)}) %collective-permute-start.9) | collective-permute-done | bytes 1048608 | tf_op jit(solution)/shard_map/ppermute | solution.py:917
  388.0 4.6 fusion.89
  398.1 3.5 multiply_convert_fusion.1
  401.5 5.6 fusion.116
  418.9 4.6 fusion.86
  429.4 21.1 %collective-permute-done.13 = bf16[256,2048]{1,0:T(8,128)(2,1)S(1)} collective-permute-done((bf16[256,2048]{1,0:T(8,128)(2,1)S(1)}, bf16[256,2048]{1,0:T(8,128)(2,1)S(1)}, u32[]{:S(2)}, u32[]{:S(2)}) %collective-permute-start.13) | collective-permute-done | bytes 1048608 | tf_op jit(solution)/shard_map/ppermute | solution.py:917
  450.5 18.8 %collective-permute-done.14 = bf16[256,2048]{1,0:T(8,128)(2,1)S(1)} collective-permute-done((bf16[256,2048]{1,0:T(8,128)(2,1)S(1)}, bf16[256,2048]{1,0:T(8,128)(2,1)S(1)}, u32[]{:S(2)}, u32[]{:S(2)}) %collective-permute-start.14) | collective-permute-done | bytes 1048608 | tf_op jit(solution)/shard_map/ppermute | solution.py:917
  481.9 4.6 fusion.83
  495.3 8.6 convolution_convert_fusion.2
  503.9 11.5 %collective-permute-done.15 = bf16[256,2048]{1,0:T(8,128)(2,1)} collective-permute-done((bf16[256,2048]{1,0:T(8,128)(2,1)}, bf16[256,2048]{1,0:T(8,128)(2,1)}, u32[]{:S(2)}, u32[]{:S(2)}) %collective-permute-start.15) | collective-permute-done | bytes 1048608 | tf_op jit(solution)/shard_map/ppermute | solution.py:920
  515.4 3.6 add_convert_fusion.7
  519.4 10.1 convolution_convert_fusion.1
  529.5 12.3 %collective-permute-done.17 = bf16[256,2048]{1,0:T(8,128)(2,1)} collective-permute-done((bf16[256,2048]{1,0:T(8,128)(2,1)}, bf16[256,2048]{1,0:T(8,128)(2,1)}, u32[]{:S(2)}, u32[]{:S(2)}) %collective-permute-start.17) | collective-permute-done | bytes 1048608 | tf_op jit(solution)/shard_map/ppermute | solution.py:920
  554.2 4.3 fusion.128
  598.7 5.3 add_convert_fusion
  604.0 4.8 add_convert_fusion.6
  608.7 10.4 %convolution_convert_fusion = bf16[1408,2048]{1,0:T(8,128)(2,1)} fusion(bf16[896,1408]{1,0:T(8,128)(2,1)S(1)} %copy-done.38, bf16[224,2048]{1,0:T(8,128)(2,1)} %fusion.186, bf16[224,2048]{1,0:T(8,128)(2,1)} %fusion.187, bf16[224,2048]{1,0:T(8,128)(2,1)} %fusion.188, bf16[224,2048]{1,0:T(8,128)(2,1)S(1)} %copy-done.71), kind=kOutput, calls=%fused_computation | convolution fusion | flops 5184946176 | bytes 11960320 | tf_op jit(solution)/shard_map/dot_general | solution.py:70
  619.1 11.7 %collective-permute-done.19 = bf16[256,2048]{1,0:T(8,128)(2,1)S(1)} collective-permute-done((bf16[256,2048]{1,0:T(8,128)(2,1)}, bf16[256,2048]{1,0:T(8,128)(2,1)S(1)}, u32[]{:S(2)}, u32[]{:S(2)}) %collective-permute-start.19) | collective-permute-done | bytes 1048608 | tf_op jit(solution)/shard_map/ppermute | solution.py:920
  641.5 5.6 convolution_convert_fusion.4
  647.1 6.4 convolution_convert_fusion.6
  654.6 3.6 all-to-all-start.1
  664.0 24.2 %collective-permute-done.23 = bf16[256,2048]{1,0:T(8,128)(2,1)S(1)} collective-permute-done((bf16[256,2048]{1,0:T(8,128)(2,1)}, bf16[256,2048]{1,0:T(8,128)(2,1)S(1)}, u32[]{:S(2)}, u32[]{:S(2)}) %collective-permute-start.23) | collective-permute-done | bytes 1048608 | tf_op jit(solution)/shard_map/ppermute | solution.py:917
  689.1 6.9 collective-permute-done.22
  696.1 4.6 all-to-all-done.1
  701.7 29.0 %attend_back.1 = (bf16[2048,512]{1,0:T(8,128)(2,1)}, bf16[2048,512]{1,0:T(8,128)(2,1)}, bf16[2048,640]{1,0:T(8,128)(2,1)}) custom-call(s32[64]{0:T(128)} %reshape.426.reach_ref, bf16[2048,512]{1,0:T(8,128)(2,1)} %get-tuple-element.104.q_ref, bf16[2048,512]{1,0:T(8,128)(2,1)} %get-tuple-element.105.k_ref, bf16[2048,256]{1,0:T(8,128)(2,1)} %get-tuple-element.106.v_ref, ...), custom_call_target="tpu_custom_call" | custom-call | bytes 90000000 | tf_op jit(solution)/shard_map/attend_back/pallas_call | solution.py:755
  730.7 3.9 convolution_convert_fusion.11
  734.9 9.0 convolution_convert_fusion.5
  748.6 3.4 add_convert_fusion.4
  753.7 19.6 %collective-permute-done.25 = bf16[256,2048]{1,0:T(8,128)(2,1)} collective-permute-done((bf16[256,2048]{1,0:T(8,128)(2,1)S(1)}, bf16[256,2048]{1,0:T(8,128)(2,1)}, u32[]{:S(2)}, u32[]{:S(2)}) %collective-permute-start.25) | collective-permute-done | bytes 1048608 | tf_op jit(solution)/shard_map/ppermute | solution.py:917
  776.2 3.4 add_convert_fusion.3
  782.3 43.3 %reduce_rows.3 = f32[256,640]{1,0:T(8,128)} custom-call(bf16[8,256,640]{2,1,0:T(8,128)(2,1)} %bitcast.446), custom_call_target="tpu_custom_call" | custom-call | bytes 300000000 | tf_op jit(solution)/shard_map/reduce_rows/pallas_call | solution.py:448
  838.9 8.4 convolution_convert_fusion.3
  847.3 94.0 %reduce_rows.4 = f32[256,2048]{1,0:T(8,128)} custom-call(bf16[8,256,2048]{2,1,0:T(8,128)(2,1)} %bitcast.426), custom_call_target="tpu_custom_call" | custom-call | bytes 300000000 | tf_op jit(solution)/shard_map/reduce_rows/pallas_call | solution.py:448
  945.7 3.5 pad_maximum_fusion.1
  949.3 5.0 all-to-all-start.2
  960.4 43.8 %reduce_rows.5 = f32[64,2688]{1,0:T(8,128)} custom-call(bf16[8,64,2688]{2,1,0:T(8,128)(2,1)} %bitcast.416), custom_call_target="tpu_custom_call" | custom-call | bytes 300000000 | tf_op jit(solution)/shard_map/reduce_rows/pallas_call | solution.py:448
  (595 shorter events, 274.8 us)
Async XLA Ops:
  7.2 165.6 %all-gather.3.cloned.1.call-start = ((), (), s32[]{:S(2)}) async-start(), calls=%async_computation.11 | async-start | bytes 2703360 | tf_op jit(solution)/shard_map/all_gather | solution.py:874
  10.4 280.5 %all-gather.5.cloned.1.call-start = ((), (), s32[]{:S(2)}) async-start(), calls=%async_computation.12 | async-start | bytes 8650752 | tf_op jit(solution)/shard_map/all_gather | solution.py:881
  19.9 148.9 %copy-start.107 = (s32[1,8]{1,0:T(1,128)S(1)}, s32[1,8]{1,0:T(1,128)}, u32[]{:S(2)}) copy-start(s32[1,8]{1,0:T(1,128)} %param.22) | copy-start | bytes 100
  198.0 26.0 %collective-permute-start = (bf16[256,2048]{1,0:T(8,128)(2,1)S(1)}, bf16[256,2048]{1,0:T(8,128)(2,1)}, u32[]{:S(2)}, u32[]{:S(2)}) collective-permute-start(bf16[256,2048]{1,0:T(8,128)(2,1)S(1)} %copy-done.32), channel_id=1, source_target_pairs={{0,2},{1,3},{2,4},{3,5},{4,6},{5,7},{6,0},{7,1},{8,10},{9,11},{10,... | collective-permute-start | bytes 3145736 | tf_op jit(solution)/shard_map/ppermute | solution.py:920
  198.6 25.4 %collective-permute-start.1 = (bf16[256,2048]{1,0:T(8,128)(2,1)S(1)}, bf16[256,2048]{1,0:T(8,128)(2,1)S(1)}, u32[]{:S(2)}, u32[]{:S(2)}) collective-permute-start(bf16[256,2048]{1,0:T(8,128)(2,1)S(1)} %copy-done.32), channel_id=1, source_target_pairs={{0,1},{1,0},{2,3},{3,2},{4,5},{5,4},{6,7},{7,6},{8,9},{9,8},{10,11... | collective-permute-start | bytes 3145736 | tf_op jit(solution)/shard_map/ppermute | solution.py:917
  226.7 52.2 %all-to-all-start = ((bf16[8,256,256]{1,2,0:T(8,128)(2,1)}), bf16[8,256,256]{1,2,0:T(8,128)(2,1)S(1)}, u32[]{:S(2)}, u32[]{:S(2)}) async-start(bf16[8,256,256]{1,2,0:T(8,128)(2,1)} %copy.109), calls=%async_computation | async-start | bytes 2097152 | tf_op jit(solution)/shard_map/all_to_all | solution.py:933
  231.7 469.0 %reduce-scatter.9.cloned.1.call-start = ((), (), s32[]{:S(2)}) async-start(), calls=%async_computation.13 | async-start | bytes 7208960 | tf_op jit(solution)/shard_map/reduce_scatter | solution.py:1060
  232.8 41.4 %collective-permute-start.2 = (bf16[256,2048]{1,0:T(8,128)(2,1)}, bf16[256,2048]{1,0:T(8,128)(2,1)S(1)}, u32[]{:S(2)}, u32[]{:S(2)}) collective-permute-start(bf16[256,2048]{1,0:T(8,128)(2,1)} %collective-permute-done), channel_id=1, source_target_pairs={{0,2},{1,3},{2,4},{3,5},{4,6},{5,7},{6,0},{7,1},{8,10},{9,11},{10,... | collective-permute-start | bytes 3145736 | tf_op jit(solution)/shard_map/ppermute | solution.py:920
  234.7 40.4 %collective-permute-start.3 = (bf16[256,2048]{1,0:T(8,128)(2,1)}, bf16[256,2048]{1,0:T(8,128)(2,1)}, u32[]{:S(2)}, u32[]{:S(2)}) collective-permute-start(bf16[256,2048]{1,0:T(8,128)(2,1)} %collective-permute-done), channel_id=1, source_target_pairs={{0,1},{1,0},{2,3},{3,2},{4,5},{5,4},{6,7},{7,6},{8,9},{9,8},{10,11... | collective-permute-start | bytes 3145736 | tf_op jit(solution)/shard_map/ppermute | solution.py:917
  278.9 24.6 %collective-permute-start.4 = (bf16[256,2048]{1,0:T(8,128)(2,1)}, bf16[256,2048]{1,0:T(8,128)(2,1)}, u32[]{:S(2)}, u32[]{:S(2)}) collective-permute-start(bf16[256,2048]{1,0:T(8,128)(2,1)} %copy-done.68), channel_id=1, source_target_pairs={{0,2},{1,3},{2,4},{3,5},{4,6},{5,7},{6,0},{7,1},{8,10},{9,11},{10,... | collective-permute-start | bytes 3145736 | tf_op jit(solution)/shard_map/ppermute | solution.py:920
  278.9 24.6 %collective-permute-start.5 = (bf16[256,2048]{1,0:T(8,128)(2,1)}, bf16[256,2048]{1,0:T(8,128)(2,1)}, u32[]{:S(2)}, u32[]{:S(2)}) collective-permute-start(bf16[256,2048]{1,0:T(8,128)(2,1)} %copy-done.68), channel_id=1, source_target_pairs={{0,1},{1,0},{2,3},{3,2},{4,5},{5,4},{6,7},{7,6},{8,9},{9,8},{10,11... | collective-permute-start | bytes 3145736 | tf_op jit(solution)/shard_map/ppermute | solution.py:917
  303.5 25.0 %collective-permute-start.6 = (bf16[256,2048]{1,0:T(8,128)(2,1)S(1)}, bf16[256,2048]{1,0:T(8,128)(2,1)S(1)}, u32[]{:S(2)}, u32[]{:S(2)}) collective-permute-start(bf16[256,2048]{1,0:T(8,128)(2,1)S(1)} %multiply_convert_fusion), channel_id=1, source_target_pairs={{0,2},{1,3},{2,4},{3,5},{4,6},{5,7},{6,0},{7,1},{8,10},{9,11},{10,... | collective-permute-start | bytes 3145736 | tf_op jit(solution)/shard_map/ppermute | solution.py:920
  305.8 26.1 %collective-permute-start.7 = (bf16[256,2048]{1,0:T(8,128)(2,1)S(1)}, bf16[256,2048]{1,0:T(8,128)(2,1)S(1)}, u32[]{:S(2)}, u32[]{:S(2)}) collective-permute-start(bf16[256,2048]{1,0:T(8,128)(2,1)S(1)} %multiply_convert_fusion), channel_id=1, source_target_pairs={{0,1},{1,0},{2,3},{3,2},{4,5},{5,4},{6,7},{7,6},{8,9},{9,8},{10,11... | collective-permute-start | bytes 3145736 | tf_op jit(solution)/shard_map/ppermute | solution.py:917
  307.5 46.9 %collective-permute-start.10 = (bf16[256,2048]{1,0:T(8,128)(2,1)}, bf16[256,2048]{1,0:T(8,128)(2,1)S(1)}, u32[]{:S(2)}, u32[]{:S(2)}) collective-permute-start(bf16[256,2048]{1,0:T(8,128)(2,1)} %collective-permute-done.4), channel_id=1, source_target_pairs={{0,1},{1,0},{2,3},{3,2},{4,5},{5,4},{6,7},{7,6},{8,9},{9,8},{10,11... | collective-permute-start | bytes 3145736 | tf_op jit(solution)/shard_map/ppermute | solution.py:917
  332.6 161.6 %copy-start.108 = (bf16[2,112,2048]{2,1,0:T(8,128)(2,1)}, bf16[2,112,2048]{2,1,0:T(8,128)(2,1)S(1)}, u32[]{:S(2)}) copy-start(bf16[2,112,2048]{2,1,0:T(8,128)(2,1)S(1)} %convolution_convert_fusion.10) | copy-start | bytes 2752516
  332.6 22.4 %collective-permute-start.8 = (bf16[256,2048]{1,0:T(8,128)(2,1)S(1)}, bf16[256,2048]{1,0:T(8,128)(2,1)S(1)}, u32[]{:S(2)}, u32[]{:S(2)}) collective-permute-start(bf16[256,2048]{1,0:T(8,128)(2,1)S(1)} %collective-permute-done.6), channel_id=1, source_target_pairs={{0,2},{1,3},{2,4},{3,5},{4,6},{5,7},{6,0},{7,1},{8,10},{9,11},{10,... | collective-permute-start | bytes 3145736 | tf_op jit(solution)/shard_map/ppermute | solution.py:920
  333.1 41.3 %collective-permute-start.9 = (bf16[256,2048]{1,0:T(8,128)(2,1)S(1)}, bf16[256,2048]{1,0:T(8,128)(2,1)S(1)}, u32[]{:S(2)}, u32[]{:S(2)}) collective-permute-start(bf16[256,2048]{1,0:T(8,128)(2,1)S(1)} %collective-permute-done.6), channel_id=1, source_target_pairs={{0,1},{1,0},{2,3},{3,2},{4,5},{5,4},{6,7},{7,6},{8,9},{9,8},{10,11... | collective-permute-start | bytes 3145736 | tf_op jit(solution)/shard_map/ppermute | solution.py:917
  343.7 148.8 %copy-start.72 = (bf16[224,1408]{1,0:T(8,128)(2,1)}, bf16[224,1408]{1,0:T(8,128)(2,1)S(1)}, u32[]{:S(2)}) copy-start(bf16[224,1408]{1,0:T(8,128)(2,1)S(1)} %get-tuple-element.191) | copy-start | bytes 1892356
  375.1 119.1 %copy-start.110 = (bf16[2,112,2048]{2,1,0:T(8,128)(2,1)}, bf16[2,112,2048]{2,1,0:T(8,128)(2,1)S(1)}, u32[]{:S(2)}) copy-start(bf16[2,112,2048]{2,1,0:T(8,128)(2,1)S(1)} %convolution_convert_fusion.9) | copy-start | bytes 2752516
  375.1 32.3 %collective-permute-start.11 = (bf16[256,2048]{1,0:T(8,128)(2,1)S(1)}, bf16[256,2048]{1,0:T(8,128)(2,1)S(1)}, u32[]{:S(2)}, u32[]{:S(2)}) collective-permute-start(bf16[256,2048]{1,0:T(8,128)(2,1)S(1)} %collective-permute-done.8), channel_id=1, source_target_pairs={{0,2},{1,3},{2,4},{3,5},{4,6},{5,7},{6,0},{7,1},{8,10},{9,11},{10,... | collective-permute-start | bytes 3145736 | tf_op jit(solution)/shard_map/ppermute | solution.py:920
  376.0 31.4 %collective-permute-start.12 = (bf16[256,2048]{1,0:T(8,128)(2,1)S(1)}, bf16[256,2048]{1,0:T(8,128)(2,1)S(1)}, u32[]{:S(2)}, u32[]{:S(2)}) collective-permute-start(bf16[256,2048]{1,0:T(8,128)(2,1)S(1)} %collective-permute-done.8), channel_id=1, source_target_pairs={{0,1},{1,0},{2,3},{3,2},{4,5},{5,4},{6,7},{7,6},{8,9},{9,8},{10,11... | collective-permute-start | bytes 3145736 | tf_op jit(solution)/shard_map/ppermute | solution.py:917
  386.0 106.4 %copy-start.74 = (bf16[224,1408]{1,0:T(8,128)(2,1)}, bf16[224,1408]{1,0:T(8,128)(2,1)S(1)}, u32[]{:S(2)}) copy-start(bf16[224,1408]{1,0:T(8,128)(2,1)S(1)} %get-tuple-element.194) | copy-start | bytes 1892356
  408.1 86.1 %copy-start.112 = (bf16[2,112,2048]{2,1,0:T(8,128)(2,1)}, bf16[2,112,2048]{2,1,0:T(8,128)(2,1)S(1)}, u32[]{:S(2)}) copy-start(bf16[2,112,2048]{2,1,0:T(8,128)(2,1)S(1)} %convolution_convert_fusion.8) | copy-start | bytes 2752516
  424.3 26.2 %collective-permute-start.13 = (bf16[256,2048]{1,0:T(8,128)(2,1)S(1)}, bf16[256,2048]{1,0:T(8,128)(2,1)S(1)}, u32[]{:S(2)}, u32[]{:S(2)}) collective-permute-start(bf16[256,2048]{1,0:T(8,128)(2,1)S(1)} %collective-permute-done.11), channel_id=1, source_target_pairs={{0,1},{1,0},{2,3},{3,2},{4,5},{5,4},{6,7},{7,6},{8,9},{9,8},{10,11... | collective-permute-start | bytes 3145736 | tf_op jit(solution)/shard_map/ppermute | solution.py:917
  424.7 44.6 %collective-permute-start.14 = (bf16[256,2048]{1,0:T(8,128)(2,1)S(1)}, bf16[256,2048]{1,0:T(8,128)(2,1)S(1)}, u32[]{:S(2)}, u32[]{:S(2)}) collective-permute-start(bf16[256,2048]{1,0:T(8,128)(2,1)S(1)} %get-tuple-element.127), channel_id=1, source_target_pairs={{0,1},{1,0},{2,3},{3,2},{4,5},{5,4},{6,7},{7,6},{8,9},{9,8},{10,11... | collective-permute-start | bytes 3145736 | tf_op jit(solution)/shard_map/ppermute | solution.py:917
  491.7 23.7 %collective-permute-start.15 = (bf16[256,2048]{1,0:T(8,128)(2,1)}, bf16[256,2048]{1,0:T(8,128)(2,1)}, u32[]{:S(2)}, u32[]{:S(2)}) collective-permute-start(bf16[256,2048]{1,0:T(8,128)(2,1)} %add_convert_fusion.8), channel_id=1, source_target_pairs={{0,2},{1,3},{2,4},{3,5},{4,6},{5,7},{6,0},{7,1},{8,10},{9,11},{10,... | collective-permute-start | bytes 3145736 | tf_op jit(solution)/shard_map/ppermute | solution.py:920
  492.1 23.3 %collective-permute-start.16 = (bf16[256,2048]{1,0:T(8,128)(2,1)}, bf16[256,2048]{1,0:T(8,128)(2,1)}, u32[]{:S(2)}, u32[]{:S(2)}) collective-permute-start(bf16[256,2048]{1,0:T(8,128)(2,1)} %get-tuple-element.133), channel_id=1, source_target_pairs={{0,1},{1,0},{2,3},{3,2},{4,5},{5,4},{6,7},{7,6},{8,9},{9,8},{10,11... | collective-permute-start | bytes 3145736 | tf_op jit(solution)/shard_map/ppermute | solution.py:917
  519.0 22.7 %collective-permute-start.17 = (bf16[256,2048]{1,0:T(8,128)(2,1)}, bf16[256,2048]{1,0:T(8,128)(2,1)}, u32[]{:S(2)}, u32[]{:S(2)}) collective-permute-start(bf16[256,2048]{1,0:T(8,128)(2,1)} %add_convert_fusion.7), channel_id=1, source_target_pairs={{0,2},{1,3},{2,4},{3,5},{4,6},{5,7},{6,0},{7,1},{8,10},{9,11},{10,... | collective-permute-start | bytes 3145736 | tf_op jit(solution)/shard_map/ppermute | solution.py:920
  519.0 22.7 %collective-permute-start.18 = (bf16[256,2048]{1,0:T(8,128)(2,1)}, bf16[256,2048]{1,0:T(8,128)(2,1)}, u32[]{:S(2)}, u32[]{:S(2)}) collective-permute-start(bf16[256,2048]{1,0:T(8,128)(2,1)} %get-tuple-element.136), channel_id=1, source_target_pairs={{0,1},{1,0},{2,3},{3,2},{4,5},{5,4},{6,7},{7,6},{8,9},{9,8},{10,11... | collective-permute-start | bytes 3145736 | tf_op jit(solution)/shard_map/ppermute | solution.py:917
  541.8 231.6 %reduce-scatter.11.cloned.1.call-start = ((), (), s32[]{:S(2)}) async-start(), calls=%async_computation.14 | async-start | bytes 7208960 | tf_op jit(solution)/shard_map/reduce_scatter | solution.py:1061
  550.9 296.4 %reduce-scatter.15.cloned.1.call-start = ((), (), s32[]{:S(2)}) async-start(), calls=%async_computation.16 | async-start | bytes 1802240 | tf_op jit(solution)/shard_map/reduce_scatter | solution.py:1063
  554.2 65.0 %collective-permute-start.20 = (bf16[256,2048]{1,0:T(8,128)(2,1)}, bf16[256,2048]{1,0:T(8,128)(2,1)}, u32[]{:S(2)}, u32[]{:S(2)}) collective-permute-start(bf16[256,2048]{1,0:T(8,128)(2,1)} %get-tuple-element.203), channel_id=1, source_target_pairs={{0,1},{1,0},{2,3},{3,2},{4,5},{5,4},{6,7},{7,6},{8,9},{9,8},{10,11... | collective-permute-start | bytes 3145736 | tf_op jit(solution)/shard_map/ppermute | solution.py:917
  608.7 22.1 %collective-permute-start.19 = (bf16[256,2048]{1,0:T(8,128)(2,1)}, bf16[256,2048]{1,0:T(8,128)(2,1)S(1)}, u32[]{:S(2)}, u32[]{:S(2)}) collective-permute-start(bf16[256,2048]{1,0:T(8,128)(2,1)} %add_convert_fusion.6), channel_id=1, source_target_pairs={{0,2},{1,3},{2,4},{3,5},{4,6},{5,7},{6,0},{7,1},{8,10},{9,11},{10,... | collective-permute-start | bytes 3145736 | tf_op jit(solution)/shard_map/ppermute | solution.py:920
  632.3 215.0 %reduce-scatter.17.cloned.1.call-start = ((), (), s32[]{:S(2)}) async-start(), calls=%async_computation.17 | async-start | bytes 3932160 | tf_op jit(solution)/shard_map/reduce_scatter | solution.py:1066
  632.9 214.4 %reduce-scatter.13.cloned.1.call-start = ((), (), s32[]{:S(2)}) async-start(), calls=%async_computation.15 | async-start | bytes 7208960 | tf_op jit(solution)/shard_map/reduce_scatter | solution.py:1062
  633.7 19.8 %collective-permute-start.21 = (bf16[256,2048]{1,0:T(8,128)(2,1)}, bf16[256,2048]{1,0:T(8,128)(2,1)}, u32[]{:S(2)}, u32[]{:S(2)}) collective-permute-start(bf16[256,2048]{1,0:T(8,128)(2,1)} %slice.231), channel_id=1, source_target_pairs={{0,1},{1,0},{2,3},{3,2},{4,5},{5,4},{6,7},{7,6},{8,9},{9,8},{10,11... | collective-permute-start | bytes 3145736 | tf_op jit(solution)/shard_map/ppermute | solution.py:917
  654.6 46.1 %all-to-all-start.1 = ((bf16[256,8,256]{2,0,1:T(8,128)(2,1)}), bf16[256,8,256]{2,0,1:T(8,128)(2,1)S(1)}, u32[]{:S(2)}, u32[]{:S(2)}) async-start(bf16[256,8,256]{2,0,1:T(8,128)(2,1)} %bitcast.375), calls=%async_computation.1 | async-start | bytes 2097152 | tf_op jit(solution)/shard_map/all_to_all | solution.py:1087
  658.1 285.0 %reduce-scatter.23.cloned.1.call-start = ((), (), s32[]{:S(2)}) async-start(), calls=%async_computation.20 | async-start | bytes 3276800 | tf_op jit(solution)/shard_map/reduce_scatter | solution.py:1066
  658.2 30.0 %collective-permute-start.23 = (bf16[256,2048]{1,0:T(8,128)(2,1)}, bf16[256,2048]{1,0:T(8,128)(2,1)S(1)}, u32[]{:S(2)}, u32[]{:S(2)}) collective-permute-start(bf16[256,2048]{1,0:T(8,128)(2,1)} %slice.232), channel_id=1, source_target_pairs={{0,1},{1,0},{2,3},{3,2},{4,5},{5,4},{6,7},{7,6},{8,9},{9,8},{10,11... | collective-permute-start | bytes 3145736 | tf_op jit(solution)/shard_map/ppermute | solution.py:917
  662.1 34.0 %collective-permute-start.22 = (bf16[256,2048]{1,0:T(8,128)(2,1)S(1)}, bf16[256,2048]{1,0:T(8,128)(2,1)}, u32[]{:S(2)}, u32[]{:S(2)}) collective-permute-start(bf16[256,2048]{1,0:T(8,128)(2,1)S(1)} %add_convert_fusion.5), channel_id=1, source_target_pairs={{0,2},{1,3},{2,4},{3,5},{4,6},{5,7},{6,0},{7,1},{8,10},{9,11},{10,... | collective-permute-start | bytes 3145736 | tf_op jit(solution)/shard_map/ppermute | solution.py:920
  745.8 199.9 %reduce-scatter.21.cloned.1.call-start = ((), (), s32[]{:S(2)}) async-start(), calls=%async_computation.19 | async-start | bytes 3276800 | tf_op jit(solution)/shard_map/reduce_scatter | solution.py:1121
  747.1 26.2 %collective-permute-start.25 = (bf16[256,2048]{1,0:T(8,128)(2,1)S(1)}, bf16[256,2048]{1,0:T(8,128)(2,1)}, u32[]{:S(2)}, u32[]{:S(2)}) collective-permute-start(bf16[256,2048]{1,0:T(8,128)(2,1)S(1)} %copy-done.66), channel_id=1, source_target_pairs={{0,1},{1,0},{2,3},{3,2},{4,5},{5,4},{6,7},{7,6},{8,9},{9,8},{10,11... | collective-permute-start | bytes 3145736 | tf_op jit(solution)/shard_map/ppermute | solution.py:917
  752.0 24.2 %collective-permute-start.24 = (bf16[256,2048]{1,0:T(8,128)(2,1)}, bf16[256,2048]{1,0:T(8,128)(2,1)}, u32[]{:S(2)}, u32[]{:S(2)}) collective-permute-start(bf16[256,2048]{1,0:T(8,128)(2,1)} %add_convert_fusion.4), channel_id=1, source_target_pairs={{0,2},{1,3},{2,4},{3,5},{4,6},{5,7},{6,0},{7,1},{8,10},{9,11},{10,... | collective-permute-start | bytes 3145736 | tf_op jit(solution)/shard_map/ppermute | solution.py:920
  752.0 73.7 %collective-permute-start.27 = (bf16[256,2048]{1,0:T(8,128)(2,1)}, bf16[256,2048]{1,0:T(8,128)(2,1)}, u32[]{:S(2)}, u32[]{:S(2)}) collective-permute-start(bf16[256,2048]{1,0:T(8,128)(2,1)} %slice.234), channel_id=1, source_target_pairs={{0,1},{1,0},{2,3},{3,2},{4,5},{5,4},{6,7},{7,6},{8,9},{9,8},{10,11... | collective-permute-start | bytes 3145736 | tf_op jit(solution)/shard_map/ppermute | solution.py:917
  779.7 46.0 %collective-permute-start.26 = (bf16[256,2048]{1,0:T(8,128)(2,1)}, bf16[256,2048]{1,0:T(8,128)(2,1)}, u32[]{:S(2)}, u32[]{:S(2)}) collective-permute-start(bf16[256,2048]{1,0:T(8,128)(2,1)} %add_convert_fusion.3), channel_id=1, source_target_pairs={{0,2},{1,3},{2,4},{3,5},{4,6},{5,7},{6,0},{7,1},{8,10},{9,11},{10,... | collective-permute-start | bytes 3145736 | tf_op jit(solution)/shard_map/ppermute | solution.py:920
  834.9 110.8 %reduce-scatter.19.cloned.1.call-start = ((), (), s32[]{:S(2)}) async-start(), calls=%async_computation.18 | async-start | bytes 10485760 | tf_op jit(solution)/shard_map/reduce_scatter | solution.py:1090
  847.3 94.0 %copy-start.62 = (bf16[512,1408]{1,0:T(8,128)(2,1)S(1)}, bf16[512,1408]{1,0:T(8,128)(2,1)}, u32[]{:S(2)}) copy-start(bf16[512,1408]{1,0:T(8,128)(2,1)} %reduce-scatter.11.cloned.1.call-done) | copy-start | bytes 4325380
  949.3 66.2 %all-to-all-start.2 = ((bf16[8,64,1408]{2,1,0:T(8,128)(2,1)}), bf16[8,64,1408]{2,1,0:T(8,128)(2,1)}, u32[]{:S(2)}, u32[]{:S(2)}) async-start(bf16[8,64,1408]{2,1,0:T(8,128)(2,1)} %bitcast.78), calls=%async_computation.10 | async-start | bytes 2883584 | tf_op jit(solution)/shard_map/all_to_all | solution.py:1146
  (150 other events, 976.0 us)
Sparse Core Ops, SparseCore 0:
  11.5 84.4 all-gather.2
  99.0 87.1 all-gather.4
  541.9 52.3 reduce-scatter.8
  596.8 54.8 reduce-scatter.10
  654.2 27.3 reduce-scatter.14
  684.1 37.9 reduce-scatter.16
  724.6 54.8 reduce-scatter.12
  782.2 34.6 reduce-scatter.22
  835.1 35.6 reduce-scatter.20
  873.3 71.7 reduce-scatter.18

commit v3 on v2

--- a/solution.py
+++ b/solution.py
@@ -200,14 +200,50 @@
     return [dma((2 * half, chunks))] * 2 + [dma((half, chunks))] * 4
 
 
-def gather_kernel(chunks, x_ref, o_ref, *sems):
-    chain = Chain(chunks, x_ref, o_ref, *sems)
-    greet(chain.rank, chain.last)
-    chain.start()
-    o_ref[chain.rank] = x_ref[...]
-    for s in range(1, chain.last + 1):
-        chain.step(s)
-    chain.finish()
+class Share:
+    def __init__(self, ref, send_out, recv_out, send_pass, recv_pass):
+        self.ref = ref
+        self.sems = (send_out, recv_out, send_pass, recv_pass)
+        self.line = lax.axis_index("dp")
+        self.count = ref.shape[0] // 2
+
+    def out(self, k):
+        peer = 2 * lax.rem(self.line // 2 + k, self.count) + self.line % 2
+        return pltpu.make_async_remote_copy(
+            src_ref=self.ref.at[self.line],
+            dst_ref=self.ref.at[self.line],
+            send_sem=self.sems[0].at[k],
+            recv_sem=self.sems[1].at[k],
+            device_id={"dp": peer},
+            device_id_type=MESH,
+        )
+
+    def hand(self, k):
+        slab = 2 * lax.rem(self.line // 2 + self.count - k, self.count) + self.line % 2
+        return pltpu.make_async_remote_copy(
+            src_ref=self.ref.at[slab],
+            dst_ref=self.ref.at[slab],
+            send_sem=self.sems[2].at[k],
+            recv_sem=self.sems[3].at[k],
+            device_id={"dp": self.line + 1 - 2 * (self.line % 2)},
+            device_id_type=MESH,
+        )
+
+    def start(self):
+        for k in range(1, self.count):
+            self.out(k).start()
+        self.hand(0).start()
+
+    def middle(self):
+        for k in range(1, self.count):
+            self.out(k).wait_recv()
+            self.hand(k).start()
+
+    def finish(self):
+        for k in range(1, self.count):
+            self.out(k).wait_send()
+        for k in range(self.count):
+            self.hand(k).wait()
 
 
 def prologue_kernel(
@@ -224,15 +260,15 @@
     wa_r,
     ta_s,
     ta_r,
-    wp_s,
-    wp_r,
-    dp_s,
-    dp_r,
+    da_s,
+    da_r,
     *sems,
 ):
     group, spread = o_ref.shape[0], pk_ref.shape[0]
-    chain = Chain(chunks, x_ref, o_ref, *sems)
-    rank, line = chain.rank, lax.axis_index("dp")
+    packs, downs = Share(pk_ref, *sems[:4]), Share(do_ref, *sems[4:8])
+    chain = Chain(chunks, x_ref, o_ref, *sems[8:])
+    rank, line = chain.rank, packs.line
+    mine = rank % 2
     barrier = pltpu.get_barrier_semaphore()
     for k in range(1, group):
         pl.semaphore_signal(
@@ -241,67 +277,61 @@
             device_id={"expert": lax.rem(rank + k, group)},
             device_id_type=MESH,
         )
-    for k in range(1, spread):
-        pl.semaphore_signal(
-            barrier, inc=1, device_id={"dp": lax.rem(line + k, spread)}, device_id_type=MESH
-        )
-    pl.semaphore_wait(barrier, group + spread - 2)
-
-    def cut(k):
-        peer = lax.rem(rank + k, group)
+    for k in range(1, packs.count):
+        peer = 2 * lax.rem(line // 2 + k, packs.count) + line % 2
+        pl.semaphore_signal(barrier, inc=1, device_id={"dp": peer}, device_id_type=MESH)
+    pl.semaphore_signal(
+        barrier, inc=1, device_id={"dp": line + 1 - 2 * (line % 2)}, device_id_type=MESH
+    )
+    pl.semaphore_wait(barrier, group - 1 + packs.count)
+
+    def far(src, dst, send, recv, peer):
         return pltpu.make_async_remote_copy(
-            src_ref=w_ref.at[peer],
-            dst_ref=pk_ref.at[line, rank],
-            send_sem=wa_s.at[k - 1],
-            recv_sem=wa_r.at[k - 1],
+            src_ref=src,
+            dst_ref=dst,
+            send_sem=send,
+            recv_sem=recv,
             device_id={"expert": peer},
             device_id_type=MESH,
         )
 
+    def cut(k):
+        peer = lax.rem(rank + k, group)
+        return far(w_ref.at[peer], pk_ref.at[line, rank], wa_s.at[k - 1], wa_r.at[k - 1], peer)
+
     def gates(k):
         peer = lax.rem(rank + k, group)
-        return pltpu.make_async_remote_copy(
-            src_ref=t_ref.at[peer],
-            dst_ref=to_ref.at[rank],
-            send_sem=ta_s.at[k - 1],
-            recv_sem=ta_r.at[k - 1],
-            device_id={"expert": peer},
-            device_id_type=MESH,
-        )
-
-    def along(src, dst, send, recv, k):
-        return pltpu.make_async_remote_copy(
-            src_ref=src,
-            dst_ref=dst,
-            send_sem=send.at[k - 1],
-            recv_sem=recv.at[k - 1],
-            device_id={"dp": lax.rem(line + k, spread)},
-            device_id_type=MESH,
-        )
-
+        return far(t_ref, to_ref.at[rank], ta_s.at[k - 1], ta_r.at[k - 1], peer)
+
+    def down():
+        return far(d_ref, do_ref.at[line, mine], da_s.at[0], da_r.at[0], chain.side)
+
+    down().start()
     for k in range(1, group):
         cut(k).start()
         gates(k).start()
     chain.start()
-    for k in range(1, spread):
-        along(d_ref, do_ref.at[line], dp_s, dp_r, k).start()
     pk_ref[line, rank] = w_ref[rank]
-    do_ref[line] = d_ref[...]
-    to_ref[rank] = t_ref[rank]
+    do_ref[line, mine] = d_ref[...]
+    to_ref[rank] = t_ref[...]
     o_ref[rank] = x_ref[...]
+    down().wait_recv()
+    downs.start()
     for k in range(1, group):
         cut(k).wait_recv()
-    for k in range(1, spread):
-        along(pk_ref.at[line], pk_ref.at[line], wp_s, wp_r, k).start()
-    for s in range(1, chain.last + 1):
+    packs.start()
+    for s in range(1, chain.last):
         chain.step(s)
+    downs.middle()
+    packs.middle()
+    chain.step(chain.last)
     chain.finish()
+    down().wait_send()
     for k in range(1, group):
         cut(k).wait_send()
         gates(k).wait()
-    for k in range(1, spread):
-        along(d_ref, do_ref.at[line], dp_s, dp_r, k).wait()
-        along(pk_ref.at[line], pk_ref.at[line], wp_s, wp_r, k).wait()
+    downs.finish()
+    packs.finish()
 
 
 def prologue(x, cuts, down, gates, spread, call_id, chunks=2):
@@ -313,13 +343,14 @@
         out_shape=[
             jax.ShapeDtypeStruct((group,) + x.shape, x.dtype),
             jax.ShapeDtypeStruct((spread,) + cuts.shape, cuts.dtype),
-            jax.ShapeDtypeStruct((spread,) + down.shape, down.dtype),
-            jax.ShapeDtypeStruct(gates.shape, gates.dtype),
+            jax.ShapeDtypeStruct((spread, 2) + down.shape, down.dtype),
+            jax.ShapeDtypeStruct((group,) + gates.shape, gates.dtype),
         ],
         in_specs=[vmem] * 4,
         out_specs=[vmem] * 4,
         scratch_shapes=[dma((group - 1,))] * 4
-        + [dma((spread - 1,))] * 4
+        + [dma((1,))] * 2
+        + [dma((spread // 2,))] * 8
         + chain_sems(group, chunks),
         compiler_params=pltpu.CompilerParams(
             collective_id=call_id, has_side_effects=True, vmem_limit_bytes=VMEM_LIMIT
@@ -329,21 +360,6 @@
     )(x, cuts, down, gates)
 
 
-def gather_rows(x, count, call_id, chunks=2):
-    return pl.pallas_call(
-        functools.partial(gather_kernel, chunks),
-        out_shape=jax.ShapeDtypeStruct((count,) + x.shape, x.dtype),
-        in_specs=[pl.BlockSpec(memory_space=pltpu.VMEM)],
-        out_specs=pl.BlockSpec(memory_space=pltpu.VMEM),
-        scratch_shapes=chain_sems(count, chunks),
-        compiler_params=pltpu.CompilerParams(
-            collective_id=call_id, has_side_effects=True, vmem_limit_bytes=VMEM_LIMIT
-        ),
-        cost_estimate=WIRE,
-        name="gather_rows",
-    )(x)
-
-
 def ring_pairs(group):
     half = group // 2
     side = [(r, r + 1 - 2 * (r % 2)) for r in range(group)]
@@ -355,18 +371,22 @@
     return lax.optimization_barrier(values)
 
 
-def reduce_kernel(chunks, p_ref, o_ref, rx, st, ru, rd, acc, sxs, rxs, sus, rus, sds, rds):
+def reduce_kernel(parts, *refs):
+    n = len(parts)
+    p_refs, o_refs = refs[:n], refs[n : 2 * n]
+    bufs = [refs[2 * n + 4 * k : 2 * n + 4 * k + 4] for k in range(n)]
+    acc, sxs, rxs, sus, rus, sds, rds = refs[6 * n :]
     rank = lax.axis_index("expert")
-    last = p_ref.shape[0] // 2 - 1
+    last = p_refs[0].shape[0] // 2 - 1
     a = rank // 2
     b = rank % 2
-    rows = p_ref.shape[1] // chunks
     greet(rank, last)
     h = a // 2
     order = [3 - 3 * h, 2 - h, 4 * h + 1 - a, a]
-
-    def cut(ref, c):
-        return ref.at[pl.ds(c * rows, rows)]
+    pieces = []
+    for k, chunks in enumerate(parts):
+        rows = p_refs[k].shape[1] // chunks
+        pieces += [(k, c * rows, rows) for c in range(chunks)]
 
     def copy(src, dst, send, recv, target):
         return pltpu.make_async_remote_copy(
@@ -378,85 +398,96 @@
             device_id_type=MESH,
         )
 
-    def across(t, c):
-        return copy(
-            cut(p_ref.at[2 * t + 1 - b], c),
-            cut(rx.at[t], c),
-            sxs.at[t, c],
-            rxs.at[t, c],
-            rank + 1 - 2 * b,
-        )
-
-    def upward(t, c):
-        return copy(cut(st.at[t], c), cut(ru.at[t], c), sus.at[t, c], rus.at[t, c], rank + 2)
-
-    def downward(t, c):
-        return copy(cut(st.at[t], c), cut(rd.at[t], c), sds.at[t, c], rds.at[t, c], rank - 2)
-
     for t in order:
-        for c in range(chunks):
-            across(t, c).start()
+        for c, (k, at, rows) in enumerate(pieces):
+            src = p_refs[k].at[2 * t + 1 - b, pl.ds(at, rows)]
+            dst = bufs[k][0].at[t, pl.ds(at, rows)]
+            copy(src, dst, sxs.at[t, c], rxs.at[t, c], rank + 1 - 2 * b).start()
+
+    def moves(t, c, k, at, rows):
+        cut = pl.ds(at, rows)
+        rx, st, ru, rd = (buf.at[t, cut] for buf in bufs[k])
+        src = p_refs[k].at[2 * t + 1 - b, cut]
+        across = copy(src, rx, sxs.at[t, c], rxs.at[t, c], rank + 1 - 2 * b)
+        upward = copy(st, ru, sus.at[t, c], rus.at[t, c], rank + 2)
+        downward = copy(st, rd, sds.at[t, c], rds.at[t, c], rank - 2)
+        return rx, st, ru, rd, across, upward, downward
+
     for t in order:
-        for c in range(chunks):
-            across(t, c).wait_recv()
-            acc[...] = cut(p_ref.at[2 * t + b], c)[...].astype(f32) + cut(rx.at[t], c)[...].astype(
-                f32
-            )
+        for c, (k, at, rows) in enumerate(pieces):
+            rx, st, ru, rd, across, upward, downward = moves(t, c, k, at, rows)
+            width = p_refs[k].shape[2]
+            total = acc.at[pl.ds(0, rows), pl.ds(0, width)]
+            across.wait_recv()
+            total[...] = p_refs[k][2 * t + b, pl.ds(at, rows)].astype(f32) + rx[...].astype(f32)
 
             @pl.when((t >= a) & (a > 0))
             def _():
-                upward(t, c).wait_recv()
-                acc[...] += cut(ru.at[t], c)[...].astype(f32)
+                upward.wait_recv()
+                total[...] += ru[...].astype(f32)
 
             @pl.when((t <= a) & (a < last))
             def _():
-                downward(t, c).wait_recv()
-                acc[...] += cut(rd.at[t], c)[...].astype(f32)
+                downward.wait_recv()
+                total[...] += rd[...].astype(f32)
 
             @pl.when(t == a)
             def _():
-                cut(o_ref, c)[...] = acc[...]
+                o_refs[k][pl.ds(at, rows)] = total[...]
 
             @pl.when(t > a)
             def _():
-                cut(st.at[t], c)[...] = acc[...].astype(st.dtype)
-                upward(t, c).start()
+                st[...] = total[...].astype(bf16)
+                upward.start()
 
             @pl.when(t < a)
             def _():
-                cut(st.at[t], c)[...] = acc[...].astype(st.dtype)
-                downward(t, c).start()
+                st[...] = total[...].astype(bf16)
+                downward.start()
 
     for t in order:
-        for c in range(chunks):
-            across(t, c).wait_send()
+        for c, (k, at, rows) in enumerate(pieces):
+            rx, st, ru, rd, across, upward, downward = moves(t, c, k, at, rows)
+            across.wait_send()
 
             @pl.when(t > a)
             def _():
-                upward(t, c).wait_send()
+                upward.wait_send()
 
             @pl.when(t < a)
             def _():
-                downward(t, c).wait_send()
-
-
-def reduce_rows(p, call_id, chunks=4):
-    count, rows, width = p.shape
-    half = count // 2
-    buf = pltpu.VMEM((half, rows, width), p.dtype)
-    sem = pltpu.SemaphoreType.DMA((half, chunks))
+                downward.wait_send()
+
+
+def reduce_rows(operands, call_id, most):
+    half = operands[0].shape[0] // 2
+    parts = [
+        max(c for c in range(1, most + 1) if p.shape[1] % (16 * c) == 0 and p.shape[1] // c >= 16)
+        if p.shape[1] > 64
+        else 1
+        for p in operands
+    ]
+    high = max(p.shape[1] // c for p, c in zip(operands, parts))
+    wide = max(p.shape[2] for p in operands)
+    sem = pltpu.SemaphoreType.DMA((half, sum(parts)))
+    vmem = pl.BlockSpec(memory_space=pltpu.VMEM)
+    bufs = [
+        pltpu.VMEM((half,) + p.shape[1:], p.dtype) for p in operands for _ in range(4)
+    ]
     return pl.pallas_call(
-        functools.partial(reduce_kernel, chunks),
-        out_shape=jax.ShapeDtypeStruct((rows, width), f32),
-        in_specs=[pl.BlockSpec(memory_space=pltpu.VMEM)],
-        out_specs=pl.BlockSpec(memory_space=pltpu.VMEM),
-        scratch_shapes=[buf] * 4 + [pltpu.VMEM((rows // chunks, width), f32)] + [sem] * 6,
+        functools.partial(reduce_kernel, parts),
+        out_shape=[jax.ShapeDtypeStruct(p.shape[1:], f32) for p in operands],
+        in_specs=[vmem] * len(operands),
+        out_specs=[vmem] * len(operands),
+        scratch_shapes=bufs + [pltpu.VMEM((high, wide), f32)] + [sem] * 6,
         compiler_params=pltpu.CompilerParams(
             collective_id=call_id, has_side_effects=True, vmem_limit_bytes=VMEM_LIMIT
         ),
-        cost_estimate=WIRE,
+        cost_estimate=pl.CostEstimate(
+            flops=0, bytes_accessed=36 * sum(p.size for p in operands) * 2, transcendentals=0
+        ),
         name="reduce_rows",
-    )(p)
+    )(*operands)
 
 
 def swap_halves(values):
@@ -820,7 +851,8 @@
     rows_w = w_query.shape[0]
     rows_l = w_expand.shape[0]
     ff_cut = shared_down.shape[0]
-    ff_own = ff_cut * spread
+    half = group // 2
+    ff_own = 2 * ff_cut * spread
     ff_pad = -(-ff_own // 128) * 128
     q_own = mine * KEY
     e_own = mine * (NOPE + VD)
@@ -832,10 +864,12 @@
     ).reshape(rows_w, group, q_own)
 
     def ff_columns(weight):
-        cut = weight.reshape(rows_w, spread, group, ff_cut).transpose(0, 2, 1, 3)
-        return jnp.pad(
-            cut.reshape(rows_w, group, ff_own), ((0, 0), (0, 0), (0, ff_pad - ff_own))
+        cut = weight.reshape(rows_w, spread, half, 2 * ff_cut).transpose(2, 0, 1, 3)
+        cut = jnp.pad(
+            cut.reshape(half, 1, rows_w, ff_own),
+            ((0, 0), (0, 0), (0, 0), (0, ff_pad - ff_own)),
         )
+        return jnp.broadcast_to(cut, (half, 2, rows_w, ff_pad)).reshape(group, rows_w, ff_pad)
 
     we_cut = (
         w_expand.reshape(rows_l, group, e_own).transpose(1, 0, 2).reshape(group, rows_w, e_fold)
@@ -844,8 +878,8 @@
         [
             wq_cut.transpose(1, 0, 2),
             we_cut,
-            ff_columns(shared_gate).transpose(1, 0, 2),
-            ff_columns(shared_up).transpose(1, 0, 2),
+            ff_columns(shared_gate),
+            ff_columns(shared_up),
         ],
         axis=2,
     )
@@ -854,10 +888,9 @@
         jnp.where(routes[:, :, None] == expert_ids[None, None, :], gate_values[:, :, None], 0.0),
         axis=1,
     ).T
-    gate_of = jnp.broadcast_to(gate_of[:, None, :], (group, 8, tok_dev))
     x_all, packed, sd, gate_of = prologue(tokens, packed, shared_down, gate_of, spread, 0)
     x_all, parents, gate_of = lax.optimization_barrier(
-        (x_all.reshape(tree, width), parents, gate_of[:, 0])
+        (x_all.reshape(tree, width), parents, gate_of)
     )
     packed = packed.reshape(width, -1)
     wq = packed[:, :q_own]
@@ -919,33 +952,51 @@
     def onward(values):
         return lax.ppermute(values, "expert", ring)
 
-    def sum_with(mine, *others):
-        total = mine.astype(f32)
-        for other in others:
-            total = total + other.astype(f32)
+    def behind(values, s, far):
+        at = 2 * lax.rem(rank // 2 - s + half, half) + lax.rem(rank + far, 2)
+        return lax.dynamic_index_in_dim(values, at, 0, keepdims=False)
+
+    def line_swap(values, m):
+        own_bit = lax.rem(lax.axis_index("dp") // (1 << m), 2)
+        at = spread.bit_length() - 2 - m
+        keep = lax.dynamic_index_in_dim(values, own_bit, at, False)
+        send = lax.dynamic_index_in_dim(values, 1 - own_bit, at, False)
+        swap = [(d, d ^ (1 << m)) for d in range(spread)]
+        return keep, lax.ppermute(send, "dp", swap)
+
+    def both_halves(keep, other):
+        return (keep.astype(f32) + other.astype(f32)).astype(bf16)
+
+    def ring_sum(values):
+        steps = list(range(1, half)) + [0]
+        arrived = across(jnp.stack([behind(values, s, 1) for s in steps]))
+        total = None
+        for k, s in enumerate(steps):
+            term = behind(values, s, 0).astype(f32) + arrived[k].astype(f32)
+            if total is not None:
+                term = term + onward(total.astype(bf16)).astype(f32)
+            total = term
         return total
 
     q_att, g0 = tie(q_att, grad_out)
-    g1, g0_side = onward(g0), across(g0)
+    g1 = onward(g0)
     attn_heads, attended, log_total = attend(reach, q_att, k_att, v_att, scale)
-    attn_heads, g1, g0_side = tie(attn_heads, g1, g0_side)
-    g2, g1_side = onward(g1), across(g1)
+    attn_heads, g1 = tie(attn_heads, g1)
+    g2 = onward(g1)
     attn_own = lax.all_to_all(attn_heads, "expert", split_axis=0, concat_axis=1, tiled=True)
-    attn_own, g2, g1_side = tie(attn_own, g2, g1_side)
-    g3, g2_side = onward(g2), across(g2)
     tokens_f = tokens.astype(f32)
     resid = tokens_f + matmul(attn_own, wo)
     second_normed, second_norm_back = jax.vjp(norm_rows, resid, f_gain)
-    h0, g3, g2_side = tie(second_normed.astype(bf16), g3, g2_side)
-
-    half = group // 2
-    h1_back, h0_side = tie(onward(h0), across(h0))
-    h2_back, h1_side, g3_side = onward(h1_back), across(h1_back), across(g3)
+    b0 = second_normed.astype(bf16)
+
+    b1 = onward(b0)
     gate_of = jnp.concatenate(
         [
-            lax.dynamic_slice_in_dim(
-                gate_of, 2 * lax.rem(rank // 2 - s + half, half) + lax.rem(rank + k, 2), 1, 0
-            )
+            lax.dynamic_slice(
+                gate_of,
+                (2 * lax.rem(rank // 2 - s + half, half) + rank % 2, rank + k - 2 * k * (rank % 2), 0),
+                (1, 1, tok_dev),
+            )[0]
             for s in range(half)
             for k in range(2)
         ],
@@ -960,107 +1011,128 @@
     chosen = (
         place[:, None, :] == jnp.arange(slots, dtype=jnp.int32)[None, :, None]
     ) & routed[:, None, :]
-    pick_all = chosen.astype(bf16)
-    gates_all = jnp.sum(jnp.where(chosen, gate_of[:, None, :], 0.0), axis=2)
-
-    def experts(s, h2, g_rows):
-        pick = pick_all[2 * s : 2 * s + 2]
-        slot_gate = gates_all[2 * s : 2 * s + 2].reshape(2 * slots, 1)
-
-        def take(rows):
-            return jnp.einsum("bst,btd->bsd", pick, rows, preferred_element_type=f32).reshape(
-                2 * slots, width
-            )
-
-        def give(rows):
-            return jnp.einsum(
-                "bst,bsd->btd", pick, rows.reshape(2, slots, width), preferred_element_type=f32
-            ).reshape(2 * tok_dev, width)
-
-        h2 = jnp.stack(h2)
-        e_rows = take(h2).astype(bf16)
+    pick_all = chosen.astype(bf16).reshape(half, 2 * slots, tok_dev)
+    gates_all = jnp.sum(jnp.where(chosen, gate_of[:, None, :], 0.0), axis=2).reshape(
+        half, 2 * slots, 1
+    )
+
+    def take(s, rows, weights=None):
+        picked = matmul(pick_all[s], rows)
+        if weights is not None:
+            picked = picked * weights
+        return picked.astype(bf16)
+
+    def shared(h2, g_rows):
+        s_act, s_gating_back = jax.vjp(gating, matmul(h2, sg), matmul(h2, su))
+        s_act = s_act.astype(bf16)
+        grad_s_act = dot_last(g_rows, sd).astype(bf16)
+        gate_part, up_part = s_gating_back(grad_s_act.astype(f32))
+        gate_part = gate_part.astype(bf16)
+        up_part = up_part.astype(bf16)
+        near = dot_last(gate_part, sg) + dot_last(up_part, su)
+        return near, s_act, gate_part, up_part
+
+    def expert(e_rows, e_grad):
         activated, e_gating_back = jax.vjp(
             gating, matmul(e_rows, expert_gate[0]), matmul(e_rows, expert_up[0])
         )
         activated = activated.astype(bf16)
-        e_result = (
-            matmul(activated, expert_down[0]).astype(bf16).astype(f32) * slot_gate
+        grad_e_act = dot_last(e_grad, expert_down[0]).astype(bf16)
+        gate_part, up_part = e_gating_back(grad_e_act.astype(f32))
+        gate_part = gate_part.astype(bf16)
+        up_part = up_part.astype(bf16)
+        grad_rows = (
+            dot_last(gate_part, expert_gate[0]) + dot_last(up_part, expert_up[0])
         ).astype(bf16)
-        h2 = h2.reshape(2 * tok_dev, width)
-        s_act, s_gating_back = jax.vjp(gating, matmul(h2, sg), matmul(h2, su))
-        s_act = s_act.astype(bf16)
-        out_part = (matmul(s_act, sd) + give(e_result)).astype(bf16)
-
-        g_rows = jnp.stack(g_rows)
-        e_grad = (take(g_rows) * slot_gate).astype(bf16)
-        g_rows = g_rows.reshape(2 * tok_dev, width)
-        grad_e_act = dot_last(e_grad, expert_down[0]).astype(bf16)
-        grad_gate_part, grad_up_part = e_gating_back(grad_e_act.astype(f32))
-        grad_gate_part = grad_gate_part.astype(bf16)
-        grad_up_part = grad_up_part.astype(bf16)
-        grad_rows = (
-            dot_last(grad_gate_part, expert_gate[0]) + dot_last(grad_up_part, expert_up[0])
-        ).astype(bf16)
-        grad_s_act = dot_last(g_rows, sd).astype(bf16)
-        grad_s_gate_part, grad_s_up_part = s_gating_back(grad_s_act.astype(f32))
-        grad_s_gate_part = grad_s_gate_part.astype(bf16)
-        grad_s_up_part = grad_s_up_part.astype(bf16)
-        second_part = (
-            give(grad_rows) + dot_last(grad_s_gate_part, sg) + dot_last(grad_s_up_part, su)
-        ).astype(bf16)
-        return (
-            out_part[:tok_dev],
-            out_part[tok_dev:],
-            second_part[:tok_dev],
-            second_part[tok_dev:],
-            (
-                e_rows,
-                activated,
-                e_grad,
-                grad_gate_part,
-                grad_up_part,
-                h2,
-                s_act,
-                g_rows,
-                jnp.concatenate([grad_s_gate_part, grad_s_up_part], axis=1),
-            ),
+        return grad_rows, activated, gate_part, up_part
+
+    def join(mine, arrived):
+        return jnp.concatenate([mine[:slots], arrived], axis=0)
+
+    def spread_back(s, near, mine, arrived, *more):
+        total = near + dot_first(pick_all[s], join(mine, arrived))
+        for other in more:
+            total = total + other.astype(f32)
+        return total
+
+    e0 = take(0, b0)
+    e0_in = across(e0[slots:])
+    w0, w1 = (take(s, g, gates_all[s]) for s, g in enumerate((g0, g1)))
+    w0_in, w1_in = (across(w[slots:]) for w in (w0, w1))
+    n0_near, *s0 = shared(b0, g0)
+    n0_near, b1, e0_in, w0_in, w1_in, g2 = tie(n0_near, b1, e0_in, w0_in, w1_in, g2)
+    b2, g3 = onward(b1), onward(g2)
+    w2 = take(2, g2, gates_all[2])
+    w2_in = across(w2[slots:])
+    e1 = take(1, b1)
+    e1_in = across(e1[slots:])
+    r0, w0 = join(e0, e0_in), join(w0, w0_in)
+    n0, *k0 = expert(r0, w0)
+    n0, b1 = tie(n0, b1)
+    n0_in = across(n0[slots:])
+    n1_near, *s1 = shared(b1, g1)
+    n1_near, b2, e1_in, n0_in, w2_in, g3 = tie(n1_near, b2, e1_in, n0_in, w2_in, g3)
+    w3 = take(3, g3, gates_all[3])
+    w3_in = across(w3[slots:])
+    b3 = onward(b2)
+    e2 = take(2, b2)
+    e2_in = across(e2[slots:])
+    r1, w1 = join(e1, e1_in), join(w1, w1_in)
+    n1, *k1 = expert(r1, w1)
+    n1, b2 = tie(n1, b2)
+    n1_in = across(n1[slots:])
+    n2_near, *s2 = shared(b2, g2)
+    n2_near, b3, e2_in, n1_in, w3_in = tie(n2_near, b3, e2_in, n1_in, w3_in)
+    ring1 = onward(spread_back(1, n1_near, n1, n1_in).astype(bf16))
+    e3 = take(3, b3)
+    e3_in = across(e3[slots:])
+    r2, w2 = join(e2, e2_in), join(w2, w2_in)
+    n2, *k2 = expert(r2, w2)
+    n2, b3 = tie(n2, b3)
+    n2_in = across(n2[slots:])
+    n3_near, *s3 = shared(b3, g3)
+    n3_near, e3_in, n2_in, ring1 = tie(n3_near, e3_in, n2_in, ring1)
+    ring2 = onward(spread_back(2, n2_near, n2, n2_in, ring1).astype(bf16))
+    r3, w3 = join(e3, e3_in), join(w3, w3_in)
+    n3, *k3 = expert(r3, w3)
+    n3, ring2 = tie(n3, ring2)
+    n3_in = across(n3[slots:])
+    s_act, s_gate_part, s_up_part = (
+        jnp.concatenate(pieces, axis=0) for pieces in zip(s0, s1, s2, s3)
+    )
+    b_all = jnp.concatenate([b0, b1, b2, b3], axis=0)
+    g_all = jnp.concatenate([g0, g1, g2, g3], axis=0)
+    grad_s_cols = dot_first(b_all, jnp.concatenate([s_gate_part, s_up_part], axis=1)).astype(bf16)
+    grad_s_cols, n3_in = tie(grad_s_cols, n3_in)
+    ring3 = onward(spread_back(3, n3_near, n3, n3_in, ring2).astype(bf16))
+    e_rows = jnp.concatenate([r0, r1, r2, r3], axis=0)
+    e_grad = jnp.concatenate([w0, w1, w2, w3], axis=0)
+    activated, gate_part, up_part = (
+        jnp.concatenate(pieces, axis=0) for pieces in zip(k0, k1, k2, k3)
+    )
+    grad_e_gate = dot_first(e_rows, gate_part).astype(bf16)
+    grad_e_up = dot_first(e_rows, up_part).astype(bf16)
+    e_result = matmul(activated, expert_down[0]).astype(bf16).reshape(half, 2 * slots, width)
+    grad_e_gate, grad_e_up, ring3, activated, s_act, e_result = tie(
+        grad_e_gate, grad_e_up, ring3, activated, s_act, e_result
+    )
+    grad_second = spread_back(0, n0_near, n0, n0_in, ring3)
+    o_in = across(e_result[:, slots:])
+    grad_e_down = dot_first(activated, e_grad).astype(bf16)
+    grad_s_down = dot_first(s_act, g_all).astype(bf16)
+
+    def out_term(s, *more):
+        weighed = (join(e_result[s], o_in[s]).astype(f32) * gates_all[s]).astype(bf16)
+        total = matmul(s_act[s * tok_dev : (s + 1) * tok_dev], sd) + dot_first(
+            pick_all[s], weighed
         )
-
-    o0, o0_far, n0, n0_far, kept0 = experts(0, (h0, h0_side), (g0, g0_side))
-    n0, h2_back, h1_side, g3_side = tie(n0, h2_back, h1_side, g3_side)
-    h3_back, h2_side = onward(h2_back), across(h2_back)
-    o1, o1_far, n1, n1_far, kept1 = experts(1, (h1_back, h1_side), (g1, g1_side))
-    n1, n1_far, h3_back, h2_side = tie(n1, n1_far, h3_back, h2_side)
-    h3_side, n1_in = across(h3_back), across(n1_far)
-    o2, o2_far, n2, n2_far, kept2 = experts(2, (h2_back, h2_side), (g2, g2_side))
-    n2, n2_far, h3_side, n1_in = tie(n2, n2_far, h3_side, n1_in)
-    ring1, n2_in = onward(sum_with(n1, n1_in).astype(bf16)), across(n2_far)
-    o3, o3_far, n3, n3_far, kept3 = experts(3, (h3_back, h3_side), (g3, g3_side))
-    kept = [kept0, kept1, kept2, kept3]
-    n3, n3_far, ring1, n2_in = tie(n3, n3_far, ring1, n2_in)
-    ring2, n3_in = onward(sum_with(n2, n2_in, ring1).astype(bf16)), across(n3_far)
-    e_rows, activated, e_grad, grad_gate_part, grad_up_part = (
-        jnp.concatenate([pieces[k] for pieces in kept], axis=0) for k in range(5)
-    )
-    grad_e_gate = dot_first(e_rows, grad_gate_part).astype(bf16)
-    grad_e_up = dot_first(e_rows, grad_up_part).astype(bf16)
-    grad_e_gate, grad_e_up, ring2, n3_in, activated = tie(
-        grad_e_gate, grad_e_up, ring2, n3_in, activated
-    )
-    ring3, n0_in = onward(sum_with(n3, n3_in, ring2).astype(bf16)), across(n0_far)
-    grad_e_down = dot_first(activated, e_grad).astype(bf16)
-    grad_s_down = sum(dot_first(pieces[6], pieces[7]) for pieces in kept).astype(bf16)
-    grad_s_cols = sum(dot_first(pieces[5], pieces[8]) for pieces in kept).astype(bf16)
-    grad_e_down, grad_s_down, grad_s_cols, ring3, n0_in, o1_far, o2_far, o3_far, o0_far = tie(
-        grad_e_down, grad_s_down, grad_s_cols, ring3, n0_in, o1_far, o2_far, o3_far, o0_far
-    )
-    grad_second = sum_with(n0, n0_in, ring3)
-    o1_in = across(o1_far)
+        for other in more:
+            total = total + other.astype(f32)
+        return total
 
     grad_e_gate = lax.psum_scatter(grad_e_gate, "dp", scatter_dimension=0, tiled=True)
     grad_e_up = lax.psum_scatter(grad_e_up, "dp", scatter_dimension=0, tiled=True)
-    grad_e_down = lax.psum_scatter(grad_e_down, "dp", scatter_dimension=1, tiled=True)
-    grad_s_down = lax.psum_scatter(grad_s_down[:ff_own], "dp", scatter_dimension=0, tiled=True)
+    grad_e_down_all, grad_s_down = grad_e_down, grad_s_down[:ff_own]
 
     def sum_columns(grads):
         return lax.psum_scatter(grads, "dp", scatter_dimension=0, tiled=True)
@@ -1068,13 +1140,8 @@
     grad_s_cols = sum_columns(grad_s_cols)
 
     def ff_restore(cut):
-        return (
-            cut[:, :, :ff_own]
-            .reshape(group, rows_w, spread, ff_cut)
-            .transpose(1, 2, 0, 3)
-            .reshape(rows_w, -1)
-            .astype(f32)
-        )
+        both = cut[:, :, :ff_own].astype(f32).reshape(half, 2, rows_w, spread, 2 * ff_cut)
+        return (both[:, 0] + both[:, 1]).transpose(1, 2, 0, 3).reshape(rows_w, -1)
 
     grad_f = grad_out.astype(f32)
     grad_resid_norm, grad_f_gain = second_norm_back(grad_second)
@@ -1082,22 +1149,50 @@
     grad_attn_out = grad_resid.astype(bf16)
     grad_w_out = dot_first(attn_own, grad_attn_out).astype(bf16)
     grad_attended = dot_last(grad_attn_out, wo).astype(bf16)
-    grad_attended, grad_w_out, o1_in = tie(grad_attended, grad_w_out, o1_in)
-    ring1, o2_in = onward(sum_with(o1, o1_in).astype(bf16)), across(o2_far)
+    grad_attended, o_in = tie(grad_attended, o_in)
     grad_heads = lax.all_to_all(grad_attended, "expert", split_axis=1, concat_axis=0, tiled=True)
-    grad_heads, grad_e_gate, ring1, o2_in = tie(grad_heads, grad_e_gate, ring1, o2_in)
-    ring2, o3_in = onward(sum_with(o2, o2_in, ring1).astype(bf16)), across(o3_far)
+    grad_heads, o1, grad_w_out, grad_s_cols, grad_e_down, grad_s_down, grad_e_gate = tie(
+        grad_heads,
+        out_term(1).astype(bf16),
+        grad_w_out,
+        grad_s_cols,
+        grad_e_down_all,
+        grad_s_down,
+        grad_e_gate,
+    )
+    s_keep, s_other = line_swap(
+        grad_s_down.reshape((2,) * (spread.bit_length() - 1) + (2, ff_cut, width)), 0
+    )
+    ring1 = onward(o1)
+    grad_s_cut = lax.all_to_all(
+        grad_s_cols.reshape(group, rows_w, -1), "expert", split_axis=0, concat_axis=0, tiled=True
+    )
     grad_w_out = lax.psum_scatter(grad_w_out, "dp", scatter_dimension=0, tiled=True)
     grad_q_lin, grad_kv, lat_part = attend_back(
         reach, q_att, k_att, v_att, grad_heads, attended, log_total, we, tables, scale
     )
-    lat_part, grad_e_up, ring2, o3_in = tie(lat_part, grad_e_up, ring2, o3_in)
-    ring3, o0_in = onward(sum_with(o3, o3_in, ring2).astype(bf16)), across(o0_far)
-    grad_w_exp = dot_first(ckv, grad_kv)
-    lat_part = lat_part.reshape(group, tok_dev, -1)
-    grad_lat_sum = reduce_rows(lat_part, 5, 2)
-    grad_lat_sum, ring3, o0_in = tie(grad_lat_sum, ring3, o0_in)
-    block_out = (resid + sum_with(o0, o0_in, ring3)).astype(bf16)
+    lat_part, grad_q_lin, ring1, grad_e_down, s_other = tie(
+        lat_part, grad_q_lin, ring1, grad_e_down, s_other
+    )
+    ring2 = onward(out_term(2, ring1).astype(bf16))
+    grad_s_down = both_halves(s_keep, s_other)
+    for m in range(1, spread.bit_length() - 1):
+        s_keep, s_other = line_swap(grad_s_down, m)
+        if m < spread.bit_length() - 2:
+            grad_s_down = both_halves(s_keep, s_other)
+    (grad_lat_sum,) = reduce_rows([lat_part.reshape(group, tok_dev, -1)], 5, 2)
+    grad_lat_sum, grad_q_lin, ring2, s_other, grad_w_out, grad_e_down = tie(
+        grad_lat_sum, grad_q_lin, ring2, s_other, grad_w_out, grad_e_down
+    )
+    grad_s_down = both_halves(s_keep, s_other)
+    own_side = rank % 2
+    s_keep = lax.dynamic_index_in_dim(grad_s_down, own_side, 0, False)
+    s_other = across(lax.dynamic_index_in_dim(grad_s_down, 1 - own_side, 0, False))
+    ring3 = onward(out_term(3, ring2).astype(bf16))
+    first_part = dot_last(grad_q_lin, wq).astype(bf16).reshape(group, tok_dev, width)
+    grad_a_cols = jnp.concatenate(
+        [dot_first(h1, grad_q_lin), dot_first(ckv, grad_kv).reshape(width, e_fold)], axis=1
+    ).astype(bf16)
 
     def latent_parts(latent_in, gain_vec):
         return (
@@ -1110,7 +1205,7 @@
         (grad_lat_sum[:, :KV], grad_lat_sum[:, KV : KV + ROPE])
     )
     grad_latent = grad_latent.astype(bf16)
-    grad_w_lat = dot_first(own(h1), grad_latent)[:, :KV + ROPE]
+    grad_w_lat = dot_first(own(h1), grad_latent)[:, : KV + ROPE]
     grad_gains = jnp.stack(
         [
             grad_f_gain,
@@ -1118,42 +1213,48 @@
         ],
         axis=1,
     )
-    lat_grads = lax.psum_scatter(
-        jnp.concatenate(
-            [grad_w_lat, jnp.pad(grad_gains, ((0, 0), (0, ROPE - 2)))], axis=1
-        ).astype(bf16),
-        "dp",
-        scatter_dimension=0,
-        tiled=True,
-    )
-
-    grad_a_cols = jnp.concatenate(
-        [dot_first(h1, grad_q_lin), grad_w_exp.reshape(width, e_fold)], axis=1
+    lat_grads_in = jnp.concatenate(
+        [grad_w_lat, jnp.pad(grad_gains, ((0, 0), (0, ROPE - 2)))], axis=1
     ).astype(bf16)
-    grad_a_cols = sum_columns(grad_a_cols)
-    first_part = dot_last(grad_q_lin, wq).astype(bf16).reshape(group, tok_dev, width)
-    first_part, grad_e_down, grad_s_down, grad_s_cols = lax.optimization_barrier(
-        (first_part, grad_e_down, grad_s_down, grad_s_cols)
-    )
-    first_sum = reduce_rows(first_part, 6)
-    first_sum, rest, cols = lax.optimization_barrier(
-        (
-            first_sum,
-            jnp.concatenate([grad_w_out, lat_grads], axis=1),
-            jnp.concatenate([grad_s_cols, grad_a_cols], axis=1),
-        )
-    )
-    cols = lax.all_to_all(
-        cols.reshape(group, rows_w, -1), "expert", split_axis=0, concat_axis=0, tiled=True
-    )
-    rest = reduce_rows(rest.reshape(group, rows_w, -1), 7, max(1, rows_w // 32))
-    grad_w_out = rest[:, :width]
-    grad_w_lat = rest[:, width : width + lat_w]
-    grad_f_gain = rest[:, width + lat_w]
-    grad_l_gain = rest[:rows_l, width + lat_w + 1]
-    grad_s_gate = ff_restore(cols[:, :, :ff_pad])
-    grad_s_up = ff_restore(cols[:, :, ff_pad : 2 * ff_pad])
-    grad_a_cols = cols[:, :, 2 * ff_pad :]
+    first_part, lat_grads, grad_a_cols = tie(first_part, lat_grads_in, grad_a_cols)
+    lat_grads = lax.psum_scatter(lat_grads, "dp", scatter_dimension=0, tiled=True)
+    grad_a_cols = lax.psum_scatter(grad_a_cols, "dp", scatter_dimension=0, tiled=True)
+    grad_e_down = lax.psum_scatter(grad_e_down, "dp", scatter_dimension=1, tiled=True)
+    first_sum, grad_w_out = reduce_rows(
+        [first_part, grad_w_out.reshape(group, rows_w, width)], 6, 4
+    )
+    (
+        first_sum,
+        lat_grads,
+        ring3,
+        s_keep,
+        s_other,
+        grad_a_cols,
+        grad_s_cut,
+        grad_e_gate,
+        grad_e_up,
+    ) = tie(
+        first_sum,
+        lat_grads,
+        ring3,
+        s_keep,
+        s_other,
+        grad_a_cols,
+        grad_s_cut,
+        grad_e_gate,
+        grad_e_up,
+    )
+    grad_s_down = s_keep.astype(f32) + s_other.astype(f32)
+    block_out = (resid + out_term(0, ring3)).astype(bf16)
+    lat_grads = ring_sum(lat_grads.reshape(group, rows_w, -1))
+    grad_w_lat = lat_grads[:, :lat_w]
+    grad_f_gain = lat_grads[:, lat_w]
+    grad_l_gain = lat_grads[:rows_l, lat_w + 1]
+    grad_s_gate = ff_restore(grad_s_cut[:, :, :ff_pad])
+    grad_s_up = ff_restore(grad_s_cut[:, :, ff_pad:])
+    grad_a_cols = lax.all_to_all(
+        grad_a_cols.reshape(group, rows_w, -1), "expert", split_axis=0, concat_axis=0, tiled=True
+    )
     grad_w_q = (
         grad_a_cols[:, :, :q_own]
         .reshape(group, rows_w, mine, KEY)[..., : NOPE + ROPE]
@@ -1191,7 +1292,7 @@
         grad_f_gain,
         grad_s_gate,
         grad_s_up,
-        grad_s_down.astype(f32),
+        grad_s_down,
         grad_e_gate.astype(f32)[None],
         grad_e_up.astype(f32)[None],
         grad_e_down.astype(f32)[None],

time: 1040 us -> 1010 us (0.971)
  waiting for transfers between devices: 210 us -> 125 us
  matrix products: 212 us -> 254 us
  other arithmetic: 82.8 us -> 56.4 us
  local copies, waits for them, and re-layouts: 71.6 us -> 91.4 us
  starting transfers between devices: 42.9 us -> 61.4 us
    ppermute x16 -> x15, waiting for transfers between devices: 107 us -> 39.6 us  [across(): return lax.ppermute(values, 'expert', side)]
    ppermute x12 -> x15, waiting for transfers between devices: 92.2 us -> 52.5 us  [onward(): return lax.ppermute(values, 'expert', ring)]
    dot_general x26 -> x31, matrix products: 48.8 us -> 83.8 us  [matmul(): return jnp.dot(left, right, preferred_element_type=f32)]
    all_to_all x1, waiting for transfers between devices: 3.76 us -> 29.7 us  [per_device(): lax.all_to_all(attn_heads, 'expert', split_axis=0, concat_axis=1, tiled=T...]
    convert_element_type x14 -> x9, other arithmetic: 33.3 us -> 8.99 us  [the longest x2 3.23 us: both_halves(): return (keep.astype(f32) + other.astype(f32)).astype(bf16)]
    dot_general x16 -> x0, matrix products: 20.5 us -> none  [the longest x8 14.3 us: take(): jnp.einsum('bst,btd->bsd', pick, rows, preferred_element_type=f32)]
    pallas_call x3 -> x2, Pallas kernels: 181 us -> 164 us  [reduce_rows(): pl.pallas_call(functools.partial(reduce_kernel, parts), out_shape=[jax.Sh...]
    pallas_call x1, Pallas kernels: 146 us -> 162 us  [prologue(): pl.pallas_call(functools.partial(prologue_kernel, chunks), out_shape=[jax...]
  transfers between devices with their start and end apart: 41 -> 45, of which waited for: 18 -> 16; matrix products, arithmetic and copies ran while one was open for 27% -> 36% of each run, Pallas kernels for 39% -> 40%
where the time goes in v3:
time: 1010 us; the launch traced here: 1000 us
  Pallas kernels  397 us (39%)
  matrix products  254 us (25%)
  waiting for transfers between devices  125 us (12%)
  local copies, waits for them, and re-layouts  91.4 us (9%)
  starting transfers between devices  61.4 us (6%)
  other arithmetic  56.4 us (6%)
  between operations  16.3 us (2%)
    pallas_call x2, Pallas kernels, reduce_rows(): pl.pallas_call(functools.partial(reduce_kernel, parts), out_shape=[jax.Sh...  164 us
    pallas_call x1, Pallas kernels, prologue(): pl.pallas_call(functools.partial(prologue_kernel, chunks), out_shape=[jax...  162 us
    dot_general x27, matrix products, dot_last(): lax.dot_general(left, right, (((1,), (1,)), ((), ())), preferred_element_...  89.3 us
    dot_general x31, matrix products, matmul(): return jnp.dot(left, right, preferred_element_type=f32)  83.8 us
    dot_general x17, matrix products, dot_first(): lax.dot_general(left, right, (((0,), (0,)), ((), ())), preferred_element_...  79.8 us
    ppermute x15, waiting for transfers between devices, onward(): return lax.ppermute(values, 'expert', ring)  52.5 us
    ppermute x15, waiting for transfers between devices, across(): return lax.ppermute(values, 'expert', side)  39.6 us
    all_to_all x1, waiting for transfers between devices, per_device(): lax.all_to_all(attn_heads, 'expert', split_axis=0, concat_axis=1, tiled=T...  29.7 us
  transfers between devices with their start and end apart: 45, of which 16 were waited for; matrix products, arithmetic and copies ran while one was open for 36% of the time, Pallas kernels for 40%

profile of v3, /device:TPU:0, one launch (start us, length us, event | category | flops | bytes accessed | tf_op | source)
XLA Modules:
  0.0 1001.2 jit_solution(13003399816847886654)
XLA Ops:
  20.7 162.2 %prologue.1 = (bf16[8,256,2048]{2,1,0:T(8,128)(2,1)}, bf16[4,8,64,2176]{3,2,1,0:T(8,128)(2,1)}, bf16[4,2,88,2048]{3,2,1,0:T(8,128)(2,1)}, f32[8,8,256]{2,1,0:T(8,128)}) custom-call(bf16[256,2048]{1,0:T(8,128)(2,1)} %x_ref.1, bf16[8,64,2176]{2,1,0:T(8,128)(2,1)} %pad_maximum_fusion.3.w_ref, bf16[88,2048]{1,0:T(8,128)(2,1)} %d_ref.1, f32[8,256]{1,0:T(8,128)} %bitcast.370), custom_call_target="tpu_custom_call" | custom-call | bytes 300000000 | tf_op jit(solution)/shard_map/prologue/pallas_call | solution.py:341
  193.3 20.2 %project.1 = (bf16[2048,2048]{1,0:T(8,128)(2,1)}, bf16[2048,512]{1,0:T(8,128)(2,1)}, bf16[2048,512]{1,0:T(8,128)(2,1)}, bf16[2048,256]{1,0:T(8,128)(2,1)}, f32[2...) custom-call(bf16[2048,2048]{1,0:T(8,128)(2,1)} %bitcast.329, bf16[2048,2176]{1,0:T(8,128)(2,1)} %bitcast.298, ...), custom_call_target="tpu_custom_call" | custom-call | bytes 60000000 | tf_op jit(solution)/shard_map/project/pallas_call | solution.py:560
  215.8 21.5 %attend.1 = (bf16[2048,256]{1,0:T(8,128)(2,1)}, f32[2048,256]{1,0:T(8,128)}, f32[2,2048]{1,0:T(2,128)}) custom-call(s32[64]{0:T(128)} %reshape.364.reach_ref, bf16[2048,512]{1,0:T(8,128)(2,1)} %get-tuple-element.115.q_ref, bf16[2048,512]{1,0:T(8,128)(2,1)} %get-tuple-element.116.k_ref, bf16[2048,256]{1,0:T(8,128)(2,1)} %get-tuple-element.117.v_ref), custom_call_target="tpu_custom_call" | custom-call | bytes 70000000 | tf_op jit(solution)/shard_map/attend/pallas_call | solution.py:652
  239.6 8.7 all-to-all-start
  262.1 29.7 %all-to-all-done = bf16[8,256,256]{1,2,0:T(8,128)(2,1)} async-done(((bf16[8,256,256]{1,2,0:T(8,128)(2,1)}), bf16[8,256,256]{1,2,0:T(8,128)(2,1)}, u32[]{:S(2)}, u32[]{:S(2)}) %all-to-all-start) | async-done | bytes 1048608 | tf_op jit(solution)/shard_map/all_to_all | solution.py:986
  291.8 6.5 multiply_reduce_fusion.2
  309.4 14.2 %collective-permute-done.1 = bf16[256,2048]{1,0:T(8,128)(2,1)S(1)} collective-permute-done((bf16[256,2048]{1,0:T(8,128)(2,1)S(1)}, bf16[256,2048]{1,0:T(8,128)(2,1)S(1)}, u32[]{:S(2)}, u32[]{:S(2)}) %collective-permute-start.1) | collective-permute-done | bytes 1048608 | tf_op jit(solution)/shard_map/ppermute | solution.py:953
  324.5 4.7 fusion.117
  333.5 5.5 multiply_convert_fusion.8
  339.0 5.0 fusion.12
  344.0 4.6 fusion.107
  365.6 4.7 fusion.123
  370.3 6.1 collective-permute-done.9
  376.5 4.9 collective-permute-done.8
  382.1 4.4 fusion.10
  386.5 5.5 multiply_convert_fusion.7
  392.0 5.0 fusion.8
  397.1 4.6 fusion.104
  414.0 4.6 fusion.129
  418.5 7.3 collective-permute-done.14
  425.8 4.9 collective-permute-done.13
  435.8 5.5 multiply_convert_fusion.6
  441.3 5.0 fusion.4
  446.4 4.6 fusion.101
  465.6 4.9 collective-permute-done.16
  470.5 7.3 collective-permute-done.17
  489.2 10.8 %collective-permute-done.18 = bf16[256,2048]{1,0:T(8,128)(2,1)} collective-permute-done((bf16[256,2048]{1,0:T(8,128)(2,1)S(1)}, bf16[256,2048]{1,0:T(8,128)(2,1)}, u32[]{:S(2)}, u32[]{:S(2)}) %collective-permute-start.18) | collective-permute-done | bytes 1048608 | tf_op jit(solution)/shard_map/ppermute | solution.py:953
  502.0 11.4 %convolution_convert_fusion.5 = bf16[2048,1536]{1,0:T(8,128)(2,1)} fusion(bf16[256,2048]{1,0:T(8,128)(2,1)S(1)} %copy-done.43, bf16[256,2048]{1,0:T(8,128)(2,1)S(1)} %copy-done.41, bf16[256,2048]{1,0:T(8,128)(2,1)S(1)} %copy-done.39, bf16[256,2048]{1,0:T(8,128)(2,1)S(1)} %multiply_convert_fusion, bf16[256,768]{1,0:T(8,128)(2,1)} %copy-done.66, ...), kind=kOutput, calls=%fused_computation.5 | convolution fusion | flops 6487539712 | bytes 13631488 | tf_op jit(solution)/shard_map/dot_general | solution.py:70
  520.8 9.7 convolution_convert_fusion.1
  530.4 10.8 %convolution_convert_fusion.2 = bf16[2048,1408]{1,0:T(8,128)(2,1)} fusion(bf16[896,2048]{1,0:T(8,128)(2,1)} %constant_dynamic-update-slice_fusion, bf16[224,1408]{1,0:T(8,128)(2,1)} %copy-done.106, bf16[224,1408]{1,0:T(8,128)(2,1)} %copy-done.105, bf16[224,1408]{1,0:T(8,128)(2,1)} %copy-done.104, bf16[224,1408]{1,0:T(8,128)(2,1)} %copy-done.103), kind=kOutput, calls=%fused_computation.2 | convolution fusion | flops 5180358656 | bytes 11960320 | tf_op jit(solution)/shard_map/dot_general | solution.py:70
  545.1 11.6 %fusion.57 = bf16[896,2048]{1,0:T(8,128)(2,1)} fusion(bf16[1,1408,2048]{2,1,0:T(8,128)(2,1)} %param.35, bf16[224,1408]{1,0:T(8,128)(2,1)S(1)} %copy-done.53, bf16[224,1408]{1,0:T(8,128)(2,1)S(1)} %copy-done.51, bf16[224,1408]{1,0:T(8,128)(2,1)S(1)} %copy-done.49, bf16[224,1408]{1,0:T(8,128)(2,1)S(1)} %copy-done.47), kind=kOutput, calls=%fused_computation.69 | convolution fusion | flops 5179310080 | bytes 11960320 | tf_op jit(solution)/shard_map/dot_general | solution.py:62
  556.7 9.3 collective-permute-done.20
  578.3 8.3 convolution_convert_fusion
  586.6 6.9 convolution_convert_fusion.7
  593.6 6.7 fusion.49
  600.2 8.4 collective-permute-done.21
  618.8 6.9 convolution_convert_fusion.4
  642.0 28.9 %attend_back.1 = (bf16[2048,512]{1,0:T(8,128)(2,1)}, bf16[2048,512]{1,0:T(8,128)(2,1)}, bf16[2048,640]{1,0:T(8,128)(2,1)}) custom-call(s32[64]{0:T(128)} %reshape.364.reach_ref, bf16[2048,512]{1,0:T(8,128)(2,1)} %get-tuple-element.115.q_ref, bf16[2048,512]{1,0:T(8,128)(2,1)} %get-tuple-element.116.k_ref, bf16[2048,256]{1,0:T(8,128)(2,1)} %get-tuple-element.117.v_ref, ...), custom_call_target="tpu_custom_call" | custom-call | bytes 90000000 | tf_op jit(solution)/shard_map/attend_back/pallas_call | solution.py:786
  670.9 5.1 fusion.83
  680.6 7.6 collective-permute-start.25
  700.3 34.9 %reduce_rows.2 = f32[256,640]{1,0:T(8,128)} custom-call(bf16[8,256,640]{2,1,0:T(8,128)(2,1)} %bitcast.335), custom_call_target="tpu_custom_call" | custom-call | bytes 94371840 | tf_op jit(solution)/shard_map/reduce_rows/pallas_call | solution.py:477
  748.0 9.5 convolution_convert_fusion.6
  759.2 10.2 %convolution_convert_fusion.3 = bf16[2048,2048]{1,0:T(8,128)(2,1)} fusion(bf16[2048,512]{1,0:T(8,128)(2,1)} %get-tuple-element.176, bf16[2048,2176]{1,0:T(8,128)(2,1)} %bitcast.299), kind=kOutput, calls=%fused_computation.3 | convolution fusion | flops 4299161600 | bytes 12582912 | tf_op jit(solution)/shard_map/dot_general | solution.py:66
  770.9 4.5 all-to-all-start.2
  788.9 129.2 %reduce_rows.3 = (f32[256,2048]{1,0:T(8,128)}, f32[64,2048]{1,0:T(8,128)}) custom-call(bf16[8,256,2048]{2,1,0:T(8,128)(2,1)} %bitcast.328, bf16[8,64,2048]{2,1,0:T(8,128)(2,1)} %bitcast.342), custom_call_target="tpu_custom_call" | custom-call | bytes 377487360 | tf_op jit(solution)/shard_map/reduce_rows/pallas_call | solution.py:477
  921.1 6.2 all-to-all-start.3
  962.4 4.4 collective-permute-done.29
  969.0 5.0 collective-permute-done.30
  (537 shorter events, 276.5 us)
Async XLA Ops:
  7.2 181.3 %all-gather.3.cloned.1.call-start = ((), (), s32[]{:S(2)}) async-start(), calls=%async_computation.11 | async-start | bytes 2703360 | tf_op jit(solution)/shard_map/all_gather | solution.py:907
  10.4 281.4 %all-gather.5.cloned.1.call-start = ((), (), s32[]{:S(2)}) async-start(), calls=%async_computation.12 | async-start | bytes 8650752 | tf_op jit(solution)/shard_map/all_gather | solution.py:914
  20.7 164.4 %copy-start.98 = (s32[1,8]{1,0:T(1,128)S(1)}, s32[1,8]{1,0:T(1,128)}, u32[]{:S(2)}) copy-start(s32[1,8]{1,0:T(1,128)} %param.22) | copy-start | bytes 100
  213.5 23.8 %collective-permute-start = (bf16[256,2048]{1,0:T(8,128)(2,1)S(1)}, bf16[256,2048]{1,0:T(8,128)(2,1)}, u32[]{:S(2)}, u32[]{:S(2)}) collective-permute-start(bf16[256,2048]{1,0:T(8,128)(2,1)S(1)} %copy-done.13), channel_id=1, source_target_pairs={{0,2},{1,3},{2,4},{3,5},{4,6},{5,7},{6,0},{7,1},{8,10},{9,11},{10,... | collective-permute-start | bytes 3145736 | tf_op jit(solution)/shard_map/ppermute | solution.py:953
  239.6 52.2 %all-to-all-start = ((bf16[8,256,256]{1,2,0:T(8,128)(2,1)}), bf16[8,256,256]{1,2,0:T(8,128)(2,1)}, u32[]{:S(2)}, u32[]{:S(2)}) async-start(bf16[8,256,256]{1,2,0:T(8,128)(2,1)} %copy.139), calls=%async_computation | async-start | bytes 2097152 | tf_op jit(solution)/shard_map/all_to_all | solution.py:986
  248.3 383.7 %reduce-scatter.8.cloned.1.call-start = ((), (), s32[]{:S(2)}) async-start(), calls=%async_computation.13 | async-start | bytes 7864320 | tf_op jit(solution)/shard_map/reduce_scatter | solution.py:1138
  248.4 156.7 %copy-start.84 = (f32[224]{0:T(256)}, f32[224]{0:T(256)S(1)}, u32[]{:S(2)}) copy-start(f32[224]{0:T(256)S(1)} %mul.627) | copy-start | bytes 2692
  248.9 292.3 %copy-start.34 = (pred[2,112,256]{2,1,0:T(8,128)(4,1)}, pred[2,112,256]{2,1,0:T(8,128)(4,1)S(1)}, u32[]{:S(2)}) copy-start(pred[2,112,256]{2,1,0:T(8,128)(4,1)S(1)} %get-tuple-element.291) | copy-start | bytes 172036
  252.0 54.5 %collective-permute-start.3 = (bf16[112,2048]{1,0:T(8,128)(2,1)}, bf16[112,2048]{1,0:T(8,128)(2,1)}, u32[]{:S(2)}, u32[]{:S(2)}) collective-permute-start(bf16[112,2048]{1,0:T(8,128)(2,1)} %get-tuple-element.262), channel_id=1, source_target_pairs={{0,1},{1,0},{2,3},{3,2},{4,5},{5,4},{6,7},{7,6},{8,9},{9,8},{10,11... | collective-permute-start | bytes 1376264 | tf_op jit(solution)/shard_map/ppermute | solution.py:950
  255.9 50.6 %collective-permute-start.5 = (bf16[256,2048]{1,0:T(8,128)(2,1)}, bf16[256,2048]{1,0:T(8,128)(2,1)}, u32[]{:S(2)}, u32[]{:S(2)}) collective-permute-start(bf16[256,2048]{1,0:T(8,128)(2,1)} %collective-permute-done), channel_id=1, source_target_pairs={{0,2},{1,3},{2,4},{3,5},{4,6},{5,7},{6,0},{7,1},{8,10},{9,11},{10,... | collective-permute-start | bytes 3145736 | tf_op jit(solution)/shard_map/ppermute | solution.py:953
  260.9 45.6 %collective-permute-start.4 = (bf16[112,2048]{1,0:T(8,128)(2,1)}, bf16[112,2048]{1,0:T(8,128)(2,1)}, u32[]{:S(2)}, u32[]{:S(2)}) collective-permute-start(bf16[112,2048]{1,0:T(8,128)(2,1)} %slice.380), channel_id=1, source_target_pairs={{0,1},{1,0},{2,3},{3,2},{4,5},{5,4},{6,7},{7,6},{8,9},{9,8},{10,11... | collective-permute-start | bytes 1376264 | tf_op jit(solution)/shard_map/ppermute | solution.py:950
  300.1 23.5 %collective-permute-start.1 = (bf16[256,2048]{1,0:T(8,128)(2,1)S(1)}, bf16[256,2048]{1,0:T(8,128)(2,1)S(1)}, u32[]{:S(2)}, u32[]{:S(2)}) collective-permute-start(bf16[256,2048]{1,0:T(8,128)(2,1)S(1)} %multiply_convert_fusion), channel_id=1, source_target_pairs={{0,2},{1,3},{2,4},{3,5},{4,6},{5,7},{6,0},{7,1},{8,10},{9,11},{10,... | collective-permute-start | bytes 3145736 | tf_op jit(solution)/shard_map/ppermute | solution.py:953
  300.3 9.1 collective-permute-start.2
  324.0 57.3 %collective-permute-start.6 = (bf16[256,2048]{1,0:T(8,128)(2,1)S(1)}, bf16[256,2048]{1,0:T(8,128)(2,1)S(1)}, u32[]{:S(2)}, u32[]{:S(2)}) collective-permute-start(bf16[256,2048]{1,0:T(8,128)(2,1)S(1)} %collective-permute-done.1), channel_id=1, source_target_pairs={{0,2},{1,3},{2,4},{3,5},{4,6},{5,7},{6,0},{7,1},{8,10},{9,11},{10,... | collective-permute-start | bytes 3145736 | tf_op jit(solution)/shard_map/ppermute | solution.py:953
  353.5 16.8 %collective-permute-start.7 = (bf16[112,2048]{1,0:T(8,128)(2,1)S(1)}, bf16[112,2048]{1,0:T(8,128)(2,1)S(1)}, u32[]{:S(2)}, u32[]{:S(2)}) collective-permute-start(bf16[112,2048]{1,0:T(8,128)(2,1)S(1)} %get-tuple-element.279), channel_id=1, source_target_pairs={{0,1},{1,0},{2,3},{3,2},{4,5},{5,4},{6,7},{7,6},{8,9},{9,8},{10,11... | collective-permute-start | bytes 1376264 | tf_op jit(solution)/shard_map/ppermute | solution.py:950
  353.6 27.8 %collective-permute-start.10 = (bf16[256,2048]{1,0:T(8,128)(2,1)}, bf16[256,2048]{1,0:T(8,128)(2,1)S(1)}, u32[]{:S(2)}, u32[]{:S(2)}) collective-permute-start(bf16[256,2048]{1,0:T(8,128)(2,1)} %collective-permute-done.5), channel_id=1, source_target_pairs={{0,2},{1,3},{2,4},{3,5},{4,6},{5,7},{6,0},{7,1},{8,10},{9,11},{10,... | collective-permute-start | bytes 3145736 | tf_op jit(solution)/shard_map/ppermute | solution.py:953
  358.1 18.4 %collective-permute-start.9 = (bf16[112,2048]{1,0:T(8,128)(2,1)S(1)}, bf16[112,2048]{1,0:T(8,128)(2,1)S(1)}, u32[]{:S(2)}, u32[]{:S(2)}) collective-permute-start(bf16[112,2048]{1,0:T(8,128)(2,1)S(1)} %get-tuple-element.257), channel_id=1, source_target_pairs={{0,1},{1,0},{2,3},{3,2},{4,5},{5,4},{6,7},{7,6},{8,9},{9,8},{10,11... | collective-permute-start | bytes 1376264 | tf_op jit(solution)/shard_map/ppermute | solution.py:950
  360.1 21.3 %collective-permute-start.8 = (bf16[112,2048]{1,0:T(8,128)(2,1)S(1)}, bf16[112,2048]{1,0:T(8,128)(2,1)S(1)}, u32[]{:S(2)}, u32[]{:S(2)}) collective-permute-start(bf16[112,2048]{1,0:T(8,128)(2,1)S(1)} %get-tuple-element.264), channel_id=1, source_target_pairs={{0,1},{1,0},{2,3},{3,2},{4,5},{5,4},{6,7},{7,6},{8,9},{9,8},{10,11... | collective-permute-start | bytes 1376264 | tf_op jit(solution)/shard_map/ppermute | solution.py:950
  381.8 48.9 %collective-permute-start.11 = (bf16[256,2048]{1,0:T(8,128)(2,1)S(1)}, bf16[256,2048]{1,0:T(8,128)(2,1)S(1)}, u32[]{:S(2)}, u32[]{:S(2)}) collective-permute-start(bf16[256,2048]{1,0:T(8,128)(2,1)S(1)} %collective-permute-done.6), channel_id=1, source_target_pairs={{0,2},{1,3},{2,4},{3,5},{4,6},{5,7},{6,0},{7,1},{8,10},{9,11},{10,... | collective-permute-start | bytes 3145736 | tf_op jit(solution)/shard_map/ppermute | solution.py:953
  403.8 14.7 %collective-permute-start.12 = (bf16[112,2048]{1,0:T(8,128)(2,1)S(1)}, bf16[112,2048]{1,0:T(8,128)(2,1)S(1)}, u32[]{:S(2)}, u32[]{:S(2)}) collective-permute-start(bf16[112,2048]{1,0:T(8,128)(2,1)S(1)} %get-tuple-element.276), channel_id=1, source_target_pairs={{0,1},{1,0},{2,3},{3,2},{4,5},{5,4},{6,7},{7,6},{8,9},{9,8},{10,11... | collective-permute-start | bytes 1376264 | tf_op jit(solution)/shard_map/ppermute | solution.py:950
  406.5 19.4 %collective-permute-start.14 = (bf16[112,2048]{1,0:T(8,128)(2,1)S(1)}, bf16[112,2048]{1,0:T(8,128)(2,1)S(1)}, u32[]{:S(2)}, u32[]{:S(2)}) collective-permute-start(bf16[112,2048]{1,0:T(8,128)(2,1)S(1)} %get-tuple-element.254), channel_id=1, source_target_pairs={{0,1},{1,0},{2,3},{3,2},{4,5},{5,4},{6,7},{7,6},{8,9},{9,8},{10,11... | collective-permute-start | bytes 1376264 | tf_op jit(solution)/shard_map/ppermute | solution.py:950
  408.2 22.6 %collective-permute-start.13 = (bf16[112,2048]{1,0:T(8,128)(2,1)S(1)}, bf16[112,2048]{1,0:T(8,128)(2,1)S(1)}, u32[]{:S(2)}, u32[]{:S(2)}) collective-permute-start(bf16[112,2048]{1,0:T(8,128)(2,1)S(1)} %get-tuple-element.273), channel_id=1, source_target_pairs={{0,1},{1,0},{2,3},{3,2},{4,5},{5,4},{6,7},{7,6},{8,9},{9,8},{10,11... | collective-permute-start | bytes 1376264 | tf_op jit(solution)/shard_map/ppermute | solution.py:950
  453.2 12.4 %collective-permute-start.15 = (bf16[112,2048]{1,0:T(8,128)(2,1)S(1)}, bf16[112,2048]{1,0:T(8,128)(2,1)S(1)}, u32[]{:S(2)}, u32[]{:S(2)}) collective-permute-start(bf16[112,2048]{1,0:T(8,128)(2,1)S(1)} %get-tuple-element.271), channel_id=1, source_target_pairs={{0,1},{1,0},{2,3},{3,2},{4,5},{5,4},{6,7},{7,6},{8,9},{9,8},{10,11... | collective-permute-start | bytes 1376264 | tf_op jit(solution)/shard_map/ppermute | solution.py:950
  455.8 22.1 %collective-permute-start.17 = (bf16[256,2048]{1,0:T(8,128)(2,1)S(1)}, bf16[256,2048]{1,0:T(8,128)(2,1)S(1)}, u32[]{:S(2)}, u32[]{:S(2)}) collective-permute-start(bf16[256,2048]{1,0:T(8,128)(2,1)S(1)} %add_convert_fusion.2), channel_id=1, source_target_pairs={{0,2},{1,3},{2,4},{3,5},{4,6},{5,7},{6,0},{7,1},{8,10},{9,11},{10,... | collective-permute-start | bytes 3145736 | tf_op jit(solution)/shard_map/ppermute | solution.py:953
  457.1 13.4 %collective-permute-start.16 = (bf16[112,2048]{1,0:T(8,128)(2,1)S(1)}, bf16[112,2048]{1,0:T(8,128)(2,1)S(1)}, u32[]{:S(2)}, u32[]{:S(2)}) collective-permute-start(bf16[112,2048]{1,0:T(8,128)(2,1)S(1)} %get-tuple-element.268), channel_id=1, source_target_pairs={{0,1},{1,0},{2,3},{3,2},{4,5},{5,4},{6,7},{7,6},{8,9},{9,8},{10,11... | collective-permute-start | bytes 1376264 | tf_op jit(solution)/shard_map/ppermute | solution.py:950
  478.9 21.1 %collective-permute-start.18 = (bf16[256,2048]{1,0:T(8,128)(2,1)S(1)}, bf16[256,2048]{1,0:T(8,128)(2,1)}, u32[]{:S(2)}, u32[]{:S(2)}) collective-permute-start(bf16[256,2048]{1,0:T(8,128)(2,1)S(1)} %add_convert_fusion.1), channel_id=1, source_target_pairs={{0,2},{1,3},{2,4},{3,5},{4,6},{5,7},{6,0},{7,1},{8,10},{9,11},{10,... | collective-permute-start | bytes 3145736 | tf_op jit(solution)/shard_map/ppermute | solution.py:953
  500.9 12.6 %collective-permute-start.19 = (bf16[112,2048]{1,0:T(8,128)(2,1)}, bf16[112,2048]{1,0:T(8,128)(2,1)}, u32[]{:S(2)}, u32[]{:S(2)}) collective-permute-start(bf16[112,2048]{1,0:T(8,128)(2,1)} %get-tuple-element.266), channel_id=1, source_target_pairs={{0,1},{1,0},{2,3},{3,2},{4,5},{5,4},{6,7},{7,6},{8,9},{9,8},{10,11... | collective-permute-start | bytes 1376264 | tf_op jit(solution)/shard_map/ppermute | solution.py:950
  513.5 118.5 %reduce-scatter.10.cloned.1.call-start = ((), (), s32[]{:S(2)}) async-start(), calls=%async_computation.14 | async-start | bytes 7208960 | tf_op jit(solution)/shard_map/reduce_scatter | solution.py:1133
  544.6 21.4 %collective-permute-start.20 = (bf16[256,2048]{1,0:T(8,128)(2,1)S(1)}, bf16[256,2048]{1,0:T(8,128)(2,1)S(1)}, u32[]{:S(2)}, u32[]{:S(2)}) collective-permute-start(bf16[256,2048]{1,0:T(8,128)(2,1)S(1)} %add_convert_fusion), channel_id=1, source_target_pairs={{0,2},{1,3},{2,4},{3,5},{4,6},{5,7},{6,0},{7,1},{8,10},{9,11},{10,... | collective-permute-start | bytes 3145736 | tf_op jit(solution)/shard_map/ppermute | solution.py:953
  573.0 35.7 %collective-permute-start.21 = (bf16[4,112,2048]{2,1,0:T(8,128)(2,1)}, bf16[4,112,2048]{2,1,0:T(8,128)(2,1)}, u32[]{:S(2)}, u32[]{:S(2)}) collective-permute-start(bf16[4,112,2048]{2,1,0:T(8,128)(2,1)} %slice.329), channel_id=1, source_target_pairs={{0,1},{1,0},{2,3},{3,2},{4,5},{5,4},{6,7},{7,6},{8,9},{9,8},{10,11... | collective-permute-start | bytes 5505032 | tf_op jit(solution)/shard_map/ppermute | solution.py:950
  609.7 22.3 %all-to-all-start.1 = ((bf16[256,8,256]{2,0,1:T(8,128)(2,1)}), bf16[256,8,256]{2,0,1:T(8,128)(2,1)S(1)}, u32[]{:S(2)}, u32[]{:S(2)}) async-start(bf16[256,8,256]{2,0,1:T(8,128)(2,1)} %bitcast.292), calls=%async_computation.1 | async-start | bytes 2097152 | tf_op jit(solution)/shard_map/all_to_all | solution.py:1153
  613.3 122.0 %reduce-scatter.12.cloned.1.call-start = ((), (), s32[]{:S(2)}) async-start(), calls=%async_computation.15 | async-start | bytes 10485760 | tf_op jit(solution)/shard_map/reduce_scatter | solution.py:1170
  632.9 285.2 %reduce-scatter.18.cloned.1.call-start = ((), (), s32[]{:S(2)}) async-start(), calls=%async_computation.18 | async-start | bytes 7208960 | tf_op jit(solution)/shard_map/reduce_scatter | solution.py:1134
  633.5 284.6 %reduce-scatter.14.cloned.1.call-start = ((), (), s32[]{:S(2)}) async-start(), calls=%async_computation.16 | async-start | bytes 3276800 | tf_op jit(solution)/shard_map/reduce_scatter | solution.py:1220
  636.4 34.5 %collective-permute-start.23 = (bf16[2,2,88,2048]{3,2,1,0:T(8,128)(2,1)}, bf16[2,2,88,2048]{3,2,1,0:T(8,128)(2,1)}, u32[]{:S(2)}, u32[]{:S(2)}) collective-permute-start(bf16[2,2,88,2048]{3,2,1,0:T(8,128)(2,1)} %dynamic-slice_bitcast_fusion), channel_id=1, source_target_pairs={{0,8},{8,0},{16,24},{24,16},{1,9},{9,1},{17,25},{25,17},{2,10},{10... | collective-permute-start | bytes 4325384 | tf_op jit(solution)/shard_map/ppermute | solution.py:965
  636.4 34.5 %collective-permute-start.22 = (bf16[256,2048]{1,0:T(8,128)(2,1)}, bf16[256,2048]{1,0:T(8,128)(2,1)}, u32[]{:S(2)}, u32[]{:S(2)}) collective-permute-start(bf16[256,2048]{1,0:T(8,128)(2,1)} %fusion.84), channel_id=1, source_target_pairs={{0,2},{1,3},{2,4},{3,5},{4,6},{5,7},{6,0},{7,1},{8,10},{9,11},{10,... | collective-permute-start | bytes 3145736 | tf_op jit(solution)/shard_map/ppermute | solution.py:953
  676.0 59.3 %collective-permute-start.24 = (bf16[256,2048]{1,0:T(8,128)(2,1)}, bf16[256,2048]{1,0:T(8,128)(2,1)}, u32[]{:S(2)}, u32[]{:S(2)}) collective-permute-start(bf16[256,2048]{1,0:T(8,128)(2,1)} %fusion.83), channel_id=1, source_target_pairs={{0,2},{1,3},{2,4},{3,5},{4,6},{5,7},{6,0},{7,1},{8,10},{9,11},{10,... | collective-permute-start | bytes 3145736 | tf_op jit(solution)/shard_map/ppermute | solution.py:953
  680.6 54.6 %collective-permute-start.25 = (bf16[2,88,2048]{2,1,0:T(8,128)(2,1)}, bf16[2,88,2048]{2,1,0:T(8,128)(2,1)}, u32[]{:S(2)}, u32[]{:S(2)}) collective-permute-start(bf16[2,88,2048]{2,1,0:T(8,128)(2,1)} %dynamic-slice_bitcast_fusion.1), channel_id=1, source_target_pairs={{0,16},{8,24},{16,0},{24,8},{1,17},{9,25},{17,1},{25,9},{2,18},{10... | collective-permute-start | bytes 2162696 | tf_op jit(solution)/shard_map/ppermute | solution.py:965
  769.4 148.8 %reduce-scatter.16.cloned.1.call-start = ((), (), s32[]{:S(2)}) async-start(), calls=%async_computation.17 | async-start | bytes 3276800 | tf_op jit(solution)/shard_map/reduce_scatter | solution.py:1221
  770.1 220.2 %reduce-scatter.20.cloned.1.call-start = ((), (), s32[]{:S(2)}) async-start(), calls=%async_computation.19 | async-start | bytes 7208960 | tf_op jit(solution)/shard_map/reduce_scatter | solution.py:1222
  770.9 147.2 %all-to-all-start.2 = ((bf16[8,64,1536]{2,1,0:T(8,128)(2,1)}), bf16[8,64,1536]{2,1,0:T(8,128)(2,1)}, u32[]{:S(2)}, u32[]{:S(2)}) async-start(bf16[8,64,1536]{2,1,0:T(8,128)(2,1)} %bitcast.346), calls=%async_computation.7 | async-start | bytes 3145728 | tf_op jit(solution)/shard_map/all_to_all | solution.py:1167
  781.0 137.2 %collective-permute-start.26 = (bf16[256,2048]{1,0:T(8,128)(2,1)}, bf16[256,2048]{1,0:T(8,128)(2,1)}, u32[]{:S(2)}, u32[]{:S(2)}) collective-permute-start(bf16[256,2048]{1,0:T(8,128)(2,1)} %fusion.82), channel_id=1, source_target_pairs={{0,2},{1,3},{2,4},{3,5},{4,6},{5,7},{6,0},{7,1},{8,10},{9,11},{10,... | collective-permute-start | bytes 3145736 | tf_op jit(solution)/shard_map/ppermute | solution.py:953
  784.3 133.8 %collective-permute-start.27 = (bf16[88,2048]{1,0:T(8,128)(2,1)S(1)}, bf16[88,2048]{1,0:T(8,128)(2,1)S(1)}, u32[]{:S(2)}, u32[]{:S(2)}) collective-permute-start(bf16[88,2048]{1,0:T(8,128)(2,1)S(1)} %get-tuple-element.283), channel_id=1, source_target_pairs={{0,1},{1,0},{2,3},{3,2},{4,5},{5,4},{6,7},{7,6},{8,9},{9,8},{10,11... | collective-permute-start | bytes 1081352 | tf_op jit(solution)/shard_map/ppermute | solution.py:950
  921.1 63.4 %all-to-all-start.3 = ((bf16[8,64,640]{2,1,0:T(8,128)(2,1)}), bf16[8,64,640]{2,1,0:T(8,128)(2,1)}, u32[]{:S(2)}, u32[]{:S(2)}) async-start(bf16[8,64,640]{2,1,0:T(8,128)(2,1)} %bitcast.336), calls=%async_computation.9 | async-start | bytes 1310720 | tf_op jit(solution)/shard_map/all_to_all | solution.py:1255
  931.3 28.3 %collective-permute-start.28 = (bf16[4,64,640]{2,1,0:T(8,128)(2,1)}, bf16[4,64,640]{2,1,0:T(8,128)(2,1)}, u32[]{:S(2)}, u32[]{:S(2)}) collective-permute-start(bf16[4,64,640]{2,1,0:T(8,128)(2,1)} %pad_maximum_fusion.17), channel_id=1, source_target_pairs={{0,1},{1,0},{2,3},{3,2},{4,5},{5,4},{6,7},{7,6},{8,9},{9,8},{10,11... | collective-permute-start | bytes 983048 | tf_op jit(solution)/shard_map/ppermute | solution.py:950
  960.5 6.3 collective-permute-start.29
  967.7 6.3 collective-permute-start.30
  974.9 6.5 collective-permute-start.31
  (121 other events, 1049.5 us)
Sparse Core Ops, SparseCore 0:
  11.5 100.5 all-gather.2
  115.1 87.7 all-gather.4
  513.6 59.7 reduce-scatter.7
  576.0 54.8 reduce-scatter.9
  633.3 92.5 reduce-scatter.11
  728.5 54.8 reduce-scatter.17
  786.5 34.6 reduce-scatter.13
  824.5 34.6 reduce-scatter.15
  861.7 54.8 reduce-scatter.19

commit v4 on v3

--- a/solution.py
+++ b/solution.py
@@ -967,17 +967,6 @@
     def both_halves(keep, other):
         return (keep.astype(f32) + other.astype(f32)).astype(bf16)
 
-    def ring_sum(values):
-        steps = list(range(1, half)) + [0]
-        arrived = across(jnp.stack([behind(values, s, 1) for s in steps]))
-        total = None
-        for k, s in enumerate(steps):
-            term = behind(values, s, 0).astype(f32) + arrived[k].astype(f32)
-            if total is not None:
-                term = term + onward(total.astype(bf16)).astype(f32)
-            total = term
-        return total
-
     q_att, g0 = tie(q_att, grad_out)
     g1 = onward(g0)
     attn_heads, attended, log_total = attend(reach, q_att, k_att, v_att, scale)
@@ -1068,7 +1057,7 @@
     e1_in = across(e1[slots:])
     r0, w0 = join(e0, e0_in), join(w0, w0_in)
     n0, *k0 = expert(r0, w0)
-    n0, b1 = tie(n0, b1)
+    n0, b1, e1_in, w2_in = tie(n0, b1, e1_in, w2_in)
     n0_in = across(n0[slots:])
     n1_near, *s1 = shared(b1, g1)
     n1_near, b2, e1_in, n0_in, w2_in, g3 = tie(n1_near, b2, e1_in, n0_in, w2_in, g3)
@@ -1079,7 +1068,7 @@
     e2_in = across(e2[slots:])
     r1, w1 = join(e1, e1_in), join(w1, w1_in)
     n1, *k1 = expert(r1, w1)
-    n1, b2 = tie(n1, b2)
+    n1, b2, e2_in, w3_in = tie(n1, b2, e2_in, w3_in)
     n1_in = across(n1[slots:])
     n2_near, *s2 = shared(b2, g2)
     n2_near, b3, e2_in, n1_in, w3_in = tie(n2_near, b3, e2_in, n1_in, w3_in)
@@ -1088,7 +1077,7 @@
     e3_in = across(e3[slots:])
     r2, w2 = join(e2, e2_in), join(w2, w2_in)
     n2, *k2 = expert(r2, w2)
-    n2, b3 = tie(n2, b3)
+    n2, b3, e3_in = tie(n2, b3, e3_in)
     n2_in = across(n2[slots:])
     n3_near, *s3 = shared(b3, g3)
     n3_near, e3_in, n2_in, ring1 = tie(n3_near, e3_in, n2_in, ring1)
@@ -1113,13 +1102,13 @@
     grad_e_gate = dot_first(e_rows, gate_part).astype(bf16)
     grad_e_up = dot_first(e_rows, up_part).astype(bf16)
     e_result = matmul(activated, expert_down[0]).astype(bf16).reshape(half, 2 * slots, width)
-    grad_e_gate, grad_e_up, ring3, activated, s_act, e_result = tie(
-        grad_e_gate, grad_e_up, ring3, activated, s_act, e_result
+    grad_s_down = dot_first(s_act, g_all).astype(bf16)
+    grad_e_gate, grad_e_up, ring3, activated, s_act, e_result, grad_s_down = tie(
+        grad_e_gate, grad_e_up, ring3, activated, s_act, e_result, grad_s_down
     )
     grad_second = spread_back(0, n0_near, n0, n0_in, ring3)
     o_in = across(e_result[:, slots:])
     grad_e_down = dot_first(activated, e_grad).astype(bf16)
-    grad_s_down = dot_first(s_act, g_all).astype(bf16)
 
     def out_term(s, *more):
         weighed = (join(e_result[s], o_in[s]).astype(f32) * gates_all[s]).astype(bf16)
@@ -1149,11 +1138,10 @@
     grad_attn_out = grad_resid.astype(bf16)
     grad_w_out = dot_first(attn_own, grad_attn_out).astype(bf16)
     grad_attended = dot_last(grad_attn_out, wo).astype(bf16)
-    grad_attended, o_in = tie(grad_attended, o_in)
     grad_heads = lax.all_to_all(grad_attended, "expert", split_axis=1, concat_axis=0, tiled=True)
-    grad_heads, o1, grad_w_out, grad_s_cols, grad_e_down, grad_s_down, grad_e_gate = tie(
+    grad_heads, o_in, grad_w_out, grad_s_cols, grad_e_down, grad_s_down, grad_e_gate = tie(
         grad_heads,
-        out_term(1).astype(bf16),
+        o_in,
         grad_w_out,
         grad_s_cols,
         grad_e_down_all,
@@ -1163,6 +1151,7 @@
     s_keep, s_other = line_swap(
         grad_s_down.reshape((2,) * (spread.bit_length() - 1) + (2, ff_cut, width)), 0
     )
+    grad_heads, o1 = tie(grad_heads, out_term(1).astype(bf16))
     ring1 = onward(o1)
     grad_s_cut = lax.all_to_all(
         grad_s_cols.reshape(group, rows_w, -1), "expert", split_axis=0, concat_axis=0, tiled=True
@@ -1190,9 +1179,15 @@
     s_other = across(lax.dynamic_index_in_dim(grad_s_down, 1 - own_side, 0, False))
     ring3 = onward(out_term(3, ring2).astype(bf16))
     first_part = dot_last(grad_q_lin, wq).astype(bf16).reshape(group, tok_dev, width)
-    grad_a_cols = jnp.concatenate(
-        [dot_first(h1, grad_q_lin), dot_first(ckv, grad_kv).reshape(width, e_fold)], axis=1
-    ).astype(bf16)
+    steps = list(range(1, half)) + [0]
+    w_blocks = grad_w_out.reshape(group, rows_w, width)
+    w_in = across(jnp.stack([behind(w_blocks, s, 1) for s in steps]))
+
+    def ring_term(blocks, arrived, k, *more):
+        total = behind(blocks, steps[k], 0).astype(f32) + arrived[k].astype(f32)
+        for other in more:
+            total = total + other.astype(f32)
+        return total
 
     def latent_parts(latent_in, gain_vec):
         return (
@@ -1216,17 +1211,22 @@
     lat_grads_in = jnp.concatenate(
         [grad_w_lat, jnp.pad(grad_gains, ((0, 0), (0, ROPE - 2)))], axis=1
     ).astype(bf16)
-    first_part, lat_grads, grad_a_cols = tie(first_part, lat_grads_in, grad_a_cols)
+    first_part, lat_grads, w_in, grad_q_lin = tie(first_part, lat_grads_in, w_in, grad_q_lin)
     lat_grads = lax.psum_scatter(lat_grads, "dp", scatter_dimension=0, tiled=True)
+    w_ring = onward(ring_term(w_blocks, w_in, 0).astype(bf16))
+    grad_a_cols = jnp.concatenate(
+        [dot_first(h1, grad_q_lin), dot_first(ckv, grad_kv).reshape(width, e_fold)], axis=1
+    ).astype(bf16)
+    first_part, grad_a_cols, w_ring = tie(first_part, grad_a_cols, w_ring)
     grad_a_cols = lax.psum_scatter(grad_a_cols, "dp", scatter_dimension=0, tiled=True)
+    w_ring = onward(ring_term(w_blocks, w_in, 1, w_ring).astype(bf16))
     grad_e_down = lax.psum_scatter(grad_e_down, "dp", scatter_dimension=1, tiled=True)
-    first_sum, grad_w_out = reduce_rows(
-        [first_part, grad_w_out.reshape(group, rows_w, width)], 6, 4
-    )
+    (first_sum,) = reduce_rows([first_part], 6, 4)
     (
         first_sum,
         lat_grads,
         ring3,
+        w_ring,
         s_keep,
         s_other,
         grad_a_cols,
@@ -1237,6 +1237,7 @@
         first_sum,
         lat_grads,
         ring3,
+        w_ring,
         s_keep,
         s_other,
         grad_a_cols,
@@ -1244,14 +1245,28 @@
         grad_e_gate,
         grad_e_up,
     )
+    w_ring = onward(ring_term(w_blocks, w_in, 2, w_ring).astype(bf16))
+    lat_blocks = lat_grads.reshape(group, rows_w, -1)
+    lat_in = across(jnp.stack([behind(lat_blocks, s, 1) for s in steps]))
+    grad_first = first_sum + dot_last(grad_latent[:, :lat_w], wl)
+    unused, first_norm_back = jax.vjp(lambda v: norm_rows(v, a_gain), tokens_f)
+    (grad_tokens_norm,) = first_norm_back(grad_first)
+    grad_tokens = grad_resid + grad_tokens_norm
+    grad_tokens, lat_in, w_ring = tie(grad_tokens, lat_in, w_ring)
+    grad_w_out = ring_term(w_blocks, w_in, 3, w_ring)
+    lat_ring = onward(ring_term(lat_blocks, lat_in, 0).astype(bf16))
+    block_out = (resid + out_term(0, ring3)).astype(bf16)
+    block_out, lat_ring = tie(block_out, lat_ring)
+    lat_ring = onward(ring_term(lat_blocks, lat_in, 1, lat_ring).astype(bf16))
+    grad_s_gate = ff_restore(grad_s_cut[:, :, :ff_pad])
+    grad_s_up = ff_restore(grad_s_cut[:, :, ff_pad:])
+    grad_s_gate, grad_s_up, lat_ring = tie(grad_s_gate, grad_s_up, lat_ring)
+    lat_ring = onward(ring_term(lat_blocks, lat_in, 2, lat_ring).astype(bf16))
+    lat_grads = ring_term(lat_blocks, lat_in, 3, lat_ring)
     grad_s_down = s_keep.astype(f32) + s_other.astype(f32)
-    block_out = (resid + out_term(0, ring3)).astype(bf16)
-    lat_grads = ring_sum(lat_grads.reshape(group, rows_w, -1))
     grad_w_lat = lat_grads[:, :lat_w]
     grad_f_gain = lat_grads[:, lat_w]
     grad_l_gain = lat_grads[:rows_l, lat_w + 1]
-    grad_s_gate = ff_restore(grad_s_cut[:, :, :ff_pad])
-    grad_s_up = ff_restore(grad_s_cut[:, :, ff_pad:])
     grad_a_cols = lax.all_to_all(
         grad_a_cols.reshape(group, rows_w, -1), "expert", split_axis=0, concat_axis=0, tiled=True
     )
@@ -1274,12 +1289,6 @@
         + jnp.sum(grad_w_lat * w_latent.astype(f32), axis=1)
     ) / attn_gain.astype(f32)
 
-    grad_first = first_sum + dot_last(grad_latent[:, :lat_w], wl)
-    unused, first_norm_back = jax.vjp(
-        lambda v: norm_rows(v, a_gain), tokens_f
-    )
-    (grad_tokens_norm,) = first_norm_back(grad_first)
-    grad_tokens = grad_resid + grad_tokens_norm
     return (
         block_out,
         grad_tokens,

time: 1010 us -> 972 us (0.962)
  waiting for transfers between devices: 125 us -> 98.3 us
  local copies, waits for them, and re-layouts: 91.4 us -> 81 us
    ppermute x15 -> x18, waiting for transfers between devices: 52.5 us -> 33.5 us  [onward(): return lax.ppermute(values, 'expert', ring)]
    pallas_call x2, Pallas kernels: 164 us -> 147 us  [reduce_rows(): pl.pallas_call(functools.partial(reduce_kernel, parts), out_shape=[jax.Sh...]
    ppermute x15 -> x18, starting transfers between devices: 13.7 us -> 24.6 us  [onward(): return lax.ppermute(values, 'expert', ring)]
    ppermute x15 -> x16, waiting for transfers between devices: 39.6 us -> 32.5 us  [across(): return lax.ppermute(values, 'expert', side)]
    unnamed x259 -> x274, local copies, waits for them, and re-layouts: 22.7 us -> 22 us
  transfers between devices with their start and end apart: 45 -> 49, of which waited for: 16 -> 14; matrix products, arithmetic and copies ran while one was open for 36% -> 38% of each run, Pallas kernels for 40% -> 40%
where the time goes in v4:
time: 972 us; the launch traced here: 957 us
  Pallas kernels  388 us (40%)
  matrix products  246 us (25%)
  waiting for transfers between devices  98.3 us (10%)
  local copies, waits for them, and re-layouts  81 us (8%)
  starting transfers between devices  64 us (7%)
  other arithmetic  63.6 us (7%)
  between operations  16.7 us (2%)
    pallas_call x1, Pallas kernels, prologue(): pl.pallas_call(functools.partial(prologue_kernel, chunks), out_shape=[jax...  162 us
    pallas_call x2, Pallas kernels, reduce_rows(): pl.pallas_call(functools.partial(reduce_kernel, parts), out_shape=[jax.Sh...  147 us
    dot_general x27, matrix products, dot_last(): lax.dot_general(left, right, (((1,), (1,)), ((), ())), preferred_element_...  87.4 us
    dot_general x31, matrix products, matmul(): return jnp.dot(left, right, preferred_element_type=f32)  80.1 us
    dot_general x17, matrix products, dot_first(): lax.dot_general(left, right, (((0,), (0,)), ((), ())), preferred_element_...  77.4 us
    ppermute x18, waiting for transfers between devices, onward(): return lax.ppermute(values, 'expert', ring)  33.5 us
    pallas_call x1, Pallas kernels, attend_back(): pl.pallas_call(functools.partial(attend_back_kernel, heads, segs, scale),...  33.3 us
    ppermute x16, waiting for transfers between devices, across(): return lax.ppermute(values, 'expert', side)  32.5 us
  transfers between devices with their start and end apart: 49, of which 14 were waited for; matrix products, arithmetic and copies ran while one was open for 38% of the time, Pallas kernels for 40%

profile of v4, /device:TPU:0, one launch (start us, length us, event | category | flops | bytes accessed | tf_op | source)
XLA Modules:
  0.0 957.2 jit_solution(2906238007262372086)
XLA Ops:
  20.8 161.9 %prologue.1 = (bf16[8,256,2048]{2,1,0:T(8,128)(2,1)}, bf16[4,8,64,2176]{3,2,1,0:T(8,128)(2,1)}, bf16[4,2,88,2048]{3,2,1,0:T(8,128)(2,1)}, f32[8,8,256]{2,1,0:T(8,128)}) custom-call(bf16[256,2048]{1,0:T(8,128)(2,1)} %x_ref.1, bf16[8,64,2176]{2,1,0:T(8,128)(2,1)} %pad_maximum_fusion.3.w_ref, bf16[88,2048]{1,0:T(8,128)(2,1)} %d_ref.1, f32[8,256]{1,0:T(8,128)} %bitcast.384), custom_call_target="tpu_custom_call" | custom-call | bytes 300000000 | tf_op jit(solution)/shard_map/prologue/pallas_call | solution.py:341
  193.1 20.3 %project.1 = (bf16[2048,2048]{1,0:T(8,128)(2,1)}, bf16[2048,512]{1,0:T(8,128)(2,1)}, bf16[2048,512]{1,0:T(8,128)(2,1)}, bf16[2048,256]{1,0:T(8,128)(2,1)}, f32[2...) custom-call(bf16[2048,2048]{1,0:T(8,128)(2,1)} %bitcast.340, bf16[2048,2176]{1,0:T(8,128)(2,1)} %bitcast.309, ...), custom_call_target="tpu_custom_call" | custom-call | bytes 60000000 | tf_op jit(solution)/shard_map/project/pallas_call | solution.py:560
  216.0 25.4 %attend.1 = (bf16[2048,256]{1,0:T(8,128)(2,1)}, f32[2048,256]{1,0:T(8,128)}, f32[2,2048]{1,0:T(2,128)}) custom-call(s32[64]{0:T(128)} %reshape.377.reach_ref, bf16[2048,512]{1,0:T(8,128)(2,1)} %get-tuple-element.132.q_ref, bf16[2048,512]{1,0:T(8,128)(2,1)} %get-tuple-element.133.k_ref, bf16[2048,256]{1,0:T(8,128)(2,1)} %get-tuple-element.134.v_ref), custom_call_target="tpu_custom_call" | custom-call | bytes 70000000 | tf_op jit(solution)/shard_map/attend/pallas_call | solution.py:652
  243.7 9.3 all-to-all-start
  269.2 26.6 %all-to-all-done = bf16[8,256,256]{1,2,0:T(8,128)(2,1)} async-done(((bf16[8,256,256]{1,2,0:T(8,128)(2,1)}), bf16[8,256,256]{1,2,0:T(8,128)(2,1)}, u32[]{:S(2)}, u32[]{:S(2)}) %all-to-all-start) | async-done | bytes 1048608 | tf_op jit(solution)/shard_map/all_to_all | solution.py:975
  295.8 6.5 multiply_reduce_fusion.2
  313.3 14.2 %collective-permute-done.1 = bf16[256,2048]{1,0:T(8,128)(2,1)S(1)} collective-permute-done((bf16[256,2048]{1,0:T(8,128)(2,1)S(1)}, bf16[256,2048]{1,0:T(8,128)(2,1)S(1)}, u32[]{:S(2)}, u32[]{:S(2)}) %collective-permute-start.1) | collective-permute-done | bytes 1048608 | tf_op jit(solution)/shard_map/ppermute | solution.py:953
  340.2 4.7 fusion.120
  345.0 4.2 fusion.14
  349.2 5.5 multiply_convert_fusion.8
  354.7 5.0 fusion.12
  359.8 4.6 fusion.110
  364.4 4.7 fusion.126
  375.5 4.9 collective-permute-done.9
  388.8 5.5 multiply_convert_fusion.7
  394.3 5.0 fusion.8
  399.3 4.6 fusion.107
  403.9 4.6 fusion.132
  414.0 9.0 collective-permute-done.14
  425.9 4.0 collective-permute-start.17
  431.6 5.6 multiply_convert_fusion.6
  439.1 4.6 fusion.104
  443.8 4.6 fusion.138
  469.6 6.3 collective-permute-done.18
  478.1 11.4 %convolution_convert_fusion.5 = bf16[2048,1536]{1,0:T(8,128)(2,1)} fusion(bf16[256,2048]{1,0:T(8,128)(2,1)S(1)} %copy-done.48, bf16[256,2048]{1,0:T(8,128)(2,1)S(1)} %copy-done.46, bf16[256,2048]{1,0:T(8,128)(2,1)S(1)} %copy-done.44, bf16[256,2048]{1,0:T(8,128)(2,1)S(1)} %multiply_convert_fusion, bf16[256,768]{1,0:T(8,128)(2,1)} %copy-done.70, ...), kind=kOutput, calls=%fused_computation.5 | convolution fusion | flops 6487539712 | bytes 13631488 | tf_op jit(solution)/shard_map/dot_general | solution.py:70
  492.5 7.6 fusion.60
  503.8 8.5 convolution_convert_fusion.1
  512.3 10.6 %convolution_convert_fusion.2 = bf16[2048,1408]{1,0:T(8,128)(2,1)} fusion(bf16[896,2048]{1,0:T(8,128)(2,1)} %copy-done.84, bf16[224,1408]{1,0:T(8,128)(2,1)} %copy-done.110, bf16[224,1408]{1,0:T(8,128)(2,1)} %copy-done.109, bf16[224,1408]{1,0:T(8,128)(2,1)} %copy-done.108, bf16[224,1408]{1,0:T(8,128)(2,1)} %copy-done.107), kind=kOutput, calls=%fused_computation.2 | convolution fusion | flops 5180358656 | bytes 11960320 | tf_op jit(solution)/shard_map/dot_general | solution.py:70
  527.0 11.7 %fusion.57 = bf16[896,2048]{1,0:T(8,128)(2,1)} fusion(bf16[1,1408,2048]{2,1,0:T(8,128)(2,1)} %param.35, bf16[224,1408]{1,0:T(8,128)(2,1)S(1)} %copy-done.57, bf16[224,1408]{1,0:T(8,128)(2,1)S(1)} %copy-done.55, bf16[224,1408]{1,0:T(8,128)(2,1)S(1)} %copy-done.53, bf16[224,1408]{1,0:T(8,128)(2,1)S(1)} %copy-done.51), kind=kOutput, calls=%fused_computation.68 | convolution fusion | flops 5179310080 | bytes 11960320 | tf_op jit(solution)/shard_map/dot_general | solution.py:62
  538.7 4.8 collective-permute-done.20
  550.6 7.4 convolution_convert_fusion.7
  559.1 3.6 all-to-all-start.1
  571.6 6.9 convolution_convert_fusion.4
  578.4 10.4 %convolution_convert_fusion = bf16[1408,2048]{1,0:T(8,128)(2,1)} fusion(bf16[896,1408]{1,0:T(8,128)(2,1)} %pad_maximum_fusion.2, bf16[896,2048]{1,0:T(8,128)(2,1)} %constant_dynamic-update-slice_fusion.8), kind=kOutput, calls=%fused_computation | convolution fusion | flops 5170266112 | bytes 11960320 | tf_op jit(solution)/shard_map/dot_general | solution.py:70
  588.8 10.4 %collective-permute-done.21 = bf16[4,112,2048]{2,1,0:T(8,128)(2,1)} collective-permute-done((bf16[4,112,2048]{2,1,0:T(8,128)(2,1)}, bf16[4,112,2048]{2,1,0:T(8,128)(2,1)}, u32[]{:S(2)}, u32[]{:S(2)}) %collective-permute-start.21) | collective-permute-done | bytes 1835040 | tf_op jit(solution)/shard_map/ppermute | solution.py:950
  599.2 4.3 reduce-scatter.10.cloned.1.call-done
  616.5 33.3 %attend_back.1 = (bf16[2048,512]{1,0:T(8,128)(2,1)}, bf16[2048,512]{1,0:T(8,128)(2,1)}, bf16[2048,640]{1,0:T(8,128)(2,1)}) custom-call(s32[64]{0:T(128)} %reshape.377.reach_ref, bf16[2048,512]{1,0:T(8,128)(2,1)} %get-tuple-element.132.q_ref, bf16[2048,512]{1,0:T(8,128)(2,1)} %get-tuple-element.133.k_ref, bf16[2048,256]{1,0:T(8,128)(2,1)} %get-tuple-element.134.v_ref, ...), custom_call_target="tpu_custom_call" | custom-call | bytes 90000000 | tf_op jit(solution)/shard_map/attend_back/pallas_call | solution.py:786
  651.7 3.5 fusion.86
  662.7 41.1 %reduce_rows.2 = f32[256,640]{1,0:T(8,128)} custom-call(bf16[8,256,640]{2,1,0:T(8,128)(2,1)} %bitcast.346), custom_call_target="tpu_custom_call" | custom-call | bytes 94371840 | tf_op jit(solution)/shard_map/reduce_rows/pallas_call | solution.py:477
  716.1 10.2 %convolution_convert_fusion.3 = bf16[2048,2048]{1,0:T(8,128)(2,1)} fusion(bf16[2048,512]{1,0:T(8,128)(2,1)} %get-tuple-element.205, bf16[2048,2176]{1,0:T(8,128)(2,1)} %bitcast.310), kind=kOutput, calls=%fused_computation.3 | convolution fusion | flops 4299161600 | bytes 12582912 | tf_op jit(solution)/shard_map/dot_general | solution.py:66
  736.8 8.6 convolution_convert_fusion.6
  747.8 4.4 all-to-all-start.2
  767.8 105.6 %reduce_rows.3 = f32[256,2048]{1,0:T(8,128)} custom-call(bf16[8,256,2048]{2,1,0:T(8,128)(2,1)} %bitcast.339), custom_call_target="tpu_custom_call" | custom-call | bytes 301989888 | tf_op jit(solution)/shard_map/reduce_rows/pallas_call | solution.py:477
  883.7 4.2 all-to-all-start.3
  891.4 4.0 reshape.409
  895.4 3.8 fusion.157
  899.3 3.6 fusion.88
  934.0 4.2 collective-permute-done.35
  (567 shorter events, 264.7 us)
Async XLA Ops:
  7.2 181.1 %all-gather.3.cloned.1.call-start = ((), (), s32[]{:S(2)}) async-start(), calls=%async_computation.11 | async-start | bytes 2703360 | tf_op jit(solution)/shard_map/all_gather | solution.py:907
  10.4 285.4 %all-gather.5.cloned.1.call-start = ((), (), s32[]{:S(2)}) async-start(), calls=%async_computation.12 | async-start | bytes 8650752 | tf_op jit(solution)/shard_map/all_gather | solution.py:914
  213.4 28.1 %collective-permute-start = (bf16[256,2048]{1,0:T(8,128)(2,1)S(1)}, bf16[256,2048]{1,0:T(8,128)(2,1)}, u32[]{:S(2)}, u32[]{:S(2)}) collective-permute-start(bf16[256,2048]{1,0:T(8,128)(2,1)S(1)} %copy-done.19), channel_id=1, source_target_pairs={{0,2},{1,3},{2,4},{3,5},{4,6},{5,7},{6,0},{7,1},{8,10},{9,11},{10,... | collective-permute-start | bytes 3145736 | tf_op jit(solution)/shard_map/ppermute | solution.py:953
  243.7 52.0 %all-to-all-start = ((bf16[8,256,256]{1,2,0:T(8,128)(2,1)}), bf16[8,256,256]{1,2,0:T(8,128)(2,1)}, u32[]{:S(2)}, u32[]{:S(2)}) async-start(bf16[8,256,256]{1,2,0:T(8,128)(2,1)} %copy.139), calls=%async_computation | async-start | bytes 2097152 | tf_op jit(solution)/shard_map/all_to_all | solution.py:975
  253.1 346.1 %reduce-scatter.8.cloned.1.call-start = ((), (), s32[]{:S(2)}) async-start(), calls=%async_computation.13 | async-start | bytes 7864320 | tf_op jit(solution)/shard_map/reduce_scatter | solution.py:1127
  256.1 54.4 %collective-permute-start.3 = (bf16[112,2048]{1,0:T(8,128)(2,1)}, bf16[112,2048]{1,0:T(8,128)(2,1)}, u32[]{:S(2)}, u32[]{:S(2)}) collective-permute-start(bf16[112,2048]{1,0:T(8,128)(2,1)} %get-tuple-element.300), channel_id=1, source_target_pairs={{0,1},{1,0},{2,3},{3,2},{4,5},{5,4},{6,7},{7,6},{8,9},{9,8},{10,11... | collective-permute-start | bytes 1376264 | tf_op jit(solution)/shard_map/ppermute | solution.py:950
  260.0 50.5 %collective-permute-start.5 = (bf16[256,2048]{1,0:T(8,128)(2,1)}, bf16[256,2048]{1,0:T(8,128)(2,1)}, u32[]{:S(2)}, u32[]{:S(2)}) collective-permute-start(bf16[256,2048]{1,0:T(8,128)(2,1)} %collective-permute-done), channel_id=1, source_target_pairs={{0,2},{1,3},{2,4},{3,5},{4,6},{5,7},{6,0},{7,1},{8,10},{9,11},{10,... | collective-permute-start | bytes 3145736 | tf_op jit(solution)/shard_map/ppermute | solution.py:953
  265.0 45.6 %collective-permute-start.4 = (bf16[112,2048]{1,0:T(8,128)(2,1)}, bf16[112,2048]{1,0:T(8,128)(2,1)}, u32[]{:S(2)}, u32[]{:S(2)}) collective-permute-start(bf16[112,2048]{1,0:T(8,128)(2,1)} %slice.396), channel_id=1, source_target_pairs={{0,1},{1,0},{2,3},{3,2},{4,5},{5,4},{6,7},{7,6},{8,9},{9,8},{10,11... | collective-permute-start | bytes 1376264 | tf_op jit(solution)/shard_map/ppermute | solution.py:950
  304.1 23.4 %collective-permute-start.1 = (bf16[256,2048]{1,0:T(8,128)(2,1)S(1)}, bf16[256,2048]{1,0:T(8,128)(2,1)S(1)}, u32[]{:S(2)}, u32[]{:S(2)}) collective-permute-start(bf16[256,2048]{1,0:T(8,128)(2,1)S(1)} %multiply_convert_fusion), channel_id=1, source_target_pairs={{0,2},{1,3},{2,4},{3,5},{4,6},{5,7},{6,0},{7,1},{8,10},{9,11},{10,... | collective-permute-start | bytes 3145736 | tf_op jit(solution)/shard_map/ppermute | solution.py:953
  304.3 9.0 collective-permute-start.2
  328.0 52.4 %collective-permute-start.8 = (bf16[256,2048]{1,0:T(8,128)(2,1)S(1)}, bf16[256,2048]{1,0:T(8,128)(2,1)S(1)}, u32[]{:S(2)}, u32[]{:S(2)}) collective-permute-start(bf16[256,2048]{1,0:T(8,128)(2,1)S(1)} %collective-permute-done.1), channel_id=1, source_target_pairs={{0,2},{1,3},{2,4},{3,5},{4,6},{5,7},{6,0},{7,1},{8,10},{9,11},{10,... | collective-permute-start | bytes 3145736 | tf_op jit(solution)/shard_map/ppermute | solution.py:953
  330.3 50.1 %collective-permute-start.10 = (bf16[256,2048]{1,0:T(8,128)(2,1)}, bf16[256,2048]{1,0:T(8,128)(2,1)S(1)}, u32[]{:S(2)}, u32[]{:S(2)}) collective-permute-start(bf16[256,2048]{1,0:T(8,128)(2,1)} %collective-permute-done.5), channel_id=1, source_target_pairs={{0,2},{1,3},{2,4},{3,5},{4,6},{5,7},{6,0},{7,1},{8,10},{9,11},{10,... | collective-permute-start | bytes 3145736 | tf_op jit(solution)/shard_map/ppermute | solution.py:953
  333.7 35.5 %collective-permute-start.6 = (bf16[112,2048]{1,0:T(8,128)(2,1)S(1)}, bf16[112,2048]{1,0:T(8,128)(2,1)S(1)}, u32[]{:S(2)}, u32[]{:S(2)}) collective-permute-start(bf16[112,2048]{1,0:T(8,128)(2,1)S(1)} %get-tuple-element.317), channel_id=1, source_target_pairs={{0,1},{1,0},{2,3},{3,2},{4,5},{5,4},{6,7},{7,6},{8,9},{9,8},{10,11... | collective-permute-start | bytes 1376264 | tf_op jit(solution)/shard_map/ppermute | solution.py:950
  338.5 30.7 %collective-permute-start.7 = (bf16[112,2048]{1,0:T(8,128)(2,1)S(1)}, bf16[112,2048]{1,0:T(8,128)(2,1)S(1)}, u32[]{:S(2)}, u32[]{:S(2)}) collective-permute-start(bf16[112,2048]{1,0:T(8,128)(2,1)S(1)} %get-tuple-element.295), channel_id=1, source_target_pairs={{0,1},{1,0},{2,3},{3,2},{4,5},{5,4},{6,7},{7,6},{8,9},{9,8},{10,11... | collective-permute-start | bytes 1376264 | tf_op jit(solution)/shard_map/ppermute | solution.py:950
  371.0 9.4 collective-permute-start.9
  381.6 41.4 %collective-permute-start.13 = (bf16[256,2048]{1,0:T(8,128)(2,1)S(1)}, bf16[256,2048]{1,0:T(8,128)(2,1)S(1)}, u32[]{:S(2)}, u32[]{:S(2)}) collective-permute-start(bf16[256,2048]{1,0:T(8,128)(2,1)S(1)} %collective-permute-done.8), channel_id=1, source_target_pairs={{0,2},{1,3},{2,4},{3,5},{4,6},{5,7},{6,0},{7,1},{8,10},{9,11},{10,... | collective-permute-start | bytes 3145736 | tf_op jit(solution)/shard_map/ppermute | solution.py:953
  382.9 25.6 %collective-permute-start.11 = (bf16[112,2048]{1,0:T(8,128)(2,1)S(1)}, bf16[112,2048]{1,0:T(8,128)(2,1)S(1)}, u32[]{:S(2)}, u32[]{:S(2)}) collective-permute-start(bf16[112,2048]{1,0:T(8,128)(2,1)S(1)} %get-tuple-element.314), channel_id=1, source_target_pairs={{0,1},{1,0},{2,3},{3,2},{4,5},{5,4},{6,7},{7,6},{8,9},{9,8},{10,11... | collective-permute-start | bytes 1376264 | tf_op jit(solution)/shard_map/ppermute | solution.py:950
  385.3 23.2 %collective-permute-start.12 = (bf16[112,2048]{1,0:T(8,128)(2,1)S(1)}, bf16[112,2048]{1,0:T(8,128)(2,1)S(1)}, u32[]{:S(2)}, u32[]{:S(2)}) collective-permute-start(bf16[112,2048]{1,0:T(8,128)(2,1)S(1)} %get-tuple-element.292), channel_id=1, source_target_pairs={{0,1},{1,0},{2,3},{3,2},{4,5},{5,4},{6,7},{7,6},{8,9},{9,8},{10,11... | collective-permute-start | bytes 1376264 | tf_op jit(solution)/shard_map/ppermute | solution.py:950
  409.6 13.4 %collective-permute-start.14 = (bf16[112,2048]{1,0:T(8,128)(2,1)S(1)}, bf16[112,2048]{1,0:T(8,128)(2,1)S(1)}, u32[]{:S(2)}, u32[]{:S(2)}) collective-permute-start(bf16[112,2048]{1,0:T(8,128)(2,1)S(1)} %get-tuple-element.311), channel_id=1, source_target_pairs={{0,1},{1,0},{2,3},{3,2},{4,5},{5,4},{6,7},{7,6},{8,9},{9,8},{10,11... | collective-permute-start | bytes 1376264 | tf_op jit(solution)/shard_map/ppermute | solution.py:950
  424.1 24.3 %collective-permute-start.15 = (bf16[112,2048]{1,0:T(8,128)(2,1)S(1)}, bf16[112,2048]{1,0:T(8,128)(2,1)S(1)}, u32[]{:S(2)}, u32[]{:S(2)}) collective-permute-start(bf16[112,2048]{1,0:T(8,128)(2,1)S(1)} %get-tuple-element.309), channel_id=1, source_target_pairs={{0,1},{1,0},{2,3},{3,2},{4,5},{5,4},{6,7},{7,6},{8,9},{9,8},{10,11... | collective-permute-start | bytes 1376264 | tf_op jit(solution)/shard_map/ppermute | solution.py:950
  425.9 32.0 %collective-permute-start.17 = (bf16[256,2048]{1,0:T(8,128)(2,1)S(1)}, bf16[256,2048]{1,0:T(8,128)(2,1)S(1)}, u32[]{:S(2)}, u32[]{:S(2)}) collective-permute-start(bf16[256,2048]{1,0:T(8,128)(2,1)S(1)} %add_convert_fusion.2), channel_id=1, source_target_pairs={{0,2},{1,3},{2,4},{3,5},{4,6},{5,7},{6,0},{7,1},{8,10},{9,11},{10,... | collective-permute-start | bytes 3145736 | tf_op jit(solution)/shard_map/ppermute | solution.py:953
  449.4 8.5 collective-permute-start.16
  459.0 16.9 %collective-permute-start.18 = (bf16[256,2048]{1,0:T(8,128)(2,1)S(1)}, bf16[256,2048]{1,0:T(8,128)(2,1)}, u32[]{:S(2)}, u32[]{:S(2)}) collective-permute-start(bf16[256,2048]{1,0:T(8,128)(2,1)S(1)} %add_convert_fusion.1), channel_id=1, source_target_pairs={{0,2},{1,3},{2,4},{3,5},{4,6},{5,7},{6,0},{7,1},{8,10},{9,11},{10,... | collective-permute-start | bytes 3145736 | tf_op jit(solution)/shard_map/ppermute | solution.py:953
  477.0 12.5 %collective-permute-start.19 = (bf16[112,2048]{1,0:T(8,128)(2,1)}, bf16[112,2048]{1,0:T(8,128)(2,1)}, u32[]{:S(2)}, u32[]{:S(2)}) collective-permute-start(bf16[112,2048]{1,0:T(8,128)(2,1)} %get-tuple-element.304), channel_id=1, source_target_pairs={{0,1},{1,0},{2,3},{3,2},{4,5},{5,4},{6,7},{7,6},{8,9},{9,8},{10,11... | collective-permute-start | bytes 1376264 | tf_op jit(solution)/shard_map/ppermute | solution.py:950
  489.6 113.8 %reduce-scatter.10.cloned.1.call-start = ((), (), s32[]{:S(2)}) async-start(), calls=%async_computation.14 | async-start | bytes 7208960 | tf_op jit(solution)/shard_map/reduce_scatter | solution.py:1122
  526.5 17.1 %collective-permute-start.20 = (bf16[256,2048]{1,0:T(8,128)(2,1)S(1)}, bf16[256,2048]{1,0:T(8,128)(2,1)S(1)}, u32[]{:S(2)}, u32[]{:S(2)}) collective-permute-start(bf16[256,2048]{1,0:T(8,128)(2,1)S(1)} %add_convert_fusion), channel_id=1, source_target_pairs={{0,2},{1,3},{2,4},{3,5},{4,6},{5,7},{6,0},{7,1},{8,10},{9,11},{10,... | collective-permute-start | bytes 3145736 | tf_op jit(solution)/shard_map/ppermute | solution.py:953
  559.1 29.7 %all-to-all-start.1 = ((bf16[256,8,256]{2,0,1:T(8,128)(2,1)}), bf16[256,8,256]{2,0,1:T(8,128)(2,1)S(1)}, u32[]{:S(2)}, u32[]{:S(2)}) async-start(bf16[256,8,256]{2,0,1:T(8,128)(2,1)} %bitcast.303), calls=%async_computation.1 | async-start | bytes 2097152 | tf_op jit(solution)/shard_map/all_to_all | solution.py:1141
  562.6 141.2 %reduce-scatter.12.cloned.1.call-start = ((), (), s32[]{:S(2)}) async-start(), calls=%async_computation.15 | async-start | bytes 10485760 | tf_op jit(solution)/shard_map/reduce_scatter | solution.py:1159
  566.1 33.1 %collective-permute-start.21 = (bf16[4,112,2048]{2,1,0:T(8,128)(2,1)}, bf16[4,112,2048]{2,1,0:T(8,128)(2,1)}, u32[]{:S(2)}, u32[]{:S(2)}) collective-permute-start(bf16[4,112,2048]{2,1,0:T(8,128)(2,1)} %slice.341), channel_id=1, source_target_pairs={{0,1},{1,0},{2,3},{3,2},{4,5},{5,4},{6,7},{7,6},{8,9},{9,8},{10,11... | collective-permute-start | bytes 5505032 | tf_op jit(solution)/shard_map/ppermute | solution.py:950
  603.5 270.0 %reduce-scatter.18.cloned.1.call-start = ((), (), s32[]{:S(2)}) async-start(), calls=%async_computation.18 | async-start | bytes 7208960 | tf_op jit(solution)/shard_map/reduce_scatter | solution.py:1123
  604.0 269.5 %reduce-scatter.14.cloned.1.call-start = ((), (), s32[]{:S(2)}) async-start(), calls=%async_computation.16 | async-start | bytes 3276800 | tf_op jit(solution)/shard_map/reduce_scatter | solution.py:1215
  608.0 42.4 %collective-permute-start.23 = (bf16[2,2,88,2048]{3,2,1,0:T(8,128)(2,1)}, bf16[2,2,88,2048]{3,2,1,0:T(8,128)(2,1)}, u32[]{:S(2)}, u32[]{:S(2)}) collective-permute-start(bf16[2,2,88,2048]{3,2,1,0:T(8,128)(2,1)} %dynamic-slice_bitcast_fusion), channel_id=1, source_target_pairs={{0,8},{8,0},{16,24},{24,16},{1,9},{9,1},{17,25},{25,17},{2,10},{10... | collective-permute-start | bytes 4325384 | tf_op jit(solution)/shard_map/ppermute | solution.py:965
  614.3 36.1 %collective-permute-start.22 = (bf16[256,2048]{1,0:T(8,128)(2,1)}, bf16[256,2048]{1,0:T(8,128)(2,1)}, u32[]{:S(2)}, u32[]{:S(2)}) collective-permute-start(bf16[256,2048]{1,0:T(8,128)(2,1)} %fusion.87), channel_id=1, source_target_pairs={{0,2},{1,3},{2,4},{3,5},{4,6},{5,7},{6,0},{7,1},{8,10},{9,11},{10,... | collective-permute-start | bytes 3145736 | tf_op jit(solution)/shard_map/ppermute | solution.py:953
  655.3 48.6 %collective-permute-start.24 = (bf16[256,2048]{1,0:T(8,128)(2,1)}, bf16[256,2048]{1,0:T(8,128)(2,1)}, u32[]{:S(2)}, u32[]{:S(2)}) collective-permute-start(bf16[256,2048]{1,0:T(8,128)(2,1)} %fusion.86), channel_id=1, source_target_pairs={{0,2},{1,3},{2,4},{3,5},{4,6},{5,7},{6,0},{7,1},{8,10},{9,11},{10,... | collective-permute-start | bytes 3145736 | tf_op jit(solution)/shard_map/ppermute | solution.py:953
  660.8 43.1 %collective-permute-start.25 = (bf16[2,88,2048]{2,1,0:T(8,128)(2,1)}, bf16[2,88,2048]{2,1,0:T(8,128)(2,1)}, u32[]{:S(2)}, u32[]{:S(2)}) collective-permute-start(bf16[2,88,2048]{2,1,0:T(8,128)(2,1)} %dynamic-slice_bitcast_fusion.1), channel_id=1, source_target_pairs={{0,16},{8,24},{16,0},{24,8},{1,17},{9,25},{17,1},{25,9},{2,18},{10... | collective-permute-start | bytes 2162696 | tf_op jit(solution)/shard_map/ppermute | solution.py:965
  708.3 20.1 %collective-permute-start.26 = (bf16[4,64,2048]{2,1,0:T(8,128)(2,1)}, bf16[4,64,2048]{2,1,0:T(8,128)(2,1)}, u32[]{:S(2)}, u32[]{:S(2)}) collective-permute-start(bf16[4,64,2048]{2,1,0:T(8,128)(2,1)} %pad_maximum_fusion.5), channel_id=1, source_target_pairs={{0,1},{1,0},{2,3},{3,2},{4,5},{5,4},{6,7},{7,6},{8,9},{9,8},{10,11... | collective-permute-start | bytes 3145736 | tf_op jit(solution)/shard_map/ppermute | solution.py:950
  728.4 145.2 %reduce-scatter.16.cloned.1.call-start = ((), (), s32[]{:S(2)}) async-start(), calls=%async_computation.17 | async-start | bytes 3276800 | tf_op jit(solution)/shard_map/reduce_scatter | solution.py:1221
  733.6 13.5 %collective-permute-start.27 = (bf16[64,2048]{1,0:T(8,128)(2,1)S(1)}, bf16[64,2048]{1,0:T(8,128)(2,1)S(1)}, u32[]{:S(2)}, u32[]{:S(2)}) collective-permute-start(bf16[64,2048]{1,0:T(8,128)(2,1)S(1)} %fusion.322), channel_id=1, source_target_pairs={{0,2},{1,3},{2,4},{3,5},{4,6},{5,7},{6,0},{7,1},{8,10},{9,11},{10,... | collective-permute-start | bytes 786440 | tf_op jit(solution)/shard_map/ppermute | solution.py:953
  747.1 200.0 %reduce-scatter.20.cloned.1.call-start = ((), (), s32[]{:S(2)}) async-start(), calls=%async_computation.19 | async-start | bytes 7208960 | tf_op jit(solution)/shard_map/reduce_scatter | solution.py:1223
  747.8 125.6 %all-to-all-start.2 = ((bf16[8,64,1536]{2,1,0:T(8,128)(2,1)}), bf16[8,64,1536]{2,1,0:T(8,128)(2,1)}, u32[]{:S(2)}, u32[]{:S(2)}) async-start(bf16[8,64,1536]{2,1,0:T(8,128)(2,1)} %bitcast.360), calls=%async_computation.7 | async-start | bytes 3145728 | tf_op jit(solution)/shard_map/all_to_all | solution.py:1156
  757.7 115.8 %collective-permute-start.28 = (bf16[256,2048]{1,0:T(8,128)(2,1)}, bf16[256,2048]{1,0:T(8,128)(2,1)}, u32[]{:S(2)}, u32[]{:S(2)}) collective-permute-start(bf16[256,2048]{1,0:T(8,128)(2,1)} %fusion.85), channel_id=1, source_target_pairs={{0,2},{1,3},{2,4},{3,5},{4,6},{5,7},{6,0},{7,1},{8,10},{9,11},{10,... | collective-permute-start | bytes 3145736 | tf_op jit(solution)/shard_map/ppermute | solution.py:953
  761.1 112.3 %collective-permute-start.30 = (bf16[88,2048]{1,0:T(8,128)(2,1)S(1)}, bf16[88,2048]{1,0:T(8,128)(2,1)S(1)}, u32[]{:S(2)}, u32[]{:S(2)}) collective-permute-start(bf16[88,2048]{1,0:T(8,128)(2,1)S(1)} %get-tuple-element.321), channel_id=1, source_target_pairs={{0,1},{1,0},{2,3},{3,2},{4,5},{5,4},{6,7},{7,6},{8,9},{9,8},{10,11... | collective-permute-start | bytes 1081352 | tf_op jit(solution)/shard_map/ppermute | solution.py:950
  764.4 109.1 %collective-permute-start.29 = (bf16[64,2048]{1,0:T(8,128)(2,1)}, bf16[64,2048]{1,0:T(8,128)(2,1)S(1)}, u32[]{:S(2)}, u32[]{:S(2)}) collective-permute-start(bf16[64,2048]{1,0:T(8,128)(2,1)} %fusion.314), channel_id=1, source_target_pairs={{0,2},{1,3},{2,4},{3,5},{4,6},{5,7},{6,0},{7,1},{8,10},{9,11},{10,... | collective-permute-start | bytes 786440 | tf_op jit(solution)/shard_map/ppermute | solution.py:953
  875.5 40.4 %collective-permute-start.32 = (bf16[64,2048]{1,0:T(8,128)(2,1)}, bf16[64,2048]{1,0:T(8,128)(2,1)}, u32[]{:S(2)}, u32[]{:S(2)}) collective-permute-start(bf16[64,2048]{1,0:T(8,128)(2,1)} %fusion.313), channel_id=1, source_target_pairs={{0,2},{1,3},{2,4},{3,5},{4,6},{5,7},{6,0},{7,1},{8,10},{9,11},{10,... | collective-permute-start | bytes 786440 | tf_op jit(solution)/shard_map/ppermute | solution.py:953
  880.4 35.5 %collective-permute-start.31 = (bf16[4,64,640]{2,1,0:T(8,128)(2,1)}, bf16[4,64,640]{2,1,0:T(8,128)(2,1)}, u32[]{:S(2)}, u32[]{:S(2)}) collective-permute-start(bf16[4,64,640]{2,1,0:T(8,128)(2,1)} %pad_maximum_fusion.18), channel_id=1, source_target_pairs={{0,1},{1,0},{2,3},{3,2},{4,5},{5,4},{6,7},{7,6},{8,9},{9,8},{10,11... | collective-permute-start | bytes 983048 | tf_op jit(solution)/shard_map/ppermute | solution.py:950
  883.7 57.6 %all-to-all-start.3 = ((bf16[8,64,640]{2,1,0:T(8,128)(2,1)}), bf16[8,64,640]{2,1,0:T(8,128)(2,1)}, u32[]{:S(2)}, u32[]{:S(2)}) async-start(bf16[8,64,640]{2,1,0:T(8,128)(2,1)} %bitcast.64), calls=%async_computation.9 | async-start | bytes 1310720 | tf_op jit(solution)/shard_map/all_to_all | solution.py:1270
  916.8 6.4 collective-permute-start.33
  924.2 6.8 collective-permute-start.34
  (133 other events, 1407.2 us)
Sparse Core Ops, SparseCore 0:
  11.5 100.7 all-gather.2
  115.2 87.7 all-gather.4
  489.7 56.2 reduce-scatter.7
  548.6 54.8 reduce-scatter.9
  605.9 85.2 reduce-scatter.11
  693.7 56.1 reduce-scatter.17
  753.0 34.6 reduce-scatter.13
  791.0 34.6 reduce-scatter.15
  828.2 54.8 reduce-scatter.19

commit v5 on v4

--- a/solution.py
+++ b/solution.py
@@ -941,17 +941,19 @@
     def own(values):
         return lax.dynamic_slice_in_dim(values, rank * tok_dev, tok_dev, 0)
 
+    side, ring = ring_pairs(group)
+
+    def across(values):
+        return lax.ppermute(values, "expert", side)
+
+    def onward(values):
+        return lax.ppermute(values, "expert", ring)
+
+    x_all, g0 = tie(x_all, grad_out)
+    g1 = onward(g0)
     h1, q_att, k_att, v_att, latent, ckv = project(
         x_all, packed, lat_pack, we, a_gain[None], l_gain[None], tables, mine
     )
-    side, ring = ring_pairs(group)
-
-    def across(values):
-        return lax.ppermute(values, "expert", side)
-
-    def onward(values):
-        return lax.ppermute(values, "expert", ring)
-
     def behind(values, s, far):
         at = 2 * lax.rem(rank // 2 - s + half, half) + lax.rem(rank + far, 2)
         return lax.dynamic_index_in_dim(values, at, 0, keepdims=False)
@@ -967,18 +969,6 @@
     def both_halves(keep, other):
         return (keep.astype(f32) + other.astype(f32)).astype(bf16)
 
-    q_att, g0 = tie(q_att, grad_out)
-    g1 = onward(g0)
-    attn_heads, attended, log_total = attend(reach, q_att, k_att, v_att, scale)
-    attn_heads, g1 = tie(attn_heads, g1)
-    g2 = onward(g1)
-    attn_own = lax.all_to_all(attn_heads, "expert", split_axis=0, concat_axis=1, tiled=True)
-    tokens_f = tokens.astype(f32)
-    resid = tokens_f + matmul(attn_own, wo)
-    second_normed, second_norm_back = jax.vjp(norm_rows, resid, f_gain)
-    b0 = second_normed.astype(bf16)
-
-    b1 = onward(b0)
     gate_of = jnp.concatenate(
         [
             lax.dynamic_slice(
@@ -1011,10 +1001,26 @@
             picked = picked * weights
         return picked.astype(bf16)
 
-    def shared(h2, g_rows):
+    q_att, g1 = tie(q_att, g1)
+    g2 = onward(g1)
+    attn_heads, attended, log_total = attend(reach, q_att, k_att, v_att, scale)
+    attn_heads, g2 = tie(attn_heads, g2)
+    attn_own = lax.all_to_all(attn_heads, "expert", split_axis=0, concat_axis=1, tiled=True)
+    w0, w1, w2 = (take(s, g, gates_all[s]) for s, g in enumerate((g0, g1, g2)))
+    far0, far1, far2 = (dot_last(g, sd).astype(bf16) for g in (g0, g1, g2))
+    attn_own, w0, w1, w2, far0, far1, far2, g2 = tie(
+        attn_own, w0, w1, w2, far0, far1, far2, g2
+    )
+    g3 = onward(g2)
+    tokens_f = tokens.astype(f32)
+    resid = tokens_f + matmul(attn_own, wo)
+    second_normed, second_norm_back = jax.vjp(norm_rows, resid, f_gain)
+    b0, g3 = tie(second_normed.astype(bf16), g3)
+
+    b1 = onward(b0)
+    def shared(h2, grad_s_act):
         s_act, s_gating_back = jax.vjp(gating, matmul(h2, sg), matmul(h2, su))
         s_act = s_act.astype(bf16)
-        grad_s_act = dot_last(g_rows, sd).astype(bf16)
         gate_part, up_part = s_gating_back(grad_s_act.astype(f32))
         gate_part = gate_part.astype(bf16)
         up_part = up_part.astype(bf16)
@@ -1046,12 +1052,10 @@
 
     e0 = take(0, b0)
     e0_in = across(e0[slots:])
-    w0, w1 = (take(s, g, gates_all[s]) for s, g in enumerate((g0, g1)))
     w0_in, w1_in = (across(w[slots:]) for w in (w0, w1))
-    n0_near, *s0 = shared(b0, g0)
-    n0_near, b1, e0_in, w0_in, w1_in, g2 = tie(n0_near, b1, e0_in, w0_in, w1_in, g2)
-    b2, g3 = onward(b1), onward(g2)
-    w2 = take(2, g2, gates_all[2])
+    n0_near, *s0 = shared(b0, far0)
+    n0_near, b1, e0_in, w0_in, w1_in = tie(n0_near, b1, e0_in, w0_in, w1_in)
+    b2 = onward(b1)
     w2_in = across(w2[slots:])
     e1 = take(1, b1)
     e1_in = across(e1[slots:])
@@ -1059,8 +1063,8 @@
     n0, *k0 = expert(r0, w0)
     n0, b1, e1_in, w2_in = tie(n0, b1, e1_in, w2_in)
     n0_in = across(n0[slots:])
-    n1_near, *s1 = shared(b1, g1)
-    n1_near, b2, e1_in, n0_in, w2_in, g3 = tie(n1_near, b2, e1_in, n0_in, w2_in, g3)
+    n1_near, *s1 = shared(b1, far1)
+    n1_near, b2, e1_in, n0_in, w2_in = tie(n1_near, b2, e1_in, n0_in, w2_in)
     w3 = take(3, g3, gates_all[3])
     w3_in = across(w3[slots:])
     b3 = onward(b2)
@@ -1070,7 +1074,7 @@
     n1, *k1 = expert(r1, w1)
     n1, b2, e2_in, w3_in = tie(n1, b2, e2_in, w3_in)
     n1_in = across(n1[slots:])
-    n2_near, *s2 = shared(b2, g2)
+    n2_near, *s2 = shared(b2, far2)
     n2_near, b3, e2_in, n1_in, w3_in = tie(n2_near, b3, e2_in, n1_in, w3_in)
     ring1 = onward(spread_back(1, n1_near, n1, n1_in).astype(bf16))
     e3 = take(3, b3)
@@ -1079,7 +1083,7 @@
     n2, *k2 = expert(r2, w2)
     n2, b3, e3_in = tie(n2, b3, e3_in)
     n2_in = across(n2[slots:])
-    n3_near, *s3 = shared(b3, g3)
+    n3_near, *s3 = shared(b3, dot_last(g3, sd).astype(bf16))
     n3_near, e3_in, n2_in, ring1 = tie(n3_near, e3_in, n2_in, ring1)
     ring2 = onward(spread_back(2, n2_near, n2, n2_in, ring1).astype(bf16))
     r3, w3 = join(e3, e3_in), join(w3, w3_in)
@@ -1139,9 +1143,8 @@
     grad_w_out = dot_first(attn_own, grad_attn_out).astype(bf16)
     grad_attended = dot_last(grad_attn_out, wo).astype(bf16)
     grad_heads = lax.all_to_all(grad_attended, "expert", split_axis=1, concat_axis=0, tiled=True)
-    grad_heads, o_in, grad_w_out, grad_s_cols, grad_e_down, grad_s_down, grad_e_gate = tie(
+    grad_heads, grad_w_out, grad_s_cols, grad_e_down, grad_s_down, grad_e_gate = tie(
         grad_heads,
-        o_in,
         grad_w_out,
         grad_s_cols,
         grad_e_down_all,
@@ -1151,8 +1154,6 @@
     s_keep, s_other = line_swap(
         grad_s_down.reshape((2,) * (spread.bit_length() - 1) + (2, ff_cut, width)), 0
     )
-    grad_heads, o1 = tie(grad_heads, out_term(1).astype(bf16))
-    ring1 = onward(o1)
     grad_s_cut = lax.all_to_all(
         grad_s_cols.reshape(group, rows_w, -1), "expert", split_axis=0, concat_axis=0, tiled=True
     )
@@ -1160,24 +1161,24 @@
     grad_q_lin, grad_kv, lat_part = attend_back(
         reach, q_att, k_att, v_att, grad_heads, attended, log_total, we, tables, scale
     )
-    lat_part, grad_q_lin, ring1, grad_e_down, s_other = tie(
-        lat_part, grad_q_lin, ring1, grad_e_down, s_other
-    )
-    ring2 = onward(out_term(2, ring1).astype(bf16))
+    lat_part, grad_q_lin, o_in, grad_e_down, s_other = tie(
+        lat_part, grad_q_lin, o_in, grad_e_down, s_other
+    )
+    ring1 = onward(out_term(1).astype(bf16))
     grad_s_down = both_halves(s_keep, s_other)
     for m in range(1, spread.bit_length() - 1):
         s_keep, s_other = line_swap(grad_s_down, m)
         if m < spread.bit_length() - 2:
             grad_s_down = both_halves(s_keep, s_other)
     (grad_lat_sum,) = reduce_rows([lat_part.reshape(group, tok_dev, -1)], 5, 2)
-    grad_lat_sum, grad_q_lin, ring2, s_other, grad_w_out, grad_e_down = tie(
-        grad_lat_sum, grad_q_lin, ring2, s_other, grad_w_out, grad_e_down
+    grad_lat_sum, grad_q_lin, ring1, s_other, grad_w_out, grad_e_down = tie(
+        grad_lat_sum, grad_q_lin, ring1, s_other, grad_w_out, grad_e_down
     )
     grad_s_down = both_halves(s_keep, s_other)
     own_side = rank % 2
     s_keep = lax.dynamic_index_in_dim(grad_s_down, own_side, 0, False)
     s_other = across(lax.dynamic_index_in_dim(grad_s_down, 1 - own_side, 0, False))
-    ring3 = onward(out_term(3, ring2).astype(bf16))
+    ring2 = onward(out_term(2, ring1).astype(bf16))
     first_part = dot_last(grad_q_lin, wq).astype(bf16).reshape(group, tok_dev, width)
     steps = list(range(1, half)) + [0]
     w_blocks = grad_w_out.reshape(group, rows_w, width)
@@ -1217,7 +1218,8 @@
     grad_a_cols = jnp.concatenate(
         [dot_first(h1, grad_q_lin), dot_first(ckv, grad_kv).reshape(width, e_fold)], axis=1
     ).astype(bf16)
-    first_part, grad_a_cols, w_ring = tie(first_part, grad_a_cols, w_ring)
+    first_part, grad_a_cols, w_ring, ring2 = tie(first_part, grad_a_cols, w_ring, ring2)
+    ring3 = onward(out_term(3, ring2).astype(bf16))
     grad_a_cols = lax.psum_scatter(grad_a_cols, "dp", scatter_dimension=0, tiled=True)
     w_ring = onward(ring_term(w_blocks, w_in, 1, w_ring).astype(bf16))
     grad_e_down = lax.psum_scatter(grad_e_down, "dp", scatter_dimension=1, tiled=True)

time: 972 us -> 974 us (level)
  waiting for transfers between devices: 98.3 us -> 118 us
  Pallas kernels: 388 us -> 377 us
    ppermute x18, waiting for transfers between devices: 33.5 us -> 63.9 us  [onward(): return lax.ppermute(values, 'expert', ring)]
    all_to_all x1, waiting for transfers between devices: 26.6 us -> 12 us  [per_device(): lax.all_to_all(attn_heads, 'expert', split_axis=0, concat_axis=1, tiled=T...]
    reduce_scatter x1, waiting for transfers between devices: 4.27 us -> 17 us  [per_device(): lax.psum_scatter(grad_e_gate, 'dp', scatter_dimension=0, tiled=True)]
    unnamed x274 -> x296, local copies, waits for them, and re-layouts: 22 us -> 22.3 us
  transfers between devices with their start and end apart: 49 -> 49, of which waited for: 14 -> 19; matrix products, arithmetic and copies ran while one was open for 38% -> 38% of each run, Pallas kernels for 40% -> 39%
where the time goes in v5:
time: 974 us; the launch traced here: 963 us
  Pallas kernels  377 us (39%)
  matrix products  240 us (25%)
  waiting for transfers between devices  118 us (12%)
  local copies, waits for them, and re-layouts  88.6 us (9%)
  other arithmetic  62.1 us (6%)
  starting transfers between devices  60.7 us (6%)
  between operations  16.4 us (2%)
    pallas_call x1, Pallas kernels, prologue(): pl.pallas_call(functools.partial(prologue_kernel, chunks), out_shape=[jax...  162 us
    pallas_call x2, Pallas kernels, reduce_rows(): pl.pallas_call(functools.partial(reduce_kernel, parts), out_shape=[jax.Sh...  147 us
    dot_general x27, matrix products, dot_last(): lax.dot_general(left, right, (((1,), (1,)), ((), ())), preferred_element_...  84.8 us
    dot_general x17, matrix products, dot_first(): lax.dot_general(left, right, (((0,), (0,)), ((), ())), preferred_element_...  78.7 us
    dot_general x31, matrix products, matmul(): return jnp.dot(left, right, preferred_element_type=f32)  75 us
    ppermute x18, waiting for transfers between devices, onward(): return lax.ppermute(values, 'expert', ring)  63.9 us
    pallas_call x1, Pallas kernels, attend_back(): pl.pallas_call(functools.partial(attend_back_kernel, heads, segs, scale),...  27.8 us
    ppermute x18, starting transfers between devices, onward(): return lax.ppermute(values, 'expert', ring)  25.8 us
  transfers between devices with their start and end apart: 49, of which 19 were waited for; matrix products, arithmetic and copies ran while one was open for 38% of the time, Pallas kernels for 39%

profile of v5, /device:TPU:0, one launch (start us, length us, event | category | flops | bytes accessed | tf_op | source)
XLA Modules:
  0.0 962.8 jit_solution(11655976859094079232)
XLA Ops:
  20.7 162.2 %prologue.1 = (bf16[8,256,2048]{2,1,0:T(8,128)(2,1)}, bf16[4,8,64,2176]{3,2,1,0:T(8,128)(2,1)}, bf16[4,2,88,2048]{3,2,1,0:T(8,128)(2,1)}, f32[8,8,256]{2,1,0:T(8,128)}) custom-call(bf16[256,2048]{1,0:T(8,128)(2,1)} %x_ref.1, bf16[8,64,2176]{2,1,0:T(8,128)(2,1)} %pad_maximum_fusion.3.w_ref, bf16[88,2048]{1,0:T(8,128)(2,1)} %d_ref.1, f32[8,256]{1,0:T(8,128)} %bitcast.384), custom_call_target="tpu_custom_call" | custom-call | bytes 300000000 | tf_op jit(solution)/shard_map/prologue/pallas_call | solution.py:341
  193.5 20.2 %project.1 = (bf16[2048,2048]{1,0:T(8,128)(2,1)}, bf16[2048,512]{1,0:T(8,128)(2,1)}, bf16[2048,512]{1,0:T(8,128)(2,1)}, bf16[2048,256]{1,0:T(8,128)(2,1)}, f32[2...) custom-call(bf16[2048,2048]{1,0:T(8,128)(2,1)} %bitcast.340, bf16[2048,2176]{1,0:T(8,128)(2,1)} %bitcast.309, ...), custom_call_target="tpu_custom_call" | custom-call | bytes 60000000 | tf_op jit(solution)/shard_map/project/pallas_call | solution.py:560
  213.7 6.6 collective-permute-done
  223.5 19.9 %attend.1 = (bf16[2048,256]{1,0:T(8,128)(2,1)}, f32[2048,256]{1,0:T(8,128)}, f32[2,2048]{1,0:T(2,128)}) custom-call(s32[64]{0:T(128)} %reshape.377.reach_ref, bf16[2048,512]{1,0:T(8,128)(2,1)} %get-tuple-element.142.q_ref, bf16[2048,512]{1,0:T(8,128)(2,1)} %get-tuple-element.143.k_ref, bf16[2048,256]{1,0:T(8,128)(2,1)} %get-tuple-element.144.v_ref), custom_call_target="tpu_custom_call" | custom-call | bytes 70000000 | tf_op jit(solution)/shard_map/attend/pallas_call | solution.py:652
  249.3 4.5 all-to-all-start
  266.0 12.0 %all-to-all-done = bf16[8,256,256]{1,2,0:T(8,128)(2,1)} async-done(((bf16[8,256,256]{1,2,0:T(8,128)(2,1)}), bf16[8,256,256]{1,2,0:T(8,128)(2,1)}, u32[]{:S(2)}, u32[]{:S(2)}) %all-to-all-start) | async-done | bytes 1048608 | tf_op jit(solution)/shard_map/all_to_all | solution.py:1008
  284.2 6.4 multiply_reduce_fusion.2
  290.9 15.3 %collective-permute-done.2 = bf16[256,2048]{1,0:T(8,128)(2,1)} collective-permute-done((bf16[256,2048]{1,0:T(8,128)(2,1)}, bf16[256,2048]{1,0:T(8,128)(2,1)}, u32[]{:S(2)}, u32[]{:S(2)}) %collective-permute-start.2) | collective-permute-done | bytes 1048608 | tf_op jit(solution)/shard_map/ppermute | solution.py:950
  322.6 11.0 %collective-permute-done.3 = bf16[256,2048]{1,0:T(8,128)(2,1)S(1)} collective-permute-done((bf16[256,2048]{1,0:T(8,128)(2,1)S(1)}, bf16[256,2048]{1,0:T(8,128)(2,1)S(1)}, u32[]{:S(2)}, u32[]{:S(2)}) %collective-permute-start.3) | collective-permute-done | bytes 1048608 | tf_op jit(solution)/shard_map/ppermute | solution.py:950
  342.2 4.9 fusion.120
  354.2 4.6 fusion.110
  358.8 4.7 fusion.126
  369.7 4.2 collective-permute-done.10
  381.8 4.2 multiply_convert_fusion.7
  389.2 5.2 fusion.107
  394.3 4.6 fusion.132
  404.4 6.9 collective-permute-done.14
  422.9 4.6 fusion.104
  427.5 4.6 fusion.138
  442.8 4.9 collective-permute-start.18
  456.0 3.9 collective-permute-done.18
  462.5 11.4 %convolution_convert_fusion.5 = bf16[2048,1536]{1,0:T(8,128)(2,1)} fusion(bf16[256,2048]{1,0:T(8,128)(2,1)S(1)} %copy-done.55, bf16[256,2048]{1,0:T(8,128)(2,1)S(1)} %copy-done.53, bf16[256,2048]{1,0:T(8,128)(2,1)S(1)} %copy-done.51, bf16[256,2048]{1,0:T(8,128)(2,1)S(1)} %multiply_convert_fusion, bf16[256,768]{1,0:T(8,128)(2,1)} %copy-done.76, ...), kind=kOutput, calls=%fused_computation.5 | convolution fusion | flops 6487539712 | bytes 13631488 | tf_op jit(solution)/shard_map/dot_general | solution.py:70
  476.8 7.8 fusion.60
  488.3 8.5 convolution_convert_fusion.1
  496.7 10.7 %convolution_convert_fusion.2 = bf16[2048,1408]{1,0:T(8,128)(2,1)} fusion(bf16[896,2048]{1,0:T(8,128)(2,1)} %copy-done.90, bf16[224,1408]{1,0:T(8,128)(2,1)} %copy-done.117, bf16[224,1408]{1,0:T(8,128)(2,1)} %copy-done.116, bf16[224,1408]{1,0:T(8,128)(2,1)} %copy-done.115, bf16[224,1408]{1,0:T(8,128)(2,1)} %copy-done.114), kind=kOutput, calls=%fused_computation.2 | convolution fusion | flops 5180358656 | bytes 11960320 | tf_op jit(solution)/shard_map/dot_general | solution.py:70
  513.5 11.7 %fusion.57 = bf16[896,2048]{1,0:T(8,128)(2,1)} fusion(bf16[1,1408,2048]{2,1,0:T(8,128)(2,1)} %param.35, bf16[224,1408]{1,0:T(8,128)(2,1)S(1)} %copy-done.66, bf16[224,1408]{1,0:T(8,128)(2,1)S(1)} %copy-done.64, bf16[224,1408]{1,0:T(8,128)(2,1)S(1)} %copy-done.62, bf16[224,1408]{1,0:T(8,128)(2,1)S(1)} %copy-done.60), kind=kOutput, calls=%fused_computation.68 | convolution fusion | flops 5179310080 | bytes 11960320 | tf_op jit(solution)/shard_map/dot_general | solution.py:62
  535.7 7.5 convolution_convert_fusion.7
  544.2 3.6 all-to-all-start.1
  549.9 3.9 slice.341
  553.8 7.1 convolution_convert_fusion.4
  560.8 10.3 %convolution_convert_fusion = bf16[1408,2048]{1,0:T(8,128)(2,1)} fusion(bf16[896,1408]{1,0:T(8,128)(2,1)} %pad_maximum_fusion.2, bf16[896,2048]{1,0:T(8,128)(2,1)} %constant_dynamic-update-slice_fusion.8), kind=kOutput, calls=%fused_computation | convolution fusion | flops 5170266112 | bytes 11960320 | tf_op jit(solution)/shard_map/dot_general | solution.py:70
  571.2 17.0 %reduce-scatter.10.cloned.1.call-done = bf16[512,1408]{1,0:T(8,128)(2,1)} async-done(((bf16[2048,1408]{1,0:T(8,128)(2,1)}), bf16[512,1408]{1,0:T(8,128)(2,1)}) %reduce-scatter.10.cloned.1.call-update) | async-done | bytes 1441808 | tf_op jit(solution)/shard_map/reduce_scatter | solution.py:1126
  599.9 27.8 %attend_back.1 = (bf16[2048,512]{1,0:T(8,128)(2,1)}, bf16[2048,512]{1,0:T(8,128)(2,1)}, bf16[2048,640]{1,0:T(8,128)(2,1)}) custom-call(s32[64]{0:T(128)} %reshape.377.reach_ref, bf16[2048,512]{1,0:T(8,128)(2,1)} %get-tuple-element.142.q_ref, bf16[2048,512]{1,0:T(8,128)(2,1)} %get-tuple-element.143.k_ref, bf16[2048,256]{1,0:T(8,128)(2,1)} %get-tuple-element.144.v_ref, ...), custom_call_target="tpu_custom_call" | custom-call | bytes 90000000 | tf_op jit(solution)/shard_map/attend_back/pallas_call | solution.py:786
  627.7 6.2 collective-permute-done.21
  648.3 40.8 %reduce_rows.2 = f32[256,640]{1,0:T(8,128)} custom-call(bf16[8,256,640]{2,1,0:T(8,128)(2,1)} %bitcast.346), custom_call_target="tpu_custom_call" | custom-call | bytes 94371840 | tf_op jit(solution)/shard_map/reduce_rows/pallas_call | solution.py:477
  702.2 10.2 %convolution_convert_fusion.3 = bf16[2048,2048]{1,0:T(8,128)(2,1)} fusion(bf16[2048,512]{1,0:T(8,128)(2,1)} %get-tuple-element.220, bf16[2048,2176]{1,0:T(8,128)(2,1)} %bitcast.311), kind=kOutput, calls=%fused_computation.3 | convolution fusion | flops 4299161600 | bytes 12582912 | tf_op jit(solution)/shard_map/dot_general | solution.py:66
  720.3 3.6 fusion.86
  726.3 8.3 convolution_convert_fusion.6
  739.3 9.6 collective-permute-done.27
  752.4 5.7 all-to-all-start.2
  759.9 3.5 fusion.85
  772.5 106.0 %reduce_rows.3 = f32[256,2048]{1,0:T(8,128)} custom-call(bf16[8,256,2048]{2,1,0:T(8,128)(2,1)} %bitcast.339), custom_call_target="tpu_custom_call" | custom-call | bytes 301989888 | tf_op jit(solution)/shard_map/reduce_rows/pallas_call | solution.py:477
  888.6 4.4 all-to-all-start.3
  896.4 4.0 reshape.409
  900.4 3.8 fusion.157
  904.4 3.6 fusion.88
  925.3 3.5 collective-permute-done.33
  939.6 4.2 collective-permute-done.35
  (590 shorter events, 286.6 us)
Async XLA Ops:
  7.2 181.5 %all-gather.3.cloned.1.call-start = ((), (), s32[]{:S(2)}) async-start(), calls=%async_computation.11 | async-start | bytes 2703360 | tf_op jit(solution)/shard_map/all_gather | solution.py:907
  10.4 273.8 %all-gather.5.cloned.1.call-start = ((), (), s32[]{:S(2)}) async-start(), calls=%async_computation.12 | async-start | bytes 8650752 | tf_op jit(solution)/shard_map/all_gather | solution.py:914
  182.9 37.4 %collective-permute-start = (bf16[256,2048]{1,0:T(8,128)(2,1)S(1)}, bf16[256,2048]{1,0:T(8,128)(2,1)S(1)}, u32[]{:S(2)}, u32[]{:S(2)}) collective-permute-start(bf16[256,2048]{1,0:T(8,128)(2,1)S(1)} %copy-done.18), channel_id=1, source_target_pairs={{0,2},{1,3},{2,4},{3,5},{4,6},{5,7},{6,0},{7,1},{8,10},{9,11},{10,... | collective-permute-start | bytes 3145736 | tf_op jit(solution)/shard_map/ppermute | solution.py:950
  220.3 25.7 %collective-permute-start.1 = (bf16[256,2048]{1,0:T(8,128)(2,1)S(1)}, bf16[256,2048]{1,0:T(8,128)(2,1)S(1)}, u32[]{:S(2)}, u32[]{:S(2)}) collective-permute-start(bf16[256,2048]{1,0:T(8,128)(2,1)S(1)} %collective-permute-done), channel_id=1, source_target_pairs={{0,2},{1,3},{2,4},{3,5},{4,6},{5,7},{6,0},{7,1},{8,10},{9,11},{10,... | collective-permute-start | bytes 3145736 | tf_op jit(solution)/shard_map/ppermute | solution.py:950
  249.3 28.7 %all-to-all-start = ((bf16[8,256,256]{1,2,0:T(8,128)(2,1)}), bf16[8,256,256]{1,2,0:T(8,128)(2,1)}, u32[]{:S(2)}, u32[]{:S(2)}) async-start(bf16[8,256,256]{1,2,0:T(8,128)(2,1)} %copy.139), calls=%async_computation | async-start | bytes 2097152 | tf_op jit(solution)/shard_map/all_to_all | solution.py:1008
  253.8 317.3 %reduce-scatter.8.cloned.1.call-start = ((), (), s32[]{:S(2)}) async-start(), calls=%async_computation.13 | async-start | bytes 7864320 | tf_op jit(solution)/shard_map/reduce_scatter | solution.py:1131
  279.8 40.7 %collective-permute-start.6 = (bf16[112,2048]{1,0:T(8,128)(2,1)}, bf16[112,2048]{1,0:T(8,128)(2,1)}, u32[]{:S(2)}, u32[]{:S(2)}) collective-permute-start(bf16[112,2048]{1,0:T(8,128)(2,1)} %slice.315), channel_id=1, source_target_pairs={{0,1},{1,0},{2,3},{3,2},{4,5},{5,4},{6,7},{7,6},{8,9},{9,8},{10,11... | collective-permute-start | bytes 1376264 | tf_op jit(solution)/shard_map/ppermute | solution.py:947
  281.0 25.1 %collective-permute-start.2 = (bf16[256,2048]{1,0:T(8,128)(2,1)}, bf16[256,2048]{1,0:T(8,128)(2,1)}, u32[]{:S(2)}, u32[]{:S(2)}) collective-permute-start(bf16[256,2048]{1,0:T(8,128)(2,1)} %copy-done.47), channel_id=1, source_target_pairs={{0,2},{1,3},{2,4},{3,5},{4,6},{5,7},{6,0},{7,1},{8,10},{9,11},{10,... | collective-permute-start | bytes 3145736 | tf_op jit(solution)/shard_map/ppermute | solution.py:950
  283.4 37.1 %collective-permute-start.5 = (bf16[112,2048]{1,0:T(8,128)(2,1)}, bf16[112,2048]{1,0:T(8,128)(2,1)}, u32[]{:S(2)}, u32[]{:S(2)}) collective-permute-start(bf16[112,2048]{1,0:T(8,128)(2,1)} %get-tuple-element.316), channel_id=1, source_target_pairs={{0,1},{1,0},{2,3},{3,2},{4,5},{5,4},{6,7},{7,6},{8,9},{9,8},{10,11... | collective-permute-start | bytes 1376264 | tf_op jit(solution)/shard_map/ppermute | solution.py:947
  309.7 23.9 %collective-permute-start.3 = (bf16[256,2048]{1,0:T(8,128)(2,1)S(1)}, bf16[256,2048]{1,0:T(8,128)(2,1)S(1)}, u32[]{:S(2)}, u32[]{:S(2)}) collective-permute-start(bf16[256,2048]{1,0:T(8,128)(2,1)S(1)} %multiply_convert_fusion), channel_id=1, source_target_pairs={{0,2},{1,3},{2,4},{3,5},{4,6},{5,7},{6,0},{7,1},{8,10},{9,11},{10,... | collective-permute-start | bytes 3145736 | tf_op jit(solution)/shard_map/ppermute | solution.py:950
  313.1 9.5 collective-permute-start.4
  334.1 40.6 %collective-permute-start.9 = (bf16[256,2048]{1,0:T(8,128)(2,1)S(1)}, bf16[256,2048]{1,0:T(8,128)(2,1)S(1)}, u32[]{:S(2)}, u32[]{:S(2)}) collective-permute-start(bf16[256,2048]{1,0:T(8,128)(2,1)S(1)} %collective-permute-done.3), channel_id=1, source_target_pairs={{0,2},{1,3},{2,4},{3,5},{4,6},{5,7},{6,0},{7,1},{8,10},{9,11},{10,... | collective-permute-start | bytes 3145736 | tf_op jit(solution)/shard_map/ppermute | solution.py:950
  339.9 23.6 %collective-permute-start.8 = (bf16[112,2048]{1,0:T(8,128)(2,1)S(1)}, bf16[112,2048]{1,0:T(8,128)(2,1)S(1)}, u32[]{:S(2)}, u32[]{:S(2)}) collective-permute-start(bf16[112,2048]{1,0:T(8,128)(2,1)S(1)} %get-tuple-element.311), channel_id=1, source_target_pairs={{0,1},{1,0},{2,3},{3,2},{4,5},{5,4},{6,7},{7,6},{8,9},{9,8},{10,11... | collective-permute-start | bytes 1376264 | tf_op jit(solution)/shard_map/ppermute | solution.py:947
  340.1 23.4 %collective-permute-start.7 = (bf16[112,2048]{1,0:T(8,128)(2,1)S(1)}, bf16[112,2048]{1,0:T(8,128)(2,1)S(1)}, u32[]{:S(2)}, u32[]{:S(2)}) collective-permute-start(bf16[112,2048]{1,0:T(8,128)(2,1)S(1)} %get-tuple-element.333), channel_id=1, source_target_pairs={{0,1},{1,0},{2,3},{3,2},{4,5},{5,4},{6,7},{7,6},{8,9},{9,8},{10,11... | collective-permute-start | bytes 1376264 | tf_op jit(solution)/shard_map/ppermute | solution.py:947
  365.4 8.5 collective-permute-start.10
  375.1 36.3 %collective-permute-start.13 = (bf16[256,2048]{1,0:T(8,128)(2,1)S(1)}, bf16[256,2048]{1,0:T(8,128)(2,1)S(1)}, u32[]{:S(2)}, u32[]{:S(2)}) collective-permute-start(bf16[256,2048]{1,0:T(8,128)(2,1)S(1)} %collective-permute-done.9), channel_id=1, source_target_pairs={{0,2},{1,3},{2,4},{3,5},{4,6},{5,7},{6,0},{7,1},{8,10},{9,11},{10,... | collective-permute-start | bytes 3145736 | tf_op jit(solution)/shard_map/ppermute | solution.py:950
  376.9 22.0 %collective-permute-start.12 = (bf16[112,2048]{1,0:T(8,128)(2,1)S(1)}, bf16[112,2048]{1,0:T(8,128)(2,1)S(1)}, u32[]{:S(2)}, u32[]{:S(2)}) collective-permute-start(bf16[112,2048]{1,0:T(8,128)(2,1)S(1)} %get-tuple-element.308), channel_id=1, source_target_pairs={{0,1},{1,0},{2,3},{3,2},{4,5},{5,4},{6,7},{7,6},{8,9},{9,8},{10,11... | collective-permute-start | bytes 1376264 | tf_op jit(solution)/shard_map/ppermute | solution.py:947
  377.4 21.5 %collective-permute-start.11 = (bf16[112,2048]{1,0:T(8,128)(2,1)S(1)}, bf16[112,2048]{1,0:T(8,128)(2,1)S(1)}, u32[]{:S(2)}, u32[]{:S(2)}) collective-permute-start(bf16[112,2048]{1,0:T(8,128)(2,1)S(1)} %get-tuple-element.330), channel_id=1, source_target_pairs={{0,1},{1,0},{2,3},{3,2},{4,5},{5,4},{6,7},{7,6},{8,9},{9,8},{10,11... | collective-permute-start | bytes 1376264 | tf_op jit(solution)/shard_map/ppermute | solution.py:947
  400.0 11.4 %collective-permute-start.14 = (bf16[112,2048]{1,0:T(8,128)(2,1)S(1)}, bf16[112,2048]{1,0:T(8,128)(2,1)S(1)}, u32[]{:S(2)}, u32[]{:S(2)}) collective-permute-start(bf16[112,2048]{1,0:T(8,128)(2,1)S(1)} %get-tuple-element.327), channel_id=1, source_target_pairs={{0,1},{1,0},{2,3},{3,2},{4,5},{5,4},{6,7},{7,6},{8,9},{9,8},{10,11... | collective-permute-start | bytes 1376264 | tf_op jit(solution)/shard_map/ppermute | solution.py:947
  412.0 20.0 %collective-permute-start.15 = (bf16[112,2048]{1,0:T(8,128)(2,1)S(1)}, bf16[112,2048]{1,0:T(8,128)(2,1)S(1)}, u32[]{:S(2)}, u32[]{:S(2)}) collective-permute-start(bf16[112,2048]{1,0:T(8,128)(2,1)S(1)} %get-tuple-element.325), channel_id=1, source_target_pairs={{0,1},{1,0},{2,3},{3,2},{4,5},{5,4},{6,7},{7,6},{8,9},{9,8},{10,11... | collective-permute-start | bytes 1376264 | tf_op jit(solution)/shard_map/ppermute | solution.py:947
  413.9 27.8 %collective-permute-start.17 = (bf16[256,2048]{1,0:T(8,128)(2,1)S(1)}, bf16[256,2048]{1,0:T(8,128)(2,1)S(1)}, u32[]{:S(2)}, u32[]{:S(2)}) collective-permute-start(bf16[256,2048]{1,0:T(8,128)(2,1)S(1)} %add_convert_fusion.2), channel_id=1, source_target_pairs={{0,2},{1,3},{2,4},{3,5},{4,6},{5,7},{6,0},{7,1},{8,10},{9,11},{10,... | collective-permute-start | bytes 3145736 | tf_op jit(solution)/shard_map/ppermute | solution.py:950
  433.2 8.5 collective-permute-start.16
  442.8 17.2 %collective-permute-start.18 = (bf16[256,2048]{1,0:T(8,128)(2,1)S(1)}, bf16[256,2048]{1,0:T(8,128)(2,1)}, u32[]{:S(2)}, u32[]{:S(2)}) collective-permute-start(bf16[256,2048]{1,0:T(8,128)(2,1)S(1)} %add_convert_fusion.1), channel_id=1, source_target_pairs={{0,2},{1,3},{2,4},{3,5},{4,6},{5,7},{6,0},{7,1},{8,10},{9,11},{10,... | collective-permute-start | bytes 3145736 | tf_op jit(solution)/shard_map/ppermute | solution.py:950
  460.9 12.9 %collective-permute-start.19 = (bf16[112,2048]{1,0:T(8,128)(2,1)}, bf16[112,2048]{1,0:T(8,128)(2,1)}, u32[]{:S(2)}, u32[]{:S(2)}) collective-permute-start(bf16[112,2048]{1,0:T(8,128)(2,1)} %get-tuple-element.320), channel_id=1, source_target_pairs={{0,1},{1,0},{2,3},{3,2},{4,5},{5,4},{6,7},{7,6},{8,9},{9,8},{10,11... | collective-permute-start | bytes 1376264 | tf_op jit(solution)/shard_map/ppermute | solution.py:947
  473.9 114.3 %reduce-scatter.10.cloned.1.call-start = ((), (), s32[]{:S(2)}) async-start(), calls=%async_computation.14 | async-start | bytes 7208960 | tf_op jit(solution)/shard_map/reduce_scatter | solution.py:1126
  511.0 17.1 %collective-permute-start.20 = (bf16[256,2048]{1,0:T(8,128)(2,1)S(1)}, bf16[256,2048]{1,0:T(8,128)(2,1)S(1)}, u32[]{:S(2)}, u32[]{:S(2)}) collective-permute-start(bf16[256,2048]{1,0:T(8,128)(2,1)S(1)} %add_convert_fusion), channel_id=1, source_target_pairs={{0,2},{1,3},{2,4},{3,5},{4,6},{5,7},{6,0},{7,1},{8,10},{9,11},{10,... | collective-permute-start | bytes 3145736 | tf_op jit(solution)/shard_map/ppermute | solution.py:950
  544.2 26.9 %all-to-all-start.1 = ((bf16[256,8,256]{2,0,1:T(8,128)(2,1)}), bf16[256,8,256]{2,0,1:T(8,128)(2,1)S(1)}, u32[]{:S(2)}, u32[]{:S(2)}) async-start(bf16[256,8,256]{2,0,1:T(8,128)(2,1)} %bitcast.303), calls=%async_computation.1 | async-start | bytes 2097152 | tf_op jit(solution)/shard_map/all_to_all | solution.py:1145
  547.8 141.3 %reduce-scatter.12.cloned.1.call-start = ((), (), s32[]{:S(2)}) async-start(), calls=%async_computation.15 | async-start | bytes 10485760 | tf_op jit(solution)/shard_map/reduce_scatter | solution.py:1160
  588.2 290.4 %reduce-scatter.18.cloned.1.call-start = ((), (), s32[]{:S(2)}) async-start(), calls=%async_computation.18 | async-start | bytes 7208960 | tf_op jit(solution)/shard_map/reduce_scatter | solution.py:1127
  588.8 289.9 %reduce-scatter.14.cloned.1.call-start = ((), (), s32[]{:S(2)}) async-start(), calls=%async_computation.16 | async-start | bytes 3276800 | tf_op jit(solution)/shard_map/reduce_scatter | solution.py:1216
  591.8 42.1 %collective-permute-start.21 = (bf16[4,112,2048]{2,1,0:T(8,128)(2,1)}, bf16[4,112,2048]{2,1,0:T(8,128)(2,1)}, u32[]{:S(2)}, u32[]{:S(2)}) collective-permute-start(bf16[4,112,2048]{2,1,0:T(8,128)(2,1)} %slice.342), channel_id=1, source_target_pairs={{0,1},{1,0},{2,3},{3,2},{4,5},{5,4},{6,7},{7,6},{8,9},{9,8},{10,11... | collective-permute-start | bytes 5505032 | tf_op jit(solution)/shard_map/ppermute | solution.py:947
  596.0 37.9 %collective-permute-start.22 = (bf16[2,2,88,2048]{3,2,1,0:T(8,128)(2,1)}, bf16[2,2,88,2048]{3,2,1,0:T(8,128)(2,1)S(1)}, u32[]{:S(2)}, u32[]{:S(2)}) collective-permute-start(bf16[2,2,88,2048]{3,2,1,0:T(8,128)(2,1)} %dynamic-slice_bitcast_fusion), channel_id=1, source_target_pairs={{0,8},{8,0},{16,24},{24,16},{1,9},{9,1},{17,25},{25,17},{2,10},{10... | collective-permute-start | bytes 4325384 | tf_op jit(solution)/shard_map/ppermute | solution.py:967
  640.4 48.7 %collective-permute-start.23 = (bf16[256,2048]{1,0:T(8,128)(2,1)}, bf16[256,2048]{1,0:T(8,128)(2,1)}, u32[]{:S(2)}, u32[]{:S(2)}) collective-permute-start(bf16[256,2048]{1,0:T(8,128)(2,1)} %fusion.87), channel_id=1, source_target_pairs={{0,2},{1,3},{2,4},{3,5},{4,6},{5,7},{6,0},{7,1},{8,10},{9,11},{10,... | collective-permute-start | bytes 3145736 | tf_op jit(solution)/shard_map/ppermute | solution.py:950
  644.4 44.6 %collective-permute-start.24 = (bf16[2,88,2048]{2,1,0:T(8,128)(2,1)}, bf16[2,88,2048]{2,1,0:T(8,128)(2,1)S(1)}, u32[]{:S(2)}, u32[]{:S(2)}) collective-permute-start(bf16[2,88,2048]{2,1,0:T(8,128)(2,1)} %dynamic-slice_bitcast_fusion.1), channel_id=1, source_target_pairs={{0,16},{8,24},{16,0},{24,8},{1,17},{9,25},{17,1},{25,9},{2,18},{10... | collective-permute-start | bytes 2162696 | tf_op jit(solution)/shard_map/ppermute | solution.py:967
  693.8 20.2 %collective-permute-start.25 = (bf16[4,64,2048]{2,1,0:T(8,128)(2,1)}, bf16[4,64,2048]{2,1,0:T(8,128)(2,1)}, u32[]{:S(2)}, u32[]{:S(2)}) collective-permute-start(bf16[4,64,2048]{2,1,0:T(8,128)(2,1)} %pad_maximum_fusion.5), channel_id=1, source_target_pairs={{0,1},{1,0},{2,3},{3,2},{4,5},{5,4},{6,7},{7,6},{8,9},{9,8},{10,11... | collective-permute-start | bytes 3145736 | tf_op jit(solution)/shard_map/ppermute | solution.py:947
  714.1 164.6 %reduce-scatter.16.cloned.1.call-start = ((), (), s32[]{:S(2)}) async-start(), calls=%async_computation.17 | async-start | bytes 3276800 | tf_op jit(solution)/shard_map/reduce_scatter | solution.py:1223
  723.9 25.0 %collective-permute-start.27 = (bf16[256,2048]{1,0:T(8,128)(2,1)}, bf16[256,2048]{1,0:T(8,128)(2,1)}, u32[]{:S(2)}, u32[]{:S(2)}) collective-permute-start(bf16[256,2048]{1,0:T(8,128)(2,1)} %fusion.86), channel_id=1, source_target_pairs={{0,2},{1,3},{2,4},{3,5},{4,6},{5,7},{6,0},{7,1},{8,10},{9,11},{10,... | collective-permute-start | bytes 3145736 | tf_op jit(solution)/shard_map/ppermute | solution.py:950
  735.7 15.8 %collective-permute-start.26 = (bf16[64,2048]{1,0:T(8,128)(2,1)S(1)}, bf16[64,2048]{1,0:T(8,128)(2,1)S(1)}, u32[]{:S(2)}, u32[]{:S(2)}) collective-permute-start(bf16[64,2048]{1,0:T(8,128)(2,1)S(1)} %fusion.316), channel_id=1, source_target_pairs={{0,2},{1,3},{2,4},{3,5},{4,6},{5,7},{6,0},{7,1},{8,10},{9,11},{10,... | collective-permute-start | bytes 786440 | tf_op jit(solution)/shard_map/ppermute | solution.py:950
  751.6 201.2 %reduce-scatter.20.cloned.1.call-start = ((), (), s32[]{:S(2)}) async-start(), calls=%async_computation.19 | async-start | bytes 7208960 | tf_op jit(solution)/shard_map/reduce_scatter | solution.py:1225
  752.4 126.2 %all-to-all-start.2 = ((bf16[8,64,1536]{2,1,0:T(8,128)(2,1)}), bf16[8,64,1536]{2,1,0:T(8,128)(2,1)}, u32[]{:S(2)}, u32[]{:S(2)}) async-start(bf16[8,64,1536]{2,1,0:T(8,128)(2,1)} %bitcast.360), calls=%async_computation.7 | async-start | bytes 3145728 | tf_op jit(solution)/shard_map/all_to_all | solution.py:1157
  763.4 115.2 %collective-permute-start.28 = (bf16[256,2048]{1,0:T(8,128)(2,1)}, bf16[256,2048]{1,0:T(8,128)(2,1)}, u32[]{:S(2)}, u32[]{:S(2)}) collective-permute-start(bf16[256,2048]{1,0:T(8,128)(2,1)} %fusion.85), channel_id=1, source_target_pairs={{0,2},{1,3},{2,4},{3,5},{4,6},{5,7},{6,0},{7,1},{8,10},{9,11},{10,... | collective-permute-start | bytes 3145736 | tf_op jit(solution)/shard_map/ppermute | solution.py:950
  765.8 112.8 %collective-permute-start.30 = (bf16[88,2048]{1,0:T(8,128)(2,1)S(1)}, bf16[88,2048]{1,0:T(8,128)(2,1)S(1)}, u32[]{:S(2)}, u32[]{:S(2)}) collective-permute-start(bf16[88,2048]{1,0:T(8,128)(2,1)S(1)} %get-tuple-element.337), channel_id=1, source_target_pairs={{0,1},{1,0},{2,3},{3,2},{4,5},{5,4},{6,7},{7,6},{8,9},{9,8},{10,11... | collective-permute-start | bytes 1081352 | tf_op jit(solution)/shard_map/ppermute | solution.py:947
  769.2 109.4 %collective-permute-start.29 = (bf16[64,2048]{1,0:T(8,128)(2,1)}, bf16[64,2048]{1,0:T(8,128)(2,1)S(1)}, u32[]{:S(2)}, u32[]{:S(2)}) collective-permute-start(bf16[64,2048]{1,0:T(8,128)(2,1)} %fusion.308), channel_id=1, source_target_pairs={{0,2},{1,3},{2,4},{3,5},{4,6},{5,7},{6,0},{7,1},{8,10},{9,11},{10,... | collective-permute-start | bytes 786440 | tf_op jit(solution)/shard_map/ppermute | solution.py:950
  880.6 40.3 %collective-permute-start.32 = (bf16[64,2048]{1,0:T(8,128)(2,1)}, bf16[64,2048]{1,0:T(8,128)(2,1)}, u32[]{:S(2)}, u32[]{:S(2)}) collective-permute-start(bf16[64,2048]{1,0:T(8,128)(2,1)} %fusion.307), channel_id=1, source_target_pairs={{0,2},{1,3},{2,4},{3,5},{4,6},{5,7},{6,0},{7,1},{8,10},{9,11},{10,... | collective-permute-start | bytes 786440 | tf_op jit(solution)/shard_map/ppermute | solution.py:950
  885.6 35.3 %collective-permute-start.31 = (bf16[4,64,640]{2,1,0:T(8,128)(2,1)}, bf16[4,64,640]{2,1,0:T(8,128)(2,1)}, u32[]{:S(2)}, u32[]{:S(2)}) collective-permute-start(bf16[4,64,640]{2,1,0:T(8,128)(2,1)} %pad_maximum_fusion.18), channel_id=1, source_target_pairs={{0,1},{1,0},{2,3},{3,2},{4,5},{5,4},{6,7},{7,6},{8,9},{9,8},{10,11... | collective-permute-start | bytes 983048 | tf_op jit(solution)/shard_map/ppermute | solution.py:947
  888.6 58.4 %all-to-all-start.3 = ((bf16[8,64,640]{2,1,0:T(8,128)(2,1)}), bf16[8,64,640]{2,1,0:T(8,128)(2,1)}, u32[]{:S(2)}, u32[]{:S(2)}) async-start(bf16[8,64,640]{2,1,0:T(8,128)(2,1)} %bitcast.63), calls=%async_computation.9 | async-start | bytes 1310720 | tf_op jit(solution)/shard_map/all_to_all | solution.py:1272
  921.8 7.1 collective-permute-start.33
  929.8 6.5 collective-permute-start.34
  (144 other events, 2062.0 us)
Sparse Core Ops, SparseCore 0:
  11.5 100.6 all-gather.2
  115.2 96.3 all-gather.4
  474.0 56.6 reduce-scatter.7
  533.3 54.8 reduce-scatter.9
  590.6 87.4 reduce-scatter.11
  680.6 55.3 reduce-scatter.17
  739.1 34.6 reduce-scatter.13
  777.1 34.6 reduce-scatter.15
  814.4 54.8 reduce-scatter.19

commit v6 on v5

--- a/solution.py
+++ b/solution.py
@@ -1015,7 +1015,7 @@
     tokens_f = tokens.astype(f32)
     resid = tokens_f + matmul(attn_own, wo)
     second_normed, second_norm_back = jax.vjp(norm_rows, resid, f_gain)
-    b0, g3 = tie(second_normed.astype(bf16), g3)
+    b0 = second_normed.astype(bf16)
 
     b1 = onward(b0)
     def shared(h2, grad_s_act):
@@ -1064,7 +1064,7 @@
     n0, b1, e1_in, w2_in = tie(n0, b1, e1_in, w2_in)
     n0_in = across(n0[slots:])
     n1_near, *s1 = shared(b1, far1)
-    n1_near, b2, e1_in, n0_in, w2_in = tie(n1_near, b2, e1_in, n0_in, w2_in)
+    n1_near, b2, e1_in, n0_in, w2_in, g3 = tie(n1_near, b2, e1_in, n0_in, w2_in, g3)
     w3 = take(3, g3, gates_all[3])
     w3_in = across(w3[slots:])
     b3 = onward(b2)
@@ -1143,13 +1143,12 @@
     grad_w_out = dot_first(attn_own, grad_attn_out).astype(bf16)
     grad_attended = dot_last(grad_attn_out, wo).astype(bf16)
     grad_heads = lax.all_to_all(grad_attended, "expert", split_axis=1, concat_axis=0, tiled=True)
-    grad_heads, grad_w_out, grad_s_cols, grad_e_down, grad_s_down, grad_e_gate = tie(
+    grad_heads, grad_w_out, grad_s_cols, grad_e_down, grad_s_down = tie(
         grad_heads,
         grad_w_out,
         grad_s_cols,
         grad_e_down_all,
         grad_s_down,
-        grad_e_gate,
     )
     s_keep, s_other = line_swap(
         grad_s_down.reshape((2,) * (spread.bit_length() - 1) + (2, ff_cut, width)), 0
@@ -1218,8 +1217,7 @@
     grad_a_cols = jnp.concatenate(
         [dot_first(h1, grad_q_lin), dot_first(ckv, grad_kv).reshape(width, e_fold)], axis=1
     ).astype(bf16)
-    first_part, grad_a_cols, w_ring, ring2 = tie(first_part, grad_a_cols, w_ring, ring2)
-    ring3 = onward(out_term(3, ring2).astype(bf16))
+    first_part, grad_a_cols, w_ring = tie(first_part, grad_a_cols, w_ring)
     grad_a_cols = lax.psum_scatter(grad_a_cols, "dp", scatter_dimension=0, tiled=True)
     w_ring = onward(ring_term(w_blocks, w_in, 1, w_ring).astype(bf16))
     grad_e_down = lax.psum_scatter(grad_e_down, "dp", scatter_dimension=1, tiled=True)
@@ -1227,7 +1225,7 @@
     (
         first_sum,
         lat_grads,
-        ring3,
+        ring2,
         w_ring,
         s_keep,
         s_other,
@@ -1238,7 +1236,7 @@
     ) = tie(
         first_sum,
         lat_grads,
-        ring3,
+        ring2,
         w_ring,
         s_keep,
         s_other,
@@ -1250,6 +1248,7 @@
     w_ring = onward(ring_term(w_blocks, w_in, 2, w_ring).astype(bf16))
     lat_blocks = lat_grads.reshape(group, rows_w, -1)
     lat_in = across(jnp.stack([behind(lat_blocks, s, 1) for s in steps]))
+    ring3 = onward(out_term(3, ring2).astype(bf16))
     grad_first = first_sum + dot_last(grad_latent[:, :lat_w], wl)
     unused, first_norm_back = jax.vjp(lambda v: norm_rows(v, a_gain), tokens_f)
     (grad_tokens_norm,) = first_norm_back(grad_first)
@@ -1257,12 +1256,12 @@
     grad_tokens, lat_in, w_ring = tie(grad_tokens, lat_in, w_ring)
     grad_w_out = ring_term(w_blocks, w_in, 3, w_ring)
     lat_ring = onward(ring_term(lat_blocks, lat_in, 0).astype(bf16))
+    grad_s_gate = ff_restore(grad_s_cut[:, :, :ff_pad])
+    grad_s_gate, grad_s_cut, lat_ring = tie(grad_s_gate, grad_s_cut, lat_ring)
+    lat_ring = onward(ring_term(lat_blocks, lat_in, 1, lat_ring).astype(bf16))
+    grad_s_up = ff_restore(grad_s_cut[:, :, ff_pad:])
+    grad_s_up, lat_ring, ring3 = tie(grad_s_up, lat_ring, ring3)
     block_out = (resid + out_term(0, ring3)).astype(bf16)
-    block_out, lat_ring = tie(block_out, lat_ring)
-    lat_ring = onward(ring_term(lat_blocks, lat_in, 1, lat_ring).astype(bf16))
-    grad_s_gate = ff_restore(grad_s_cut[:, :, :ff_pad])
-    grad_s_up = ff_restore(grad_s_cut[:, :, ff_pad:])
-    grad_s_gate, grad_s_up, lat_ring = tie(grad_s_gate, grad_s_up, lat_ring)
     lat_ring = onward(ring_term(lat_blocks, lat_in, 2, lat_ring).astype(bf16))
     lat_grads = ring_term(lat_blocks, lat_in, 3, lat_ring)
     grad_s_down = s_keep.astype(f32) + s_other.astype(f32)

time: 974 us -> 959 us (0.985)
  waiting for transfers between devices: 118 us -> 86.8 us
    ppermute x18, waiting for transfers between devices: 63.9 us -> 35.2 us  [onward(): return lax.ppermute(values, 'expert', ring)]
    reduce_scatter x1, waiting for transfers between devices: 17 us -> 0.02 us  [per_device(): lax.psum_scatter(grad_e_gate, 'dp', scatter_dimension=0, tiled=True)]
    reduce_scatter x1, waiting for transfers between devices: 0.02 us -> 11 us  [per_device(): lax.psum_scatter(grad_a_cols, 'dp', scatter_dimension=0, tiled=True)]
  transfers between devices with their start and end apart: 49 -> 49, of which waited for: 19 -> 13; matrix products, arithmetic and copies ran while one was open for 38% -> 40% of each run, Pallas kernels for 39% -> 40%
where the time goes in v6:
time: 959 us; the launch traced here: 944 us
  Pallas kernels  380 us (40%)
  matrix products  243 us (25%)
  local copies, waits for them, and re-layouts  91.1 us (9%)
  waiting for transfers between devices  86.8 us (9%)
  starting transfers between devices  65.5 us (7%)
  other arithmetic  60.6 us (6%)
  between operations  16.6 us (2%)
    pallas_call x1, Pallas kernels, prologue(): pl.pallas_call(functools.partial(prologue_kernel, chunks), out_shape=[jax...  162 us
    pallas_call x2, Pallas kernels, reduce_rows(): pl.pallas_call(functools.partial(reduce_kernel, parts), out_shape=[jax.Sh...  143 us
    dot_general x31, matrix products, matmul(): return jnp.dot(left, right, preferred_element_type=f32)  81.2 us
    dot_general x17, matrix products, dot_first(): lax.dot_general(left, right, (((0,), (0,)), ((), ())), preferred_element_...  80.8 us
    dot_general x27, matrix products, dot_last(): lax.dot_general(left, right, (((1,), (1,)), ((), ())), preferred_element_...  80 us
    ppermute x18, waiting for transfers between devices, onward(): return lax.ppermute(values, 'expert', ring)  35.2 us
    pallas_call x1, Pallas kernels, attend_back(): pl.pallas_call(functools.partial(attend_back_kernel, heads, segs, scale),...  31.4 us
    ppermute x16, waiting for transfers between devices, across(): return lax.ppermute(values, 'expert', side)  27.8 us
  transfers between devices with their start and end apart: 49, of which 13 were waited for; matrix products, arithmetic and copies ran while one was open for 40% of the time, Pallas kernels for 40%

profile of v6, /device:TPU:0, one launch (start us, length us, event | category | flops | bytes accessed | tf_op | source)
XLA Modules:
  0.0 943.5 jit_solution(10962042314096328978)
XLA Ops:
  20.7 162.3 %prologue.1 = (bf16[8,256,2048]{2,1,0:T(8,128)(2,1)}, bf16[4,8,64,2176]{3,2,1,0:T(8,128)(2,1)}, bf16[4,2,88,2048]{3,2,1,0:T(8,128)(2,1)}, f32[8,8,256]{2,1,0:T(8,128)}) custom-call(bf16[256,2048]{1,0:T(8,128)(2,1)} %x_ref.1, bf16[8,64,2176]{2,1,0:T(8,128)(2,1)} %pad_maximum_fusion.3.w_ref, bf16[88,2048]{1,0:T(8,128)(2,1)} %d_ref.1, f32[8,256]{1,0:T(8,128)} %bitcast.386), custom_call_target="tpu_custom_call" | custom-call | bytes 300000000 | tf_op jit(solution)/shard_map/prologue/pallas_call | solution.py:341
  193.6 20.2 %project.1 = (bf16[2048,2048]{1,0:T(8,128)(2,1)}, bf16[2048,512]{1,0:T(8,128)(2,1)}, bf16[2048,512]{1,0:T(8,128)(2,1)}, bf16[2048,256]{1,0:T(8,128)(2,1)}, f32[2...) custom-call(bf16[2048,2048]{1,0:T(8,128)(2,1)} %bitcast.342, bf16[2048,2176]{1,0:T(8,128)(2,1)} %bitcast.309, ...), custom_call_target="tpu_custom_call" | custom-call | bytes 60000000 | tf_op jit(solution)/shard_map/project/pallas_call | solution.py:560
  213.8 6.5 collective-permute-done
  223.7 23.1 %attend.1 = (bf16[2048,256]{1,0:T(8,128)(2,1)}, f32[2048,256]{1,0:T(8,128)}, f32[2,2048]{1,0:T(2,128)}) custom-call(s32[64]{0:T(128)} %reshape.377.reach_ref, bf16[2048,512]{1,0:T(8,128)(2,1)} %get-tuple-element.140.q_ref, bf16[2048,512]{1,0:T(8,128)(2,1)} %get-tuple-element.141.k_ref, bf16[2048,256]{1,0:T(8,128)(2,1)} %get-tuple-element.142.v_ref), custom_call_target="tpu_custom_call" | custom-call | bytes 70000000 | tf_op jit(solution)/shard_map/attend/pallas_call | solution.py:652
  250.0 5.5 all-to-all-start
  267.6 10.3 %all-to-all-done = bf16[8,256,256]{1,2,0:T(8,128)(2,1)} async-done(((bf16[8,256,256]{1,2,0:T(8,128)(2,1)}), bf16[8,256,256]{1,2,0:T(8,128)(2,1)}, u32[]{:S(2)}, u32[]{:S(2)}) %all-to-all-start) | async-done | bytes 1048608 | tf_op jit(solution)/shard_map/all_to_all | solution.py:1008
  284.1 6.5 multiply_reduce_fusion.2
  303.3 5.8 collective-permute-done.3
  309.1 18.7 %collective-permute-done.2 = bf16[256,2048]{1,0:T(8,128)(2,1)S(1)} collective-permute-done((bf16[256,2048]{1,0:T(8,128)(2,1)S(1)}, bf16[256,2048]{1,0:T(8,128)(2,1)S(1)}, u32[]{:S(2)}, u32[]{:S(2)}) %collective-permute-start.2) | collective-permute-done | bytes 1048608 | tf_op jit(solution)/shard_map/ppermute | solution.py:950
  336.5 4.8 fusion.120
  343.0 5.7 multiply_convert_fusion.8
  350.6 4.6 fusion.110
  355.2 4.7 fusion.126
  366.5 3.8 collective-permute-done.9
  383.2 4.2 multiply_convert_fusion.7
  390.6 5.2 fusion.107
  395.7 4.6 fusion.132
  406.4 6.9 collective-permute-done.14
  424.2 4.6 fusion.104
  428.8 4.6 fusion.138
  444.1 4.2 collective-permute-start.18
  456.8 4.3 collective-permute-done.18
  463.2 11.6 %convolution_convert_fusion.5 = bf16[2048,1536]{1,0:T(8,128)(2,1)} fusion(bf16[256,2048]{1,0:T(8,128)(2,1)S(1)} %copy-done.53, bf16[256,2048]{1,0:T(8,128)(2,1)S(1)} %copy-done.51, bf16[256,2048]{1,0:T(8,128)(2,1)S(1)} %copy-done.49, bf16[256,2048]{1,0:T(8,128)(2,1)S(1)} %multiply_convert_fusion, bf16[256,768]{1,0:T(8,128)(2,1)} %copy-done.77, ...), kind=kOutput, calls=%fused_computation.5 | convolution fusion | flops 6487539712 | bytes 13631488 | tf_op jit(solution)/shard_map/dot_general | solution.py:70
  479.3 6.7 fusion.60
  490.2 8.5 convolution_convert_fusion.1
  498.7 11.6 %convolution_convert_fusion.2 = bf16[2048,1408]{1,0:T(8,128)(2,1)} fusion(bf16[896,2048]{1,0:T(8,128)(2,1)} %copy-done.91, bf16[224,1408]{1,0:T(8,128)(2,1)} %copy-done.117, bf16[224,1408]{1,0:T(8,128)(2,1)} %copy-done.116, bf16[224,1408]{1,0:T(8,128)(2,1)} %copy-done.115, bf16[224,1408]{1,0:T(8,128)(2,1)} %copy-done.114), kind=kOutput, calls=%fused_computation.2 | convolution fusion | flops 5180358656 | bytes 11960320 | tf_op jit(solution)/shard_map/dot_general | solution.py:70
  516.3 11.7 %fusion.57 = bf16[896,2048]{1,0:T(8,128)(2,1)} fusion(bf16[1,1408,2048]{2,1,0:T(8,128)(2,1)} %param.35, bf16[224,1408]{1,0:T(8,128)(2,1)S(1)} %copy-done.63, bf16[224,1408]{1,0:T(8,128)(2,1)S(1)} %copy-done.61, bf16[224,1408]{1,0:T(8,128)(2,1)S(1)} %copy-done.59, bf16[224,1408]{1,0:T(8,128)(2,1)S(1)} %copy-done.57), kind=kOutput, calls=%fused_computation.68 | convolution fusion | flops 5179310080 | bytes 11960320 | tf_op jit(solution)/shard_map/dot_general | solution.py:62
  536.6 4.3 all-to-all-start.1
  542.7 3.9 slice.341
  546.6 6.9 convolution_convert_fusion.4
  553.5 10.3 %convolution_convert_fusion = bf16[1408,2048]{1,0:T(8,128)(2,1)} fusion(bf16[896,1408]{1,0:T(8,128)(2,1)} %pad_maximum_fusion.2, bf16[896,2048]{1,0:T(8,128)(2,1)} %constant_dynamic-update-slice_fusion.8), kind=kOutput, calls=%fused_computation | convolution fusion | flops 5170266112 | bytes 11960320 | tf_op jit(solution)/shard_map/dot_general | solution.py:70
  577.6 31.4 %attend_back.1 = (bf16[2048,512]{1,0:T(8,128)(2,1)}, bf16[2048,512]{1,0:T(8,128)(2,1)}, bf16[2048,640]{1,0:T(8,128)(2,1)}) custom-call(s32[64]{0:T(128)} %reshape.377.reach_ref, bf16[2048,512]{1,0:T(8,128)(2,1)} %get-tuple-element.140.q_ref, bf16[2048,512]{1,0:T(8,128)(2,1)} %get-tuple-element.141.k_ref, bf16[2048,256]{1,0:T(8,128)(2,1)} %get-tuple-element.142.v_ref, ...), custom_call_target="tpu_custom_call" | custom-call | bytes 90000000 | tf_op jit(solution)/shard_map/attend_back/pallas_call | solution.py:786
  619.0 4.6 collective-permute-start.24
  626.9 35.9 %reduce_rows.2 = f32[256,640]{1,0:T(8,128)} custom-call(bf16[8,256,640]{2,1,0:T(8,128)(2,1)} %bitcast.348), custom_call_target="tpu_custom_call" | custom-call | bytes 94371840 | tf_op jit(solution)/shard_map/reduce_rows/pallas_call | solution.py:477
  676.1 10.2 %convolution_convert_fusion.3 = bf16[2048,2048]{1,0:T(8,128)(2,1)} fusion(bf16[2048,512]{1,0:T(8,128)(2,1)} %get-tuple-element.216, bf16[2048,2176]{1,0:T(8,128)(2,1)} %bitcast.311), kind=kOutput, calls=%fused_computation.3 | convolution fusion | flops 4299161600 | bytes 12582912 | tf_op jit(solution)/shard_map/dot_general | solution.py:66
  686.3 6.4 collective-permute-done.25
  692.7 3.6 convolution_convert_fusion.12
  698.8 8.7 convolution_convert_fusion.6
  709.9 5.6 all-to-all-start.2
  719.5 3.5 fusion.86
  732.2 106.8 %reduce_rows.3 = f32[256,2048]{1,0:T(8,128)} custom-call(bf16[8,256,2048]{2,1,0:T(8,128)(2,1)} %bitcast.341), custom_call_target="tpu_custom_call" | custom-call | bytes 301989888 | tf_op jit(solution)/shard_map/reduce_rows/pallas_call | solution.py:477
  839.1 11.0 %reduce-scatter.14.cloned.1.call-done = bf16[512,640]{0,1:T(8,128)(2,1)} async-done(((bf16[2048,640]{0,1:T(8,128)(2,1)}), bf16[512,640]{0,1:T(8,128)(2,1)}) %reduce-scatter.14.cloned.1.call-update) | async-done | bytes 655376 | tf_op jit(solution)/shard_map/reduce_scatter | solution.py:1221
  859.7 4.3 all-to-all-start.3
  863.9 5.1 fusion.85
  873.3 4.1 reshape.405
  884.6 3.8 fusion.157
  907.6 3.9 reshape.408
  919.4 4.9 fusion.88
  (591 shorter events, 276.6 us)
Async XLA Ops:
  7.2 181.6 %all-gather.3.cloned.1.call-start = ((), (), s32[]{:S(2)}) async-start(), calls=%async_computation.11 | async-start | bytes 2703360 | tf_op jit(solution)/shard_map/all_gather | solution.py:907
  10.4 273.7 %all-gather.5.cloned.1.call-start = ((), (), s32[]{:S(2)}) async-start(), calls=%async_computation.12 | async-start | bytes 8650752 | tf_op jit(solution)/shard_map/all_gather | solution.py:914
  183.1 37.3 %collective-permute-start = (bf16[256,2048]{1,0:T(8,128)(2,1)S(1)}, bf16[256,2048]{1,0:T(8,128)(2,1)S(1)}, u32[]{:S(2)}, u32[]{:S(2)}) collective-permute-start(bf16[256,2048]{1,0:T(8,128)(2,1)S(1)} %copy-done.16), channel_id=1, source_target_pairs={{0,2},{1,3},{2,4},{3,5},{4,6},{5,7},{6,0},{7,1},{8,10},{9,11},{10,... | collective-permute-start | bytes 3145736 | tf_op jit(solution)/shard_map/ppermute | solution.py:950
  220.3 26.4 %collective-permute-start.1 = (bf16[256,2048]{1,0:T(8,128)(2,1)S(1)}, bf16[256,2048]{1,0:T(8,128)(2,1)S(1)}, u32[]{:S(2)}, u32[]{:S(2)}) collective-permute-start(bf16[256,2048]{1,0:T(8,128)(2,1)S(1)} %collective-permute-done), channel_id=1, source_target_pairs={{0,2},{1,3},{2,4},{3,5},{4,6},{5,7},{6,0},{7,1},{8,10},{9,11},{10,... | collective-permute-start | bytes 3145736 | tf_op jit(solution)/shard_map/ppermute | solution.py:950
  250.0 27.9 %all-to-all-start = ((bf16[8,256,256]{1,2,0:T(8,128)(2,1)}), bf16[8,256,256]{1,2,0:T(8,128)(2,1)}, u32[]{:S(2)}, u32[]{:S(2)}) async-start(bf16[8,256,256]{1,2,0:T(8,128)(2,1)} %copy.139), calls=%async_computation | async-start | bytes 2097152 | tf_op jit(solution)/shard_map/all_to_all | solution.py:1008
  255.5 308.3 %reduce-scatter.8.cloned.1.call-start = ((), (), s32[]{:S(2)}) async-start(), calls=%async_computation.13 | async-start | bytes 7864320 | tf_op jit(solution)/shard_map/reduce_scatter | solution.py:1131
  279.7 22.0 %collective-permute-start.5 = (bf16[112,2048]{1,0:T(8,128)(2,1)}, bf16[112,2048]{1,0:T(8,128)(2,1)}, u32[]{:S(2)}, u32[]{:S(2)}) collective-permute-start(bf16[112,2048]{1,0:T(8,128)(2,1)} %slice.315), channel_id=1, source_target_pairs={{0,1},{1,0},{2,3},{3,2},{4,5},{5,4},{6,7},{7,6},{8,9},{9,8},{10,11... | collective-permute-start | bytes 1376264 | tf_op jit(solution)/shard_map/ppermute | solution.py:947
  280.9 85.5 %collective-permute-start.10 = (bf16[256,2048]{1,0:T(8,128)(2,1)}, bf16[256,2048]{1,0:T(8,128)(2,1)}, u32[]{:S(2)}, u32[]{:S(2)}) collective-permute-start(bf16[256,2048]{1,0:T(8,128)(2,1)} %copy-done.45), channel_id=1, source_target_pairs={{0,2},{1,3},{2,4},{3,5},{4,6},{5,7},{6,0},{7,1},{8,10},{9,11},{10,... | collective-permute-start | bytes 3145736 | tf_op jit(solution)/shard_map/ppermute | solution.py:950
  283.3 20.0 %collective-permute-start.4 = (bf16[112,2048]{1,0:T(8,128)(2,1)}, bf16[112,2048]{1,0:T(8,128)(2,1)}, u32[]{:S(2)}, u32[]{:S(2)}) collective-permute-start(bf16[112,2048]{1,0:T(8,128)(2,1)} %get-tuple-element.310), channel_id=1, source_target_pairs={{0,1},{1,0},{2,3},{3,2},{4,5},{5,4},{6,7},{7,6},{8,9},{9,8},{10,11... | collective-permute-start | bytes 1376264 | tf_op jit(solution)/shard_map/ppermute | solution.py:947
  294.7 33.1 %collective-permute-start.2 = (bf16[256,2048]{1,0:T(8,128)(2,1)S(1)}, bf16[256,2048]{1,0:T(8,128)(2,1)S(1)}, u32[]{:S(2)}, u32[]{:S(2)}) collective-permute-start(bf16[256,2048]{1,0:T(8,128)(2,1)S(1)} %multiply_convert_fusion), channel_id=1, source_target_pairs={{0,2},{1,3},{2,4},{3,5},{4,6},{5,7},{6,0},{7,1},{8,10},{9,11},{10,... | collective-permute-start | bytes 3145736 | tf_op jit(solution)/shard_map/ppermute | solution.py:950
  295.3 13.8 %collective-permute-start.3 = (bf16[112,2048]{1,0:T(8,128)(2,1)S(1)}, bf16[112,2048]{1,0:T(8,128)(2,1)S(1)}, u32[]{:S(2)}, u32[]{:S(2)}) collective-permute-start(bf16[112,2048]{1,0:T(8,128)(2,1)S(1)} %get-tuple-element.330), channel_id=1, source_target_pairs={{0,1},{1,0},{2,3},{3,2},{4,5},{5,4},{6,7},{7,6},{8,9},{9,8},{10,11... | collective-permute-start | bytes 1376264 | tf_op jit(solution)/shard_map/ppermute | solution.py:947
  328.2 42.1 %collective-permute-start.8 = (bf16[256,2048]{1,0:T(8,128)(2,1)S(1)}, bf16[256,2048]{1,0:T(8,128)(2,1)S(1)}, u32[]{:S(2)}, u32[]{:S(2)}) collective-permute-start(bf16[256,2048]{1,0:T(8,128)(2,1)S(1)} %collective-permute-done.2), channel_id=1, source_target_pairs={{0,2},{1,3},{2,4},{3,5},{4,6},{5,7},{6,0},{7,1},{8,10},{9,11},{10,... | collective-permute-start | bytes 3145736 | tf_op jit(solution)/shard_map/ppermute | solution.py:950
  334.2 25.8 %collective-permute-start.7 = (bf16[112,2048]{1,0:T(8,128)(2,1)S(1)}, bf16[112,2048]{1,0:T(8,128)(2,1)S(1)}, u32[]{:S(2)}, u32[]{:S(2)}) collective-permute-start(bf16[112,2048]{1,0:T(8,128)(2,1)S(1)} %get-tuple-element.305), channel_id=1, source_target_pairs={{0,1},{1,0},{2,3},{3,2},{4,5},{5,4},{6,7},{7,6},{8,9},{9,8},{10,11... | collective-permute-start | bytes 1376264 | tf_op jit(solution)/shard_map/ppermute | solution.py:947
  334.7 25.3 %collective-permute-start.6 = (bf16[112,2048]{1,0:T(8,128)(2,1)S(1)}, bf16[112,2048]{1,0:T(8,128)(2,1)S(1)}, u32[]{:S(2)}, u32[]{:S(2)}) collective-permute-start(bf16[112,2048]{1,0:T(8,128)(2,1)S(1)} %get-tuple-element.327), channel_id=1, source_target_pairs={{0,1},{1,0},{2,3},{3,2},{4,5},{5,4},{6,7},{7,6},{8,9},{9,8},{10,11... | collective-permute-start | bytes 1376264 | tf_op jit(solution)/shard_map/ppermute | solution.py:947
  361.8 8.5 collective-permute-start.9
  371.5 41.7 %collective-permute-start.13 = (bf16[256,2048]{1,0:T(8,128)(2,1)S(1)}, bf16[256,2048]{1,0:T(8,128)(2,1)S(1)}, u32[]{:S(2)}, u32[]{:S(2)}) collective-permute-start(bf16[256,2048]{1,0:T(8,128)(2,1)S(1)} %collective-permute-done.8), channel_id=1, source_target_pairs={{0,2},{1,3},{2,4},{3,5},{4,6},{5,7},{6,0},{7,1},{8,10},{9,11},{10,... | collective-permute-start | bytes 3145736 | tf_op jit(solution)/shard_map/ppermute | solution.py:950
  374.9 25.4 %collective-permute-start.11 = (bf16[112,2048]{1,0:T(8,128)(2,1)S(1)}, bf16[112,2048]{1,0:T(8,128)(2,1)S(1)}, u32[]{:S(2)}, u32[]{:S(2)}) collective-permute-start(bf16[112,2048]{1,0:T(8,128)(2,1)S(1)} %get-tuple-element.324), channel_id=1, source_target_pairs={{0,1},{1,0},{2,3},{3,2},{4,5},{5,4},{6,7},{7,6},{8,9},{9,8},{10,11... | collective-permute-start | bytes 1376264 | tf_op jit(solution)/shard_map/ppermute | solution.py:947
  379.0 21.4 %collective-permute-start.12 = (bf16[112,2048]{1,0:T(8,128)(2,1)S(1)}, bf16[112,2048]{1,0:T(8,128)(2,1)S(1)}, u32[]{:S(2)}, u32[]{:S(2)}) collective-permute-start(bf16[112,2048]{1,0:T(8,128)(2,1)S(1)} %get-tuple-element.302), channel_id=1, source_target_pairs={{0,1},{1,0},{2,3},{3,2},{4,5},{5,4},{6,7},{7,6},{8,9},{9,8},{10,11... | collective-permute-start | bytes 1376264 | tf_op jit(solution)/shard_map/ppermute | solution.py:947
  401.4 11.8 %collective-permute-start.14 = (bf16[112,2048]{1,0:T(8,128)(2,1)S(1)}, bf16[112,2048]{1,0:T(8,128)(2,1)S(1)}, u32[]{:S(2)}, u32[]{:S(2)}) collective-permute-start(bf16[112,2048]{1,0:T(8,128)(2,1)S(1)} %get-tuple-element.321), channel_id=1, source_target_pairs={{0,1},{1,0},{2,3},{3,2},{4,5},{5,4},{6,7},{7,6},{8,9},{9,8},{10,11... | collective-permute-start | bytes 1376264 | tf_op jit(solution)/shard_map/ppermute | solution.py:947
  413.9 19.5 %collective-permute-start.15 = (bf16[112,2048]{1,0:T(8,128)(2,1)S(1)}, bf16[112,2048]{1,0:T(8,128)(2,1)S(1)}, u32[]{:S(2)}, u32[]{:S(2)}) collective-permute-start(bf16[112,2048]{1,0:T(8,128)(2,1)S(1)} %get-tuple-element.319), channel_id=1, source_target_pairs={{0,1},{1,0},{2,3},{3,2},{4,5},{5,4},{6,7},{7,6},{8,9},{9,8},{10,11... | collective-permute-start | bytes 1376264 | tf_op jit(solution)/shard_map/ppermute | solution.py:947
  415.8 27.3 %collective-permute-start.17 = (bf16[256,2048]{1,0:T(8,128)(2,1)S(1)}, bf16[256,2048]{1,0:T(8,128)(2,1)S(1)}, u32[]{:S(2)}, u32[]{:S(2)}) collective-permute-start(bf16[256,2048]{1,0:T(8,128)(2,1)S(1)} %add_convert_fusion.2), channel_id=1, source_target_pairs={{0,2},{1,3},{2,4},{3,5},{4,6},{5,7},{6,0},{7,1},{8,10},{9,11},{10,... | collective-permute-start | bytes 3145736 | tf_op jit(solution)/shard_map/ppermute | solution.py:950
  434.5 8.5 collective-permute-start.16
  444.1 16.9 %collective-permute-start.18 = (bf16[256,2048]{1,0:T(8,128)(2,1)S(1)}, bf16[256,2048]{1,0:T(8,128)(2,1)}, u32[]{:S(2)}, u32[]{:S(2)}) collective-permute-start(bf16[256,2048]{1,0:T(8,128)(2,1)S(1)} %add_convert_fusion.1), channel_id=1, source_target_pairs={{0,2},{1,3},{2,4},{3,5},{4,6},{5,7},{6,0},{7,1},{8,10},{9,11},{10,... | collective-permute-start | bytes 3145736 | tf_op jit(solution)/shard_map/ppermute | solution.py:950
  462.0 12.7 %collective-permute-start.19 = (bf16[112,2048]{1,0:T(8,128)(2,1)}, bf16[112,2048]{1,0:T(8,128)(2,1)}, u32[]{:S(2)}, u32[]{:S(2)}) collective-permute-start(bf16[112,2048]{1,0:T(8,128)(2,1)} %get-tuple-element.314), channel_id=1, source_target_pairs={{0,1},{1,0},{2,3},{3,2},{4,5},{5,4},{6,7},{7,6},{8,9},{9,8},{10,11... | collective-permute-start | bytes 1376264 | tf_op jit(solution)/shard_map/ppermute | solution.py:947
  514.0 16.9 %collective-permute-start.20 = (bf16[256,2048]{1,0:T(8,128)(2,1)S(1)}, bf16[256,2048]{1,0:T(8,128)(2,1)S(1)}, u32[]{:S(2)}, u32[]{:S(2)}) collective-permute-start(bf16[256,2048]{1,0:T(8,128)(2,1)S(1)} %add_convert_fusion), channel_id=1, source_target_pairs={{0,2},{1,3},{2,4},{3,5},{4,6},{5,7},{6,0},{7,1},{8,10},{9,11},{10,... | collective-permute-start | bytes 3145736 | tf_op jit(solution)/shard_map/ppermute | solution.py:950
  536.6 27.2 %all-to-all-start.1 = ((bf16[256,8,256]{2,0,1:T(8,128)(2,1)}), bf16[256,8,256]{2,0,1:T(8,128)(2,1)S(1)}, u32[]{:S(2)}, u32[]{:S(2)}) async-start(bf16[256,8,256]{2,0,1:T(8,128)(2,1)} %bitcast.303), calls=%async_computation.1 | async-start | bytes 2097152 | tf_op jit(solution)/shard_map/all_to_all | solution.py:1145
  540.8 122.1 %reduce-scatter.10.cloned.1.call-start = ((), (), s32[]{:S(2)}) async-start(), calls=%async_computation.14 | async-start | bytes 10485760 | tf_op jit(solution)/shard_map/reduce_scatter | solution.py:1159
  564.8 274.2 %reduce-scatter.16.cloned.1.call-start = ((), (), s32[]{:S(2)}) async-start(), calls=%async_computation.17 | async-start | bytes 7208960 | tf_op jit(solution)/shard_map/reduce_scatter | solution.py:1126
  565.3 273.7 %reduce-scatter.18.cloned.1.call-start = ((), (), s32[]{:S(2)}) async-start(), calls=%async_computation.18 | async-start | bytes 7208960 | tf_op jit(solution)/shard_map/reduce_scatter | solution.py:1127
  565.9 273.2 %reduce-scatter.12.cloned.1.call-start = ((), (), s32[]{:S(2)}) async-start(), calls=%async_computation.15 | async-start | bytes 3276800 | tf_op jit(solution)/shard_map/reduce_scatter | solution.py:1215
  568.9 40.1 %collective-permute-start.21 = (bf16[4,112,2048]{2,1,0:T(8,128)(2,1)}, bf16[4,112,2048]{2,1,0:T(8,128)(2,1)}, u32[]{:S(2)}, u32[]{:S(2)}) collective-permute-start(bf16[4,112,2048]{2,1,0:T(8,128)(2,1)} %slice.342), channel_id=1, source_target_pairs={{0,1},{1,0},{2,3},{3,2},{4,5},{5,4},{6,7},{7,6},{8,9},{9,8},{10,11... | collective-permute-start | bytes 5505032 | tf_op jit(solution)/shard_map/ppermute | solution.py:947
  573.5 35.5 %collective-permute-start.22 = (bf16[2,2,88,2048]{3,2,1,0:T(8,128)(2,1)}, bf16[2,2,88,2048]{3,2,1,0:T(8,128)(2,1)S(1)}, u32[]{:S(2)}, u32[]{:S(2)}) collective-permute-start(bf16[2,2,88,2048]{3,2,1,0:T(8,128)(2,1)} %dynamic-slice_bitcast_fusion), channel_id=1, source_target_pairs={{0,8},{8,0},{16,24},{24,16},{1,9},{9,1},{17,25},{25,17},{2,10},{10... | collective-permute-start | bytes 4325384 | tf_op jit(solution)/shard_map/ppermute | solution.py:967
  615.5 47.4 %collective-permute-start.23 = (bf16[256,2048]{1,0:T(8,128)(2,1)}, bf16[256,2048]{1,0:T(8,128)(2,1)}, u32[]{:S(2)}, u32[]{:S(2)}) collective-permute-start(bf16[256,2048]{1,0:T(8,128)(2,1)} %fusion.87), channel_id=1, source_target_pairs={{0,2},{1,3},{2,4},{3,5},{4,6},{5,7},{6,0},{7,1},{8,10},{9,11},{10,... | collective-permute-start | bytes 3145736 | tf_op jit(solution)/shard_map/ppermute | solution.py:950
  619.0 43.9 %collective-permute-start.24 = (bf16[2,88,2048]{2,1,0:T(8,128)(2,1)}, bf16[2,88,2048]{2,1,0:T(8,128)(2,1)S(1)}, u32[]{:S(2)}, u32[]{:S(2)}) collective-permute-start(bf16[2,88,2048]{2,1,0:T(8,128)(2,1)} %dynamic-slice_bitcast_fusion.1), channel_id=1, source_target_pairs={{0,16},{8,24},{16,0},{24,8},{1,17},{9,25},{17,1},{25,9},{2,18},{10... | collective-permute-start | bytes 2162696 | tf_op jit(solution)/shard_map/ppermute | solution.py:967
  667.1 25.5 %collective-permute-start.25 = (bf16[4,64,2048]{2,1,0:T(8,128)(2,1)}, bf16[4,64,2048]{2,1,0:T(8,128)(2,1)}, u32[]{:S(2)}, u32[]{:S(2)}) collective-permute-start(bf16[4,64,2048]{2,1,0:T(8,128)(2,1)} %pad_maximum_fusion.5), channel_id=1, source_target_pairs={{0,1},{1,0},{2,3},{3,2},{4,5},{5,4},{6,7},{7,6},{8,9},{9,8},{10,11... | collective-permute-start | bytes 3145736 | tf_op jit(solution)/shard_map/ppermute | solution.py:947
  692.7 157.4 %reduce-scatter.14.cloned.1.call-start = ((), (), s32[]{:S(2)}) async-start(), calls=%async_computation.16 | async-start | bytes 3276800 | tf_op jit(solution)/shard_map/reduce_scatter | solution.py:1221
  698.0 11.2 %collective-permute-start.26 = (bf16[64,2048]{1,0:T(8,128)(2,1)S(1)}, bf16[64,2048]{1,0:T(8,128)(2,1)S(1)}, u32[]{:S(2)}, u32[]{:S(2)}) collective-permute-start(bf16[64,2048]{1,0:T(8,128)(2,1)S(1)} %fusion.316), channel_id=1, source_target_pairs={{0,2},{1,3},{2,4},{3,5},{4,6},{5,7},{6,0},{7,1},{8,10},{9,11},{10,... | collective-permute-start | bytes 786440 | tf_op jit(solution)/shard_map/ppermute | solution.py:950
  709.9 129.2 %all-to-all-start.2 = ((bf16[8,64,1536]{2,1,0:T(8,128)(2,1)}), bf16[8,64,1536]{2,1,0:T(8,128)(2,1)}, u32[]{:S(2)}, u32[]{:S(2)}) async-start(bf16[8,64,1536]{2,1,0:T(8,128)(2,1)} %bitcast.362), calls=%async_computation.6 | async-start | bytes 3145728 | tf_op jit(solution)/shard_map/all_to_all | solution.py:1156
  715.5 217.7 %reduce-scatter.20.cloned.1.call-start = ((), (), s32[]{:S(2)}) async-start(), calls=%async_computation.19 | async-start | bytes 7208960 | tf_op jit(solution)/shard_map/reduce_scatter | solution.py:1223
  723.0 116.1 %collective-permute-start.27 = (bf16[256,2048]{1,0:T(8,128)(2,1)}, bf16[256,2048]{1,0:T(8,128)(2,1)}, u32[]{:S(2)}, u32[]{:S(2)}) collective-permute-start(bf16[256,2048]{1,0:T(8,128)(2,1)} %fusion.86), channel_id=1, source_target_pairs={{0,2},{1,3},{2,4},{3,5},{4,6},{5,7},{6,0},{7,1},{8,10},{9,11},{10,... | collective-permute-start | bytes 3145736 | tf_op jit(solution)/shard_map/ppermute | solution.py:950
  725.3 113.7 %collective-permute-start.29 = (bf16[88,2048]{1,0:T(8,128)(2,1)S(1)}, bf16[88,2048]{1,0:T(8,128)(2,1)S(1)}, u32[]{:S(2)}, u32[]{:S(2)}) collective-permute-start(bf16[88,2048]{1,0:T(8,128)(2,1)S(1)} %get-tuple-element.331), channel_id=1, source_target_pairs={{0,1},{1,0},{2,3},{3,2},{4,5},{5,4},{6,7},{7,6},{8,9},{9,8},{10,11... | collective-permute-start | bytes 1081352 | tf_op jit(solution)/shard_map/ppermute | solution.py:947
  728.9 110.2 %collective-permute-start.28 = (bf16[64,2048]{1,0:T(8,128)(2,1)}, bf16[64,2048]{1,0:T(8,128)(2,1)S(1)}, u32[]{:S(2)}, u32[]{:S(2)}) collective-permute-start(bf16[64,2048]{1,0:T(8,128)(2,1)} %fusion.308), channel_id=1, source_target_pairs={{0,2},{1,3},{2,4},{3,5},{4,6},{5,7},{6,0},{7,1},{8,10},{9,11},{10,... | collective-permute-start | bytes 786440 | tf_op jit(solution)/shard_map/ppermute | solution.py:950
  853.5 42.9 %collective-permute-start.31 = (bf16[64,2048]{1,0:T(8,128)(2,1)}, bf16[64,2048]{1,0:T(8,128)(2,1)}, u32[]{:S(2)}, u32[]{:S(2)}) collective-permute-start(bf16[64,2048]{1,0:T(8,128)(2,1)} %fusion.307), channel_id=1, source_target_pairs={{0,2},{1,3},{2,4},{3,5},{4,6},{5,7},{6,0},{7,1},{8,10},{9,11},{10,... | collective-permute-start | bytes 786440 | tf_op jit(solution)/shard_map/ppermute | solution.py:950
  855.9 40.6 %collective-permute-start.30 = (bf16[4,64,640]{2,1,0:T(8,128)(2,1)}, bf16[4,64,640]{2,1,0:T(8,128)(2,1)}, u32[]{:S(2)}, u32[]{:S(2)}) collective-permute-start(bf16[4,64,640]{2,1,0:T(8,128)(2,1)} %pad_maximum_fusion.18), channel_id=1, source_target_pairs={{0,1},{1,0},{2,3},{3,2},{4,5},{5,4},{6,7},{7,6},{8,9},{9,8},{10,11... | collective-permute-start | bytes 983048 | tf_op jit(solution)/shard_map/ppermute | solution.py:947
  859.7 67.8 %all-to-all-start.3 = ((bf16[8,64,640]{2,1,0:T(8,128)(2,1)}), bf16[8,64,640]{2,1,0:T(8,128)(2,1)}, u32[]{:S(2)}, u32[]{:S(2)}) async-start(bf16[8,64,640]{2,1,0:T(8,128)(2,1)} %bitcast.68), calls=%async_computation.9 | async-start | bytes 1310720 | tf_op jit(solution)/shard_map/all_to_all | solution.py:1271
  869.0 47.4 %collective-permute-start.34 = (bf16[256,2048]{1,0:T(8,128)(2,1)}, bf16[256,2048]{1,0:T(8,128)(2,1)}, u32[]{:S(2)}, u32[]{:S(2)}) collective-permute-start(bf16[256,2048]{1,0:T(8,128)(2,1)} %fusion.85), channel_id=1, source_target_pairs={{0,2},{1,3},{2,4},{3,5},{4,6},{5,7},{6,0},{7,1},{8,10},{9,11},{10,... | collective-permute-start | bytes 3145736 | tf_op jit(solution)/shard_map/ppermute | solution.py:950
  904.8 11.7 %collective-permute-start.33 = (bf16[64,640]{1,0:T(8,128)(2,1)S(1)}, bf16[64,640]{1,0:T(8,128)(2,1)S(1)}, u32[]{:S(2)}, u32[]{:S(2)}) collective-permute-start(bf16[64,640]{1,0:T(8,128)(2,1)S(1)} %fusion.319), channel_id=1, source_target_pairs={{0,2},{1,3},{2,4},{3,5},{4,6},{5,7},{6,0},{7,1},{8,10},{9,11},{10,... | collective-permute-start | bytes 245768 | tf_op jit(solution)/shard_map/ppermute | solution.py:950
  917.4 6.9 collective-permute-start.35
  (144 other events, 2354.2 us)
Sparse Core Ops, SparseCore 0:
  11.5 100.6 all-gather.2
  115.2 96.3 all-gather.4
  474.9 61.9 reduce-scatter.7
  564.0 95.5 reduce-scatter.9
  661.9 54.8 reduce-scatter.15
  719.4 54.8 reduce-scatter.17
  777.4 34.6 reduce-scatter.11
  815.4 34.6 reduce-scatter.13
  852.6 54.8 reduce-scatter.19
